TPU v7x, 32 devices: a whole 2x2x4 slice. The times are simulated.
32 devices in a mesh: dp: 4 (over y, x), expert: 8 (over z, core).
Axes of the slice: x: 2, y: 2, z: 4, core: 2. Of those that a mesh axis runs over, the one named last changes fastest.
Arguments:
- tokens: bfloat16 [4096, 1536], P(('dp', 'expert')), may hold values from -6 to 6
- grad_out: bfloat16 [4096, 1536], P(('dp', 'expert')), may hold values from -6 to 6
- expert_ids: int32 [4096, 4], P(('dp', 'expert')), may hold values from 0 to 7, all different within a row; in each aligned block of 128 rows (0 to 127, 128 to 255, ...) at most 96 rows name the same one
- gate_q: int32 [4096, 4], P(('dp', 'expert')), may hold values from 1 to 65535
- w_up: bfloat16 [8, 1536, 768], P('expert', 'dp'), may hold values from -0.15625 to 0.15625
- w_down: bfloat16 [8, 768, 1536], P('expert', None, 'dp'), may hold values from -0.21875 to 0.21875
Outputs:
- dw_up: bfloat16 [8, 1536, 768], P('expert', 'dp')
- dw_down: bfloat16 [8, 768, 1536], P('expert', None, 'dp')
Inputs may be any that keep to these rules, and one draw needn't show every extreme that they name: `expert_ids`: within the rows of one device no expert is named by more than 96 rows, a bound that some block reaches; the 4 ids of a row differ.
All inputs are finite; a program needn't handle non-finite values.
Results may differ from a plain program's by a relative error of at most 0.0064.
Values may be sent and summed in bfloat16 or wider, within the bound.
No kernel may reach another device: no remote copies, remote signals or barrier semaphores. Data moves between devices by JAX's collectives and lax.ppermute only.
A program may use at most 64 MiB of HBM per device.

v0:
```python
import jax
import jax.numpy as jnp
from jax import lax
from jax.sharding import PartitionSpec as P


F32 = jnp.float32
BF16 = jnp.bfloat16
FIRST = (((0,), (0,)), ((), ()))
LAST = (((1,), (1,)), ((), ()))


def silu_slope(values):
    sigmoid_part = jax.nn.sigmoid(values)
    return sigmoid_part * (1.0 + values * (1.0 - sigmoid_part))


def summed_up(recv_rows, projected_grad):
    partial_value = lax.dot_general(recv_rows, projected_grad, FIRST, preferred_element_type=F32).astype(BF16)
    pieces = lax.all_to_all(partial_value[None], "dp", split_axis=1, concat_axis=0, tiled=True)
    return jnp.sum(pieces.astype(F32), axis=0, keepdims=True).astype(BF16)


def summed_down(activated, grad_rows):
    partial_value = lax.dot_general(activated, grad_rows, FIRST, preferred_element_type=F32).astype(BF16)
    pieces = lax.all_to_all(partial_value[None], "dp", split_axis=2, concat_axis=0, tiled=True)
    return jnp.sum(pieces.astype(F32), axis=0, keepdims=True).astype(BF16)


def sparse_shards(tokens, grad_out, expert_ids, gate_q, w_up, w_down, capacity):
    devices = lax.axis_size("expert")
    top_count = expert_ids.shape[1]
    model_width = tokens.shape[1]
    slot_expert = expert_ids.reshape(-1)
    onehot_table = (slot_expert[:, None] == jnp.arange(devices, dtype=jnp.int32)[None, :]).astype(jnp.int32)
    earlier = jnp.cumsum(onehot_table, axis=0) - onehot_table
    slot_rank = jnp.sum(earlier * onehot_table, axis=1)
    slot_target = slot_expert * capacity + slot_rank
    gate_values = gate_q.reshape(-1).astype(F32) * (1.0 / 65536.0)
    token_rows = jnp.repeat(tokens, top_count, axis=0)
    slot_grads = (gate_values[:, None] * jnp.repeat(grad_out, top_count, axis=0).astype(F32)).astype(BF16)
    empty_rows = jnp.zeros((devices * capacity, model_width), BF16)
    send_tokens = empty_rows.at[slot_target].set(token_rows).reshape(devices, capacity, model_width)
    grad_slots = empty_rows.at[slot_target].set(slot_grads).reshape(devices, capacity, model_width)
    up_whole = lax.all_gather(w_up, "dp", axis=1, tiled=True)[0]
    down_whole = lax.all_gather(w_down, "dp", axis=2, tiled=True)[0]
    recv_tokens = lax.all_to_all(send_tokens, "expert", split_axis=0, concat_axis=0, tiled=True)
    recv_rows = recv_tokens.reshape(-1, model_width)
    projected = jnp.dot(recv_rows, up_whole, preferred_element_type=F32)
    recv_grads = lax.all_to_all(grad_slots, "expert", split_axis=0, concat_axis=0, tiled=True)
    activated = jax.nn.silu(projected).astype(BF16)
    grad_rows = recv_grads.reshape(-1, model_width)
    act_grad = lax.dot_general(grad_rows, down_whole, LAST, preferred_element_type=F32)
    projected_grad = (act_grad * silu_slope(projected)).astype(BF16)
    return summed_up(recv_rows, projected_grad), summed_down(activated, grad_rows)


def xor_perm(count, bits):
    return [(i, i ^ bits) for i in range(count)]


def dense_shards(tokens, grad_out, expert_ids, gate_q, w_up, w_down):
    return dense_body(tokens, grad_out, expert_ids, gate_q, w_up[0], w_down[0])


def dense_body(tokens, grad_out, expert_ids, gate_q, w_up, w_down):
    devices = lax.axis_size("expert")
    block, hidden = w_up.shape
    dp_index = lax.axis_index("dp")
    ex_index = lax.axis_index("expert")
    upper = ex_index >= devices // 2

    def ex(value, perm):
        return lax.ppermute(value, "expert", perm)

    def dp(value, bits):
        return lax.ppermute(value, "dp", xor_perm(4, bits))

    swap = xor_perm(devices, 1)

    def ring(hops):
        return [(i, (i + 2 * hops) % devices) for i in range(devices)]

    up_mid = [(i, i + 2) for i in range(2, devices - 2)]
    down_mid = [(i, i - 2) for i in range(2, devices - 2)]

    t1 = ex(tokens, ring(1))
    t3 = ex(tokens, ring(-1))
    up_x = dp(w_up, 1)
    down_y = dp(w_down, 2)
    g1 = ex(grad_out, ring(1))
    g3 = ex(grad_out, ring(-1))
    up_y = dp(w_up, 2)
    down_x = dp(w_down, 1)

    experts = jnp.arange(devices, dtype=jnp.int32)
    named = expert_ids[:, :, None] == experts[None, None, :]
    gate_table = jnp.sum(jnp.where(named, gate_q[:, :, None], 0), axis=1).astype(F32) * (1.0 / 65536.0)
    c0 = jnp.concatenate([gate_table, ex(gate_table, swap)], axis=0)
    c1 = ex(c0, ring(1))
    c2 = ex(c0, ring(2))
    c3 = ex(c0, ring(3))
    t0b = ex(tokens, swap)
    g0b = ex(grad_out, swap)

    up_d = dp(up_x, 2)
    down_d = dp(down_y, 1)
    t2u = ex(t1, up_mid)
    t2d = ex(t3, down_mid)
    t1b = ex(t1, swap)
    t3b = ex(t3, swap)
    g2u = ex(g1, up_mid)
    g2d = ex(g3, down_mid)
    g1b = ex(g1, swap)
    g3b = ex(g3, swap)

    up_all = jnp.zeros((4 * block, hidden), BF16)
    down_all = jnp.zeros((hidden, 4 * block), BF16)
    for bits, up_part, down_part in ((0, w_up, w_down), (1, up_x, down_x), (2, up_y, down_y), (3, up_d, down_d)):
        where = (dp_index ^ bits) * block
        up_all = lax.dynamic_update_slice(up_all, up_part, (where, 0))
        down_all = lax.dynamic_update_slice(down_all, down_part, (0, where))

    pick = (experts == ex_index).astype(F32)

    def gate_of(*tables):
        table = jnp.concatenate(tables, axis=0)
        return jnp.sum(table * pick, axis=1)

    def scaled(gate, g):
        return (gate[:, None] * g.astype(F32)).astype(BF16)

    def backward(pre, g):
        act_grad = lax.dot_general(g, down_all, LAST, preferred_element_type=F32)
        return (act_grad * silu_slope(pre)).astype(BF16)

    def outer(left, right):
        return lax.dot_general(left, right, FIRST, preferred_element_type=F32)

    x_a = jnp.concatenate([tokens, t0b], axis=0)
    x_b = jnp.concatenate([t1, t1b, t3, t3b], axis=0)
    pre_a = jnp.dot(x_a, up_all, preferred_element_type=F32)
    pre_b = jnp.dot(x_b, up_all, preferred_element_type=F32)
    act_a = jax.nn.silu(pre_a).astype(BF16)
    act_b = jax.nn.silu(pre_b).astype(BF16)
    gate_a = gate_of(c0)
    gate_b = gate_of(c1, c3)
    gate_c = gate_of(c2)
    g_a = scaled(gate_a, jnp.concatenate([grad_out, g0b], axis=0))
    g_b = scaled(gate_b, jnp.concatenate([g1, g1b, g3, g3b], axis=0))
    back_a = backward(pre_a, g_a)
    back_b = backward(pre_b, g_b)
    up_acc = outer(x_a, back_a) + outer(x_b, back_b)
    down_acc = outer(act_a, g_a) + outer(act_b, g_b)
    t2 = jnp.where(upper, t2u, t2d)
    t2b = ex(t2, swap)
    x_c = jnp.concatenate([t2, t2b], axis=0)
    pre_c = jnp.dot(x_c, up_all, preferred_element_type=F32)
    act_c = jax.nn.silu(pre_c).astype(BF16)
    up_acc, down_acc, act_c, pre_c, g2u, g2d = lax.optimization_barrier((up_acc, down_acc, act_c, pre_c, g2u, g2d))
    g2 = jnp.where(upper, g2u, g2d)
    g2b = ex(g2, swap)
    g_c = scaled(gate_c, jnp.concatenate([g2, g2b], axis=0))
    back_c = backward(pre_c, g_c)

    def up_block(bits):
        where = (dp_index ^ bits) * block
        cols = lax.dynamic_slice(x_c, (0, where), (x_c.shape[0], block))
        return outer(cols, back_c) + lax.dynamic_slice(up_acc, (where, 0), (block, hidden))

    def down_block(bits):
        where = (dp_index ^ bits) * block
        cols = lax.dynamic_slice(g_c, (0, where), (g_c.shape[0], block))
        return outer(act_c, cols) + lax.dynamic_slice(down_acc, (0, where), (hidden, block))

    up_far = dp(up_block(3).astype(BF16), 2)
    down_far = dp(down_block(3).astype(BF16), 1)
    up_near = dp(up_block(2).astype(BF16), 2)
    down_near = dp(down_block(1).astype(BF16), 1)
    up_side, down_side = up_block(1), down_block(2)
    up_own, down_own = up_block(0), down_block(0)
    up_side, down_side, up_own, down_own = lax.optimization_barrier((up_side, down_side, up_own, down_own))
    up_fwd = dp((up_side + up_far.astype(F32)).astype(BF16), 1)
    down_fwd = dp((down_side + down_far.astype(F32)).astype(BF16), 2)
    dw_up = (up_own + up_near.astype(F32) + up_fwd.astype(F32)).astype(BF16)
    dw_down = (down_own + down_near.astype(F32) + down_fwd.astype(F32)).astype(BF16)
    return dw_up[None], dw_down[None]


def shards(tokens, grad_out, expert_ids, gate_q, w_up, w_down):
    devices = lax.axis_size("expert")
    token_count, top_count = expert_ids.shape
    capacity = max(2, token_count * top_count * 3 // (2 * devices))
    if 2 * capacity >= token_count and devices == 8 and lax.axis_size("dp") == 4:
        return dense_shards(tokens, grad_out, expert_ids, gate_q, w_up, w_down)
    return sparse_shards(tokens, grad_out, expert_ids, gate_q, w_up, w_down, capacity)


def solution(mesh):
    in_specs = (
        P(("dp", "expert"), None),
        P(("dp", "expert"), None),
        P(("dp", "expert"), None),
        P(("dp", "expert"), None),
        P("expert", "dp", None),
        P("expert", None, "dp"),
    )
    out_specs = (P("expert", "dp", None), P("expert", None, "dp"))
    return jax.shard_map(shards, mesh=mesh, in_specs=in_specs, out_specs=out_specs, check_vma=False)
```

profile of v0, /device:TPU:0, one launch (start us, length us, event | category | flops | bytes accessed | tf_op | source)
XLA Modules:
  0.0 179.6 jit_solution(9918349032667248687)
XLA Ops:
  0.6 5.1 %collective-permute-start.2 = (bf16[128,1536]{1,0:T(8,128)(2,1)}, bf16[128,1536]{1,0:T(8,128)(2,1)}, u32[]{:S(2)}, u32[]{:S(2)}) collective-permute-start(bf16[128,1536]{1,0:T(8,128)(2,1)} %param.6), channel_id=1, source_target_pairs={{0,6},{1,7},{2,0},{3,1},{4,2},{5,3},{6,4},{7,5},{8,14},{9,15},{10,... | collective-permute-start | bytes 1179656 | tf_op jit(solution)/shard_map/ppermute | solution.py:74
  7.1 1.5 broadcast_in_dim.36
  11.9 3.8 %collective-permute-start.18 = (f32[256,8]{0,1:T(8,128)}, f32[256,8]{0,1:T(8,128)}, u32[]{:S(2)}, u32[]{:S(2)}) collective-permute-start(f32[256,8]{0,1:T(8,128)} %pad_maximum_fusion.2), channel_id=1, source_target_pairs={{0,6},{1,7},{2,0},{3,1},{4,2},{5,3},{6,4},{7,5},{8,14},{9,15},{10,... | collective-permute-start | bytes 24584 | tf_op jit(solution)/shard_map/ppermute | solution.py:74
  16.2 7.8 %collective-permute-done.17 = f32[256,8]{0,1:T(8,128)S(1)} collective-permute-done((f32[256,8]{0,1:T(8,128)}, f32[256,8]{0,1:T(8,128)S(1)}, u32[]{:S(2)}, u32[]{:S(2)}) %collective-permute-start.17) | collective-permute-done | bytes 8224 | tf_op jit(solution)/shard_map/ppermute | solution.py:74
  27.5 2.8 %collective-permute-done.6 = f32[256,8]{0,1:T(8,128)S(1)} collective-permute-done((f32[256,8]{0,1:T(8,128)}, f32[256,8]{0,1:T(8,128)S(1)}, u32[]{:S(2)}, u32[]{:S(2)}) %collective-permute-start.6) | collective-permute-done | bytes 8224 | tf_op jit(solution)/shard_map/ppermute | solution.py:74
  30.3 1.5 collective-permute-start.13
  33.0 1.8 constant_dynamic-update-slice_fusion.5
  35.3 1.8 constant_dynamic-update-slice_fusion
  37.1 3.1 %collective-permute-done.12 = bf16[384,768]{1,0:T(8,128)(2,1)S(1)} collective-permute-done((bf16[384,768]{1,0:T(8,128)(2,1)S(1)}, bf16[384,768]{1,0:T(8,128)(2,1)S(1)}, u32[]{:S(2)}, u32[]{:S(2)}) %collective-permute-start.12) | collective-permute-done | bytes 589856 | tf_op jit(solution)/shard_map/ppermute | solution.py:77
  41.1 9.8 %collective-permute-done.9 = bf16[768,384]{1,0:T(8,128)(2,1)S(1)} collective-permute-done((bf16[768,384]{1,0:T(8,128)(2,1)S(1)}, bf16[768,384]{1,0:T(8,128)(2,1)S(1)}, u32[]{:S(2)}, u32[]{:S(2)}) %collective-permute-start.9) | collective-permute-done | bytes 589856 | tf_op jit(solution)/shard_map/ppermute | solution.py:77
  53.5 2.1 %collective-permute-done.10 = bf16[768,384]{1,0:T(8,128)(2,1)S(1)} collective-permute-done((bf16[768,384]{1,0:T(8,128)(2,1)S(1)}, bf16[768,384]{1,0:T(8,128)(2,1)S(1)}, u32[]{:S(2)}, u32[]{:S(2)}) %collective-permute-start.10) | collective-permute-done | bytes 589856 | tf_op jit(solution)/shard_map/ppermute | solution.py:77
  58.6 1.8 %constant_dynamic-update-slice_fusion.3 = bf16[512,1536]{1,0:T(8,128)(2,1)} fusion(bf16[512,1536]{1,0:T(8,128)(2,1)} %constant_dynamic-update-slice_fusion.4, bf16[128,1536]{1,0:T(8,128)(2,1)} %collective-permute-done.2), kind=kLoop, calls=%fused_computation.71 | loop fusion | bytes 786432
  60.4 1.5 collective-permute-start.14
  63.1 5.1 %collective-permute-start.19 = (bf16[128,1536]{1,0:T(8,128)(2,1)S(1)}, bf16[128,1536]{1,0:T(8,128)(2,1)}, u32[]{:S(2)}, u32[]{:S(2)}) collective-permute-start(bf16[128,1536]{1,0:T(8,128)(2,1)S(1)} %copy-done.3), channel_id=1, source_target_pairs={{0,2},{1,3},{2,4},{3,5},{4,6},{5,7},{6,0},{7,1},{8,10},{9,11},{10,... | collective-permute-start | bytes 1179656 | tf_op jit(solution)/shard_map/ppermute | solution.py:74
  68.2 11.2 %collective-permute-done.3 = bf16[128,1536]{1,0:T(8,128)(2,1)S(1)} collective-permute-done((bf16[128,1536]{1,0:T(8,128)(2,1)}, bf16[128,1536]{1,0:T(8,128)(2,1)S(1)}, u32[]{:S(2)}, u32[]{:S(2)}) %collective-permute-start.3) | collective-permute-done | bytes 393248 | tf_op jit(solution)/shard_map/ppermute | solution.py:74
  80.7 1.6 collective-permute-start.11
  84.7 11.0 %collective-permute-done.11 = bf16[768,384]{1,0:T(8,128)(2,1)S(1)} collective-permute-done((bf16[768,384]{1,0:T(8,128)(2,1)S(1)}, bf16[768,384]{1,0:T(8,128)(2,1)S(1)}, u32[]{:S(2)}, u32[]{:S(2)}) %collective-permute-start.11) | collective-permute-done | bytes 589856 | tf_op jit(solution)/shard_map/ppermute | solution.py:77
  95.8 2.4 %fusion.61 = f32[256,768]{1,0:T(8,128)S(1)} fusion(bf16[256,1536]{1,0:T(8,128)(2,1)S(1)} %copy-done.7, bf16[1536,768]{1,0:T(8,128)(2,1)} %constant_dynamic-update-slice_fusion.6), kind=kOutput, calls=%fused_computation.106 | convolution fusion | flops 603979776 | bytes 3932160 | tf_op jit(solution)/shard_map/dot_general | solution.py:142
  99.2 3.1 %fusion.13 = f32[768,1536]{1,0:T(8,128)} fusion(f32[256,768]{1,0:T(8,128)S(1)} %fusion.61, bf16[128,1536]{1,0:T(8,128)(2,1)S(1)} %collective-permute-done.8, bf16[128,1536]{1,0:T(8,128)(2,1)S(1)} %copy-done.3, f32[256]{0:T(256)S(1)} %get-tuple-element.23), kind=kOutput, calls=%fused_computation.47 | convolution fusion | flops 607322112 | bytes 6292480 | tf_op jit(solution)/shard_map/dot_general | solution.py:138
  102.3 5.3 %fusion.4 = f32[1536,768]{1,0:T(8,128)} fusion(bf16[256,1536]{1,0:T(8,128)(2,1)} %constant_dynamic-update-slice_fusion, bf16[768,1536]{1,0:T(8,128)(2,1)S(1)} %constant_dynamic-update-slice_fusion.10, f32[256,768]{1,0:T(8,128)} %copy-done, bf16[128,1536]{1,0:T(8,128)(2,1)} %copy-done.5, bf16[128,1536]{1,0:T(8,128)(2,1)S(1)} %copy-done.4, ...), kind=kOutput, calls=%fused_computation.18 | convolution fusion | flops 1212088320 | bytes 9438208 | tf_op jit(solution)/shard_map/dot_general | solution.py:138
  107.6 4.7 %fusion.62 = f32[512,768]{1,0:T(8,128)} fusion(bf16[512,1536]{1,0:T(8,128)(2,1)} %constant_dynamic-update-slice_fusion.2, bf16[1536,768]{1,0:T(8,128)(2,1)} %constant_dynamic-update-slice_fusion.6), kind=kOutput, calls=%fused_computation.107 | convolution fusion | flops 1207959552 | bytes 5505024 | tf_op jit(solution)/shard_map/dot_general | solution.py:143
  112.3 8.8 %convolution_add_fusion.1 = f32[1536,768]{1,0:T(8,128)} fusion(f32[1536,768]{1,0:T(8,128)} %fusion.4, bf16[512,1536]{1,0:T(8,128)(2,1)} %constant_dynamic-update-slice_fusion.2, f32[512,768]{1,0:T(8,128)} %fusion.62, bf16[768,1536]{1,0:T(8,128)(2,1)S(1)} %constant_dynamic-update-slice_fusion.10, bf16[128,1536]{1,0:T(8,128)(2,1)} %collective-permute-done.22, ...), kind=kOutput, calls=%fused_computation.1 | convolution fusion | flops 2428502016 | bytes 16517120 | tf_op jit(solution)/shard_map/dot_general | solution.py:138
  121.1 4.9 %convolution_add_fusion = f32[768,1536]{1,0:T(8,128)S(1)} fusion(f32[768,1536]{1,0:T(8,128)} %fusion.13, f32[512,768]{1,0:T(8,128)} %fusion.62, bf16[128,1536]{1,0:T(8,128)(2,1)} %collective-permute-done.22, bf16[128,1536]{1,0:T(8,128)(2,1)} %collective-permute-done.21, bf16[128,1536]{1,0:T(8,128)(2,1)} %collective-permute-done.20, ...), kind=kOutput, calls=%fused_computation | convolution fusion | flops 1218969600 | bytes 12584960 | tf_op jit(solution)/shard_map/dot_general | solution.py:138
  126.0 2.5 %multiply_convert_fusion.6 = (bf16[256,768]{1,0:T(8,128)(2,1)S(1)}, f32[256,768]{1,0:T(8,128)S(1)}) fusion(bf16[1536,768]{1,0:T(8,128)(2,1)} %constant_dynamic-update-slice_fusion.6, bf16[128,1536]{1,0:T(8,128)(2,1)S(1)} %collective-permute-done.4, bf16[128,1536]{1,0:T(8,128)(2,1)S(1)} %broadcast_select_fusion.1), kind=kOutput, calls=%fused_computation.37 | convolution fusion | flops 606535680 | bytes 4325376 | tf_op jit(solution)/shard_map/dot_general | solution.py:158
  135.3 1.6 collective-permute-start.27
  137.9 1.5 collective-permute-start.30
  140.1 11.5 %collective-permute-done.27 = bf16[384,768]{1,0:T(8,128)(2,1)S(1)} collective-permute-done((bf16[384,768]{1,0:T(8,128)(2,1)S(1)}, bf16[384,768]{1,0:T(8,128)(2,1)S(1)}, u32[]{:S(2)}, u32[]{:S(2)}) %collective-permute-start.27) | collective-permute-done | bytes 589856 | tf_op jit(solution)/shard_map/ppermute | solution.py:77
  151.7 1.6 collective-permute-start.28
  154.4 1.6 collective-permute-start.31
  156.0 8.2 %collective-permute-done.26 = bf16[384,768]{1,0:T(8,128)(2,1)S(1)} collective-permute-done((bf16[384,768]{1,0:T(8,128)(2,1)S(1)}, bf16[384,768]{1,0:T(8,128)(2,1)S(1)}, u32[]{:S(2)}, u32[]{:S(2)}) %collective-permute-start.26) | collective-permute-done | bytes 589856 | tf_op jit(solution)/shard_map/ppermute | solution.py:77
  164.3 3.8 %collective-permute-done.28 = bf16[384,768]{1,0:T(8,128)(2,1)S(1)} collective-permute-done((bf16[384,768]{1,0:T(8,128)(2,1)S(1)}, bf16[384,768]{1,0:T(8,128)(2,1)S(1)}, u32[]{:S(2)}, u32[]{:S(2)}) %collective-permute-start.28) | collective-permute-done | bytes 589856 | tf_op jit(solution)/shard_map/ppermute | solution.py:77
  169.0 9.6 %collective-permute-done.29 = bf16[768,384]{1,0:T(8,128)(2,1)S(1)} collective-permute-done((bf16[768,384]{1,0:T(8,128)(2,1)S(1)}, bf16[768,384]{1,0:T(8,128)(2,1)S(1)}, u32[]{:S(2)}, u32[]{:S(2)}) %collective-permute-start.29) | collective-permute-done | bytes 589856 | tf_op jit(solution)/shard_map/ppermute | solution.py:77
  (100 shorter events, 34.3 us)
Async XLA Ops:
  0.6 50.3 %collective-permute-start.2 = (bf16[128,1536]{1,0:T(8,128)(2,1)}, bf16[128,1536]{1,0:T(8,128)(2,1)}, u32[]{:S(2)}, u32[]{:S(2)}) collective-permute-start(bf16[128,1536]{1,0:T(8,128)(2,1)} %param.6), channel_id=1, source_target_pairs={{0,6},{1,7},{2,0},{3,1},{4,2},{5,3},{6,4},{7,5},{8,14},{9,15},{10,... | collective-permute-start | bytes 1179656 | tf_op jit(solution)/shard_map/ppermute | solution.py:74
  5.8 26.7 %collective-permute-start = (bf16[128,1536]{1,0:T(8,128)(2,1)}, bf16[128,1536]{1,0:T(8,128)(2,1)}, u32[]{:S(2)}, u32[]{:S(2)}) collective-permute-start(bf16[128,1536]{1,0:T(8,128)(2,1)} %param.6), channel_id=1, source_target_pairs={{0,2},{1,3},{2,4},{3,5},{4,6},{5,7},{6,0},{7,1},{8,10},{9,11},{10,... | collective-permute-start | bytes 1179656 | tf_op jit(solution)/shard_map/ppermute | solution.py:74
  5.8 29.0 %collective-permute-start.7 = (bf16[128,1536]{1,0:T(8,128)(2,1)}, bf16[128,1536]{1,0:T(8,128)(2,1)}, u32[]{:S(2)}, u32[]{:S(2)}) collective-permute-start(bf16[128,1536]{1,0:T(8,128)(2,1)} %param.6), channel_id=1, source_target_pairs={{0,1},{1,0},{2,3},{3,2},{4,5},{5,4},{6,7},{7,6},{8,9},{9,8},{10,11... | collective-permute-start | bytes 1179656 | tf_op jit(solution)/shard_map/ppermute | solution.py:74
  6.5 4.8 %collective-permute-start.5 = (f32[128,8]{0,1:T(8,128)S(1)}, f32[128,8]{0,1:T(8,128)S(1)}, u32[]{:S(2)}, u32[]{:S(2)}) collective-permute-start(f32[128,8]{0,1:T(8,128)S(1)} %convert_multiply_fusion), channel_id=1, source_target_pairs={{0,1},{1,0},{2,3},{3,2},{4,5},{5,4},{6,7},{7,6},{8,9},{9,8},{10,11... | collective-permute-start | bytes 12296 | tf_op jit(solution)/shard_map/ppermute | solution.py:74
  11.9 12.1 %collective-permute-start.17 = (f32[256,8]{0,1:T(8,128)}, f32[256,8]{0,1:T(8,128)S(1)}, u32[]{:S(2)}, u32[]{:S(2)}) collective-permute-start(f32[256,8]{0,1:T(8,128)} %pad_maximum_fusion.2), channel_id=1, source_target_pairs={{0,2},{1,3},{2,4},{3,5},{4,6},{5,7},{6,0},{7,1},{8,10},{9,11},{10,... | collective-permute-start | bytes 24584 | tf_op jit(solution)/shard_map/ppermute | solution.py:74
  11.9 13.6 %collective-permute-start.18 = (f32[256,8]{0,1:T(8,128)}, f32[256,8]{0,1:T(8,128)}, u32[]{:S(2)}, u32[]{:S(2)}) collective-permute-start(f32[256,8]{0,1:T(8,128)} %pad_maximum_fusion.2), channel_id=1, source_target_pairs={{0,6},{1,7},{2,0},{3,1},{4,2},{5,3},{6,4},{7,5},{8,14},{9,15},{10,... | collective-permute-start | bytes 24584 | tf_op jit(solution)/shard_map/ppermute | solution.py:74
  24.0 16.2 %collective-permute-start.12 = (bf16[384,768]{1,0:T(8,128)(2,1)S(1)}, bf16[384,768]{1,0:T(8,128)(2,1)S(1)}, u32[]{:S(2)}, u32[]{:S(2)}) collective-permute-start(bf16[384,768]{1,0:T(8,128)(2,1)S(1)} %bitcast.29), channel_id=1, source_target_pairs={{0,8},{8,0},{16,24},{24,16},{1,9},{9,1},{17,25},{25,17},{2,10},{10... | collective-permute-start | bytes 1769480 | tf_op jit(solution)/shard_map/ppermute | solution.py:77
  25.5 4.8 %collective-permute-start.6 = (f32[256,8]{0,1:T(8,128)}, f32[256,8]{0,1:T(8,128)S(1)}, u32[]{:S(2)}, u32[]{:S(2)}) collective-permute-start(f32[256,8]{0,1:T(8,128)} %pad_maximum_fusion.2), channel_id=1, source_target_pairs={{0,4},{1,5},{2,6},{3,7},{4,0},{5,1},{6,2},{7,3},{8,12},{9,13},{10,... | collective-permute-start | bytes 24584 | tf_op jit(solution)/shard_map/ppermute | solution.py:74
  30.3 22.2 %collective-permute-start.13 = (bf16[384,768]{1,0:T(8,128)(2,1)S(1)}, bf16[384,768]{1,0:T(8,128)(2,1)S(1)}, u32[]{:S(2)}, u32[]{:S(2)}) collective-permute-start(bf16[384,768]{1,0:T(8,128)(2,1)S(1)} %bitcast.30), channel_id=1, source_target_pairs={{0,16},{8,24},{16,0},{24,8},{1,17},{9,25},{17,1},{25,9},{2,18},{10... | collective-permute-start | bytes 1769480 | tf_op jit(solution)/shard_map/ppermute | solution.py:77
  32.4 18.4 %collective-permute-start.9 = (bf16[768,384]{1,0:T(8,128)(2,1)S(1)}, bf16[768,384]{1,0:T(8,128)(2,1)S(1)}, u32[]{:S(2)}, u32[]{:S(2)}) collective-permute-start(bf16[768,384]{1,0:T(8,128)(2,1)S(1)} %bitcast.31), channel_id=1, source_target_pairs={{0,8},{8,0},{16,24},{24,16},{1,9},{9,1},{17,25},{25,17},{2,10},{10... | collective-permute-start | bytes 1769480 | tf_op jit(solution)/shard_map/ppermute | solution.py:77
  34.8 20.9 %collective-permute-start.10 = (bf16[768,384]{1,0:T(8,128)(2,1)S(1)}, bf16[768,384]{1,0:T(8,128)(2,1)S(1)}, u32[]{:S(2)}, u32[]{:S(2)}) collective-permute-start(bf16[768,384]{1,0:T(8,128)(2,1)S(1)} %bitcast.32), channel_id=1, source_target_pairs={{0,16},{8,24},{16,0},{24,8},{1,17},{9,25},{17,1},{25,9},{2,18},{10... | collective-permute-start | bytes 1769480 | tf_op jit(solution)/shard_map/ppermute | solution.py:77
  40.2 16.9 %collective-permute-start.15 = (bf16[128,1536]{1,0:T(8,128)(2,1)}, bf16[128,1536]{1,0:T(8,128)(2,1)S(1)}, u32[]{:S(2)}, u32[]{:S(2)}) collective-permute-start(bf16[128,1536]{1,0:T(8,128)(2,1)} %collective-permute-done), channel_id=1, source_target_pairs={{0,1},{1,0},{2,3},{3,2},{4,5},{5,4},{6,7},{7,6},{8,9},{9,8},{10,11... | collective-permute-start | bytes 1179656 | tf_op jit(solution)/shard_map/ppermute | solution.py:74
  50.9 47.4 %collective-permute-start.8 = (bf16[128,1536]{1,0:T(8,128)(2,1)S(1)}, bf16[128,1536]{1,0:T(8,128)(2,1)S(1)}, u32[]{:S(2)}, u32[]{:S(2)}) collective-permute-start(bf16[128,1536]{1,0:T(8,128)(2,1)S(1)} %copy-done.3), channel_id=1, source_target_pairs={{0,1},{1,0},{2,3},{3,2},{4,5},{5,4},{6,7},{7,6},{8,9},{9,8},{10,11... | collective-permute-start | bytes 1179656 | tf_op jit(solution)/shard_map/ppermute | solution.py:74
  51.0 12.1 %collective-permute-start.21 = (bf16[128,1536]{1,0:T(8,128)(2,1)S(1)}, bf16[128,1536]{1,0:T(8,128)(2,1)}, u32[]{:S(2)}, u32[]{:S(2)}) collective-permute-start(bf16[128,1536]{1,0:T(8,128)(2,1)S(1)} %copy-done.3), channel_id=1, source_target_pairs={{0,6},{1,7},{2,0},{3,1},{4,2},{5,3},{6,4},{7,5},{8,14},{9,15},{10,... | collective-permute-start | bytes 1179656 | tf_op jit(solution)/shard_map/ppermute | solution.py:74
  52.5 7.9 %collective-permute-start.16 = (bf16[128,1536]{1,0:T(8,128)(2,1)}, bf16[128,1536]{1,0:T(8,128)(2,1)S(1)}, u32[]{:S(2)}, u32[]{:S(2)}) collective-permute-start(bf16[128,1536]{1,0:T(8,128)(2,1)} %collective-permute-done.2), channel_id=1, source_target_pairs={{0,1},{1,0},{2,3},{3,2},{4,5},{5,4},{6,7},{7,6},{8,9},{9,8},{10,11... | collective-permute-start | bytes 1179656 | tf_op jit(solution)/shard_map/ppermute | solution.py:74
  55.7 23.7 %collective-permute-start.3 = (bf16[128,1536]{1,0:T(8,128)(2,1)}, bf16[128,1536]{1,0:T(8,128)(2,1)S(1)}, u32[]{:S(2)}, u32[]{:S(2)}) collective-permute-start(bf16[128,1536]{1,0:T(8,128)(2,1)} %collective-permute-done.2), channel_id=1, source_target_pairs={{2,0},{3,1},{4,2},{5,3},{10,8},{11,9},{12,10},{13,11},{18,16},{19,... | collective-permute-start | bytes 1179656 | tf_op jit(solution)/shard_map/ppermute | solution.py:74
  57.1 23.6 %collective-permute-start.1 = (bf16[128,1536]{1,0:T(8,128)(2,1)}, bf16[128,1536]{1,0:T(8,128)(2,1)S(1)}, u32[]{:S(2)}, u32[]{:S(2)}) collective-permute-start(bf16[128,1536]{1,0:T(8,128)(2,1)} %collective-permute-done), channel_id=1, source_target_pairs={{2,4},{3,5},{4,6},{5,7},{10,12},{11,13},{12,14},{13,15},{18,20},{1... | collective-permute-start | bytes 1179656 | tf_op jit(solution)/shard_map/ppermute | solution.py:74
  60.4 22.0 %collective-permute-start.14 = (bf16[384,768]{1,0:T(8,128)(2,1)S(1)}, bf16[384,768]{1,0:T(8,128)(2,1)S(1)}, u32[]{:S(2)}, u32[]{:S(2)}) collective-permute-start(bf16[384,768]{1,0:T(8,128)(2,1)S(1)} %collective-permute-done.12), channel_id=1, source_target_pairs={{0,16},{8,24},{16,0},{24,8},{1,17},{9,25},{17,1},{25,9},{2,18},{10... | collective-permute-start | bytes 1769480 | tf_op jit(solution)/shard_map/ppermute | solution.py:77
  63.1 19.2 %collective-permute-start.19 = (bf16[128,1536]{1,0:T(8,128)(2,1)S(1)}, bf16[128,1536]{1,0:T(8,128)(2,1)}, u32[]{:S(2)}, u32[]{:S(2)}) collective-permute-start(bf16[128,1536]{1,0:T(8,128)(2,1)S(1)} %copy-done.3), channel_id=1, source_target_pairs={{0,2},{1,3},{2,4},{3,5},{4,6},{5,7},{6,0},{7,1},{8,10},{9,11},{10,... | collective-permute-start | bytes 1179656 | tf_op jit(solution)/shard_map/ppermute | solution.py:74
  79.4 49.2 %collective-permute-start.24 = (bf16[128,1536]{1,0:T(8,128)(2,1)}, bf16[128,1536]{1,0:T(8,128)(2,1)}, u32[]{:S(2)}, u32[]{:S(2)}) collective-permute-start(bf16[128,1536]{1,0:T(8,128)(2,1)} %collective-permute-done.21), channel_id=1, source_target_pairs={{2,0},{3,1},{4,2},{5,3},{10,8},{11,9},{12,10},{13,11},{18,16},{19,... | collective-permute-start | bytes 1179656 | tf_op jit(solution)/shard_map/ppermute | solution.py:74
  80.7 14.9 %collective-permute-start.11 = (bf16[768,384]{1,0:T(8,128)(2,1)S(1)}, bf16[768,384]{1,0:T(8,128)(2,1)S(1)}, u32[]{:S(2)}, u32[]{:S(2)}) collective-permute-start(bf16[768,384]{1,0:T(8,128)(2,1)S(1)} %collective-permute-done.10), channel_id=1, source_target_pairs={{0,8},{8,0},{16,24},{24,16},{1,9},{9,1},{17,25},{25,17},{2,10},{10... | collective-permute-start | bytes 1769480 | tf_op jit(solution)/shard_map/ppermute | solution.py:77
  82.3 30.0 %collective-permute-start.22 = (bf16[128,1536]{1,0:T(8,128)(2,1)}, bf16[128,1536]{1,0:T(8,128)(2,1)}, u32[]{:S(2)}, u32[]{:S(2)}) collective-permute-start(bf16[128,1536]{1,0:T(8,128)(2,1)} %collective-permute-done.21), channel_id=1, source_target_pairs={{0,1},{1,0},{2,3},{3,2},{4,5},{5,4},{6,7},{7,6},{8,9},{9,8},{10,11... | collective-permute-start | bytes 1179656 | tf_op jit(solution)/shard_map/ppermute | solution.py:74
  82.4 46.2 %collective-permute-start.23 = (bf16[128,1536]{1,0:T(8,128)(2,1)}, bf16[128,1536]{1,0:T(8,128)(2,1)}, u32[]{:S(2)}, u32[]{:S(2)}) collective-permute-start(bf16[128,1536]{1,0:T(8,128)(2,1)} %collective-permute-done.19), channel_id=1, source_target_pairs={{2,4},{3,5},{4,6},{5,7},{10,12},{11,13},{12,14},{13,15},{18,20},{1... | collective-permute-start | bytes 1179656 | tf_op jit(solution)/shard_map/ppermute | solution.py:74
  95.7 16.6 %collective-permute-start.20 = (bf16[128,1536]{1,0:T(8,128)(2,1)}, bf16[128,1536]{1,0:T(8,128)(2,1)}, u32[]{:S(2)}, u32[]{:S(2)}) collective-permute-start(bf16[128,1536]{1,0:T(8,128)(2,1)} %collective-permute-done.19), channel_id=1, source_target_pairs={{0,1},{1,0},{2,3},{3,2},{4,5},{5,4},{6,7},{7,6},{8,9},{9,8},{10,11... | collective-permute-start | bytes 1179656 | tf_op jit(solution)/shard_map/ppermute | solution.py:74
  98.3 27.8 %collective-permute-start.4 = (bf16[128,1536]{1,0:T(8,128)(2,1)S(1)}, bf16[128,1536]{1,0:T(8,128)(2,1)S(1)}, u32[]{:S(2)}, u32[]{:S(2)}) collective-permute-start(bf16[128,1536]{1,0:T(8,128)(2,1)S(1)} %broadcast_select_fusion.1), channel_id=1, source_target_pairs={{0,1},{1,0},{2,3},{3,2},{4,5},{5,4},{6,7},{7,6},{8,9},{9,8},{10,11... | collective-permute-start | bytes 1179656 | tf_op jit(solution)/shard_map/ppermute | solution.py:74
  129.6 1.9 %collective-permute-start.25 = (bf16[128,1536]{1,0:T(8,128)(2,1)S(1)}, bf16[128,1536]{1,0:T(8,128)(2,1)S(1)}, u32[]{:S(2)}, u32[]{:S(2)}) collective-permute-start(bf16[128,1536]{1,0:T(8,128)(2,1)S(1)} %broadcast_select_fusion), channel_id=1, source_target_pairs={{0,1},{1,0},{2,3},{3,2},{4,5},{5,4},{6,7},{7,6},{8,9},{9,8},{10,11... | collective-permute-start | bytes 1179656 | tf_op jit(solution)/shard_map/ppermute | solution.py:74
  135.3 16.3 %collective-permute-start.27 = (bf16[384,768]{1,0:T(8,128)(2,1)S(1)}, bf16[384,768]{1,0:T(8,128)(2,1)S(1)}, u32[]{:S(2)}, u32[]{:S(2)}) collective-permute-start(bf16[384,768]{1,0:T(8,128)(2,1)S(1)} %add_convert_fusion.4), channel_id=1, source_target_pairs={{0,16},{8,24},{16,0},{24,8},{1,17},{9,25},{17,1},{25,9},{2,18},{10... | collective-permute-start | bytes 1769480 | tf_op jit(solution)/shard_map/ppermute | solution.py:77
  137.3 27.0 %collective-permute-start.26 = (bf16[384,768]{1,0:T(8,128)(2,1)S(1)}, bf16[384,768]{1,0:T(8,128)(2,1)S(1)}, u32[]{:S(2)}, u32[]{:S(2)}) collective-permute-start(bf16[384,768]{1,0:T(8,128)(2,1)S(1)} %add_convert_fusion.5), channel_id=1, source_target_pairs={{0,16},{8,24},{16,0},{24,8},{1,17},{9,25},{17,1},{25,9},{2,18},{10... | collective-permute-start | bytes 1769480 | tf_op jit(solution)/shard_map/ppermute | solution.py:77
  137.9 16.4 %collective-permute-start.30 = (bf16[768,384]{1,0:T(8,128)(2,1)S(1)}, bf16[768,384]{1,0:T(8,128)(2,1)S(1)}, u32[]{:S(2)}, u32[]{:S(2)}) collective-permute-start(bf16[768,384]{1,0:T(8,128)(2,1)S(1)} %fusion.1), channel_id=1, source_target_pairs={{0,8},{8,0},{16,24},{24,16},{1,9},{9,1},{17,25},{25,17},{2,10},{10... | collective-permute-start | bytes 1769480 | tf_op jit(solution)/shard_map/ppermute | solution.py:77
  151.7 16.3 %collective-permute-start.28 = (bf16[384,768]{1,0:T(8,128)(2,1)S(1)}, bf16[384,768]{1,0:T(8,128)(2,1)S(1)}, u32[]{:S(2)}, u32[]{:S(2)}) collective-permute-start(bf16[384,768]{1,0:T(8,128)(2,1)S(1)} %add_convert_fusion.3), channel_id=1, source_target_pairs={{0,8},{8,0},{16,24},{24,16},{1,9},{9,1},{17,25},{25,17},{2,10},{10... | collective-permute-start | bytes 1769480 | tf_op jit(solution)/shard_map/ppermute | solution.py:77
  153.7 24.9 %collective-permute-start.29 = (bf16[768,384]{1,0:T(8,128)(2,1)S(1)}, bf16[768,384]{1,0:T(8,128)(2,1)S(1)}, u32[]{:S(2)}, u32[]{:S(2)}) collective-permute-start(bf16[768,384]{1,0:T(8,128)(2,1)S(1)} %fusion), channel_id=1, source_target_pairs={{0,8},{8,0},{16,24},{24,16},{1,9},{9,1},{17,25},{25,17},{2,10},{10... | collective-permute-start | bytes 1769480 | tf_op jit(solution)/shard_map/ppermute | solution.py:77
  154.4 24.2 %collective-permute-start.31 = (bf16[768,384]{1,0:T(8,128)(2,1)S(1)}, bf16[768,384]{1,0:T(8,128)(2,1)S(1)}, u32[]{:S(2)}, u32[]{:S(2)}) collective-permute-start(bf16[768,384]{1,0:T(8,128)(2,1)S(1)} %add_convert_fusion.1), channel_id=1, source_target_pairs={{0,16},{8,24},{16,0},{24,8},{1,17},{9,25},{17,1},{25,9},{2,18},{10... | collective-permute-start | bytes 1769480 | tf_op jit(solution)/shard_map/ppermute | solution.py:77
  (11 other events, 91.9 us)
where the time goes:
time: 180 us
  waiting for transfers between devices  82.8 us (46%)
  starting transfers between devices  37.4 us (21%)
  matrix products  35.6 us (20%)
  local copies, waits for them, and re-layouts  15.5 us (9%)
  other arithmetic  7.38 us (4%)
    ppermute x12, waiting for transfers between devices, dp(): return lax.ppermute(value, 'dp', xor_perm(4, bits))  59.1 us
    dot_general x12, matrix products, outer(): return lax.dot_general(left, right, FIRST, preferred_element_type=F32)  25.1 us
    ppermute x20, waiting for transfers between devices, ex(): return lax.ppermute(value, 'expert', perm)  23.7 us
    ppermute x20, starting transfers between devices, ex(): return lax.ppermute(value, 'expert', perm)  22.8 us
    ppermute x12, starting transfers between devices, dp(): return lax.ppermute(value, 'dp', xor_perm(4, bits))  14.6 us
    unnamed x26, local copies, waits for them, and re-layouts  7.47 us
    dot_general x1, matrix products, dense_body(): pre_b = jnp.dot(x_b, up_all, preferred_element_type=F32)  4.68 us
  transfers between devices with their start and end apart: 32, of which 13 were waited for; matrix products, arithmetic and copies ran while one was open for 29% of the time, Pallas kernels for 0%

commit v1 on v0

--- a/solution.py
+++ b/solution.py
@@ -65,7 +65,7 @@
 
 def dense_body(tokens, grad_out, expert_ids, gate_q, w_up, w_down):
     devices = lax.axis_size("expert")
-    block, hidden = w_up.shape
+    block, _ = w_up.shape
     dp_index = lax.axis_index("dp")
     ex_index = lax.axis_index("expert")
     upper = ex_index >= devices // 2
@@ -114,14 +114,9 @@
     g1b = ex(g1, swap)
     g3b = ex(g3, swap)
 
-    up_all = jnp.zeros((4 * block, hidden), BF16)
-    down_all = jnp.zeros((hidden, 4 * block), BF16)
-    for bits, up_part, down_part in ((0, w_up, w_down), (1, up_x, down_x), (2, up_y, down_y), (3, up_d, down_d)):
-        where = (dp_index ^ bits) * block
-        up_all = lax.dynamic_update_slice(up_all, up_part, (where, 0))
-        down_all = lax.dynamic_update_slice(down_all, down_part, (0, where))
-
     pick = (experts == ex_index).astype(F32)
+    ups = (w_up, up_x, up_y, up_d)
+    downs = (w_down, down_x, down_y, down_d)
 
     def gate_of(*tables):
         table = jnp.concatenate(tables, axis=0)
@@ -130,51 +125,60 @@
     def scaled(gate, g):
         return (gate[:, None] * g.astype(F32)).astype(BF16)
 
-    def backward(pre, g):
-        act_grad = lax.dot_general(g, down_all, LAST, preferred_element_type=F32)
-        return (act_grad * silu_slope(pre)).astype(BF16)
+    def columns(rows, bits):
+        return lax.dynamic_slice(rows, (0, (dp_index ^ bits) * block), (rows.shape[0], block))
+
+    def forward_part(x, bits, total):
+        part = jnp.dot(columns(x, bits), ups[bits], preferred_element_type=F32)
+        return part if total is None else total + part
+
+    def backward_part(g, bits, total):
+        part = lax.dot_general(columns(g, bits), downs[bits], LAST, preferred_element_type=F32)
+        return part if total is None else total + part
 
     def outer(left, right):
         return lax.dot_general(left, right, FIRST, preferred_element_type=F32)
 
-    x_a = jnp.concatenate([tokens, t0b], axis=0)
-    x_b = jnp.concatenate([t1, t1b, t3, t3b], axis=0)
-    pre_a = jnp.dot(x_a, up_all, preferred_element_type=F32)
-    pre_b = jnp.dot(x_b, up_all, preferred_element_type=F32)
-    act_a = jax.nn.silu(pre_a).astype(BF16)
-    act_b = jax.nn.silu(pre_b).astype(BF16)
-    gate_a = gate_of(c0)
-    gate_b = gate_of(c1, c3)
-    gate_c = gate_of(c2)
-    g_a = scaled(gate_a, jnp.concatenate([grad_out, g0b], axis=0))
-    g_b = scaled(gate_b, jnp.concatenate([g1, g1b, g3, g3b], axis=0))
-    back_a = backward(pre_a, g_a)
-    back_b = backward(pre_b, g_b)
-    up_acc = outer(x_a, back_a) + outer(x_b, back_b)
-    down_acc = outer(act_a, g_a) + outer(act_b, g_b)
+    x_ab = jnp.concatenate([tokens, t0b, t1, t1b, t3, t3b], axis=0)
+    pre = None
+    for bits in (0, 1, 2, 3):
+        pre = forward_part(x_ab, bits, pre)
+    g_ab = scaled(gate_of(c0, c1, c3), jnp.concatenate([grad_out, g0b, g1, g1b, g3, g3b], axis=0))
+    act_grad = None
+    for bits in (0, 1, 2, 3):
+        act_grad = backward_part(g_ab, bits, act_grad)
+    act_ab = jax.nn.silu(pre).astype(BF16)
+    back_ab = (act_grad * silu_slope(pre)).astype(BF16)
+    up_acc = [outer(columns(x_ab, bits), back_ab) for bits in range(4)]
+    down_acc = [outer(act_ab, columns(g_ab, bits)) for bits in range(4)]
     t2 = jnp.where(upper, t2u, t2d)
     t2b = ex(t2, swap)
     x_c = jnp.concatenate([t2, t2b], axis=0)
-    pre_c = jnp.dot(x_c, up_all, preferred_element_type=F32)
+    pre_c = None
+    for bits in (0, 1, 2, 3):
+        pre_c = forward_part(x_c, bits, pre_c)
     act_c = jax.nn.silu(pre_c).astype(BF16)
-    up_acc, down_acc, act_c, pre_c, g2u, g2d = lax.optimization_barrier((up_acc, down_acc, act_c, pre_c, g2u, g2d))
+    slope_c = silu_slope(pre_c)
+    gate_c = gate_of(c2)
+    up_acc, down_acc, act_c, slope_c, gate_c, g2u, g2d = lax.optimization_barrier(
+        (up_acc, down_acc, act_c, slope_c, gate_c, g2u, g2d)
+    )
     g2 = jnp.where(upper, g2u, g2d)
     g2b = ex(g2, swap)
     g_c = scaled(gate_c, jnp.concatenate([g2, g2b], axis=0))
-    back_c = backward(pre_c, g_c)
+    act_grad_c = None
+    for bits in (0, 1, 2, 3):
+        act_grad_c = backward_part(g_c, bits, act_grad_c)
+    back_c = (act_grad_c * slope_c).astype(BF16)
 
     def up_block(bits):
-        where = (dp_index ^ bits) * block
-        cols = lax.dynamic_slice(x_c, (0, where), (x_c.shape[0], block))
-        return outer(cols, back_c) + lax.dynamic_slice(up_acc, (where, 0), (block, hidden))
+        return outer(columns(x_c, bits), back_c) + up_acc[bits]
 
     def down_block(bits):
-        where = (dp_index ^ bits) * block
-        cols = lax.dynamic_slice(g_c, (0, where), (g_c.shape[0], block))
-        return outer(act_c, cols) + lax.dynamic_slice(down_acc, (0, where), (hidden, block))
-
+        return outer(act_c, columns(g_c, bits)) + down_acc[bits]
+
+    down_far = dp(down_block(3).astype(BF16), 1)
     up_far = dp(up_block(3).astype(BF16), 2)
-    down_far = dp(down_block(3).astype(BF16), 1)
     up_near = dp(up_block(2).astype(BF16), 2)
     down_near = dp(down_block(1).astype(BF16), 1)
     up_side, down_side = up_block(1), down_block(2)

time: 180 us -> 151 us (0.84)
  matrix products: 35.6 us -> 19.5 us
  local copies, waits for them, and re-layouts: 15.5 us -> 6.59 us
  starting transfers between devices: 37.4 us -> 33.4 us
  other arithmetic: 7.38 us -> 4.49 us
  waiting for transfers between devices: 82.8 us -> 85.4 us
    dot_general x12 -> x16, matrix products: 25.1 us -> 8.99 us  [outer(): return lax.dot_general(left, right, FIRST, preferred_element_type=F32)]
    ppermute x20, waiting for transfers between devices: 23.7 us -> 32.4 us  [ex(): return lax.ppermute(value, 'expert', perm)]
    ppermute x12, waiting for transfers between devices: 59.1 us -> 53 us  [dp(): return lax.ppermute(value, 'dp', xor_perm(4, bits))]
    ppermute x20, starting transfers between devices: 22.8 us -> 18.1 us  [ex(): return lax.ppermute(value, 'expert', perm)]
    dynamic_update_slice x8 -> x0, local copies, waits for them, and re-layouts: 3.79 us -> none  [the longest x4 3.41 us: dense_body(): up_all = lax.dynamic_update_slice(up_all, up_part, (where, 0))]
    concatenate x2, local copies, waits for them, and re-layouts: 2.53 us -> 0.05 us  [the longest x1 0.03 us: dense_body(): jnp.concatenate([grad_out, g0b, g1, g1b, g3, g3b], axis=0)]
    reduce_sum x2, other arithmetic: 2.02 us -> 0.16 us  [gate_of(): return jnp.sum(table * pick, axis=1)]
    unnamed x26 -> x16, local copies, waits for them, and re-layouts: 7.47 us -> 6.54 us
  transfers between devices with their start and end apart: 32 -> 32, of which waited for: 13 -> 11; matrix products, arithmetic and copies ran while one was open for 29% -> 19% of each run, Pallas kernels for 0% -> 0%
where the time goes in v1:
time: 151 us; the launch traced here: 150 us
  waiting for transfers between devices  85.4 us (57%)
  starting transfers between devices  33.4 us (22%)
  matrix products  19.5 us (13%)
  local copies, waits for them, and re-layouts  6.59 us (4%)
  other arithmetic  4.49 us (3%)
    ppermute x12, waiting for transfers between devices, dp(): return lax.ppermute(value, 'dp', xor_perm(4, bits))  53 us
    ppermute x20, waiting for transfers between devices, ex(): return lax.ppermute(value, 'expert', perm)  32.4 us
    ppermute x20, starting transfers between devices, ex(): return lax.ppermute(value, 'expert', perm)  18.1 us
    ppermute x12, starting transfers between devices, dp(): return lax.ppermute(value, 'dp', xor_perm(4, bits))  15.3 us
    dot_general x16, matrix products, outer(): return lax.dot_general(left, right, FIRST, preferred_element_type=F32)  8.99 us
    unnamed x16, local copies, waits for them, and re-layouts  6.54 us
    dot_general x8, matrix products, backward_part(): lax.dot_general(columns(g, bits), downs[bits], LAST, preferred_element_ty...  5.47 us
    dot_general x8, matrix products, forward_part(): part = jnp.dot(columns(x, bits), ups[bits], preferred_element_type=F32)  5.01 us
  transfers between devices with their start and end apart: 32, of which 11 were waited for; matrix products, arithmetic and copies ran while one was open for 19% of the time, Pallas kernels for 0%

profile of v1, /device:TPU:0, one launch (start us, length us, event | category | flops | bytes accessed | tf_op | source)
XLA Modules:
  0.0 150.5 jit_solution(17252100947072080285)
XLA Ops:
  0.6 3.1 %collective-permute-start = (bf16[128,1536]{1,0:T(8,128)(2,1)}, bf16[128,1536]{1,0:T(8,128)(2,1)S(1)}, u32[]{:S(2)}, u32[]{:S(2)}) collective-permute-start(bf16[128,1536]{1,0:T(8,128)(2,1)} %param.6), channel_id=1, source_target_pairs={{0,2},{1,3},{2,4},{3,5},{4,6},{5,7},{6,0},{7,1},{8,10},{9,11},{10,... | collective-permute-start | bytes 1179656 | tf_op jit(solution)/shard_map/ppermute | solution.py:74
  5.1 1.8 %constant_dynamic-update-slice_fusion.5 = bf16[768,1536]{1,0:T(8,128)(2,1)} fusion(bf16[128,1536]{1,0:T(8,128)(2,1)} %param.6), kind=kLoop, calls=%fused_computation.89 | loop fusion | bytes 786432
  6.9 1.0 constant_dynamic-update-slice_fusion.11
  7.9 2.2 %collective-permute-start.10 = (f32[256,8]{0,1:T(8,128)S(1)}, f32[256,8]{0,1:T(8,128)S(1)}, u32[]{:S(2)}, u32[]{:S(2)}) collective-permute-start(f32[256,8]{0,1:T(8,128)S(1)} %pad_maximum_fusion), channel_id=1, source_target_pairs={{0,6},{1,7},{2,0},{3,1},{4,2},{5,3},{6,4},{7,5},{8,14},{9,15},{10,... | collective-permute-start | bytes 24584 | tf_op jit(solution)/shard_map/ppermute | solution.py:74
  10.1 5.3 %collective-permute-done.10 = f32[256,8]{0,1:T(8,128)S(1)} collective-permute-done((f32[256,8]{0,1:T(8,128)S(1)}, f32[256,8]{0,1:T(8,128)S(1)}, u32[]{:S(2)}, u32[]{:S(2)}) %collective-permute-start.10) | collective-permute-done | bytes 8224 | tf_op jit(solution)/shard_map/ppermute | solution.py:74
  15.9 1.6 %collective-permute-start.22 = (f32[256,8]{0,1:T(8,128)S(1)}, f32[256,8]{0,1:T(8,128)S(1)}, u32[]{:S(2)}, u32[]{:S(2)}) collective-permute-start(f32[256,8]{0,1:T(8,128)S(1)} %pad_maximum_fusion), channel_id=1, source_target_pairs={{0,4},{1,5},{2,6},{3,7},{4,0},{5,1},{6,2},{7,3},{8,12},{9,13},{10,... | collective-permute-start | bytes 24584 | tf_op jit(solution)/shard_map/ppermute | solution.py:74
  17.6 6.4 %collective-permute-done.22 = f32[256,8]{0,1:T(8,128)S(1)} collective-permute-done((f32[256,8]{0,1:T(8,128)S(1)}, f32[256,8]{0,1:T(8,128)S(1)}, u32[]{:S(2)}, u32[]{:S(2)}) %collective-permute-start.22) | collective-permute-done | bytes 8224 | tf_op jit(solution)/shard_map/ppermute | solution.py:74
  24.1 3.5 %collective-permute-start.2 = (bf16[128,1536]{1,0:T(8,128)(2,1)}, bf16[128,1536]{1,0:T(8,128)(2,1)S(1)}, u32[]{:S(2)}, u32[]{:S(2)}) collective-permute-start(bf16[128,1536]{1,0:T(8,128)(2,1)} %param.6), channel_id=1, source_target_pairs={{0,6},{1,7},{2,0},{3,1},{4,2},{5,3},{6,4},{7,5},{8,14},{9,15},{10,... | collective-permute-start | bytes 1179656 | tf_op jit(solution)/shard_map/ppermute | solution.py:74
  27.6 1.4 collective-permute-start.14
  29.0 1.0 constant_dynamic-update-slice_fusion.10
  30.1 1.3 collective-permute-start.19
  31.5 1.8 %constant_dynamic-update-slice_fusion.4 = bf16[768,1536]{1,0:T(8,128)(2,1)} fusion(bf16[768,1536]{1,0:T(8,128)(2,1)} %constant_dynamic-update-slice_fusion.5, bf16[128,1536]{1,0:T(8,128)(2,1)} %collective-permute-done.5), kind=kLoop, calls=%fused_computation.88 | loop fusion | bytes 786432
  33.3 1.5 %collective-permute-start.20 = (bf16[384,768]{1,0:T(8,128)(2,1)S(1)}, bf16[384,768]{1,0:T(8,128)(2,1)S(1)}, u32[]{:S(2)}, u32[]{:S(2)}) collective-permute-start(bf16[384,768]{1,0:T(8,128)(2,1)S(1)} %bitcast.45), channel_id=1, source_target_pairs={{0,16},{8,24},{16,0},{24,8},{1,17},{9,25},{17,1},{25,9},{2,18},{10... | collective-permute-start | bytes 1769480 | tf_op jit(solution)/shard_map/ppermute | solution.py:77
  35.6 9.0 %collective-permute-done.14 = bf16[128,1536]{1,0:T(8,128)(2,1)S(1)} collective-permute-done((bf16[128,1536]{1,0:T(8,128)(2,1)}, bf16[128,1536]{1,0:T(8,128)(2,1)S(1)}, u32[]{:S(2)}, u32[]{:S(2)}) %collective-permute-start.14) | collective-permute-done | bytes 393248 | tf_op jit(solution)/shard_map/ppermute | solution.py:74
  47.6 1.4 collective-permute-start.3
  49.1 1.4 collective-permute-start.17
  50.5 1.6 %collective-permute-start.16 = (bf16[768,384]{1,0:T(8,128)(2,1)S(1)}, bf16[768,384]{1,0:T(8,128)(2,1)S(1)}, u32[]{:S(2)}, u32[]{:S(2)}) collective-permute-start(bf16[768,384]{1,0:T(8,128)(2,1)S(1)} %bitcast.43), channel_id=1, source_target_pairs={{0,8},{8,0},{16,24},{24,16},{1,9},{9,1},{17,25},{25,17},{2,10},{10... | collective-permute-start | bytes 1769480 | tf_op jit(solution)/shard_map/ppermute | solution.py:77
  52.1 8.9 %collective-permute-done.3 = bf16[128,1536]{1,0:T(8,128)(2,1)S(1)} collective-permute-done((bf16[128,1536]{1,0:T(8,128)(2,1)S(1)}, bf16[128,1536]{1,0:T(8,128)(2,1)S(1)}, u32[]{:S(2)}, u32[]{:S(2)}) %collective-permute-start.3) | collective-permute-done | bytes 393248 | tf_op jit(solution)/shard_map/ppermute | solution.py:74
  63.3 1.5 collective-permute-start.24
  65.6 1.4 collective-permute-start.21
  67.7 1.6 %collective-permute-start.18 = (bf16[768,384]{1,0:T(8,128)(2,1)S(1)}, bf16[768,384]{1,0:T(8,128)(2,1)S(1)}, u32[]{:S(2)}, u32[]{:S(2)}) collective-permute-start(bf16[768,384]{1,0:T(8,128)(2,1)S(1)} %collective-permute-done.17), channel_id=1, source_target_pairs={{0,8},{8,0},{16,24},{24,16},{1,9},{9,1},{17,25},{25,17},{2,10},{10... | collective-permute-start | bytes 1769480 | tf_op jit(solution)/shard_map/ppermute | solution.py:77
  71.0 9.4 %collective-permute-done.21 = bf16[384,768]{1,0:T(8,128)(2,1)S(1)} collective-permute-done((bf16[384,768]{1,0:T(8,128)(2,1)S(1)}, bf16[384,768]{1,0:T(8,128)(2,1)S(1)}, u32[]{:S(2)}, u32[]{:S(2)}) %collective-permute-start.21) | collective-permute-done | bytes 589856 | tf_op jit(solution)/shard_map/ppermute | solution.py:77
  80.4 1.1 multiply_convert_fusion.1
  82.3 1.3 multiply_convert_fusion.2
  91.3 1.7 %collective-permute-done.25 = bf16[128,1536]{1,0:T(8,128)(2,1)S(1)} collective-permute-done((bf16[128,1536]{1,0:T(8,128)(2,1)S(1)}, bf16[128,1536]{1,0:T(8,128)(2,1)S(1)}, u32[]{:S(2)}, u32[]{:S(2)}) %collective-permute-start.25) | collective-permute-done | bytes 393248 | tf_op jit(solution)/shard_map/ppermute | solution.py:74
  94.0 1.6 %collective-permute-start.29 = (bf16[768,384]{1,0:T(8,128)(2,1)S(1)}, bf16[768,384]{1,0:T(8,128)(2,1)S(1)}, u32[]{:S(2)}, u32[]{:S(2)}) collective-permute-start(bf16[768,384]{1,0:T(8,128)(2,1)S(1)} %fusion), channel_id=1, source_target_pairs={{0,8},{8,0},{16,24},{24,16},{1,9},{9,1},{17,25},{25,17},{2,10},{10... | collective-permute-start | bytes 1769480 | tf_op jit(solution)/shard_map/ppermute | solution.py:77
  101.5 20.6 %collective-permute-done.30 = bf16[768,384]{1,0:T(8,128)(2,1)S(1)} collective-permute-done((bf16[768,384]{1,0:T(8,128)(2,1)S(1)}, bf16[768,384]{1,0:T(8,128)(2,1)S(1)}, u32[]{:S(2)}, u32[]{:S(2)}) %collective-permute-start.30) | collective-permute-done | bytes 589856 | tf_op jit(solution)/shard_map/ppermute | solution.py:77
  123.2 1.4 collective-permute-start.26
  124.7 1.6 %collective-permute-start.28 = (bf16[384,768]{1,0:T(8,128)(2,1)S(1)}, bf16[384,768]{1,0:T(8,128)(2,1)S(1)}, u32[]{:S(2)}, u32[]{:S(2)}) collective-permute-start(bf16[384,768]{1,0:T(8,128)(2,1)S(1)} %add_convert_fusion.3), channel_id=1, source_target_pairs={{0,8},{8,0},{16,24},{24,16},{1,9},{9,1},{17,25},{25,17},{2,10},{10... | collective-permute-start | bytes 1769480 | tf_op jit(solution)/shard_map/ppermute | solution.py:77
  126.2 12.3 %collective-permute-done.31 = bf16[768,384]{1,0:T(8,128)(2,1)S(1)} collective-permute-done((bf16[768,384]{1,0:T(8,128)(2,1)S(1)}, bf16[768,384]{1,0:T(8,128)(2,1)S(1)}, u32[]{:S(2)}, u32[]{:S(2)}) %collective-permute-start.31) | collective-permute-done | bytes 589856 | tf_op jit(solution)/shard_map/ppermute | solution.py:77
  138.5 1.0 fusion.6
  139.5 9.9 %collective-permute-done.26 = bf16[384,768]{1,0:T(8,128)(2,1)S(1)} collective-permute-done((bf16[384,768]{1,0:T(8,128)(2,1)S(1)}, bf16[384,768]{1,0:T(8,128)(2,1)S(1)}, u32[]{:S(2)}, u32[]{:S(2)}) %collective-permute-start.26) | collective-permute-done | bytes 589856 | tf_op jit(solution)/shard_map/ppermute | solution.py:77
  (100 shorter events, 28.9 us)
Async XLA Ops:
  0.6 32.7 %collective-permute-start = (bf16[128,1536]{1,0:T(8,128)(2,1)}, bf16[128,1536]{1,0:T(8,128)(2,1)S(1)}, u32[]{:S(2)}, u32[]{:S(2)}) collective-permute-start(bf16[128,1536]{1,0:T(8,128)(2,1)} %param.6), channel_id=1, source_target_pairs={{0,2},{1,3},{2,4},{3,5},{4,6},{5,7},{6,0},{7,1},{8,10},{9,11},{10,... | collective-permute-start | bytes 1179656 | tf_op jit(solution)/shard_map/ppermute | solution.py:74
  3.7 27.7 %collective-permute-start.5 = (bf16[128,1536]{1,0:T(8,128)(2,1)}, bf16[128,1536]{1,0:T(8,128)(2,1)}, u32[]{:S(2)}, u32[]{:S(2)}) collective-permute-start(bf16[128,1536]{1,0:T(8,128)(2,1)} %param.6), channel_id=1, source_target_pairs={{0,1},{1,0},{2,3},{3,2},{4,5},{5,4},{6,7},{7,6},{8,9},{9,8},{10,11... | collective-permute-start | bytes 1179656 | tf_op jit(solution)/shard_map/ppermute | solution.py:74
  4.5 3.5 %collective-permute-start.8 = (f32[128,8]{0,1:T(8,128)S(1)}, f32[128,8]{0,1:T(8,128)S(1)}, u32[]{:S(2)}, u32[]{:S(2)}) collective-permute-start(f32[128,8]{0,1:T(8,128)S(1)} %convert_multiply_fusion), channel_id=1, source_target_pairs={{0,1},{1,0},{2,3},{3,2},{4,5},{5,4},{6,7},{7,6},{8,9},{9,8},{10,11... | collective-permute-start | bytes 12296 | tf_op jit(solution)/shard_map/ppermute | solution.py:74
  5.0 22.6 %collective-permute-start.11 = (bf16[128,1536]{1,0:T(8,128)(2,1)}, bf16[128,1536]{1,0:T(8,128)(2,1)}, u32[]{:S(2)}, u32[]{:S(2)}) collective-permute-start(bf16[128,1536]{1,0:T(8,128)(2,1)} %param.7), channel_id=1, source_target_pairs={{0,1},{1,0},{2,3},{3,2},{4,5},{5,4},{6,7},{7,6},{8,9},{9,8},{10,11... | collective-permute-start | bytes 1179656 | tf_op jit(solution)/shard_map/ppermute | solution.py:74
  7.9 7.4 %collective-permute-start.10 = (f32[256,8]{0,1:T(8,128)S(1)}, f32[256,8]{0,1:T(8,128)S(1)}, u32[]{:S(2)}, u32[]{:S(2)}) collective-permute-start(f32[256,8]{0,1:T(8,128)S(1)} %pad_maximum_fusion), channel_id=1, source_target_pairs={{0,6},{1,7},{2,0},{3,1},{4,2},{5,3},{6,4},{7,5},{8,14},{9,15},{10,... | collective-permute-start | bytes 24584 | tf_op jit(solution)/shard_map/ppermute | solution.py:74
  10.1 5.8 %collective-permute-start.9 = (f32[256,8]{0,1:T(8,128)S(1)}, f32[256,8]{0,1:T(8,128)S(1)}, u32[]{:S(2)}, u32[]{:S(2)}) collective-permute-start(f32[256,8]{0,1:T(8,128)S(1)} %pad_maximum_fusion), channel_id=1, source_target_pairs={{0,2},{1,3},{2,4},{3,5},{4,6},{5,7},{6,0},{7,1},{8,10},{9,11},{10,... | collective-permute-start | bytes 24584 | tf_op jit(solution)/shard_map/ppermute | solution.py:74
  15.4 14.7 %collective-permute-start.12 = (bf16[128,1536]{1,0:T(8,128)(2,1)}, bf16[128,1536]{1,0:T(8,128)(2,1)S(1)}, u32[]{:S(2)}, u32[]{:S(2)}) collective-permute-start(bf16[128,1536]{1,0:T(8,128)(2,1)} %param.7), channel_id=1, source_target_pairs={{0,2},{1,3},{2,4},{3,5},{4,6},{5,7},{6,0},{7,1},{8,10},{9,11},{10,... | collective-permute-start | bytes 1179656 | tf_op jit(solution)/shard_map/ppermute | solution.py:74
  15.9 8.1 %collective-permute-start.22 = (f32[256,8]{0,1:T(8,128)S(1)}, f32[256,8]{0,1:T(8,128)S(1)}, u32[]{:S(2)}, u32[]{:S(2)}) collective-permute-start(f32[256,8]{0,1:T(8,128)S(1)} %pad_maximum_fusion), channel_id=1, source_target_pairs={{0,4},{1,5},{2,6},{3,7},{4,0},{5,1},{6,2},{7,3},{8,12},{9,13},{10,... | collective-permute-start | bytes 24584 | tf_op jit(solution)/shard_map/ppermute | solution.py:74
  24.1 21.1 %collective-permute-start.2 = (bf16[128,1536]{1,0:T(8,128)(2,1)}, bf16[128,1536]{1,0:T(8,128)(2,1)S(1)}, u32[]{:S(2)}, u32[]{:S(2)}) collective-permute-start(bf16[128,1536]{1,0:T(8,128)(2,1)} %param.6), channel_id=1, source_target_pairs={{0,6},{1,7},{2,0},{3,1},{4,2},{5,3},{6,4},{7,5},{8,14},{9,15},{10,... | collective-permute-start | bytes 1179656 | tf_op jit(solution)/shard_map/ppermute | solution.py:74
  27.6 17.0 %collective-permute-start.14 = (bf16[128,1536]{1,0:T(8,128)(2,1)}, bf16[128,1536]{1,0:T(8,128)(2,1)S(1)}, u32[]{:S(2)}, u32[]{:S(2)}) collective-permute-start(bf16[128,1536]{1,0:T(8,128)(2,1)} %param.7), channel_id=1, source_target_pairs={{0,6},{1,7},{2,0},{3,1},{4,2},{5,3},{6,4},{7,5},{8,14},{9,15},{10,... | collective-permute-start | bytes 1179656 | tf_op jit(solution)/shard_map/ppermute | solution.py:74
  30.1 33.2 %collective-permute-start.19 = (bf16[384,768]{1,0:T(8,128)(2,1)S(1)}, bf16[384,768]{1,0:T(8,128)(2,1)S(1)}, u32[]{:S(2)}, u32[]{:S(2)}) collective-permute-start(bf16[384,768]{1,0:T(8,128)(2,1)S(1)} %bitcast.44), channel_id=1, source_target_pairs={{0,8},{8,0},{16,24},{24,16},{1,9},{9,1},{17,25},{25,17},{2,10},{10... | collective-permute-start | bytes 1769480 | tf_op jit(solution)/shard_map/ppermute | solution.py:77
  31.5 13.2 %collective-permute-start.13 = (bf16[128,1536]{1,0:T(8,128)(2,1)S(1)}, bf16[128,1536]{1,0:T(8,128)(2,1)S(1)}, u32[]{:S(2)}, u32[]{:S(2)}) collective-permute-start(bf16[128,1536]{1,0:T(8,128)(2,1)S(1)} %collective-permute-done.12), channel_id=1, source_target_pairs={{0,1},{1,0},{2,3},{3,2},{4,5},{5,4},{6,7},{7,6},{8,9},{9,8},{10,11... | collective-permute-start | bytes 1179656 | tf_op jit(solution)/shard_map/ppermute | solution.py:74
  33.3 34.4 %collective-permute-start.20 = (bf16[384,768]{1,0:T(8,128)(2,1)S(1)}, bf16[384,768]{1,0:T(8,128)(2,1)S(1)}, u32[]{:S(2)}, u32[]{:S(2)}) collective-permute-start(bf16[384,768]{1,0:T(8,128)(2,1)S(1)} %bitcast.45), channel_id=1, source_target_pairs={{0,16},{8,24},{16,0},{24,8},{1,17},{9,25},{17,1},{25,9},{2,18},{10... | collective-permute-start | bytes 1769480 | tf_op jit(solution)/shard_map/ppermute | solution.py:77
  44.6 2.9 %collective-permute-start.6 = (bf16[128,1536]{1,0:T(8,128)(2,1)S(1)}, bf16[128,1536]{1,0:T(8,128)(2,1)S(1)}, u32[]{:S(2)}, u32[]{:S(2)}) collective-permute-start(bf16[128,1536]{1,0:T(8,128)(2,1)S(1)} %collective-permute-done), channel_id=1, source_target_pairs={{0,1},{1,0},{2,3},{3,2},{4,5},{5,4},{6,7},{7,6},{8,9},{9,8},{10,11... | collective-permute-start | bytes 1179656 | tf_op jit(solution)/shard_map/ppermute | solution.py:74
  44.6 2.3 %collective-permute-start.15 = (bf16[128,1536]{1,0:T(8,128)(2,1)S(1)}, bf16[128,1536]{1,0:T(8,128)(2,1)S(1)}, u32[]{:S(2)}, u32[]{:S(2)}) collective-permute-start(bf16[128,1536]{1,0:T(8,128)(2,1)S(1)} %collective-permute-done.14), channel_id=1, source_target_pairs={{0,1},{1,0},{2,3},{3,2},{4,5},{5,4},{6,7},{7,6},{8,9},{9,8},{10,11... | collective-permute-start | bytes 1179656 | tf_op jit(solution)/shard_map/ppermute | solution.py:74
  45.2 5.3 %collective-permute-start.1 = (bf16[128,1536]{1,0:T(8,128)(2,1)S(1)}, bf16[128,1536]{1,0:T(8,128)(2,1)S(1)}, u32[]{:S(2)}, u32[]{:S(2)}) collective-permute-start(bf16[128,1536]{1,0:T(8,128)(2,1)S(1)} %collective-permute-done), channel_id=1, source_target_pairs={{2,4},{3,5},{4,6},{5,7},{10,12},{11,13},{12,14},{13,15},{18,20},{1... | collective-permute-start | bytes 1179656 | tf_op jit(solution)/shard_map/ppermute | solution.py:74
  46.9 2.2 %collective-permute-start.7 = (bf16[128,1536]{1,0:T(8,128)(2,1)S(1)}, bf16[128,1536]{1,0:T(8,128)(2,1)S(1)}, u32[]{:S(2)}, u32[]{:S(2)}) collective-permute-start(bf16[128,1536]{1,0:T(8,128)(2,1)S(1)} %collective-permute-done.2), channel_id=1, source_target_pairs={{0,1},{1,0},{2,3},{3,2},{4,5},{5,4},{6,7},{7,6},{8,9},{9,8},{10,11... | collective-permute-start | bytes 1179656 | tf_op jit(solution)/shard_map/ppermute | solution.py:74
  47.6 13.4 %collective-permute-start.3 = (bf16[128,1536]{1,0:T(8,128)(2,1)S(1)}, bf16[128,1536]{1,0:T(8,128)(2,1)S(1)}, u32[]{:S(2)}, u32[]{:S(2)}) collective-permute-start(bf16[128,1536]{1,0:T(8,128)(2,1)S(1)} %collective-permute-done.2), channel_id=1, source_target_pairs={{2,0},{3,1},{4,2},{5,3},{10,8},{11,9},{12,10},{13,11},{18,16},{19,... | collective-permute-start | bytes 1179656 | tf_op jit(solution)/shard_map/ppermute | solution.py:74
  49.1 16.5 %collective-permute-start.17 = (bf16[768,384]{1,0:T(8,128)(2,1)S(1)}, bf16[768,384]{1,0:T(8,128)(2,1)S(1)}, u32[]{:S(2)}, u32[]{:S(2)}) collective-permute-start(bf16[768,384]{1,0:T(8,128)(2,1)S(1)} %bitcast.42), channel_id=1, source_target_pairs={{0,16},{8,24},{16,0},{24,8},{1,17},{9,25},{17,1},{25,9},{2,18},{10... | collective-permute-start | bytes 1769480 | tf_op jit(solution)/shard_map/ppermute | solution.py:77
  50.5 19.6 %collective-permute-start.16 = (bf16[768,384]{1,0:T(8,128)(2,1)S(1)}, bf16[768,384]{1,0:T(8,128)(2,1)S(1)}, u32[]{:S(2)}, u32[]{:S(2)}) collective-permute-start(bf16[768,384]{1,0:T(8,128)(2,1)S(1)} %bitcast.43), channel_id=1, source_target_pairs={{0,8},{8,0},{16,24},{24,16},{1,9},{9,1},{17,25},{25,17},{2,10},{10... | collective-permute-start | bytes 1769480 | tf_op jit(solution)/shard_map/ppermute | solution.py:77
  61.0 30.2 %collective-permute-start.23 = (bf16[128,1536]{1,0:T(8,128)(2,1)S(1)}, bf16[128,1536]{1,0:T(8,128)(2,1)S(1)}, u32[]{:S(2)}, u32[]{:S(2)}) collective-permute-start(bf16[128,1536]{1,0:T(8,128)(2,1)S(1)} %collective-permute-done.12), channel_id=1, source_target_pairs={{2,4},{3,5},{4,6},{5,7},{10,12},{11,13},{12,14},{13,15},{18,20},{1... | collective-permute-start | bytes 1179656 | tf_op jit(solution)/shard_map/ppermute | solution.py:74
  63.3 27.9 %collective-permute-start.24 = (bf16[128,1536]{1,0:T(8,128)(2,1)S(1)}, bf16[128,1536]{1,0:T(8,128)(2,1)S(1)}, u32[]{:S(2)}, u32[]{:S(2)}) collective-permute-start(bf16[128,1536]{1,0:T(8,128)(2,1)S(1)} %collective-permute-done.14), channel_id=1, source_target_pairs={{2,0},{3,1},{4,2},{5,3},{10,8},{11,9},{12,10},{13,11},{18,16},{19,... | collective-permute-start | bytes 1179656 | tf_op jit(solution)/shard_map/ppermute | solution.py:74
  65.6 14.8 %collective-permute-start.21 = (bf16[384,768]{1,0:T(8,128)(2,1)S(1)}, bf16[384,768]{1,0:T(8,128)(2,1)S(1)}, u32[]{:S(2)}, u32[]{:S(2)}) collective-permute-start(bf16[384,768]{1,0:T(8,128)(2,1)S(1)} %collective-permute-done.19), channel_id=1, source_target_pairs={{0,16},{8,24},{16,0},{24,8},{1,17},{9,25},{17,1},{25,9},{2,18},{10... | collective-permute-start | bytes 1769480 | tf_op jit(solution)/shard_map/ppermute | solution.py:77
  67.7 14.5 %collective-permute-start.18 = (bf16[768,384]{1,0:T(8,128)(2,1)S(1)}, bf16[768,384]{1,0:T(8,128)(2,1)S(1)}, u32[]{:S(2)}, u32[]{:S(2)}) collective-permute-start(bf16[768,384]{1,0:T(8,128)(2,1)S(1)} %collective-permute-done.17), channel_id=1, source_target_pairs={{0,8},{8,0},{16,24},{24,16},{1,9},{9,1},{17,25},{25,17},{2,10},{10... | collective-permute-start | bytes 1769480 | tf_op jit(solution)/shard_map/ppermute | solution.py:77
  70.1 18.7 %collective-permute-start.4 = (bf16[128,1536]{1,0:T(8,128)(2,1)S(1)}, bf16[128,1536]{1,0:T(8,128)(2,1)S(1)}, u32[]{:S(2)}, u32[]{:S(2)}) collective-permute-start(bf16[128,1536]{1,0:T(8,128)(2,1)S(1)} %broadcast_select_fusion.1), channel_id=1, source_target_pairs={{0,1},{1,0},{2,3},{3,2},{4,5},{5,4},{6,7},{7,6},{8,9},{9,8},{10,11... | collective-permute-start | bytes 1179656 | tf_op jit(solution)/shard_map/ppermute | solution.py:74
  91.3 1.8 %collective-permute-start.25 = (bf16[128,1536]{1,0:T(8,128)(2,1)S(1)}, bf16[128,1536]{1,0:T(8,128)(2,1)S(1)}, u32[]{:S(2)}, u32[]{:S(2)}) collective-permute-start(bf16[128,1536]{1,0:T(8,128)(2,1)S(1)} %broadcast_select_fusion), channel_id=1, source_target_pairs={{0,1},{1,0},{2,3},{3,2},{4,5},{5,4},{6,7},{7,6},{8,9},{9,8},{10,11... | collective-permute-start | bytes 1179656 | tf_op jit(solution)/shard_map/ppermute | solution.py:74
  94.0 32.2 %collective-permute-start.29 = (bf16[768,384]{1,0:T(8,128)(2,1)S(1)}, bf16[768,384]{1,0:T(8,128)(2,1)S(1)}, u32[]{:S(2)}, u32[]{:S(2)}) collective-permute-start(bf16[768,384]{1,0:T(8,128)(2,1)S(1)} %fusion), channel_id=1, source_target_pairs={{0,8},{8,0},{16,24},{24,16},{1,9},{9,1},{17,25},{25,17},{2,10},{10... | collective-permute-start | bytes 1769480 | tf_op jit(solution)/shard_map/ppermute | solution.py:77
  96.0 26.1 %collective-permute-start.30 = (bf16[768,384]{1,0:T(8,128)(2,1)S(1)}, bf16[768,384]{1,0:T(8,128)(2,1)S(1)}, u32[]{:S(2)}, u32[]{:S(2)}) collective-permute-start(bf16[768,384]{1,0:T(8,128)(2,1)S(1)} %fusion.1), channel_id=1, source_target_pairs={{0,8},{8,0},{16,24},{24,16},{1,9},{9,1},{17,25},{25,17},{2,10},{10... | collective-permute-start | bytes 1769480 | tf_op jit(solution)/shard_map/ppermute | solution.py:77
  98.9 25.6 %collective-permute-start.27 = (bf16[384,768]{1,0:T(8,128)(2,1)S(1)}, bf16[384,768]{1,0:T(8,128)(2,1)S(1)}, u32[]{:S(2)}, u32[]{:S(2)}) collective-permute-start(bf16[384,768]{1,0:T(8,128)(2,1)S(1)} %add_convert_fusion.4), channel_id=1, source_target_pairs={{0,16},{8,24},{16,0},{24,8},{1,17},{9,25},{17,1},{25,9},{2,18},{10... | collective-permute-start | bytes 1769480 | tf_op jit(solution)/shard_map/ppermute | solution.py:77
  122.2 16.3 %collective-permute-start.31 = (bf16[768,384]{1,0:T(8,128)(2,1)S(1)}, bf16[768,384]{1,0:T(8,128)(2,1)S(1)}, u32[]{:S(2)}, u32[]{:S(2)}) collective-permute-start(bf16[768,384]{1,0:T(8,128)(2,1)S(1)} %add_convert_fusion.1), channel_id=1, source_target_pairs={{0,16},{8,24},{16,0},{24,8},{1,17},{9,25},{17,1},{25,9},{2,18},{10... | collective-permute-start | bytes 1769480 | tf_op jit(solution)/shard_map/ppermute | solution.py:77
  123.2 26.3 %collective-permute-start.26 = (bf16[384,768]{1,0:T(8,128)(2,1)S(1)}, bf16[384,768]{1,0:T(8,128)(2,1)S(1)}, u32[]{:S(2)}, u32[]{:S(2)}) collective-permute-start(bf16[384,768]{1,0:T(8,128)(2,1)S(1)} %add_convert_fusion.5), channel_id=1, source_target_pairs={{0,16},{8,24},{16,0},{24,8},{1,17},{9,25},{17,1},{25,9},{2,18},{10... | collective-permute-start | bytes 1769480 | tf_op jit(solution)/shard_map/ppermute | solution.py:77
  124.7 24.8 %collective-permute-start.28 = (bf16[384,768]{1,0:T(8,128)(2,1)S(1)}, bf16[384,768]{1,0:T(8,128)(2,1)S(1)}, u32[]{:S(2)}, u32[]{:S(2)}) collective-permute-start(bf16[384,768]{1,0:T(8,128)(2,1)S(1)} %add_convert_fusion.3), channel_id=1, source_target_pairs={{0,8},{8,0},{16,24},{24,16},{1,9},{9,1},{17,25},{25,17},{2,10},{10... | collective-permute-start | bytes 1769480 | tf_op jit(solution)/shard_map/ppermute | solution.py:77
  (3 other events, 33.4 us)

commit v2 on v1

--- a/solution.py
+++ b/solution.py
@@ -1,6 +1,10 @@
+import functools
+
 import jax
 import jax.numpy as jnp
 from jax import lax
+from jax.experimental import pallas as pl
+from jax.experimental.pallas import tpu as pltpu
 from jax.sharding import PartitionSpec as P
 
 
@@ -59,6 +63,247 @@
     return [(i, i ^ bits) for i in range(count)]
 
 
+MIB = 1 << 20
+
+
+def pick_gate(table_ref, part, expert):
+    table = table_ref[:, part * SHARD : (part + 1) * SHARD]
+    mine = lax.broadcasted_iota(jnp.int32, table.shape, 0) == expert
+    row = jnp.sum(jnp.where(mine, table, 0.0), axis=0, keepdims=True)
+    return jnp.transpose(jnp.broadcast_to(row, (SHARD, SHARD)))
+
+
+SHARD = 128
+
+
+def scale_rows(gate, rows):
+    wide = jnp.concatenate([gate] * (rows.shape[1] // gate.shape[1]), axis=1)
+    return (wide * rows.astype(F32)).astype(BF16)
+
+
+def dot_rows(left, right):
+    return jnp.dot(left, right, preferred_element_type=F32)
+
+
+def dot_last(left, right):
+    return lax.dot_general(left, right, LAST, preferred_element_type=F32)
+
+
+def dot_first(left, right):
+    return lax.dot_general(left, right, FIRST, preferred_element_type=F32)
+
+
+def most_kernel(block, *refs):
+    count = 6
+    xs, gs, tables = refs[0:count], refs[count : 2 * count], refs[12:15]
+    ups, downs = refs[15:19], refs[19:23]
+    up_out, down_out = refs[23:27], refs[27:31]
+    x, g, up, down, act, back, up_stage, down_stage, x_sem, g_sem, w_sem, o_sem = refs[31:]
+    me = lax.axis_index("dp")
+    expert = lax.axis_index("expert")
+    x_copies, g_copies, w_copies = [], [], []
+    for i in range(4):
+        w_copies.append(pltpu.make_async_copy(ups[i], up.at[pl.ds(i * block, block), :], w_sem.at[i]))
+    for i in range(4):
+        w_copies.append(pltpu.make_async_copy(downs[i], down.at[:, pl.ds(i * block, block)], w_sem.at[4 + i]))
+    for i in range(count):
+        for bits in range(4):
+            where = pl.multiple_of((me ^ bits) * block, block)
+            rows, cols = pl.ds(i * SHARD, SHARD), pl.ds(bits * block, block)
+            x_copies.append(pltpu.make_async_copy(xs[i].at[:, pl.ds(where, block)], x.at[rows, cols], x_sem.at[i, bits]))
+            g_copies.append(pltpu.make_async_copy(gs[i].at[:, pl.ds(where, block)], g.at[rows, cols], g_sem.at[i, bits]))
+    for c in x_copies[:8] + w_copies[:4] + g_copies[:8] + w_copies[4:]:
+        c.start()
+    for c in x_copies[8:] + g_copies[8:]:
+        c.start()
+    for c in w_copies[:4]:
+        c.wait()
+    for pair in range(count // 2):
+        rows = slice(pair * 2 * SHARD, (pair + 1) * 2 * SHARD)
+        for c in x_copies[pair * 8 : pair * 8 + 8]:
+            c.wait()
+        pre = dot_rows(x[rows, :], up[...])
+        sig = jax.nn.sigmoid(pre)
+        act[rows, :] = (pre * sig).astype(BF16)
+        slope = sig * (1.0 + pre * (1.0 - sig))
+        for c in g_copies[pair * 8 : pair * 8 + 8]:
+            c.wait()
+        for half in range(2):
+            own = slice((pair * 2 + half) * SHARD, (pair * 2 + half + 1) * SHARD)
+            g[own, :] = scale_rows(pick_gate(tables[pair], half, expert), g[own, :])
+        if pair == 0:
+            for c in w_copies[4:]:
+                c.wait()
+        back[rows, :] = (dot_last(g[rows, :], down[...]) * slope).astype(BF16)
+    outs = []
+    for n, bits in enumerate((3, 2, 1, 0)):
+        slot = n % 2
+        if n >= 2:
+            outs[2 * (n - 2)].wait()
+            outs[2 * (n - 2) + 1].wait()
+        cols = slice(bits * block, (bits + 1) * block)
+        up_stage[slot] = dot_first(x[:, cols], back[...])
+        outs.append(pltpu.make_async_copy(up_stage.at[slot], up_out[bits], o_sem.at[bits]))
+        outs[-1].start()
+        down_stage[slot] = dot_first(act[...], g[:, cols])
+        outs.append(pltpu.make_async_copy(down_stage.at[slot], down_out[bits], o_sem.at[4 + bits]))
+        outs[-1].start()
+    for c in outs[4:]:
+        c.wait()
+
+
+def last_forward_kernel(block, *refs):
+    shards, ups = refs[0:4], refs[4:8]
+    x_out, act_out, slope_out = refs[8:11]
+    parts, up, sems = refs[11:]
+    me = lax.axis_index("dp")
+    copies = []
+    for i in range(4):
+        for bits in range(4):
+            where = pl.multiple_of((me ^ bits) * block, block)
+            copies.append(
+                pltpu.make_async_copy(
+                    shards[i].at[:, pl.ds(where, block)], parts.at[i, :, pl.ds(bits * block, block)], sems.at[i, bits]
+                )
+            )
+    for i in range(4):
+        copies.append(pltpu.make_async_copy(ups[i], up.at[pl.ds(i * block, block), :], sems.at[4, i]))
+    for c in copies:
+        c.start()
+    for c in copies:
+        c.wait()
+    x_out[:SHARD, :] = parts[0] + parts[1]
+    x_out[SHARD:, :] = parts[2] + parts[3]
+    pre = dot_rows(x_out[...], up[...])
+    sig = jax.nn.sigmoid(pre)
+    act_out[...] = (pre * sig).astype(BF16)
+    slope_out[...] = sig * (1.0 + pre * (1.0 - sig))
+
+
+def last_backward_kernel(block, *refs):
+    shards, downs = refs[0:4], refs[4:8]
+    table, x_ref, act, slope, up_acc, down_acc = refs[8:14]
+    up_far, down_far, back, g = refs[14:18]
+    parts, down, up_part, down_part, x_part, sems = refs[18:]
+    me = lax.axis_index("dp")
+    expert = lax.axis_index("expert")
+    copies = []
+    for i in range(4):
+        for bits in range(4):
+            where = pl.multiple_of((me ^ bits) * block, block)
+            copies.append(
+                pltpu.make_async_copy(
+                    shards[i].at[:, pl.ds(where, block)], parts.at[i, :, pl.ds(bits * block, block)], sems.at[i, bits]
+                )
+            )
+    down_copy = pltpu.make_async_copy(down_acc, down_part, sems.at[5, 0])
+    up_copy = pltpu.make_async_copy(up_acc, up_part, sems.at[5, 1])
+    x_copy = pltpu.make_async_copy(x_ref.at[:, pl.ds(3 * block, block)], x_part, sems.at[5, 2])
+    w_copies = []
+    for i in range(4):
+        w_copies.append(pltpu.make_async_copy(downs[i], down.at[:, pl.ds(i * block, block)], sems.at[4, i]))
+    for c in copies + [down_copy] + w_copies + [x_copy, up_copy]:
+        c.start()
+    for c in copies:
+        c.wait()
+    for half in range(2):
+        own = slice(half * SHARD, (half + 1) * SHARD)
+        g[own, :] = scale_rows(pick_gate(table, half, expert), parts[2 * half] + parts[2 * half + 1])
+    down_copy.wait()
+    far = slice(3 * block, 4 * block)
+    down_far[...] = (dot_first(act[...], g[:, far]) + down_part[...]).astype(BF16)
+    for c in w_copies:
+        c.wait()
+    back[...] = (dot_last(g[...], down[...]) * slope[...]).astype(BF16)
+    x_copy.wait()
+    up_copy.wait()
+    up_far[...] = (dot_first(x_part[...], back[...]) + up_part[...]).astype(BF16)
+
+
+ANY = pl.BlockSpec(memory_space=pl.ANY)
+VMEM = pl.BlockSpec(memory_space=pltpu.VMEM)
+
+
+def most_of(xs, gs, tables, ups, downs):
+    block, hidden = ups[0].shape
+    rows, width = 6 * SHARD, 4 * block
+    out = [jax.ShapeDtypeStruct((block, hidden), F32)] * 4 + [jax.ShapeDtypeStruct((hidden, block), F32)] * 4
+    got = pl.pallas_call(
+        functools.partial(most_kernel, block),
+        out_shape=out,
+        in_specs=[ANY] * 12 + [VMEM] * 3 + [ANY] * 8,
+        out_specs=[ANY] * 8,
+        scratch_shapes=[
+            pltpu.VMEM((rows, width), BF16),
+            pltpu.VMEM((rows, width), BF16),
+            pltpu.VMEM((width, hidden), BF16),
+            pltpu.VMEM((hidden, width), BF16),
+            pltpu.VMEM((rows, hidden), BF16),
+            pltpu.VMEM((rows, hidden), BF16),
+            pltpu.VMEM((2, block, hidden), F32),
+            pltpu.VMEM((2, hidden, block), F32),
+            pltpu.SemaphoreType.DMA((6, 4)),
+            pltpu.SemaphoreType.DMA((6, 4)),
+            pltpu.SemaphoreType.DMA((8,)),
+            pltpu.SemaphoreType.DMA((8,)),
+        ],
+        compiler_params=pltpu.CompilerParams(vmem_limit_bytes=32 * MIB),
+        cost_estimate=pl.CostEstimate(flops=8 * rows * width * hidden, bytes_accessed=20 * MIB, transcendentals=rows * hidden),
+        name="most",
+    )(*xs, *gs, *tables, *ups, *downs)
+    return got[:4], got[4:]
+
+
+def last_forward(shards, ups):
+    block, hidden = ups[0].shape
+    rows, width = 2 * SHARD, 4 * block
+    return pl.pallas_call(
+        functools.partial(last_forward_kernel, block),
+        out_shape=[
+            jax.ShapeDtypeStruct((rows, width), BF16),
+            jax.ShapeDtypeStruct((rows, hidden), BF16),
+            jax.ShapeDtypeStruct((rows, hidden), F32),
+        ],
+        in_specs=[ANY] * 8,
+        out_specs=[VMEM] * 3,
+        scratch_shapes=[
+            pltpu.VMEM((4, SHARD, width), BF16),
+            pltpu.VMEM((width, hidden), BF16),
+            pltpu.SemaphoreType.DMA((5, 4)),
+        ],
+        compiler_params=pltpu.CompilerParams(vmem_limit_bytes=16 * MIB),
+        cost_estimate=pl.CostEstimate(flops=2 * rows * width * hidden, bytes_accessed=5 * MIB, transcendentals=rows * hidden),
+        name="last_forward",
+    )(*shards, *ups)
+
+
+def last_backward(shards, downs, table, x, act, slope, up_acc, down_acc):
+    hidden, block = downs[0].shape
+    rows, width = 2 * SHARD, 4 * block
+    return pl.pallas_call(
+        functools.partial(last_backward_kernel, block),
+        out_shape=[
+            jax.ShapeDtypeStruct((block, hidden), BF16),
+            jax.ShapeDtypeStruct((hidden, block), BF16),
+            jax.ShapeDtypeStruct((rows, hidden), BF16),
+            jax.ShapeDtypeStruct((rows, width), BF16),
+        ],
+        in_specs=[ANY] * 8 + [VMEM, ANY, VMEM, VMEM, ANY, ANY],
+        out_specs=[VMEM] * 4,
+        scratch_shapes=[
+            pltpu.VMEM((4, SHARD, width), BF16),
+            pltpu.VMEM((hidden, width), BF16),
+            pltpu.VMEM((block, hidden), F32),
+            pltpu.VMEM((hidden, block), F32),
+            pltpu.VMEM((rows, block), BF16),
+            pltpu.SemaphoreType.DMA((6, 4)),
+        ],
+        compiler_params=pltpu.CompilerParams(vmem_limit_bytes=20 * MIB),
+        cost_estimate=pl.CostEstimate(flops=4 * rows * width * hidden, bytes_accessed=8 * MIB, transcendentals=0),
+        name="last_backward",
+    )(*shards, *downs, table, x, act, slope, up_acc, down_acc)
+
+
 def dense_shards(tokens, grad_out, expert_ids, gate_q, w_up, w_down):
     return dense_body(tokens, grad_out, expert_ids, gate_q, w_up[0], w_down[0])
 
@@ -66,9 +311,6 @@
 def dense_body(tokens, grad_out, expert_ids, gate_q, w_up, w_down):
     devices = lax.axis_size("expert")
     block, _ = w_up.shape
-    dp_index = lax.axis_index("dp")
-    ex_index = lax.axis_index("expert")
-    upper = ex_index >= devices // 2
 
     def ex(value, perm):
         return lax.ppermute(value, "expert", perm)
@@ -94,9 +336,9 @@
     down_x = dp(w_down, 1)
 
     experts = jnp.arange(devices, dtype=jnp.int32)
-    named = expert_ids[:, :, None] == experts[None, None, :]
-    gate_table = jnp.sum(jnp.where(named, gate_q[:, :, None], 0), axis=1).astype(F32) * (1.0 / 65536.0)
-    c0 = jnp.concatenate([gate_table, ex(gate_table, swap)], axis=0)
+    named = expert_ids.T[None, :, :] == experts[:, None, None]
+    gate_table = jnp.sum(jnp.where(named, gate_q.T[None, :, :], 0), axis=1).astype(F32) * (1.0 / 65536.0)
+    c0 = jnp.concatenate([gate_table, ex(gate_table, swap)], axis=1)
     c1 = ex(c0, ring(1))
     c2 = ex(c0, ring(2))
     c3 = ex(c0, ring(3))
@@ -113,72 +355,30 @@
     g2d = ex(g3, down_mid)
     g1b = ex(g1, swap)
     g3b = ex(g3, swap)
-
-    pick = (experts == ex_index).astype(F32)
+    t2ub = ex(t2u, swap)
+    t2db = ex(t2d, swap)
+    g2ub = ex(g2u, swap)
+    g2db = ex(g2d, swap)
+
     ups = (w_up, up_x, up_y, up_d)
     downs = (w_down, down_x, down_y, down_d)
-
-    def gate_of(*tables):
-        table = jnp.concatenate(tables, axis=0)
-        return jnp.sum(table * pick, axis=1)
-
-    def scaled(gate, g):
-        return (gate[:, None] * g.astype(F32)).astype(BF16)
+    up_acc, down_acc = most_of((tokens, t0b, t1, t1b, t3, t3b), (grad_out, g0b, g1, g1b, g3, g3b), (c0, c1, c3), ups, downs)
+    x_c, act_c, slope_c = last_forward((t2u, t2d, t2ub, t2db), ups)
+    up_first, down_first, back_c, g_c = last_backward(
+        (g2u, g2d, g2ub, g2db), downs, c2, x_c, act_c, slope_c, up_acc[3], down_acc[3]
+    )
 
     def columns(rows, bits):
-        return lax.dynamic_slice(rows, (0, (dp_index ^ bits) * block), (rows.shape[0], block))
-
-    def forward_part(x, bits, total):
-        part = jnp.dot(columns(x, bits), ups[bits], preferred_element_type=F32)
-        return part if total is None else total + part
-
-    def backward_part(g, bits, total):
-        part = lax.dot_general(columns(g, bits), downs[bits], LAST, preferred_element_type=F32)
-        return part if total is None else total + part
-
-    def outer(left, right):
-        return lax.dot_general(left, right, FIRST, preferred_element_type=F32)
-
-    x_ab = jnp.concatenate([tokens, t0b, t1, t1b, t3, t3b], axis=0)
-    pre = None
-    for bits in (0, 1, 2, 3):
-        pre = forward_part(x_ab, bits, pre)
-    g_ab = scaled(gate_of(c0, c1, c3), jnp.concatenate([grad_out, g0b, g1, g1b, g3, g3b], axis=0))
-    act_grad = None
-    for bits in (0, 1, 2, 3):
-        act_grad = backward_part(g_ab, bits, act_grad)
-    act_ab = jax.nn.silu(pre).astype(BF16)
-    back_ab = (act_grad * silu_slope(pre)).astype(BF16)
-    up_acc = [outer(columns(x_ab, bits), back_ab) for bits in range(4)]
-    down_acc = [outer(act_ab, columns(g_ab, bits)) for bits in range(4)]
-    t2 = jnp.where(upper, t2u, t2d)
-    t2b = ex(t2, swap)
-    x_c = jnp.concatenate([t2, t2b], axis=0)
-    pre_c = None
-    for bits in (0, 1, 2, 3):
-        pre_c = forward_part(x_c, bits, pre_c)
-    act_c = jax.nn.silu(pre_c).astype(BF16)
-    slope_c = silu_slope(pre_c)
-    gate_c = gate_of(c2)
-    up_acc, down_acc, act_c, slope_c, gate_c, g2u, g2d = lax.optimization_barrier(
-        (up_acc, down_acc, act_c, slope_c, gate_c, g2u, g2d)
-    )
-    g2 = jnp.where(upper, g2u, g2d)
-    g2b = ex(g2, swap)
-    g_c = scaled(gate_c, jnp.concatenate([g2, g2b], axis=0))
-    act_grad_c = None
-    for bits in (0, 1, 2, 3):
-        act_grad_c = backward_part(g_c, bits, act_grad_c)
-    back_c = (act_grad_c * slope_c).astype(BF16)
+        return rows[:, bits * block : (bits + 1) * block]
 
     def up_block(bits):
-        return outer(columns(x_c, bits), back_c) + up_acc[bits]
+        return dot_first(columns(x_c, bits), back_c) + up_acc[bits]
 
     def down_block(bits):
-        return outer(act_c, columns(g_c, bits)) + down_acc[bits]
-
-    down_far = dp(down_block(3).astype(BF16), 1)
-    up_far = dp(up_block(3).astype(BF16), 2)
+        return dot_first(act_c, columns(g_c, bits)) + down_acc[bits]
+
+    down_far = dp(down_first, 1)
+    up_far = dp(up_first, 2)
     up_near = dp(up_block(2).astype(BF16), 2)
     down_near = dp(down_block(1).astype(BF16), 1)
     up_side, down_side = up_block(1), down_block(2)
@@ -195,7 +395,7 @@
     devices = lax.axis_size("expert")
     token_count, top_count = expert_ids.shape
     capacity = max(2, token_count * top_count * 3 // (2 * devices))
-    if 2 * capacity >= token_count and devices == 8 and lax.axis_size("dp") == 4:
+    if 2 * capacity >= token_count and devices == 8 and lax.axis_size("dp") == 4 and token_count == SHARD:
         return dense_shards(tokens, grad_out, expert_ids, gate_q, w_up, w_down)
     return sparse_shards(tokens, grad_out, expert_ids, gate_q, w_up, w_down, capacity)
 

time: 151 us -> 165 us (1.093)
  Pallas kernels: 0 us -> 21.8 us
  matrix products: 19.5 us -> 2.25 us
  waiting for transfers between devices: 85.4 us -> 92.6 us
  starting transfers between devices: 33.4 us -> 40.1 us
  local copies, waits for them, and re-layouts: 6.59 us -> 4.12 us
    pallas_call x0 -> x3, Pallas kernels: none -> 21.8 us  [the longest x1 16.4 us: most_of(): pl.pallas_call(functools.partial(most_kernel, block), out_shape=out, in_s...]
    dot_general x32 -> x6, matrix products: 19.5 us -> 2.25 us  [dot_first(): return lax.dot_general(left, right, FIRST, preferred_element_type=F32)]
    ppermute x20 -> x22, starting transfers between devices: 18.1 us -> 24.7 us  [ex(): return lax.ppermute(value, 'expert', perm)]
    ppermute x12, waiting for transfers between devices: 53 us -> 58.2 us  [dp(): return lax.ppermute(value, 'dp', xor_perm(4, bits))]
    unnamed x16 -> x8, local copies, waits for them, and re-layouts: 6.54 us -> 4.12 us
    ppermute x20 -> x22, waiting for transfers between devices: 32.4 us -> 34.4 us  [ex(): return lax.ppermute(value, 'expert', perm)]
  transfers between devices with their start and end apart: 32 -> 34, of which waited for: 11 -> 12; matrix products, arithmetic and copies ran while one was open for 19% -> 2% of each run, Pallas kernels for 0% -> 11%
where the time goes in v2:
time: 165 us
  waiting for transfers between devices  92.6 us (56%)
  starting transfers between devices  40.1 us (24%)
  Pallas kernels  21.8 us (13%)
  local copies, waits for them, and re-layouts  4.12 us (2%)
  other arithmetic  3.05 us (2%)
  matrix products  2.25 us (1%)
    ppermute x12, waiting for transfers between devices, dp(): return lax.ppermute(value, 'dp', xor_perm(4, bits))  58.2 us
    ppermute x22, waiting for transfers between devices, ex(): return lax.ppermute(value, 'expert', perm)  34.4 us
    ppermute x22, starting transfers between devices, ex(): return lax.ppermute(value, 'expert', perm)  24.7 us
    pallas_call x1, Pallas kernels, most_of(): pl.pallas_call(functools.partial(most_kernel, block), out_shape=out, in_s...  16.4 us
    ppermute x12, starting transfers between devices, dp(): return lax.ppermute(value, 'dp', xor_perm(4, bits))  15.4 us
    unnamed x8, local copies, waits for them, and re-layouts  4.12 us
    pallas_call x1, Pallas kernels, last_backward(): pl.pallas_call(functools.partial(last_backward_kernel, block), out_shape=...  3.57 us
  transfers between devices with their start and end apart: 34, of which 12 were waited for; matrix products, arithmetic and copies ran while one was open for 2% of the time, Pallas kernels for 11%

profile of v2, /device:TPU:0, one launch (start us, length us, event | category | flops | bytes accessed | tf_op | source)
XLA Modules:
  0.0 164.8 jit_solution(8663933229609179786)
XLA Ops:
  0.6 3.1 %collective-permute-start = (bf16[128,1536]{1,0:T(8,128)(2,1)}, bf16[128,1536]{1,0:T(8,128)(2,1)S(1)}, u32[]{:S(2)}, u32[]{:S(2)}) collective-permute-start(bf16[128,1536]{1,0:T(8,128)(2,1)} %refs_0_.1), channel_id=1, source_target_pairs={{0,2},{1,3},{2,4},{3,5},{4,6},{5,7},{6,0},{7,1},{8,10},{9,11},{10,... | collective-permute-start | bytes 1179656 | tf_op jit(solution)/shard_map/ppermute | solution.py:316
  4.5 1.2 collective-permute-done.18
  5.7 1.6 collective-permute-start.26
  7.3 2.2 %collective-permute-start.27 = (f32[8,256]{1,0:T(8,128)S(1)}, f32[8,256]{1,0:T(8,128)S(1)}, u32[]{:S(2)}, u32[]{:S(2)}) collective-permute-start(f32[8,256]{1,0:T(8,128)S(1)} %pad_maximum_fusion.refs_12_), channel_id=1, source_target_pairs={{0,6},{1,7},{2,0},{3,1},{4,2},{5,3},{6,4},{7,5},{8,14},{9,15},{10,... | collective-permute-start | bytes 24584 | tf_op jit(solution)/shard_map/ppermute | solution.py:316
  9.8 1.8 %collective-permute-start.9 = (bf16[128,1536]{1,0:T(8,128)(2,1)}, bf16[128,1536]{1,0:T(8,128)(2,1)S(1)}, u32[]{:S(2)}, u32[]{:S(2)}) collective-permute-start(bf16[128,1536]{1,0:T(8,128)(2,1)} %refs_6_.1), channel_id=1, source_target_pairs={{0,2},{1,3},{2,4},{3,5},{4,6},{5,7},{6,0},{7,1},{8,10},{9,11},{10,... | collective-permute-start | bytes 1179656 | tf_op jit(solution)/shard_map/ppermute | solution.py:316
  11.5 4.6 %collective-permute-done.26.refs_13_ = f32[8,256]{1,0:T(8,128)S(1)} collective-permute-done((f32[8,256]{1,0:T(8,128)S(1)}, f32[8,256]{1,0:T(8,128)S(1)}, u32[]{:S(2)}, u32[]{:S(2)}) %collective-permute-start.26) | collective-permute-done | bytes 8224 | tf_op jit(solution)/shard_map/ppermute | solution.py:316
  16.2 10.6 %collective-permute-start.11 = (bf16[128,1536]{1,0:T(8,128)(2,1)}, bf16[128,1536]{1,0:T(8,128)(2,1)S(1)}, u32[]{:S(2)}, u32[]{:S(2)}) collective-permute-start(bf16[128,1536]{1,0:T(8,128)(2,1)} %refs_6_.1), channel_id=1, source_target_pairs={{0,6},{1,7},{2,0},{3,1},{4,2},{5,3},{6,4},{7,5},{8,14},{9,15},{10,... | collective-permute-start | bytes 1179656 | tf_op jit(solution)/shard_map/ppermute | solution.py:316
  26.7 1.6 collective-permute-start.16
  28.3 1.5 collective-permute-start.6
  29.8 3.4 %collective-permute-done.9.refs_8_ = bf16[128,1536]{1,0:T(8,128)(2,1)S(1)} collective-permute-done((bf16[128,1536]{1,0:T(8,128)(2,1)}, bf16[128,1536]{1,0:T(8,128)(2,1)S(1)}, u32[]{:S(2)}, u32[]{:S(2)}) %collective-permute-start.9) | collective-permute-done | bytes 393248 | tf_op jit(solution)/shard_map/ppermute | solution.py:316
  33.2 1.7 %collective-permute-start.15 = (bf16[768,384]{1,0:T(8,128)(2,1)}, bf16[768,384]{1,0:T(8,128)(2,1)S(1)}, u32[]{:S(2)}, u32[]{:S(2)}) collective-permute-start(bf16[768,384]{1,0:T(8,128)(2,1)} %bitcast.15), channel_id=1, source_target_pairs={{0,8},{8,0},{16,24},{24,16},{1,9},{9,1},{17,25},{25,17},{2,10},{10... | collective-permute-start | bytes 1769480 | tf_op jit(solution)/shard_map/ppermute | solution.py:319
  34.9 5.8 %collective-permute-done.11.refs_10_ = bf16[128,1536]{1,0:T(8,128)(2,1)S(1)} collective-permute-done((bf16[128,1536]{1,0:T(8,128)(2,1)}, bf16[128,1536]{1,0:T(8,128)(2,1)S(1)}, u32[]{:S(2)}, u32[]{:S(2)}) %collective-permute-start.11) | collective-permute-done | bytes 393248 | tf_op jit(solution)/shard_map/ppermute | solution.py:316
  40.7 1.5 collective-permute-start.7
  42.2 1.9 %collective-permute-done.23.refs_7_ = bf16[128,1536]{1,0:T(8,128)(2,1)S(1)} collective-permute-done((bf16[128,1536]{1,0:T(8,128)(2,1)}, bf16[128,1536]{1,0:T(8,128)(2,1)S(1)}, u32[]{:S(2)}, u32[]{:S(2)}) %collective-permute-start.23) | collective-permute-done | bytes 393248 | tf_op jit(solution)/shard_map/ppermute | solution.py:316
  44.8 11.7 %collective-permute-done.15.refs_20_.refs_5_ = bf16[768,384]{1,0:T(8,128)(2,1)S(1)} collective-permute-done((bf16[768,384]{1,0:T(8,128)(2,1)}, bf16[768,384]{1,0:T(8,128)(2,1)S(1)}, u32[]{:S(2)}, u32[]{:S(2)}) %collective-permute-start.15) | collective-permute-done | bytes 589856 | tf_op jit(solution)/shard_map/ppermute | solution.py:319
  57.3 1.6 collective-permute-start.17
  58.8 1.1 collective-permute-start.8
  59.9 1.3 collective-permute-start.3
  61.9 1.3 collective-permute-start.12
  63.2 10.6 %collective-permute-done.3.refs_1_ = bf16[128,1536]{1,0:T(8,128)(2,1)S(1)} collective-permute-done((bf16[128,1536]{1,0:T(8,128)(2,1)S(1)}, bf16[128,1536]{1,0:T(8,128)(2,1)S(1)}, u32[]{:S(2)}, u32[]{:S(2)}) %collective-permute-start.3) | collective-permute-done | bytes 393248 | tf_op jit(solution)/shard_map/ppermute | solution.py:316
  73.8 6.9 %collective-permute-done.12.refs_1_ = bf16[128,1536]{1,0:T(8,128)(2,1)S(1)} collective-permute-done((bf16[128,1536]{1,0:T(8,128)(2,1)S(1)}, bf16[128,1536]{1,0:T(8,128)(2,1)S(1)}, u32[]{:S(2)}, u32[]{:S(2)}) %collective-permute-start.12) | collective-permute-done | bytes 393248 | tf_op jit(solution)/shard_map/ppermute | solution.py:316
  81.3 1.1 copy-done
  82.4 1.1 copy-done.1
  85.4 16.4 %most.1 = (f32[384,768]{1,0:T(8,128)S(1)}, f32[384,768]{1,0:T(8,128)S(1)}, f32[384,768]{1,0:T(8,128)S(1)}, f32[384,768]{1,0:T(8,128)S(1)}, f32[768,384]{1,0:T(8,...) custom-call(bf16[128,1536]{1,0:T(8,128)(2,1)S(1)} %copy-done.2, ...), custom_call_target="tpu_custom_call" | custom-call | flops 7247757312 | bytes 20971520 | tf_op jit(solution)/shard_map/most/pallas_call | solution.py:231
  101.9 1.8 %last_forward.1 = (bf16[256,1536]{1,0:T(8,128)(2,1)S(1)}, bf16[256,768]{1,0:T(8,128)(2,1)S(1)}, f32[256,768]{1,0:T(8,128)S(1)}) custom-call(bf16[128,1536]{1,0:T(8,128)(2,1)S(1)} %collective-permute-done.1.refs_0_, bf16[128,1536]{1,0:T(8,128)(2,1)S(1)} %collective-permute-done.3.refs_1_, bf16[128,1536]{1,0:T(8,128)(2,1)S(1)} %collective-permute-done.4.refs_2_, ...), custom_call_target="tpu_custom_call" | custom-call | flops 603979776 | bytes 5242880 | tf_op jit(solution)/shard_map/last_forward/pallas_call | solution.py:260
  103.7 3.6 %last_backward.1 = (bf16[384,768]{1,0:T(8,128)(2,1)S(1)}, bf16[768,384]{1,0:T(8,128)(2,1)S(1)}, bf16[256,768]{1,0:T(8,128)(2,1)S(1)}, bf16[256,1536]{1,0:T(8,128)(2,1)S(1)}) custom-call(bf16[128,1536]{1,0:T(8,128)(2,1)S(1)} %collective-permute-done.10.refs_0_, bf16[128,1536]{1,0:T(8,128)(2,1)S(1)} %collective-permute-done.12.refs_1_, ...), custom_call_target="tpu_custom_call" | custom-call | flops 1207959552 | bytes 8388608 | tf_op jit(solution)/shard_map/last_backward/pallas_call | solution.py:283
  109.1 1.6 collective-permute-start.32
  110.6 1.5 collective-permute-start.29
  112.9 23.2 %collective-permute-done.32 = bf16[768,384]{1,0:T(8,128)(2,1)S(1)} collective-permute-done((bf16[768,384]{1,0:T(8,128)(2,1)S(1)}, bf16[768,384]{1,0:T(8,128)(2,1)S(1)}, u32[]{:S(2)}, u32[]{:S(2)}) %collective-permute-start.32) | collective-permute-done | bytes 589856 | tf_op jit(solution)/shard_map/ppermute | solution.py:319
  136.2 1.6 collective-permute-start.33
  139.4 13.0 %collective-permute-done.33 = bf16[768,384]{1,0:T(8,128)(2,1)S(1)} collective-permute-done((bf16[768,384]{1,0:T(8,128)(2,1)S(1)}, bf16[768,384]{1,0:T(8,128)(2,1)S(1)}, u32[]{:S(2)}, u32[]{:S(2)}) %collective-permute-start.33) | collective-permute-done | bytes 589856 | tf_op jit(solution)/shard_map/ppermute | solution.py:319
  153.5 10.2 %collective-permute-done.28 = bf16[384,768]{1,0:T(8,128)(2,1)S(1)} collective-permute-done((bf16[384,768]{1,0:T(8,128)(2,1)S(1)}, bf16[384,768]{1,0:T(8,128)(2,1)S(1)}, u32[]{:S(2)}, u32[]{:S(2)}) %collective-permute-start.28) | collective-permute-done | bytes 589856 | tf_op jit(solution)/shard_map/ppermute | solution.py:319
  (60 shorter events, 12.0 us)
Async XLA Ops:
  0.6 26.1 %collective-permute-start = (bf16[128,1536]{1,0:T(8,128)(2,1)}, bf16[128,1536]{1,0:T(8,128)(2,1)S(1)}, u32[]{:S(2)}, u32[]{:S(2)}) collective-permute-start(bf16[128,1536]{1,0:T(8,128)(2,1)} %refs_0_.1), channel_id=1, source_target_pairs={{0,2},{1,3},{2,4},{3,5},{4,6},{5,7},{6,0},{7,1},{8,10},{9,11},{10,... | collective-permute-start | bytes 1179656 | tf_op jit(solution)/shard_map/ppermute | solution.py:316
  5.7 10.5 %collective-permute-start.26 = (f32[8,256]{1,0:T(8,128)S(1)}, f32[8,256]{1,0:T(8,128)S(1)}, u32[]{:S(2)}, u32[]{:S(2)}) collective-permute-start(f32[8,256]{1,0:T(8,128)S(1)} %pad_maximum_fusion.refs_12_), channel_id=1, source_target_pairs={{0,2},{1,3},{2,4},{3,5},{4,6},{5,7},{6,0},{7,1},{8,10},{9,11},{10,... | collective-permute-start | bytes 24584 | tf_op jit(solution)/shard_map/ppermute | solution.py:316
  7.3 19.5 %collective-permute-start.27 = (f32[8,256]{1,0:T(8,128)S(1)}, f32[8,256]{1,0:T(8,128)S(1)}, u32[]{:S(2)}, u32[]{:S(2)}) collective-permute-start(f32[8,256]{1,0:T(8,128)S(1)} %pad_maximum_fusion.refs_12_), channel_id=1, source_target_pairs={{0,6},{1,7},{2,0},{3,1},{4,2},{5,3},{6,4},{7,5},{8,14},{9,15},{10,... | collective-permute-start | bytes 24584 | tf_op jit(solution)/shard_map/ppermute | solution.py:316
  9.5 18.8 %collective-permute-start.2 = (bf16[128,1536]{1,0:T(8,128)(2,1)}, bf16[128,1536]{1,0:T(8,128)(2,1)S(1)}, u32[]{:S(2)}, u32[]{:S(2)}) collective-permute-start(bf16[128,1536]{1,0:T(8,128)(2,1)} %refs_0_.1), channel_id=1, source_target_pairs={{0,6},{1,7},{2,0},{3,1},{4,2},{5,3},{6,4},{7,5},{8,14},{9,15},{10,... | collective-permute-start | bytes 1179656 | tf_op jit(solution)/shard_map/ppermute | solution.py:316
  9.8 23.5 %collective-permute-start.9 = (bf16[128,1536]{1,0:T(8,128)(2,1)}, bf16[128,1536]{1,0:T(8,128)(2,1)S(1)}, u32[]{:S(2)}, u32[]{:S(2)}) collective-permute-start(bf16[128,1536]{1,0:T(8,128)(2,1)} %refs_6_.1), channel_id=1, source_target_pairs={{0,2},{1,3},{2,4},{3,5},{4,6},{5,7},{6,0},{7,1},{8,10},{9,11},{10,... | collective-permute-start | bytes 1179656 | tf_op jit(solution)/shard_map/ppermute | solution.py:316
  16.2 24.6 %collective-permute-start.11 = (bf16[128,1536]{1,0:T(8,128)(2,1)}, bf16[128,1536]{1,0:T(8,128)(2,1)S(1)}, u32[]{:S(2)}, u32[]{:S(2)}) collective-permute-start(bf16[128,1536]{1,0:T(8,128)(2,1)} %refs_6_.1), channel_id=1, source_target_pairs={{0,6},{1,7},{2,0},{3,1},{4,2},{5,3},{6,4},{7,5},{8,14},{9,15},{10,... | collective-permute-start | bytes 1179656 | tf_op jit(solution)/shard_map/ppermute | solution.py:316
  26.7 15.5 %collective-permute-start.20 = (bf16[128,1536]{1,0:T(8,128)(2,1)}, bf16[128,1536]{1,0:T(8,128)(2,1)S(1)}, u32[]{:S(2)}, u32[]{:S(2)}) collective-permute-start(bf16[128,1536]{1,0:T(8,128)(2,1)} %refs_0_.1), channel_id=1, source_target_pairs={{0,1},{1,0},{2,3},{3,2},{4,5},{5,4},{6,7},{7,6},{8,9},{9,8},{10,11... | collective-permute-start | bytes 1179656 | tf_op jit(solution)/shard_map/ppermute | solution.py:316
  26.7 17.6 %collective-permute-start.16 = (bf16[768,384]{1,0:T(8,128)(2,1)}, bf16[768,384]{1,0:T(8,128)(2,1)S(1)}, u32[]{:S(2)}, u32[]{:S(2)}) collective-permute-start(bf16[768,384]{1,0:T(8,128)(2,1)} %bitcast.14), channel_id=1, source_target_pairs={{0,16},{8,24},{16,0},{24,8},{1,17},{9,25},{17,1},{25,9},{2,18},{10... | collective-permute-start | bytes 1769480 | tf_op jit(solution)/shard_map/ppermute | solution.py:319
  28.3 16.4 %collective-permute-start.6 = (bf16[384,768]{1,0:T(8,128)(2,1)}, bf16[384,768]{1,0:T(8,128)(2,1)S(1)}, u32[]{:S(2)}, u32[]{:S(2)}) collective-permute-start(bf16[384,768]{1,0:T(8,128)(2,1)} %bitcast.18), channel_id=1, source_target_pairs={{0,8},{8,0},{16,24},{24,16},{1,9},{9,1},{17,25},{25,17},{2,10},{10... | collective-permute-start | bytes 1769480 | tf_op jit(solution)/shard_map/ppermute | solution.py:319
  33.2 23.3 %collective-permute-start.15 = (bf16[768,384]{1,0:T(8,128)(2,1)}, bf16[768,384]{1,0:T(8,128)(2,1)S(1)}, u32[]{:S(2)}, u32[]{:S(2)}) collective-permute-start(bf16[768,384]{1,0:T(8,128)(2,1)} %bitcast.15), channel_id=1, source_target_pairs={{0,8},{8,0},{16,24},{24,16},{1,9},{9,1},{17,25},{25,17},{2,10},{10... | collective-permute-start | bytes 1769480 | tf_op jit(solution)/shard_map/ppermute | solution.py:319
  40.7 15.9 %collective-permute-start.7 = (bf16[384,768]{1,0:T(8,128)(2,1)}, bf16[384,768]{1,0:T(8,128)(2,1)S(1)}, u32[]{:S(2)}, u32[]{:S(2)}) collective-permute-start(bf16[384,768]{1,0:T(8,128)(2,1)} %bitcast.19), channel_id=1, source_target_pairs={{0,16},{8,24},{16,0},{24,8},{1,17},{9,25},{17,1},{25,9},{2,18},{10... | collective-permute-start | bytes 1769480 | tf_op jit(solution)/shard_map/ppermute | solution.py:319
  44.2 13.1 %collective-permute-start.21 = (bf16[128,1536]{1,0:T(8,128)(2,1)S(1)}, bf16[128,1536]{1,0:T(8,128)(2,1)S(1)}, u32[]{:S(2)}, u32[]{:S(2)}) collective-permute-start(bf16[128,1536]{1,0:T(8,128)(2,1)S(1)} %collective-permute-done.refs_2_), channel_id=1, source_target_pairs={{0,1},{1,0},{2,3},{3,2},{4,5},{5,4},{6,7},{7,6},{8,9},{9,8},{10,11... | collective-permute-start | bytes 1179656 | tf_op jit(solution)/shard_map/ppermute | solution.py:316
  44.3 14.5 %collective-permute-start.22 = (bf16[128,1536]{1,0:T(8,128)(2,1)S(1)}, bf16[128,1536]{1,0:T(8,128)(2,1)S(1)}, u32[]{:S(2)}, u32[]{:S(2)}) collective-permute-start(bf16[128,1536]{1,0:T(8,128)(2,1)S(1)} %collective-permute-done.2.refs_4_), channel_id=1, source_target_pairs={{0,1},{1,0},{2,3},{3,2},{4,5},{5,4},{6,7},{7,6},{8,9},{9,8},{10,11... | collective-permute-start | bytes 1179656 | tf_op jit(solution)/shard_map/ppermute | solution.py:316
  44.7 15.2 %collective-permute-start.24 = (bf16[128,1536]{1,0:T(8,128)(2,1)S(1)}, bf16[128,1536]{1,0:T(8,128)(2,1)S(1)}, u32[]{:S(2)}, u32[]{:S(2)}) collective-permute-start(bf16[128,1536]{1,0:T(8,128)(2,1)S(1)} %collective-permute-done.9.refs_8_), channel_id=1, source_target_pairs={{0,1},{1,0},{2,3},{3,2},{4,5},{5,4},{6,7},{7,6},{8,9},{9,8},{10,11... | collective-permute-start | bytes 1179656 | tf_op jit(solution)/shard_map/ppermute | solution.py:316
  56.6 4.6 %collective-permute-start.25 = (bf16[128,1536]{1,0:T(8,128)(2,1)S(1)}, bf16[128,1536]{1,0:T(8,128)(2,1)S(1)}, u32[]{:S(2)}, u32[]{:S(2)}) collective-permute-start(bf16[128,1536]{1,0:T(8,128)(2,1)S(1)} %collective-permute-done.11.refs_10_), channel_id=1, source_target_pairs={{0,1},{1,0},{2,3},{3,2},{4,5},{5,4},{6,7},{7,6},{8,9},{9,8},{10,11... | collective-permute-start | bytes 1179656 | tf_op jit(solution)/shard_map/ppermute | solution.py:316
  56.6 5.3 %collective-permute-start.1 = (bf16[128,1536]{1,0:T(8,128)(2,1)S(1)}, bf16[128,1536]{1,0:T(8,128)(2,1)S(1)}, u32[]{:S(2)}, u32[]{:S(2)}) collective-permute-start(bf16[128,1536]{1,0:T(8,128)(2,1)S(1)} %collective-permute-done.refs_2_), channel_id=1, source_target_pairs={{2,4},{3,5},{4,6},{5,7},{10,12},{11,13},{12,14},{13,15},{18,20},{1... | collective-permute-start | bytes 1179656 | tf_op jit(solution)/shard_map/ppermute | solution.py:316
  57.3 23.4 %collective-permute-start.17 = (bf16[768,384]{1,0:T(8,128)(2,1)S(1)}, bf16[768,384]{1,0:T(8,128)(2,1)S(1)}, u32[]{:S(2)}, u32[]{:S(2)}) collective-permute-start(bf16[768,384]{1,0:T(8,128)(2,1)S(1)} %collective-permute-done.16.refs_21_.refs_6_), channel_id=1, source_target_pairs={{0,8},{8,0},{16,24},{24,16},{1,9},{9,1},{17,25},{25,17},{2,10},{10... | collective-permute-start | bytes 1769480 | tf_op jit(solution)/shard_map/ppermute | solution.py:319
  58.8 22.4 %collective-permute-start.8 = (bf16[384,768]{1,0:T(8,128)(2,1)S(1)}, bf16[384,768]{1,0:T(8,128)(2,1)S(1)}, u32[]{:S(2)}, u32[]{:S(2)}) collective-permute-start(bf16[384,768]{1,0:T(8,128)(2,1)S(1)} %collective-permute-done.6.refs_5_.refs_16_), channel_id=1, source_target_pairs={{0,16},{8,24},{16,0},{24,8},{1,17},{9,25},{17,1},{25,9},{2,18},{10... | collective-permute-start | bytes 1769480 | tf_op jit(solution)/shard_map/ppermute | solution.py:319
  59.9 13.9 %collective-permute-start.3 = (bf16[128,1536]{1,0:T(8,128)(2,1)S(1)}, bf16[128,1536]{1,0:T(8,128)(2,1)S(1)}, u32[]{:S(2)}, u32[]{:S(2)}) collective-permute-start(bf16[128,1536]{1,0:T(8,128)(2,1)S(1)} %collective-permute-done.2.refs_4_), channel_id=1, source_target_pairs={{2,0},{3,1},{4,2},{5,3},{10,8},{11,9},{12,10},{13,11},{18,16},{19,... | collective-permute-start | bytes 1179656 | tf_op jit(solution)/shard_map/ppermute | solution.py:316
  61.2 12.6 %collective-permute-start.10 = (bf16[128,1536]{1,0:T(8,128)(2,1)S(1)}, bf16[128,1536]{1,0:T(8,128)(2,1)S(1)}, u32[]{:S(2)}, u32[]{:S(2)}) collective-permute-start(bf16[128,1536]{1,0:T(8,128)(2,1)S(1)} %collective-permute-done.9.refs_8_), channel_id=1, source_target_pairs={{2,4},{3,5},{4,6},{5,7},{10,12},{11,13},{12,14},{13,15},{18,20},{1... | collective-permute-start | bytes 1179656 | tf_op jit(solution)/shard_map/ppermute | solution.py:316
  61.9 18.8 %collective-permute-start.12 = (bf16[128,1536]{1,0:T(8,128)(2,1)S(1)}, bf16[128,1536]{1,0:T(8,128)(2,1)S(1)}, u32[]{:S(2)}, u32[]{:S(2)}) collective-permute-start(bf16[128,1536]{1,0:T(8,128)(2,1)S(1)} %collective-permute-done.11.refs_10_), channel_id=1, source_target_pairs={{2,0},{3,1},{4,2},{5,3},{10,8},{11,9},{12,10},{13,11},{18,16},{19,... | collective-permute-start | bytes 1179656 | tf_op jit(solution)/shard_map/ppermute | solution.py:316
  73.8 29.9 %collective-permute-start.19 = (f32[8,256]{1,0:T(8,128)S(1)}, f32[8,256]{1,0:T(8,128)S(1)}, u32[]{:S(2)}, u32[]{:S(2)}) collective-permute-start(f32[8,256]{1,0:T(8,128)S(1)} %pad_maximum_fusion.refs_12_), channel_id=1, source_target_pairs={{0,4},{1,5},{2,6},{3,7},{4,0},{5,1},{6,2},{7,3},{8,12},{9,13},{10,... | collective-permute-start | bytes 24584 | tf_op jit(solution)/shard_map/ppermute | solution.py:316
  73.8 28.1 %collective-permute-start.4 = (bf16[128,1536]{1,0:T(8,128)(2,1)S(1)}, bf16[128,1536]{1,0:T(8,128)(2,1)S(1)}, u32[]{:S(2)}, u32[]{:S(2)}) collective-permute-start(bf16[128,1536]{1,0:T(8,128)(2,1)S(1)} %collective-permute-done.1.refs_0_), channel_id=1, source_target_pairs={{0,1},{1,0},{2,3},{3,2},{4,5},{5,4},{6,7},{7,6},{8,9},{9,8},{10,11... | collective-permute-start | bytes 1179656 | tf_op jit(solution)/shard_map/ppermute | solution.py:316
  80.7 21.2 %collective-permute-start.5 = (bf16[128,1536]{1,0:T(8,128)(2,1)S(1)}, bf16[128,1536]{1,0:T(8,128)(2,1)S(1)}, u32[]{:S(2)}, u32[]{:S(2)}) collective-permute-start(bf16[128,1536]{1,0:T(8,128)(2,1)S(1)} %collective-permute-done.3.refs_1_), channel_id=1, source_target_pairs={{0,1},{1,0},{2,3},{3,2},{4,5},{5,4},{6,7},{7,6},{8,9},{9,8},{10,11... | collective-permute-start | bytes 1179656 | tf_op jit(solution)/shard_map/ppermute | solution.py:316
  80.7 23.0 %collective-permute-start.13 = (bf16[128,1536]{1,0:T(8,128)(2,1)S(1)}, bf16[128,1536]{1,0:T(8,128)(2,1)S(1)}, u32[]{:S(2)}, u32[]{:S(2)}) collective-permute-start(bf16[128,1536]{1,0:T(8,128)(2,1)S(1)} %collective-permute-done.10.refs_0_), channel_id=1, source_target_pairs={{0,1},{1,0},{2,3},{3,2},{4,5},{5,4},{6,7},{7,6},{8,9},{9,8},{10,11... | collective-permute-start | bytes 1179656 | tf_op jit(solution)/shard_map/ppermute | solution.py:316
  81.2 22.5 %collective-permute-start.14 = (bf16[128,1536]{1,0:T(8,128)(2,1)S(1)}, bf16[128,1536]{1,0:T(8,128)(2,1)S(1)}, u32[]{:S(2)}, u32[]{:S(2)}) collective-permute-start(bf16[128,1536]{1,0:T(8,128)(2,1)S(1)} %collective-permute-done.12.refs_1_), channel_id=1, source_target_pairs={{0,1},{1,0},{2,3},{3,2},{4,5},{5,4},{6,7},{7,6},{8,9},{9,8},{10,11... | collective-permute-start | bytes 1179656 | tf_op jit(solution)/shard_map/ppermute | solution.py:316
  107.7 31.8 %collective-permute-start.31 = (bf16[768,384]{1,0:T(8,128)(2,1)S(1)}, bf16[768,384]{1,0:T(8,128)(2,1)S(1)}, u32[]{:S(2)}, u32[]{:S(2)}) collective-permute-start(bf16[768,384]{1,0:T(8,128)(2,1)S(1)} %fusion.1), channel_id=1, source_target_pairs={{0,8},{8,0},{16,24},{24,16},{1,9},{9,1},{17,25},{25,17},{2,10},{10... | collective-permute-start | bytes 1769480 | tf_op jit(solution)/shard_map/ppermute | solution.py:319
  109.1 27.0 %collective-permute-start.32 = (bf16[768,384]{1,0:T(8,128)(2,1)S(1)}, bf16[768,384]{1,0:T(8,128)(2,1)S(1)}, u32[]{:S(2)}, u32[]{:S(2)}) collective-permute-start(bf16[768,384]{1,0:T(8,128)(2,1)S(1)} %get-tuple-element.39), channel_id=1, source_target_pairs={{0,8},{8,0},{16,24},{24,16},{1,9},{9,1},{17,25},{25,17},{2,10},{10... | collective-permute-start | bytes 1769480 | tf_op jit(solution)/shard_map/ppermute | solution.py:319
  110.6 28.1 %collective-permute-start.29 = (bf16[384,768]{1,0:T(8,128)(2,1)S(1)}, bf16[384,768]{1,0:T(8,128)(2,1)S(1)}, u32[]{:S(2)}, u32[]{:S(2)}) collective-permute-start(bf16[384,768]{1,0:T(8,128)(2,1)S(1)} %get-tuple-element.35), channel_id=1, source_target_pairs={{0,16},{8,24},{16,0},{24,8},{1,17},{9,25},{17,1},{25,9},{2,18},{10... | collective-permute-start | bytes 1769480 | tf_op jit(solution)/shard_map/ppermute | solution.py:319
  136.2 16.3 %collective-permute-start.33 = (bf16[768,384]{1,0:T(8,128)(2,1)S(1)}, bf16[768,384]{1,0:T(8,128)(2,1)S(1)}, u32[]{:S(2)}, u32[]{:S(2)}) collective-permute-start(bf16[768,384]{1,0:T(8,128)(2,1)S(1)} %add_convert_fusion.1), channel_id=1, source_target_pairs={{0,16},{8,24},{16,0},{24,8},{1,17},{9,25},{17,1},{25,9},{2,18},{10... | collective-permute-start | bytes 1769480 | tf_op jit(solution)/shard_map/ppermute | solution.py:319
  138.2 25.6 %collective-permute-start.28 = (bf16[384,768]{1,0:T(8,128)(2,1)S(1)}, bf16[384,768]{1,0:T(8,128)(2,1)S(1)}, u32[]{:S(2)}, u32[]{:S(2)}) collective-permute-start(bf16[384,768]{1,0:T(8,128)(2,1)S(1)} %fusion), channel_id=1, source_target_pairs={{0,16},{8,24},{16,0},{24,8},{1,17},{9,25},{17,1},{25,9},{2,18},{10... | collective-permute-start | bytes 1769480 | tf_op jit(solution)/shard_map/ppermute | solution.py:319
  138.8 24.9 %collective-permute-start.30 = (bf16[384,768]{1,0:T(8,128)(2,1)S(1)}, bf16[384,768]{1,0:T(8,128)(2,1)S(1)}, u32[]{:S(2)}, u32[]{:S(2)}) collective-permute-start(bf16[384,768]{1,0:T(8,128)(2,1)S(1)} %add_convert_fusion.3), channel_id=1, source_target_pairs={{0,8},{8,0},{16,24},{24,16},{1,9},{9,1},{17,25},{25,17},{2,10},{10... | collective-permute-start | bytes 1769480 | tf_op jit(solution)/shard_map/ppermute | solution.py:319
  (6 other events, 7.3 us)

commit v3 on v1

--- a/solution.py
+++ b/solution.py
@@ -1,6 +1,10 @@
+import functools
+
 import jax
 import jax.numpy as jnp
 from jax import lax
+from jax.experimental import pallas as pl
+from jax.experimental.pallas import tpu as pltpu
 from jax.sharding import PartitionSpec as P
 
 
@@ -59,6 +63,210 @@
     return [(i, i ^ bits) for i in range(count)]
 
 
+MIB = 1 << 20
+
+
+def pick_gate(table_ref, part, expert):
+    table = table_ref[:, part * SHARD : (part + 1) * SHARD]
+    mine = lax.broadcasted_iota(jnp.int32, table.shape, 0) == expert
+    row = jnp.sum(jnp.where(mine, table, 0.0), axis=0, keepdims=True)
+    return jnp.transpose(jnp.broadcast_to(row, (SHARD, SHARD)))
+
+
+SHARD = 128
+
+
+def scale_rows(gate, rows):
+    wide = jnp.concatenate([gate] * (rows.shape[1] // gate.shape[1]), axis=1)
+    return (wide * rows.astype(F32)).astype(BF16)
+
+
+def dot_rows(left, right):
+    return jnp.dot(left, right, preferred_element_type=F32)
+
+
+def dot_last(left, right):
+    return lax.dot_general(left, right, LAST, preferred_element_type=F32)
+
+
+def owner_columns(block, bits):
+    return pl.ds(pl.multiple_of((lax.axis_index("dp") ^ bits) * block, block), block)
+
+
+def early_forward_kernel(block, shards, *refs):
+    xs, ups = refs[0:shards], refs[shards : shards + 3]
+    x_last, x_turned, part = refs[shards + 3 : shards + 6]
+    x = refs[shards + 6]
+    for pair in range(shards // 2):
+        rows = slice(pair * 2 * SHARD, (pair + 1) * 2 * SHARD)
+        for half in range(2):
+            for bits in range(4):
+                x[half * SHARD : (half + 1) * SHARD, bits * block : (bits + 1) * block] = xs[pair * 2 + half][
+                    :, owner_columns(block, bits)
+                ]
+        total = dot_rows(x[:, :block], ups[0][...])
+        for bits in (1, 2):
+            total = total + dot_rows(x[:, bits * block : (bits + 1) * block], ups[bits][...])
+        part[rows, :] = total
+        x_last[rows, :] = x[:, 3 * block :]
+        x_turned[:, rows] = jnp.transpose(x[...])
+
+
+def early_backward_kernel(block, shards, *refs):
+    gs, tables, downs = refs[0:shards], refs[shards : shards + shards // 2], refs[shards + shards // 2 : shards + shards // 2 + 3]
+    g, part = refs[shards + shards // 2 + 3 :]
+    expert = lax.axis_index("expert")
+    for pair in range(shards // 2):
+        rows = slice(pair * 2 * SHARD, (pair + 1) * 2 * SHARD)
+        for half in range(2):
+            own = slice((pair * 2 + half) * SHARD, (pair * 2 + half + 1) * SHARD)
+            gate = pick_gate(tables[pair], half, expert)
+            for bits in range(4):
+                g[own, bits * block : (bits + 1) * block] = scale_rows(gate, gs[pair * 2 + half][:, owner_columns(block, bits)])
+        total = dot_last(g[rows, :block], downs[0][...])
+        for bits in (1, 2):
+            total = total + dot_last(g[rows, bits * block : (bits + 1) * block], downs[bits][...])
+        part[rows, :] = total
+
+
+def most_kernel(block, *refs):
+    x_last, x_turned, g, pre_part, grad_part, up, down = refs[0:7]
+    up_out, down_out = refs[7:11], refs[11:15]
+    act_turned, back = refs[15:]
+    for pair in range(g.shape[0] // (2 * SHARD)):
+        rows = slice(pair * 2 * SHARD, (pair + 1) * 2 * SHARD)
+        pre = pre_part[rows, :] + dot_rows(x_last[rows, :], up[...])
+        grad = grad_part[rows, :] + dot_last(g[rows, 3 * block :], down[...])
+        sig = jax.nn.sigmoid(pre)
+        act_turned[:, rows] = jnp.transpose((pre * sig).astype(BF16))
+        back[rows, :] = (grad * (sig * (1.0 + pre * (1.0 - sig)))).astype(BF16)
+    for bits in range(4):
+        cols = slice(bits * block, (bits + 1) * block)
+        up_out[bits][...] = dot_rows(x_turned[cols, :], back[...])
+        down_out[bits][...] = dot_rows(act_turned[...], g[:, cols])
+
+
+def last_forward_kernel(block, *refs):
+    shards, ups = refs[0:4], refs[4:8]
+    x_turned, act_turned, slope, x = refs[8:]
+    for half in range(2):
+        for bits in range(4):
+            cols = owner_columns(block, bits)
+            x[half * SHARD : (half + 1) * SHARD, bits * block : (bits + 1) * block] = (
+                shards[2 * half][:, cols] + shards[2 * half + 1][:, cols]
+            )
+    pre = dot_rows(x[:, :block], ups[0][...])
+    for bits in (1, 2, 3):
+        pre = pre + dot_rows(x[:, bits * block : (bits + 1) * block], ups[bits][...])
+    x_turned[...] = jnp.transpose(x[...])
+    sig = jax.nn.sigmoid(pre)
+    act_turned[...] = jnp.transpose((pre * sig).astype(BF16))
+    slope[...] = sig * (1.0 + pre * (1.0 - sig))
+
+
+def last_backward_kernel(block, *refs):
+    shards, downs = refs[0:4], refs[4:8]
+    table, x_turned, act_turned, slope, up_acc, down_acc = refs[8:14]
+    up_far, down_far, back, g = refs[14:18]
+    expert = lax.axis_index("expert")
+    for half in range(2):
+        gate = pick_gate(table, half, expert)
+        for bits in range(4):
+            cols = owner_columns(block, bits)
+            g[half * SHARD : (half + 1) * SHARD, bits * block : (bits + 1) * block] = scale_rows(
+                gate, shards[2 * half][:, cols] + shards[2 * half + 1][:, cols]
+            )
+    far = slice(3 * block, 4 * block)
+    grad = dot_last(g[:, :block], downs[0][...])
+    for bits in (1, 2, 3):
+        grad = grad + dot_last(g[:, bits * block : (bits + 1) * block], downs[bits][...])
+    back[...] = (grad * slope[...]).astype(BF16)
+    down_far[...] = (dot_rows(act_turned[...], g[:, far]) + down_acc[...]).astype(BF16)
+    up_far[...] = (dot_rows(x_turned[far, :], back[...]) + up_acc[...]).astype(BF16)
+
+
+VMEM = pl.BlockSpec(memory_space=pltpu.VMEM)
+
+
+def local_call(kernel, outs, args, scratch=(), flops=0):
+    moved = sum(v.size * v.dtype.itemsize for v in (*args, *outs))
+    return pl.pallas_call(
+        kernel,
+        out_shape=outs,
+        in_specs=[VMEM] * len(args),
+        out_specs=[VMEM] * len(outs),
+        scratch_shapes=list(scratch),
+        compiler_params=pltpu.CompilerParams(vmem_limit_bytes=GRANT * MIB),
+        cost_estimate=pl.CostEstimate(flops=flops, bytes_accessed=moved, transcendentals=0),
+    )(*args)
+
+
+GRANT = 24
+
+
+def shape(rows, cols, dtype):
+    return jax.ShapeDtypeStruct((rows, cols), dtype)
+
+
+def early_forward(xs, ups):
+    block, hidden = ups[0].shape
+    rows, width = len(xs) * SHARD, 4 * block
+    return local_call(
+        functools.partial(early_forward_kernel, block, len(xs)),
+        [shape(rows, block, BF16), shape(width, rows, BF16), shape(rows, hidden, F32)],
+        (*xs, *ups[:3]),
+        [pltpu.VMEM((2 * SHARD, width), BF16)],
+        flops=6 * rows * block * hidden,
+    )
+
+
+def early_backward(gs, tables, downs):
+    hidden, block = downs[0].shape
+    rows, width = len(gs) * SHARD, 4 * block
+    return local_call(
+        functools.partial(early_backward_kernel, block, len(gs)),
+        [shape(rows, width, BF16), shape(rows, hidden, F32)],
+        (*gs, *tables, *downs[:3]),
+        flops=6 * rows * block * hidden,
+    )
+
+
+def most_of(x_last, x_turned, g, pre_part, grad_part, up, down):
+    block, hidden = up.shape
+    rows = g.shape[0]
+    got = local_call(
+        functools.partial(most_kernel, block),
+        [shape(block, hidden, F32)] * 4 + [shape(hidden, block, F32)] * 4,
+        (x_last, x_turned, g, pre_part, grad_part, up, down),
+        [pltpu.VMEM((hidden, rows), BF16), pltpu.VMEM((rows, hidden), BF16)],
+        flops=20 * rows * block * hidden,
+    )
+    return got[:4], got[4:]
+
+
+def last_forward(shards, ups):
+    block, hidden = ups[0].shape
+    rows, width = 2 * SHARD, 4 * block
+    return local_call(
+        functools.partial(last_forward_kernel, block),
+        [shape(width, rows, BF16), shape(hidden, rows, BF16), shape(rows, hidden, F32)],
+        (*shards, *ups),
+        [pltpu.VMEM((rows, width), BF16)],
+        flops=2 * rows * width * hidden,
+    )
+
+
+def last_backward(shards, downs, table, x, act, slope, up_acc, down_acc):
+    hidden, block = downs[0].shape
+    rows, width = 2 * SHARD, 4 * block
+    return local_call(
+        functools.partial(last_backward_kernel, block),
+        [shape(block, hidden, BF16), shape(hidden, block, BF16), shape(rows, hidden, BF16), shape(rows, width, BF16)],
+        (*shards, *downs, table, x, act, slope, up_acc, down_acc),
+        flops=4 * rows * width * hidden,
+    )
+
+
 def dense_shards(tokens, grad_out, expert_ids, gate_q, w_up, w_down):
     return dense_body(tokens, grad_out, expert_ids, gate_q, w_up[0], w_down[0])
 
@@ -66,9 +274,6 @@
 def dense_body(tokens, grad_out, expert_ids, gate_q, w_up, w_down):
     devices = lax.axis_size("expert")
     block, _ = w_up.shape
-    dp_index = lax.axis_index("dp")
-    ex_index = lax.axis_index("expert")
-    upper = ex_index >= devices // 2
 
     def ex(value, perm):
         return lax.ppermute(value, "expert", perm)
@@ -94,9 +299,9 @@
     down_x = dp(w_down, 1)
 
     experts = jnp.arange(devices, dtype=jnp.int32)
-    named = expert_ids[:, :, None] == experts[None, None, :]
-    gate_table = jnp.sum(jnp.where(named, gate_q[:, :, None], 0), axis=1).astype(F32) * (1.0 / 65536.0)
-    c0 = jnp.concatenate([gate_table, ex(gate_table, swap)], axis=0)
+    named = expert_ids.T[None, :, :] == experts[:, None, None]
+    gate_table = jnp.sum(jnp.where(named, gate_q.T[None, :, :], 0), axis=1).astype(F32) * (1.0 / 65536.0)
+    c0 = jnp.concatenate([gate_table, ex(gate_table, swap)], axis=1)
     c1 = ex(c0, ring(1))
     c2 = ex(c0, ring(2))
     c3 = ex(c0, ring(3))
@@ -113,74 +318,32 @@
     g2d = ex(g3, down_mid)
     g1b = ex(g1, swap)
     g3b = ex(g3, swap)
-
-    pick = (experts == ex_index).astype(F32)
+    t2ub = ex(t2u, swap)
+    t2db = ex(t2d, swap)
+    g2ub = ex(g2u, swap)
+    g2db = ex(g2d, swap)
+
     ups = (w_up, up_x, up_y, up_d)
     downs = (w_down, down_x, down_y, down_d)
-
-    def gate_of(*tables):
-        table = jnp.concatenate(tables, axis=0)
-        return jnp.sum(table * pick, axis=1)
-
-    def scaled(gate, g):
-        return (gate[:, None] * g.astype(F32)).astype(BF16)
-
-    def columns(rows, bits):
-        return lax.dynamic_slice(rows, (0, (dp_index ^ bits) * block), (rows.shape[0], block))
-
-    def forward_part(x, bits, total):
-        part = jnp.dot(columns(x, bits), ups[bits], preferred_element_type=F32)
-        return part if total is None else total + part
-
-    def backward_part(g, bits, total):
-        part = lax.dot_general(columns(g, bits), downs[bits], LAST, preferred_element_type=F32)
-        return part if total is None else total + part
-
-    def outer(left, right):
-        return lax.dot_general(left, right, FIRST, preferred_element_type=F32)
-
-    x_ab = jnp.concatenate([tokens, t0b, t1, t1b, t3, t3b], axis=0)
-    pre = None
-    for bits in (0, 1, 2, 3):
-        pre = forward_part(x_ab, bits, pre)
-    g_ab = scaled(gate_of(c0, c1, c3), jnp.concatenate([grad_out, g0b, g1, g1b, g3, g3b], axis=0))
-    act_grad = None
-    for bits in (0, 1, 2, 3):
-        act_grad = backward_part(g_ab, bits, act_grad)
-    act_ab = jax.nn.silu(pre).astype(BF16)
-    back_ab = (act_grad * silu_slope(pre)).astype(BF16)
-    up_acc = [outer(columns(x_ab, bits), back_ab) for bits in range(4)]
-    down_acc = [outer(act_ab, columns(g_ab, bits)) for bits in range(4)]
-    t2 = jnp.where(upper, t2u, t2d)
-    t2b = ex(t2, swap)
-    x_c = jnp.concatenate([t2, t2b], axis=0)
-    pre_c = None
-    for bits in (0, 1, 2, 3):
-        pre_c = forward_part(x_c, bits, pre_c)
-    act_c = jax.nn.silu(pre_c).astype(BF16)
-    slope_c = silu_slope(pre_c)
-    gate_c = gate_of(c2)
-    up_acc, down_acc, act_c, slope_c, gate_c, g2u, g2d = lax.optimization_barrier(
-        (up_acc, down_acc, act_c, slope_c, gate_c, g2u, g2d)
-    )
-    g2 = jnp.where(upper, g2u, g2d)
-    g2b = ex(g2, swap)
-    g_c = scaled(gate_c, jnp.concatenate([g2, g2b], axis=0))
-    act_grad_c = None
-    for bits in (0, 1, 2, 3):
-        act_grad_c = backward_part(g_c, bits, act_grad_c)
-    back_c = (act_grad_c * slope_c).astype(BF16)
+    x_last, x_turned, pre_part = early_forward((tokens, t0b, t1, t1b, t3, t3b), ups)
+    g_ab, grad_part = early_backward((grad_out, g0b, g1, g1b, g3, g3b), (c0, c1, c3), downs)
+    up_acc, down_acc = most_of(x_last, x_turned, g_ab, pre_part, grad_part, up_d, down_d)
+    x_c, act_c, slope_c = last_forward((t2u, t2d, t2ub, t2db), ups)
+    up_first, down_first, back_c, g_c = last_backward(
+        (g2u, g2d, g2ub, g2db), downs, c2, x_c, act_c, slope_c, up_acc[3], down_acc[3]
+    )
 
     def up_block(bits):
-        return outer(columns(x_c, bits), back_c) + up_acc[bits]
+        return dot_rows(x_c[bits * block : (bits + 1) * block, :], back_c) + up_acc[bits]
 
     def down_block(bits):
-        return outer(act_c, columns(g_c, bits)) + down_acc[bits]
-
-    down_far = dp(down_block(3).astype(BF16), 1)
-    up_far = dp(up_block(3).astype(BF16), 2)
-    up_near = dp(up_block(2).astype(BF16), 2)
-    down_near = dp(down_block(1).astype(BF16), 1)
+        return dot_rows(act_c, g_c[:, bits * block : (bits + 1) * block]) + down_acc[bits]
+
+    down_far = dp(down_first, 1)
+    up_far = dp(up_first, 2)
+    up_second, down_second = up_block(2).astype(BF16), down_block(1).astype(BF16)
+    up_near = dp(up_second, 2)
+    down_near = dp(down_second, 1)
     up_side, down_side = up_block(1), down_block(2)
     up_own, down_own = up_block(0), down_block(0)
     up_side, down_side, up_own, down_own = lax.optimization_barrier((up_side, down_side, up_own, down_own))
@@ -195,7 +358,7 @@
     devices = lax.axis_size("expert")
     token_count, top_count = expert_ids.shape
     capacity = max(2, token_count * top_count * 3 // (2 * devices))
-    if 2 * capacity >= token_count and devices == 8 and lax.axis_size("dp") == 4:
+    if 2 * capacity >= token_count and devices == 8 and lax.axis_size("dp") == 4 and token_count == SHARD:
         return dense_shards(tokens, grad_out, expert_ids, gate_q, w_up, w_down)
     return sparse_shards(tokens, grad_out, expert_ids, gate_q, w_up, w_down, capacity)
 

time: 151 us -> 145 us (0.960)
  matrix products: 19.5 us -> 2.07 us
  Pallas kernels: 0 us -> 13.3 us
  starting transfers between devices: 33.4 us -> 38.3 us
  local copies, waits for them, and re-layouts: 6.59 us -> 2.07 us
  other arithmetic: 4.49 us -> 2.93 us
    dot_general x32 -> x6, matrix products: 19.5 us -> 2.07 us  [dot_rows(): return jnp.dot(left, right, preferred_element_type=F32)]
    pallas_call x0 -> x5, Pallas kernels: none -> 13.3 us  [local_call(): pl.pallas_call(kernel, out_shape=outs, in_specs=[VMEM] * len(args), out_s...]
    ppermute x20 -> x22, starting transfers between devices: 18.1 us -> 24.5 us  [ex(): return lax.ppermute(value, 'expert', perm)]
    unnamed x16 -> x10, local copies, waits for them, and re-layouts: 6.54 us -> 2.07 us
    ppermute x12, waiting for transfers between devices: 53 us -> 57.1 us  [dp(): return lax.ppermute(value, 'dp', xor_perm(4, bits))]
    ppermute x20 -> x22, waiting for transfers between devices: 32.4 us -> 28.5 us  [ex(): return lax.ppermute(value, 'expert', perm)]
    ppermute x12, starting transfers between devices: 15.3 us -> 13.8 us  [dp(): return lax.ppermute(value, 'dp', xor_perm(4, bits))]
  transfers between devices with their start and end apart: 32 -> 34, of which waited for: 11 -> 11; matrix products, arithmetic and copies ran while one was open for 19% -> 3% of each run, Pallas kernels for 0% -> 8%
where the time goes in v3:
time: 145 us
  waiting for transfers between devices  85.6 us (59%)
  starting transfers between devices  38.3 us (26%)
  Pallas kernels  13.3 us (9%)
  other arithmetic  2.93 us (2%)
  local copies, waits for them, and re-layouts  2.07 us (1%)
  matrix products  2.07 us (1%)
    ppermute x12, waiting for transfers between devices, dp(): return lax.ppermute(value, 'dp', xor_perm(4, bits))  57.1 us
    ppermute x22, waiting for transfers between devices, ex(): return lax.ppermute(value, 'expert', perm)  28.5 us
    ppermute x22, starting transfers between devices, ex(): return lax.ppermute(value, 'expert', perm)  24.5 us
    ppermute x12, starting transfers between devices, dp(): return lax.ppermute(value, 'dp', xor_perm(4, bits))  13.8 us
    pallas_call x5, Pallas kernels, local_call(): pl.pallas_call(kernel, out_shape=outs, in_specs=[VMEM] * len(args), out_s...  13.3 us
  transfers between devices with their start and end apart: 34, of which 11 were waited for; matrix products, arithmetic and copies ran while one was open for 3% of the time, Pallas kernels for 8%

profile of v3, /device:TPU:0, one launch (start us, length us, event | category | flops | bytes accessed | tf_op | source)
XLA Modules:
  0.0 145.0 jit_solution(9829896317862475391)
XLA Ops:
  0.6 3.1 %collective-permute-start.9 = (bf16[128,1536]{1,0:T(8,128)(2,1)}, bf16[128,1536]{1,0:T(8,128)(2,1)S(1)}, u32[]{:S(2)}, u32[]{:S(2)}) collective-permute-start(bf16[128,1536]{1,0:T(8,128)(2,1)} %refs_0_.3), channel_id=1, source_target_pairs={{0,2},{1,3},{2,4},{3,5},{4,6},{5,7},{6,0},{7,1},{8,10},{9,11},{10,... | collective-permute-start | bytes 1179656 | tf_op jit(solution)/shard_map/ppermute | solution.py:279
  4.5 1.2 collective-permute-done.18
  5.7 1.6 %collective-permute-start.26 = (f32[8,256]{1,0:T(8,128)S(1)}, f32[8,256]{1,0:T(8,128)S(1)}, u32[]{:S(2)}, u32[]{:S(2)}) collective-permute-start(f32[8,256]{1,0:T(8,128)S(1)} %pad_maximum_fusion.refs_6_), channel_id=1, source_target_pairs={{0,2},{1,3},{2,4},{3,5},{4,6},{5,7},{6,0},{7,1},{8,10},{9,11},{10,... | collective-permute-start | bytes 24584 | tf_op jit(solution)/shard_map/ppermute | solution.py:279
  7.3 2.2 %collective-permute-start.27 = (f32[8,256]{1,0:T(8,128)S(1)}, f32[8,256]{1,0:T(8,128)S(1)}, u32[]{:S(2)}, u32[]{:S(2)}) collective-permute-start(f32[8,256]{1,0:T(8,128)S(1)} %pad_maximum_fusion.refs_6_), channel_id=1, source_target_pairs={{0,6},{1,7},{2,0},{3,1},{4,2},{5,3},{6,4},{7,5},{8,14},{9,15},{10,... | collective-permute-start | bytes 24584 | tf_op jit(solution)/shard_map/ppermute | solution.py:279
  9.8 6.4 %collective-permute-done.26.refs_7_ = f32[8,256]{1,0:T(8,128)S(1)} collective-permute-done((f32[8,256]{1,0:T(8,128)S(1)}, f32[8,256]{1,0:T(8,128)S(1)}, u32[]{:S(2)}, u32[]{:S(2)}) %collective-permute-start.26) | collective-permute-done | bytes 8224 | tf_op jit(solution)/shard_map/ppermute | solution.py:279
  16.2 8.7 %collective-permute-start.2 = (bf16[128,1536]{1,0:T(8,128)(2,1)}, bf16[128,1536]{1,0:T(8,128)(2,1)S(1)}, u32[]{:S(2)}, u32[]{:S(2)}) collective-permute-start(bf16[128,1536]{1,0:T(8,128)(2,1)} %refs_0_.2), channel_id=1, source_target_pairs={{0,6},{1,7},{2,0},{3,1},{4,2},{5,3},{6,4},{7,5},{8,14},{9,15},{10,... | collective-permute-start | bytes 1179656 | tf_op jit(solution)/shard_map/ppermute | solution.py:279
  24.9 1.5 %collective-permute-start.16 = (bf16[768,384]{1,0:T(8,128)(2,1)}, bf16[768,384]{1,0:T(8,128)(2,1)S(1)}, u32[]{:S(2)}, u32[]{:S(2)}) collective-permute-start(bf16[768,384]{1,0:T(8,128)(2,1)} %bitcast.14), channel_id=1, source_target_pairs={{0,16},{8,24},{16,0},{24,8},{1,17},{9,25},{17,1},{25,9},{2,18},{10... | collective-permute-start | bytes 1769480 | tf_op jit(solution)/shard_map/ppermute | solution.py:282
  26.4 1.5 %collective-permute-start.15 = (bf16[768,384]{1,0:T(8,128)(2,1)}, bf16[768,384]{1,0:T(8,128)(2,1)S(1)}, u32[]{:S(2)}, u32[]{:S(2)}) collective-permute-start(bf16[768,384]{1,0:T(8,128)(2,1)} %bitcast.15), channel_id=1, source_target_pairs={{0,8},{8,0},{16,24},{24,16},{1,9},{9,1},{17,25},{25,17},{2,10},{10... | collective-permute-start | bytes 1769480 | tf_op jit(solution)/shard_map/ppermute | solution.py:282
  28.5 6.6 %collective-permute-done.refs_2_ = bf16[128,1536]{1,0:T(8,128)(2,1)S(1)} collective-permute-done((bf16[128,1536]{1,0:T(8,128)(2,1)}, bf16[128,1536]{1,0:T(8,128)(2,1)S(1)}, u32[]{:S(2)}, u32[]{:S(2)}) %collective-permute-start) | collective-permute-done | bytes 393248 | tf_op jit(solution)/shard_map/ppermute | solution.py:279
  35.1 1.5 %collective-permute-start.7 = (bf16[384,768]{1,0:T(8,128)(2,1)}, bf16[384,768]{1,0:T(8,128)(2,1)S(1)}, u32[]{:S(2)}, u32[]{:S(2)}) collective-permute-start(bf16[384,768]{1,0:T(8,128)(2,1)} %bitcast.19), channel_id=1, source_target_pairs={{0,16},{8,24},{16,0},{24,8},{1,17},{9,25},{17,1},{25,9},{2,18},{10... | collective-permute-start | bytes 1769480 | tf_op jit(solution)/shard_map/ppermute | solution.py:282
  36.6 4.1 %collective-permute-done.2.refs_4_ = bf16[128,1536]{1,0:T(8,128)(2,1)S(1)} collective-permute-done((bf16[128,1536]{1,0:T(8,128)(2,1)}, bf16[128,1536]{1,0:T(8,128)(2,1)S(1)}, u32[]{:S(2)}, u32[]{:S(2)}) %collective-permute-start.2) | collective-permute-done | bytes 393248 | tf_op jit(solution)/shard_map/ppermute | solution.py:279
  40.7 1.9 %collective-permute-done.20.refs_1_ = bf16[128,1536]{1,0:T(8,128)(2,1)S(1)} collective-permute-done((bf16[128,1536]{1,0:T(8,128)(2,1)}, bf16[128,1536]{1,0:T(8,128)(2,1)S(1)}, u32[]{:S(2)}, u32[]{:S(2)}) %collective-permute-start.20) | collective-permute-done | bytes 393248 | tf_op jit(solution)/shard_map/ppermute | solution.py:279
  43.3 9.4 %collective-permute-done.6.refs_5_.refs_7_ = bf16[384,768]{1,0:T(8,128)(2,1)S(1)} collective-permute-done((bf16[384,768]{1,0:T(8,128)(2,1)}, bf16[384,768]{1,0:T(8,128)(2,1)S(1)}, u32[]{:S(2)}, u32[]{:S(2)}) %collective-permute-start.6) | collective-permute-done | bytes 589856 | tf_op jit(solution)/shard_map/ppermute | solution.py:282
  53.4 1.8 %collective-permute-start.17 = (bf16[768,384]{1,0:T(8,128)(2,1)S(1)}, bf16[768,384]{1,0:T(8,128)(2,1)S(1)}, u32[]{:S(2)}, u32[]{:S(2)}) collective-permute-start(bf16[768,384]{1,0:T(8,128)(2,1)S(1)} %collective-permute-done.16.refs_11_.refs_6_), channel_id=1, source_target_pairs={{0,8},{8,0},{16,24},{24,16},{1,9},{9,1},{17,25},{25,17},{2,10},{10... | collective-permute-start | bytes 1769480 | tf_op jit(solution)/shard_map/ppermute | solution.py:282
  55.2 1.5 %collective-permute-start.8 = (bf16[384,768]{1,0:T(8,128)(2,1)S(1)}, bf16[384,768]{1,0:T(8,128)(2,1)S(1)}, u32[]{:S(2)}, u32[]{:S(2)}) collective-permute-start(bf16[384,768]{1,0:T(8,128)(2,1)S(1)} %collective-permute-done.6.refs_5_.refs_7_), channel_id=1, source_target_pairs={{0,16},{8,24},{16,0},{24,8},{1,17},{9,25},{17,1},{25,9},{2,18},{10... | collective-permute-start | bytes 1769480 | tf_op jit(solution)/shard_map/ppermute | solution.py:282
  56.7 1.3 collective-permute-start.3
  58.7 1.3 collective-permute-start.12
  60.0 1.1 copy-done.1
  62.1 2.2 %shard_map.78 = (bf16[768,384]{1,0:T(8,128)(2,1)S(1)}, bf16[1536,768]{1,0:T(8,128)(2,1)S(1)}, f32[768,768]{1,0:T(8,128)S(1)}) custom-call(bf16[128,1536]{1,0:T(8,128)(2,1)S(1)} %copy-done.3, bf16[128,1536]{1,0:T(8,128)(2,1)S(1)} %collective-permute-done.20.refs_1_, bf16[128,1536]{1,0:T(8,128)(2,1)S(1)} %collective-permute-done.refs_2_, ...), custom_call_target="tpu_custom_call" | custom-call | flops 1358954496 | bytes 9437184 | tf_op jit(solution)/shard_map/pallas_call | solution.py:193
  64.3 2.2 %shard_map.79 = (bf16[768,1536]{1,0:T(8,128)(2,1)S(1)}, f32[768,768]{1,0:T(8,128)S(1)}) custom-call(bf16[128,1536]{1,0:T(8,128)(2,1)S(1)} %copy-done.4, bf16[128,1536]{1,0:T(8,128)(2,1)S(1)} %collective-permute-done.23.refs_1_, bf16[128,1536]{1,0:T(8,128)(2,1)S(1)} %collective-permute-done.9.refs_2_, bf16[128,1536]{1,0:T(8,128)(2,1)S(1)} %collective-permute-done.24.refs_3_, ...), custom_call_target="tpu_custom_call" | custom-call | flops 1358954496 | bytes 8871936 | tf_op jit(solution)/shard_map/pallas_call | solution.py:193
  66.5 4.1 %collective-permute-done.3.refs_1_ = bf16[128,1536]{1,0:T(8,128)(2,1)S(1)} collective-permute-done((bf16[128,1536]{1,0:T(8,128)(2,1)S(1)}, bf16[128,1536]{1,0:T(8,128)(2,1)S(1)}, u32[]{:S(2)}, u32[]{:S(2)}) %collective-permute-start.3) | collective-permute-done | bytes 393248 | tf_op jit(solution)/shard_map/ppermute | solution.py:279
  70.6 3.4 %collective-permute-start.19 = (f32[8,256]{1,0:T(8,128)S(1)}, f32[8,256]{1,0:T(8,128)S(1)}, u32[]{:S(2)}, u32[]{:S(2)}) collective-permute-start(f32[8,256]{1,0:T(8,128)S(1)} %pad_maximum_fusion.refs_6_), channel_id=1, source_target_pairs={{0,4},{1,5},{2,6},{3,7},{4,0},{5,1},{6,2},{7,3},{8,12},{9,13},{10,... | collective-permute-start | bytes 24584 | tf_op jit(solution)/shard_map/ppermute | solution.py:279
  73.9 4.1 %collective-permute-done.12.refs_1_ = bf16[128,1536]{1,0:T(8,128)(2,1)S(1)} collective-permute-done((bf16[128,1536]{1,0:T(8,128)(2,1)S(1)}, bf16[128,1536]{1,0:T(8,128)(2,1)S(1)}, u32[]{:S(2)}, u32[]{:S(2)}) %collective-permute-start.12) | collective-permute-done | bytes 393248 | tf_op jit(solution)/shard_map/ppermute | solution.py:279
  78.7 6.1 %shard_map.80 = (f32[384,768]{1,0:T(8,128)S(1)}, f32[384,768]{1,0:T(8,128)S(1)}, f32[384,768]{1,0:T(8,128)S(1)}, f32[384,768]{1,0:T(8,128)S(1)}, f32[768,384]{1,...) custom-call(bf16[768,384]{1,0:T(8,128)(2,1)S(1)} %get-tuple-element.29.refs_0_, ...), custom_call_target="tpu_custom_call" | custom-call | flops 4529848320 | bytes 20643840 | tf_op jit(solution)/shard_map/pallas_call | solution.py:193
  84.8 1.2 shard_map.77
  86.0 1.6 %shard_map.81 = (bf16[384,768]{1,0:T(8,128)(2,1)S(1)}, bf16[768,384]{1,0:T(8,128)(2,1)S(1)}, bf16[256,768]{1,0:T(8,128)(2,1)S(1)}, bf16[256,1536]{1,0:T(8,128)(2,1)S(1)}) custom-call(bf16[128,1536]{1,0:T(8,128)(2,1)S(1)} %collective-permute-done.10.refs_0_, bf16[128,1536]{1,0:T(8,128)(2,1)S(1)} %collective-permute-done.12.refs_1_, ...), custom_call_target="tpu_custom_call" | custom-call | flops 1207959552 | bytes 10625024 | tf_op jit(solution)/shard_map/pallas_call | solution.py:193
  89.4 1.6 %collective-permute-start.32 = (bf16[768,384]{1,0:T(8,128)(2,1)S(1)}, bf16[768,384]{1,0:T(8,128)(2,1)S(1)}, u32[]{:S(2)}, u32[]{:S(2)}) collective-permute-start(bf16[768,384]{1,0:T(8,128)(2,1)S(1)} %get-tuple-element.49), channel_id=1, source_target_pairs={{0,8},{8,0},{16,24},{24,16},{1,9},{9,1},{17,25},{25,17},{2,10},{10... | collective-permute-start | bytes 1769480 | tf_op jit(solution)/shard_map/ppermute | solution.py:282
  92.1 24.3 %collective-permute-done.32 = bf16[768,384]{1,0:T(8,128)(2,1)S(1)} collective-permute-done((bf16[768,384]{1,0:T(8,128)(2,1)S(1)}, bf16[768,384]{1,0:T(8,128)(2,1)S(1)}, u32[]{:S(2)}, u32[]{:S(2)}) %collective-permute-start.32) | collective-permute-done | bytes 589856 | tf_op jit(solution)/shard_map/ppermute | solution.py:282
  117.4 1.6 %collective-permute-start.28 = (bf16[384,768]{1,0:T(8,128)(2,1)S(1)}, bf16[384,768]{1,0:T(8,128)(2,1)S(1)}, u32[]{:S(2)}, u32[]{:S(2)}) collective-permute-start(bf16[384,768]{1,0:T(8,128)(2,1)S(1)} %fusion), channel_id=1, source_target_pairs={{0,16},{8,24},{16,0},{24,8},{1,17},{9,25},{17,1},{25,9},{2,18},{10... | collective-permute-start | bytes 1769480 | tf_op jit(solution)/shard_map/ppermute | solution.py:282
  119.7 13.1 %collective-permute-done.33 = bf16[768,384]{1,0:T(8,128)(2,1)S(1)} collective-permute-done((bf16[768,384]{1,0:T(8,128)(2,1)S(1)}, bf16[768,384]{1,0:T(8,128)(2,1)S(1)}, u32[]{:S(2)}, u32[]{:S(2)}) %collective-permute-start.33) | collective-permute-done | bytes 589856 | tf_op jit(solution)/shard_map/ppermute | solution.py:282
  132.8 1.0 fusion.3
  133.8 10.3 %collective-permute-done.28 = bf16[384,768]{1,0:T(8,128)(2,1)S(1)} collective-permute-done((bf16[384,768]{1,0:T(8,128)(2,1)S(1)}, bf16[384,768]{1,0:T(8,128)(2,1)S(1)}, u32[]{:S(2)}, u32[]{:S(2)}) %collective-permute-start.28) | collective-permute-done | bytes 589856 | tf_op jit(solution)/shard_map/ppermute | solution.py:282
  (64 shorter events, 10.8 us)
Async XLA Ops:
  0.6 24.3 %collective-permute-start.9 = (bf16[128,1536]{1,0:T(8,128)(2,1)}, bf16[128,1536]{1,0:T(8,128)(2,1)S(1)}, u32[]{:S(2)}, u32[]{:S(2)}) collective-permute-start(bf16[128,1536]{1,0:T(8,128)(2,1)} %refs_0_.3), channel_id=1, source_target_pairs={{0,2},{1,3},{2,4},{3,5},{4,6},{5,7},{6,0},{7,1},{8,10},{9,11},{10,... | collective-permute-start | bytes 1179656 | tf_op jit(solution)/shard_map/ppermute | solution.py:279
  5.7 10.5 %collective-permute-start.26 = (f32[8,256]{1,0:T(8,128)S(1)}, f32[8,256]{1,0:T(8,128)S(1)}, u32[]{:S(2)}, u32[]{:S(2)}) collective-permute-start(f32[8,256]{1,0:T(8,128)S(1)} %pad_maximum_fusion.refs_6_), channel_id=1, source_target_pairs={{0,2},{1,3},{2,4},{3,5},{4,6},{5,7},{6,0},{7,1},{8,10},{9,11},{10,... | collective-permute-start | bytes 24584 | tf_op jit(solution)/shard_map/ppermute | solution.py:279
  7.3 8.9 %collective-permute-start.27 = (f32[8,256]{1,0:T(8,128)S(1)}, f32[8,256]{1,0:T(8,128)S(1)}, u32[]{:S(2)}, u32[]{:S(2)}) collective-permute-start(f32[8,256]{1,0:T(8,128)S(1)} %pad_maximum_fusion.refs_6_), channel_id=1, source_target_pairs={{0,6},{1,7},{2,0},{3,1},{4,2},{5,3},{6,4},{7,5},{8,14},{9,15},{10,... | collective-permute-start | bytes 24584 | tf_op jit(solution)/shard_map/ppermute | solution.py:279
  9.5 16.9 %collective-permute-start.11 = (bf16[128,1536]{1,0:T(8,128)(2,1)}, bf16[128,1536]{1,0:T(8,128)(2,1)S(1)}, u32[]{:S(2)}, u32[]{:S(2)}) collective-permute-start(bf16[128,1536]{1,0:T(8,128)(2,1)} %refs_0_.3), channel_id=1, source_target_pairs={{0,6},{1,7},{2,0},{3,1},{4,2},{5,3},{6,4},{7,5},{8,14},{9,15},{10,... | collective-permute-start | bytes 1179656 | tf_op jit(solution)/shard_map/ppermute | solution.py:279
  9.8 18.2 %collective-permute-start.23 = (bf16[128,1536]{1,0:T(8,128)(2,1)}, bf16[128,1536]{1,0:T(8,128)(2,1)S(1)}, u32[]{:S(2)}, u32[]{:S(2)}) collective-permute-start(bf16[128,1536]{1,0:T(8,128)(2,1)} %refs_0_.3), channel_id=1, source_target_pairs={{0,1},{1,0},{2,3},{3,2},{4,5},{5,4},{6,7},{7,6},{8,9},{9,8},{10,11... | collective-permute-start | bytes 1179656 | tf_op jit(solution)/shard_map/ppermute | solution.py:279
  16.2 18.9 %collective-permute-start = (bf16[128,1536]{1,0:T(8,128)(2,1)}, bf16[128,1536]{1,0:T(8,128)(2,1)S(1)}, u32[]{:S(2)}, u32[]{:S(2)}) collective-permute-start(bf16[128,1536]{1,0:T(8,128)(2,1)} %refs_0_.2), channel_id=1, source_target_pairs={{0,2},{1,3},{2,4},{3,5},{4,6},{5,7},{6,0},{7,1},{8,10},{9,11},{10,... | collective-permute-start | bytes 1179656 | tf_op jit(solution)/shard_map/ppermute | solution.py:279
  16.2 24.6 %collective-permute-start.2 = (bf16[128,1536]{1,0:T(8,128)(2,1)}, bf16[128,1536]{1,0:T(8,128)(2,1)S(1)}, u32[]{:S(2)}, u32[]{:S(2)}) collective-permute-start(bf16[128,1536]{1,0:T(8,128)(2,1)} %refs_0_.2), channel_id=1, source_target_pairs={{0,6},{1,7},{2,0},{3,1},{4,2},{5,3},{6,4},{7,5},{8,14},{9,15},{10,... | collective-permute-start | bytes 1179656 | tf_op jit(solution)/shard_map/ppermute | solution.py:279
  24.9 17.9 %collective-permute-start.16 = (bf16[768,384]{1,0:T(8,128)(2,1)}, bf16[768,384]{1,0:T(8,128)(2,1)S(1)}, u32[]{:S(2)}, u32[]{:S(2)}) collective-permute-start(bf16[768,384]{1,0:T(8,128)(2,1)} %bitcast.14), channel_id=1, source_target_pairs={{0,16},{8,24},{16,0},{24,8},{1,17},{9,25},{17,1},{25,9},{2,18},{10... | collective-permute-start | bytes 1769480 | tf_op jit(solution)/shard_map/ppermute | solution.py:282
  26.4 16.8 %collective-permute-start.15 = (bf16[768,384]{1,0:T(8,128)(2,1)}, bf16[768,384]{1,0:T(8,128)(2,1)S(1)}, u32[]{:S(2)}, u32[]{:S(2)}) collective-permute-start(bf16[768,384]{1,0:T(8,128)(2,1)} %bitcast.15), channel_id=1, source_target_pairs={{0,8},{8,0},{16,24},{24,16},{1,9},{9,1},{17,25},{25,17},{2,10},{10... | collective-permute-start | bytes 1769480 | tf_op jit(solution)/shard_map/ppermute | solution.py:282
  27.9 24.8 %collective-permute-start.6 = (bf16[384,768]{1,0:T(8,128)(2,1)}, bf16[384,768]{1,0:T(8,128)(2,1)S(1)}, u32[]{:S(2)}, u32[]{:S(2)}) collective-permute-start(bf16[384,768]{1,0:T(8,128)(2,1)} %bitcast.18), channel_id=1, source_target_pairs={{0,8},{8,0},{16,24},{24,16},{1,9},{9,1},{17,25},{25,17},{2,10},{10... | collective-permute-start | bytes 1769480 | tf_op jit(solution)/shard_map/ppermute | solution.py:282
  35.1 17.6 %collective-permute-start.7 = (bf16[384,768]{1,0:T(8,128)(2,1)}, bf16[384,768]{1,0:T(8,128)(2,1)S(1)}, u32[]{:S(2)}, u32[]{:S(2)}) collective-permute-start(bf16[384,768]{1,0:T(8,128)(2,1)} %bitcast.19), channel_id=1, source_target_pairs={{0,16},{8,24},{16,0},{24,8},{1,17},{9,25},{17,1},{25,9},{2,18},{10... | collective-permute-start | bytes 1769480 | tf_op jit(solution)/shard_map/ppermute | solution.py:282
  42.7 10.7 %collective-permute-start.24 = (bf16[128,1536]{1,0:T(8,128)(2,1)S(1)}, bf16[128,1536]{1,0:T(8,128)(2,1)S(1)}, u32[]{:S(2)}, u32[]{:S(2)}) collective-permute-start(bf16[128,1536]{1,0:T(8,128)(2,1)S(1)} %collective-permute-done.9.refs_2_), channel_id=1, source_target_pairs={{0,1},{1,0},{2,3},{3,2},{4,5},{5,4},{6,7},{7,6},{8,9},{9,8},{10,11... | collective-permute-start | bytes 1179656 | tf_op jit(solution)/shard_map/ppermute | solution.py:279
  42.8 12.4 %collective-permute-start.25 = (bf16[128,1536]{1,0:T(8,128)(2,1)S(1)}, bf16[128,1536]{1,0:T(8,128)(2,1)S(1)}, u32[]{:S(2)}, u32[]{:S(2)}) collective-permute-start(bf16[128,1536]{1,0:T(8,128)(2,1)S(1)} %collective-permute-done.11.refs_4_), channel_id=1, source_target_pairs={{0,1},{1,0},{2,3},{3,2},{4,5},{5,4},{6,7},{7,6},{8,9},{9,8},{10,11... | collective-permute-start | bytes 1179656 | tf_op jit(solution)/shard_map/ppermute | solution.py:279
  43.2 13.5 %collective-permute-start.21 = (bf16[128,1536]{1,0:T(8,128)(2,1)S(1)}, bf16[128,1536]{1,0:T(8,128)(2,1)S(1)}, u32[]{:S(2)}, u32[]{:S(2)}) collective-permute-start(bf16[128,1536]{1,0:T(8,128)(2,1)S(1)} %collective-permute-done.refs_2_), channel_id=1, source_target_pairs={{0,1},{1,0},{2,3},{3,2},{4,5},{5,4},{6,7},{7,6},{8,9},{9,8},{10,11... | collective-permute-start | bytes 1179656 | tf_op jit(solution)/shard_map/ppermute | solution.py:279
  52.7 5.3 %collective-permute-start.22 = (bf16[128,1536]{1,0:T(8,128)(2,1)S(1)}, bf16[128,1536]{1,0:T(8,128)(2,1)S(1)}, u32[]{:S(2)}, u32[]{:S(2)}) collective-permute-start(bf16[128,1536]{1,0:T(8,128)(2,1)S(1)} %collective-permute-done.2.refs_4_), channel_id=1, source_target_pairs={{0,1},{1,0},{2,3},{3,2},{4,5},{5,4},{6,7},{7,6},{8,9},{9,8},{10,11... | collective-permute-start | bytes 1179656 | tf_op jit(solution)/shard_map/ppermute | solution.py:279
  52.7 6.0 %collective-permute-start.1 = (bf16[128,1536]{1,0:T(8,128)(2,1)S(1)}, bf16[128,1536]{1,0:T(8,128)(2,1)S(1)}, u32[]{:S(2)}, u32[]{:S(2)}) collective-permute-start(bf16[128,1536]{1,0:T(8,128)(2,1)S(1)} %collective-permute-done.refs_2_), channel_id=1, source_target_pairs={{2,4},{3,5},{4,6},{5,7},{10,12},{11,13},{12,14},{13,15},{18,20},{1... | collective-permute-start | bytes 1179656 | tf_op jit(solution)/shard_map/ppermute | solution.py:279
  53.4 24.7 %collective-permute-start.17 = (bf16[768,384]{1,0:T(8,128)(2,1)S(1)}, bf16[768,384]{1,0:T(8,128)(2,1)S(1)}, u32[]{:S(2)}, u32[]{:S(2)}) collective-permute-start(bf16[768,384]{1,0:T(8,128)(2,1)S(1)} %collective-permute-done.16.refs_11_.refs_6_), channel_id=1, source_target_pairs={{0,8},{8,0},{16,24},{24,16},{1,9},{9,1},{17,25},{25,17},{2,10},{10... | collective-permute-start | bytes 1769480 | tf_op jit(solution)/shard_map/ppermute | solution.py:282
  55.2 23.4 %collective-permute-start.8 = (bf16[384,768]{1,0:T(8,128)(2,1)S(1)}, bf16[384,768]{1,0:T(8,128)(2,1)S(1)}, u32[]{:S(2)}, u32[]{:S(2)}) collective-permute-start(bf16[384,768]{1,0:T(8,128)(2,1)S(1)} %collective-permute-done.6.refs_5_.refs_7_), channel_id=1, source_target_pairs={{0,16},{8,24},{16,0},{24,8},{1,17},{9,25},{17,1},{25,9},{2,18},{10... | collective-permute-start | bytes 1769480 | tf_op jit(solution)/shard_map/ppermute | solution.py:282
  56.7 13.9 %collective-permute-start.3 = (bf16[128,1536]{1,0:T(8,128)(2,1)S(1)}, bf16[128,1536]{1,0:T(8,128)(2,1)S(1)}, u32[]{:S(2)}, u32[]{:S(2)}) collective-permute-start(bf16[128,1536]{1,0:T(8,128)(2,1)S(1)} %collective-permute-done.2.refs_4_), channel_id=1, source_target_pairs={{2,0},{3,1},{4,2},{5,3},{10,8},{11,9},{12,10},{13,11},{18,16},{19,... | collective-permute-start | bytes 1179656 | tf_op jit(solution)/shard_map/ppermute | solution.py:279
  58.0 15.9 %collective-permute-start.10 = (bf16[128,1536]{1,0:T(8,128)(2,1)S(1)}, bf16[128,1536]{1,0:T(8,128)(2,1)S(1)}, u32[]{:S(2)}, u32[]{:S(2)}) collective-permute-start(bf16[128,1536]{1,0:T(8,128)(2,1)S(1)} %collective-permute-done.9.refs_2_), channel_id=1, source_target_pairs={{2,4},{3,5},{4,6},{5,7},{10,12},{11,13},{12,14},{13,15},{18,20},{1... | collective-permute-start | bytes 1179656 | tf_op jit(solution)/shard_map/ppermute | solution.py:279
  58.7 19.4 %collective-permute-start.12 = (bf16[128,1536]{1,0:T(8,128)(2,1)S(1)}, bf16[128,1536]{1,0:T(8,128)(2,1)S(1)}, u32[]{:S(2)}, u32[]{:S(2)}) collective-permute-start(bf16[128,1536]{1,0:T(8,128)(2,1)S(1)} %collective-permute-done.11.refs_4_), channel_id=1, source_target_pairs={{2,0},{3,1},{4,2},{5,3},{10,8},{11,9},{12,10},{13,11},{18,16},{19,... | collective-permute-start | bytes 1179656 | tf_op jit(solution)/shard_map/ppermute | solution.py:279
  70.6 15.4 %collective-permute-start.19 = (f32[8,256]{1,0:T(8,128)S(1)}, f32[8,256]{1,0:T(8,128)S(1)}, u32[]{:S(2)}, u32[]{:S(2)}) collective-permute-start(f32[8,256]{1,0:T(8,128)S(1)} %pad_maximum_fusion.refs_6_), channel_id=1, source_target_pairs={{0,4},{1,5},{2,6},{3,7},{4,0},{5,1},{6,2},{7,3},{8,12},{9,13},{10,... | collective-permute-start | bytes 24584 | tf_op jit(solution)/shard_map/ppermute | solution.py:279
  73.9 10.9 %collective-permute-start.4 = (bf16[128,1536]{1,0:T(8,128)(2,1)S(1)}, bf16[128,1536]{1,0:T(8,128)(2,1)S(1)}, u32[]{:S(2)}, u32[]{:S(2)}) collective-permute-start(bf16[128,1536]{1,0:T(8,128)(2,1)S(1)} %collective-permute-done.1.refs_0_), channel_id=1, source_target_pairs={{0,1},{1,0},{2,3},{3,2},{4,5},{5,4},{6,7},{7,6},{8,9},{9,8},{10,11... | collective-permute-start | bytes 1179656 | tf_op jit(solution)/shard_map/ppermute | solution.py:279
  78.1 6.7 %collective-permute-start.5 = (bf16[128,1536]{1,0:T(8,128)(2,1)S(1)}, bf16[128,1536]{1,0:T(8,128)(2,1)S(1)}, u32[]{:S(2)}, u32[]{:S(2)}) collective-permute-start(bf16[128,1536]{1,0:T(8,128)(2,1)S(1)} %collective-permute-done.3.refs_1_), channel_id=1, source_target_pairs={{0,1},{1,0},{2,3},{3,2},{4,5},{5,4},{6,7},{7,6},{8,9},{9,8},{10,11... | collective-permute-start | bytes 1179656 | tf_op jit(solution)/shard_map/ppermute | solution.py:279
  78.1 7.9 %collective-permute-start.13 = (bf16[128,1536]{1,0:T(8,128)(2,1)S(1)}, bf16[128,1536]{1,0:T(8,128)(2,1)S(1)}, u32[]{:S(2)}, u32[]{:S(2)}) collective-permute-start(bf16[128,1536]{1,0:T(8,128)(2,1)S(1)} %collective-permute-done.10.refs_0_), channel_id=1, source_target_pairs={{0,1},{1,0},{2,3},{3,2},{4,5},{5,4},{6,7},{7,6},{8,9},{9,8},{10,11... | collective-permute-start | bytes 1179656 | tf_op jit(solution)/shard_map/ppermute | solution.py:279
  78.6 7.4 %collective-permute-start.14 = (bf16[128,1536]{1,0:T(8,128)(2,1)S(1)}, bf16[128,1536]{1,0:T(8,128)(2,1)S(1)}, u32[]{:S(2)}, u32[]{:S(2)}) collective-permute-start(bf16[128,1536]{1,0:T(8,128)(2,1)S(1)} %collective-permute-done.12.refs_1_), channel_id=1, source_target_pairs={{0,1},{1,0},{2,3},{3,2},{4,5},{5,4},{6,7},{7,6},{8,9},{9,8},{10,11... | collective-permute-start | bytes 1179656 | tf_op jit(solution)/shard_map/ppermute | solution.py:279
  88.0 31.7 %collective-permute-start.31 = (bf16[768,384]{1,0:T(8,128)(2,1)S(1)}, bf16[768,384]{1,0:T(8,128)(2,1)S(1)}, u32[]{:S(2)}, u32[]{:S(2)}) collective-permute-start(bf16[768,384]{1,0:T(8,128)(2,1)S(1)} %fusion.1), channel_id=1, source_target_pairs={{0,8},{8,0},{16,24},{24,16},{1,9},{9,1},{17,25},{25,17},{2,10},{10... | collective-permute-start | bytes 1769480 | tf_op jit(solution)/shard_map/ppermute | solution.py:282
  89.4 27.0 %collective-permute-start.32 = (bf16[768,384]{1,0:T(8,128)(2,1)S(1)}, bf16[768,384]{1,0:T(8,128)(2,1)S(1)}, u32[]{:S(2)}, u32[]{:S(2)}) collective-permute-start(bf16[768,384]{1,0:T(8,128)(2,1)S(1)} %get-tuple-element.49), channel_id=1, source_target_pairs={{0,8},{8,0},{16,24},{24,16},{1,9},{9,1},{17,25},{25,17},{2,10},{10... | collective-permute-start | bytes 1769480 | tf_op jit(solution)/shard_map/ppermute | solution.py:282
  90.9 28.1 %collective-permute-start.29 = (bf16[384,768]{1,0:T(8,128)(2,1)S(1)}, bf16[384,768]{1,0:T(8,128)(2,1)S(1)}, u32[]{:S(2)}, u32[]{:S(2)}) collective-permute-start(bf16[384,768]{1,0:T(8,128)(2,1)S(1)} %get-tuple-element.45), channel_id=1, source_target_pairs={{0,16},{8,24},{16,0},{24,8},{1,17},{9,25},{17,1},{25,9},{2,18},{10... | collective-permute-start | bytes 1769480 | tf_op jit(solution)/shard_map/ppermute | solution.py:282
  116.5 16.3 %collective-permute-start.33 = (bf16[768,384]{1,0:T(8,128)(2,1)S(1)}, bf16[768,384]{1,0:T(8,128)(2,1)S(1)}, u32[]{:S(2)}, u32[]{:S(2)}) collective-permute-start(bf16[768,384]{1,0:T(8,128)(2,1)S(1)} %add_convert_fusion.1), channel_id=1, source_target_pairs={{0,16},{8,24},{16,0},{24,8},{1,17},{9,25},{17,1},{25,9},{2,18},{10... | collective-permute-start | bytes 1769480 | tf_op jit(solution)/shard_map/ppermute | solution.py:282
  117.4 26.6 %collective-permute-start.28 = (bf16[384,768]{1,0:T(8,128)(2,1)S(1)}, bf16[384,768]{1,0:T(8,128)(2,1)S(1)}, u32[]{:S(2)}, u32[]{:S(2)}) collective-permute-start(bf16[384,768]{1,0:T(8,128)(2,1)S(1)} %fusion), channel_id=1, source_target_pairs={{0,16},{8,24},{16,0},{24,8},{1,17},{9,25},{17,1},{25,9},{2,18},{10... | collective-permute-start | bytes 1769480 | tf_op jit(solution)/shard_map/ppermute | solution.py:282
  119.1 24.9 %collective-permute-start.30 = (bf16[384,768]{1,0:T(8,128)(2,1)S(1)}, bf16[384,768]{1,0:T(8,128)(2,1)S(1)}, u32[]{:S(2)}, u32[]{:S(2)}) collective-permute-start(bf16[384,768]{1,0:T(8,128)(2,1)S(1)} %add_convert_fusion.3), channel_id=1, source_target_pairs={{0,8},{8,0},{16,24},{24,16},{1,9},{9,1},{17,25},{25,17},{2,10},{10... | collective-permute-start | bytes 1769480 | tf_op jit(solution)/shard_map/ppermute | solution.py:282
  (7 other events, 49.9 us)

commit v4 on v3

v4 whole, which is shorter than its diff:
```python
import functools

import jax
import jax.numpy as jnp
from jax import lax
from jax.experimental import pallas as pl
from jax.experimental.pallas import tpu as pltpu
from jax.sharding import PartitionSpec as P


F32 = jnp.float32
BF16 = jnp.bfloat16
FIRST = (((0,), (0,)), ((), ()))
LAST = (((1,), (1,)), ((), ()))


def silu_slope(values):
    sigmoid_part = jax.nn.sigmoid(values)
    return sigmoid_part * (1.0 + values * (1.0 - sigmoid_part))


def summed_up(recv_rows, projected_grad):
    partial_value = lax.dot_general(recv_rows, projected_grad, FIRST, preferred_element_type=F32).astype(BF16)
    pieces = lax.all_to_all(partial_value[None], "dp", split_axis=1, concat_axis=0, tiled=True)
    return jnp.sum(pieces.astype(F32), axis=0, keepdims=True).astype(BF16)


def summed_down(activated, grad_rows):
    partial_value = lax.dot_general(activated, grad_rows, FIRST, preferred_element_type=F32).astype(BF16)
    pieces = lax.all_to_all(partial_value[None], "dp", split_axis=2, concat_axis=0, tiled=True)
    return jnp.sum(pieces.astype(F32), axis=0, keepdims=True).astype(BF16)


def sparse_shards(tokens, grad_out, expert_ids, gate_q, w_up, w_down, capacity):
    devices = lax.axis_size("expert")
    top_count = expert_ids.shape[1]
    model_width = tokens.shape[1]
    slot_expert = expert_ids.reshape(-1)
    onehot_table = (slot_expert[:, None] == jnp.arange(devices, dtype=jnp.int32)[None, :]).astype(jnp.int32)
    earlier = jnp.cumsum(onehot_table, axis=0) - onehot_table
    slot_rank = jnp.sum(earlier * onehot_table, axis=1)
    slot_target = slot_expert * capacity + slot_rank
    gate_values = gate_q.reshape(-1).astype(F32) * (1.0 / 65536.0)
    token_rows = jnp.repeat(tokens, top_count, axis=0)
    slot_grads = (gate_values[:, None] * jnp.repeat(grad_out, top_count, axis=0).astype(F32)).astype(BF16)
    empty_rows = jnp.zeros((devices * capacity, model_width), BF16)
    send_tokens = empty_rows.at[slot_target].set(token_rows).reshape(devices, capacity, model_width)
    grad_slots = empty_rows.at[slot_target].set(slot_grads).reshape(devices, capacity, model_width)
    up_whole = lax.all_gather(w_up, "dp", axis=1, tiled=True)[0]
    down_whole = lax.all_gather(w_down, "dp", axis=2, tiled=True)[0]
    recv_tokens = lax.all_to_all(send_tokens, "expert", split_axis=0, concat_axis=0, tiled=True)
    recv_rows = recv_tokens.reshape(-1, model_width)
    projected = jnp.dot(recv_rows, up_whole, preferred_element_type=F32)
    recv_grads = lax.all_to_all(grad_slots, "expert", split_axis=0, concat_axis=0, tiled=True)
    activated = jax.nn.silu(projected).astype(BF16)
    grad_rows = recv_grads.reshape(-1, model_width)
    act_grad = lax.dot_general(grad_rows, down_whole, LAST, preferred_element_type=F32)
    projected_grad = (act_grad * silu_slope(projected)).astype(BF16)
    return summed_up(recv_rows, projected_grad), summed_down(activated, grad_rows)


def xor_perm(count, bits):
    return [(i, i ^ bits) for i in range(count)]


MIB = 1 << 20


def pick_gate(table_ref, part, expert):
    table = table_ref[:, part * SHARD : (part + 1) * SHARD]
    mine = lax.broadcasted_iota(jnp.int32, table.shape, 0) == expert
    row = jnp.sum(jnp.where(mine, table, 0.0), axis=0, keepdims=True)
    return jnp.transpose(jnp.broadcast_to(row, (SHARD, SHARD)))


SHARD = 128


def scale_rows(gate, rows):
    wide = jnp.concatenate([gate] * (rows.shape[1] // gate.shape[1]), axis=1)
    return (wide * rows.astype(F32)).astype(BF16)


def dot_rows(left, right):
    return jnp.dot(left, right, preferred_element_type=F32)


def dot_last(left, right):
    return lax.dot_general(left, right, LAST, preferred_element_type=F32)


def owner_columns(block, bits):
    return pl.ds(pl.multiple_of((lax.axis_index("dp") ^ bits) * block, block), block)


SENT = (3, 1, 2)


def prepare_kernel(block, grad, tokens, up, down, sent, kept, tokens_copy, up_copy, down_copy):
    for place, bits in enumerate(SENT):
        sent[:, place * block : (place + 1) * block] = grad[:, owner_columns(block, bits)]
    kept[...] = grad[:, owner_columns(block, 0)]
    tokens_copy[...] = tokens[...]
    up_copy[...] = up[...]
    down_copy[...] = down[...]


def early_forward_kernel(block, shards, *refs):
    xs, ups = refs[0:shards], refs[shards : shards + 2]
    x_tail, x_turned, part = refs[shards + 2 : shards + 5]
    x = refs[shards + 5]
    for pair in range(shards // 2):
        rows = slice(pair * 2 * SHARD, (pair + 1) * 2 * SHARD)
        for half in range(2):
            for bits in range(4):
                x[half * SHARD : (half + 1) * SHARD, bits * block : (bits + 1) * block] = xs[pair * 2 + half][
                    :, owner_columns(block, bits)
                ]
        part[rows, :] = dot_rows(x[:, :block], ups[0][...]) + dot_rows(x[:, block : 2 * block], ups[1][...])
        x_tail[rows, :] = x[:, 2 * block :]
        x_turned[:, rows] = jnp.transpose(x[...])


def activate(pre):
    sig = jax.nn.sigmoid(pre)
    return (pre * sig).astype(BF16), sig * (1.0 + pre * (1.0 - sig))


def most_down_kernel(block, shards, *refs):
    gs, tables = refs[0:shards], refs[shards : shards + shards // 2]
    x_tail, part, up_y, up_d = refs[shards + shards // 2 : shards + shards // 2 + 4]
    g, act_turned, slope, *sums = refs[shards + shards // 2 + 4 :]
    expert = lax.axis_index("expert")
    for pair in range(shards // 2):
        rows = slice(pair * 2 * SHARD, (pair + 1) * 2 * SHARD)
        for half in range(2):
            own = slice((pair * 2 + half) * SHARD, (pair * 2 + half + 1) * SHARD)
            g[own, :] = scale_rows(pick_gate(tables[pair], half, expert), gs[pair * 2 + half][...])
        pre = part[rows, :] + dot_rows(x_tail[rows, :block], up_y[...]) + dot_rows(x_tail[rows, block:], up_d[...])
        act, slope[rows, :] = activate(pre)
        act_turned[:, rows] = jnp.transpose(act)
    for place in range(3):
        sums[place][...] = dot_rows(act_turned[...], g[:, place * block : (place + 1) * block])


def last_forward_kernel(block, *refs):
    shards, ups = refs[0:4], refs[4:8]
    x_turned, act_turned, slope, x = refs[8:]
    for half in range(2):
        for bits in range(4):
            cols = owner_columns(block, bits)
            x[half * SHARD : (half + 1) * SHARD, bits * block : (bits + 1) * block] = (
                shards[2 * half][:, cols] + shards[2 * half + 1][:, cols]
            )
    pre = dot_rows(x[:, :block], ups[0][...])
    for bits in (1, 2, 3):
        pre = pre + dot_rows(x[:, bits * block : (bits + 1) * block], ups[bits][...])
    x_turned[...] = jnp.transpose(x[...])
    act, slope[...] = activate(pre)
    act_turned[...] = jnp.transpose(act)


def last_down_kernel(block, *refs):
    shards, table, act_turned, sums = refs[0:4], refs[4], refs[5], refs[6:9]
    g, far_a, far_b, near_a, near_b, side_a, side_b = refs[9:]
    expert = lax.axis_index("expert")
    for half in range(2):
        gate = pick_gate(table, half, expert)
        g[half * SHARD : (half + 1) * SHARD, :] = scale_rows(gate, shards[2 * half][...] + shards[2 * half + 1][...])
    middle = act_turned.shape[0] // 2
    total = dot_rows(act_turned[...], g[:, :block]) + sums[0][...]
    far_a[...] = total[:middle].astype(BF16)
    far_b[...] = total[middle:].astype(BF16)
    total = dot_rows(act_turned[...], g[:, block : 2 * block]) + sums[1][...]
    near_a[...] = total[:middle].astype(BF16)
    side_b[...] = total[middle:]
    total = dot_rows(act_turned[...], g[:, 2 * block :]) + sums[2][...]
    side_a[...] = total[:middle]
    near_b[...] = total[middle:].astype(BF16)


def early_backward_kernel(block, g, *refs):
    downs, part = refs[0:3], refs[3]
    for pair in range(g.shape[0] // (2 * SHARD)):
        rows = slice(pair * 2 * SHARD, (pair + 1) * 2 * SHARD)
        total = dot_last(g[rows, :block], downs[0][...])
        for place in (1, 2):
            total = total + dot_last(g[rows, place * block : (place + 1) * block], downs[place][...])
        part[rows, :] = total


def most_up_kernel(block, shards, *refs):
    gs, tables = refs[0:shards], refs[shards : shards + shards // 2]
    part, slope, x_turned, act_turned, down = refs[shards + shards // 2 : shards + shards // 2 + 5]
    sums, down_own = refs[shards + shards // 2 + 5 : shards + shards // 2 + 9], refs[shards + shards // 2 + 9]
    g, back = refs[shards + shards // 2 + 10 :]
    expert = lax.axis_index("expert")
    for pair in range(shards // 2):
        rows = slice(pair * 2 * SHARD, (pair + 1) * 2 * SHARD)
        for half in range(2):
            own = slice((pair * 2 + half) * SHARD, (pair * 2 + half + 1) * SHARD)
            g[own, :] = scale_rows(pick_gate(tables[pair], half, expert), gs[pair * 2 + half][...])
        back[rows, :] = ((part[rows, :] + dot_last(g[rows, :], down[...])) * slope[rows, :]).astype(BF16)
    for bits in range(4):
        sums[bits][...] = dot_rows(x_turned[bits * block : (bits + 1) * block, :], back[...])
    down_own[...] = dot_rows(act_turned[...], g[...])


def last_up_kernel(block, *refs):
    shards, table, g, slope, x_turned, act_turned = refs[0:2], refs[2], refs[3], refs[4], refs[5], refs[6]
    downs, sums, down_sum = refs[7:11], refs[11:15], refs[15]
    far_a, far_b, near_a, near_b, side_a, side_b, up_own, down_own = refs[16:24]
    kept, back = refs[24:]
    expert = lax.axis_index("expert")
    for half in range(2):
        gate = pick_gate(table, half, expert)
        kept[half * SHARD : (half + 1) * SHARD, :] = scale_rows(gate, shards[half][...])
    grad = dot_last(kept[...], downs[0][...])
    for place, bits in enumerate(SENT):
        grad = grad + dot_last(g[:, place * block : (place + 1) * block], downs[bits][...])
    back[...] = (grad * slope[...]).astype(BF16)
    middle = block // 2
    total = dot_rows(x_turned[3 * block :, :], back[...]) + sums[3][...]
    far_a[...] = total[:middle].astype(BF16)
    far_b[...] = total[middle:].astype(BF16)
    total = dot_rows(x_turned[block : 2 * block, :], back[...]) + sums[1][...]
    near_a[...] = total[:middle].astype(BF16)
    side_b[...] = total[middle:]
    total = dot_rows(x_turned[2 * block : 3 * block, :], back[...]) + sums[2][...]
    side_a[...] = total[:middle]
    near_b[...] = total[middle:].astype(BF16)
    up_own[...] = dot_rows(x_turned[:block, :], back[...]) + sums[0][...]
    down_own[...] = dot_rows(act_turned[...], kept[...]) + down_sum[...]


def finish_kernel(own, near_a, near_b, far_a, far_b, out):
    middle = own.shape[0] // 2
    out[:middle, :] = (own[:middle, :] + near_a[...].astype(F32) + far_a[...].astype(F32)).astype(BF16)
    out[middle:, :] = (own[middle:, :] + near_b[...].astype(F32) + far_b[...].astype(F32)).astype(BF16)


VMEM = pl.BlockSpec(memory_space=pltpu.VMEM)


def local_call(kernel, outs, args, scratch=(), flops=0):
    moved = sum(v.size * v.dtype.itemsize for v in (*args, *outs))
    return pl.pallas_call(
        kernel,
        out_shape=outs,
        in_specs=[VMEM] * len(args),
        out_specs=[VMEM] * len(outs),
        scratch_shapes=list(scratch),
        compiler_params=pltpu.CompilerParams(vmem_limit_bytes=GRANT * MIB),
        cost_estimate=pl.CostEstimate(flops=flops, bytes_accessed=moved, transcendentals=0),
    )(*args)


GRANT = 24


def shape(rows, cols, dtype):
    return jax.ShapeDtypeStruct((rows, cols), dtype)


def prepare(grad, tokens, up, down):
    rows, width = grad.shape
    block = width // 4
    outs = [shape(rows, 3 * block, BF16), shape(rows, block, BF16)] + [shape(*v.shape, BF16) for v in (tokens, up, down)]
    return local_call(functools.partial(prepare_kernel, block), outs, (grad, tokens, up, down))


def early_forward(xs, ups):
    block, hidden = ups[0].shape
    rows, width = len(xs) * SHARD, 4 * block
    return local_call(
        functools.partial(early_forward_kernel, block, len(xs)),
        [shape(rows, 2 * block, BF16), shape(width, rows, BF16), shape(rows, hidden, F32)],
        (*xs, *ups[:2]),
        [pltpu.VMEM((2 * SHARD, width), BF16)],
        flops=4 * rows * block * hidden,
    )


def most_down(gs, tables, x_tail, part, up_y, up_d):
    block, hidden = up_y.shape
    rows = len(gs) * SHARD
    return local_call(
        functools.partial(most_down_kernel, block, len(gs)),
        [shape(rows, 3 * block, BF16), shape(hidden, rows, BF16), shape(rows, hidden, F32)] + [shape(hidden, block, F32)] * 3,
        (*gs, *tables, x_tail, part, up_y, up_d),
        flops=10 * rows * block * hidden,
    )


def last_forward(shards, ups):
    block, hidden = ups[0].shape
    rows, width = 2 * SHARD, 4 * block
    return local_call(
        functools.partial(last_forward_kernel, block),
        [shape(width, rows, BF16), shape(hidden, rows, BF16), shape(rows, hidden, F32)],
        (*shards, *ups),
        [pltpu.VMEM((rows, width), BF16)],
        flops=2 * rows * width * hidden,
    )


def exchanged(rows, cols):
    return [shape(rows // 2, cols, BF16)] * 4 + [shape(rows // 2, cols, F32)] * 2


def last_down(shards, table, act_turned, sums):
    hidden, block = sums[0].shape
    return local_call(
        functools.partial(last_down_kernel, block),
        [shape(2 * SHARD, 3 * block, BF16)] + exchanged(hidden, block),
        (*shards, table, act_turned, *sums),
        flops=12 * SHARD * block * hidden,
    )


def early_backward(g, downs):
    hidden, block = downs[0].shape
    rows = g.shape[0]
    return local_call(
        functools.partial(early_backward_kernel, block),
        [shape(rows, hidden, F32)],
        (g, *(downs[bits] for bits in SENT)),
        flops=6 * rows * block * hidden,
    )[0]


def most_up(gs, tables, part, slope, x_turned, act_turned, down):
    hidden, block = down.shape
    rows = len(gs) * SHARD
    got = local_call(
        functools.partial(most_up_kernel, block, len(gs)),
        [shape(block, hidden, F32)] * 4 + [shape(hidden, block, F32)],
        (*gs, *tables, part, slope, x_turned, act_turned, down),
        [pltpu.VMEM((rows, block), BF16), pltpu.VMEM((rows, hidden), BF16)],
        flops=12 * rows * block * hidden,
    )
    return got[:4], got[4]


def last_up(shards, table, g, slope, x_turned, act_turned, downs, sums, down_sum):
    hidden, block = downs[0].shape
    rows = 2 * SHARD
    return local_call(
        functools.partial(last_up_kernel, block),
        exchanged(block, hidden) + [shape(block, hidden, F32), shape(hidden, block, F32)],
        (*shards, table, g, slope, x_turned, act_turned, *downs, *sums, down_sum),
        [pltpu.VMEM((rows, block), BF16), pltpu.VMEM((rows, hidden), BF16)],
        flops=18 * rows * block * hidden,
    )


def finish(own, near_a, near_b, far_a, far_b):
    return local_call(finish_kernel, [shape(*own.shape, BF16)], (own, near_a, near_b, far_a, far_b))[0]


def dense_shards(tokens, grad_out, expert_ids, gate_q, w_up, w_down):
    return dense_body(tokens, grad_out, expert_ids, gate_q, w_up[0], w_down[0])


def dense_body(tokens, grad_out, expert_ids, gate_q, w_up, w_down):
    devices = lax.axis_size("expert")

    def ex(value, perm):
        return lax.ppermute(value, "expert", perm)

    def dp(value, bits):
        return lax.ppermute(value, "dp", xor_perm(4, bits))

    swap = xor_perm(devices, 1)

    def ring(hops):
        return [(i, (i + 2 * hops) % devices) for i in range(devices)]

    up_mid = [(i, i + 2) for i in range(2, devices - 2)]
    down_mid = [(i, i - 2) for i in range(2, devices - 2)]

    ga, gb, tokens_here, up_here, down_here = prepare(grad_out, tokens, w_up, w_down)

    t1 = ex(tokens, ring(1))
    t3 = ex(tokens, ring(-1))
    up_x = dp(w_up, 1)
    down_y = dp(w_down, 2)
    ga1 = ex(ga, ring(1))
    ga3 = ex(ga, ring(-1))
    up_y = dp(w_up, 2)
    down_x = dp(w_down, 1)

    experts = jnp.arange(devices, dtype=jnp.int32)
    named = expert_ids.T[None, :, :] == experts[:, None, None]
    gate_table = jnp.sum(jnp.where(named, gate_q.T[None, :, :], 0), axis=1).astype(F32) * (1.0 / 65536.0)
    c0 = jnp.concatenate([gate_table, ex(gate_table, swap)], axis=1)
    c1 = ex(c0, ring(1))
    c2 = ex(c0, ring(2))
    c3 = ex(c0, ring(3))
    t0b = ex(tokens, swap)
    ga0b = ex(ga, swap)
    gb0b = ex(gb, swap)

    up_d = dp(up_x, 2)
    down_d = dp(down_y, 1)
    t2u = ex(t1, up_mid)
    t2d = ex(t3, down_mid)
    t1b = ex(t1, swap)
    t3b = ex(t3, swap)
    ga2u = ex(ga1, up_mid)
    ga2d = ex(ga3, down_mid)
    ga1b = ex(ga1, swap)
    ga3b = ex(ga3, swap)
    gb1 = ex(gb, ring(1))
    gb3 = ex(gb, ring(-1))
    gb2 = ex(gb, ring(2))
    t2ub = ex(t2u, swap)
    t2db = ex(t2d, swap)
    ga2ub = ex(ga2u, swap)
    ga2db = ex(ga2d, swap)
    gb1b = ex(gb1, swap)
    gb3b = ex(gb3, swap)
    gb2b = ex(gb2, swap)

    ups = (up_here, up_x, up_y, up_d)
    downs = (down_here, down_x, down_y, down_d)
    tables = (c0, c1, c3)
    x_tail, x_turned, pre_part = early_forward((tokens_here, t0b, t1, t1b, t3, t3b), ups)
    g_ab, act_ab, slope_ab, *down_sums = most_down((ga, ga0b, ga1, ga1b, ga3, ga3b), tables, x_tail, pre_part, up_y, up_d)
    x_c, act_c, slope_c = last_forward((t2u, t2d, t2ub, t2db), ups)
    g_c, *down_parts = last_down((ga2u, ga2d, ga2ub, ga2db), c2, act_c, down_sums)
    grad_part = early_backward(g_ab, downs)
    up_sums, down_sum = most_up((gb, gb0b, gb1, gb1b, gb3, gb3b), tables, grad_part, slope_ab, x_turned, act_ab, down_here)
    *up_parts, up_own, down_own = last_up((gb2, gb2b), c2, g_c, slope_c, x_c, act_c, downs, up_sums, down_sum)

    def exchange(far_a, far_b, near_a, near_b, side_a, side_b):
        far_a = dp(far_a, 1)
        far_b = dp(far_b, 2)
        near_a = dp(near_a, 1)
        near_b = dp(near_b, 2)
        side_a = (side_a + far_a.astype(F32)).astype(BF16)
        side_b = (side_b + far_b.astype(F32)).astype(BF16)
        return near_a, near_b, dp(side_a, 2), dp(side_b, 1)

    down_got = exchange(*down_parts)
    up_got = exchange(*up_parts)
    dw_down = finish(down_own, *down_got)
    dw_up = finish(up_own, *up_got)
    return dw_up[None], dw_down[None]


def shards(tokens, grad_out, expert_ids, gate_q, w_up, w_down):
    devices = lax.axis_size("expert")
    token_count, top_count = expert_ids.shape
    capacity = max(2, token_count * top_count * 3 // (2 * devices))
    if 2 * capacity >= token_count and devices == 8 and lax.axis_size("dp") == 4 and token_count == SHARD:
        return dense_shards(tokens, grad_out, expert_ids, gate_q, w_up, w_down)
    return sparse_shards(tokens, grad_out, expert_ids, gate_q, w_up, w_down, capacity)


def solution(mesh):
    in_specs = (
        P(("dp", "expert"), None),
        P(("dp", "expert"), None),
        P(("dp", "expert"), None),
        P(("dp", "expert"), None),
        P("expert", "dp", None),
        P("expert", None, "dp"),
    )
    out_specs = (P("expert", "dp", None), P("expert", None, "dp"))
    return jax.shard_map(shards, mesh=mesh, in_specs=in_specs, out_specs=out_specs, check_vma=False)
```

time: 145 us -> 145 us (level)
  Pallas kernels: 13.3 us -> 18.5 us
  waiting for transfers between devices: 85.6 us -> 82.5 us
  other arithmetic: 2.93 us -> 0.26 us
  matrix products: 2.07 us -> 0 us
  starting transfers between devices: 38.3 us -> 40.3 us
    ppermute x12 -> x18, waiting for transfers between devices: 57.1 us -> 35.4 us  [dp(): return lax.ppermute(value, 'dp', xor_perm(4, bits))]
    ppermute x22 -> x29, waiting for transfers between devices: 28.5 us -> 47.1 us  [ex(): return lax.ppermute(value, 'expert', perm)]
    ppermute x12 -> x18, starting transfers between devices: 13.8 us -> 19.5 us  [dp(): return lax.ppermute(value, 'dp', xor_perm(4, bits))]
    pallas_call x5 -> x10, Pallas kernels: 13.3 us -> 18.5 us  [local_call(): pl.pallas_call(kernel, out_shape=outs, in_specs=[VMEM] * len(args), out_s...]
    ppermute x22 -> x29, starting transfers between devices: 24.5 us -> 20.7 us  [ex(): return lax.ppermute(value, 'expert', perm)]
    dot_general x6 -> x0, matrix products: 2.07 us -> none  [dot_rows(): return jnp.dot(left, right, preferred_element_type=F32)]
    broadcast_in_dim x2 -> x0, other arithmetic: 1.99 us -> none  [dense_body(): return (dw_up[None], dw_down[None])]
  transfers between devices with their start and end apart: 34 -> 47, of which waited for: 11 -> 17; matrix products, arithmetic and copies ran while one was open for 3% -> 0% of each run, Pallas kernels for 8% -> 11%
where the time goes in v4:
time: 145 us; the launch traced here: 144 us
  waiting for transfers between devices  82.5 us (57%)
  starting transfers between devices  40.3 us (28%)
  Pallas kernels  18.5 us (13%)
  local copies, waits for them, and re-layouts  2.07 us (1%)
    ppermute x29, waiting for transfers between devices, ex(): return lax.ppermute(value, 'expert', perm)  47.1 us
    ppermute x18, waiting for transfers between devices, dp(): return lax.ppermute(value, 'dp', xor_perm(4, bits))  35.4 us
    ppermute x29, starting transfers between devices, ex(): return lax.ppermute(value, 'expert', perm)  20.7 us
    ppermute x18, starting transfers between devices, dp(): return lax.ppermute(value, 'dp', xor_perm(4, bits))  19.5 us
    pallas_call x10, Pallas kernels, local_call(): pl.pallas_call(kernel, out_shape=outs, in_specs=[VMEM] * len(args), out_s...  18.5 us
  transfers between devices with their start and end apart: 47, of which 17 were waited for; matrix products, arithmetic and copies ran while one was open for 0% of the time, Pallas kernels for 11%

profile of v4, /device:TPU:0, one launch (start us, length us, event | category | flops | bytes accessed | tf_op | source)
XLA Modules:
  0.0 144.5 jit_solution(4214504387145304137)
XLA Ops:
  4.1 3.1 %collective-permute-start.4 = (bf16[128,1152]{1,0:T(8,128)(2,1)S(1)}, bf16[128,1152]{1,0:T(8,128)(2,1)S(1)}, u32[]{:S(2)}, u32[]{:S(2)}) collective-permute-start(bf16[128,1152]{1,0:T(8,128)(2,1)S(1)} %get-tuple-element.40.refs_0_), channel_id=1, source_target_pairs={{0,2},{1,3},{2,4},{3,5},{4,6},{5,7},{6,0},{7,1},{8,10},{9,11},{10,... | collective-permute-start | bytes 884744 | tf_op jit(solution)/shard_map/ppermute | solution.py:369
  7.2 2.1 %collective-permute-start.6 = (bf16[128,1152]{1,0:T(8,128)(2,1)S(1)}, bf16[128,1152]{1,0:T(8,128)(2,1)S(1)}, u32[]{:S(2)}, u32[]{:S(2)}) collective-permute-start(bf16[128,1152]{1,0:T(8,128)(2,1)S(1)} %get-tuple-element.40.refs_0_), channel_id=1, source_target_pairs={{0,6},{1,7},{2,0},{3,1},{4,2},{5,3},{6,4},{7,5},{8,14},{9,15},{10,... | collective-permute-start | bytes 884744 | tf_op jit(solution)/shard_map/ppermute | solution.py:369
  10.9 3.4 %collective-permute-start.23 = (f32[8,256]{1,0:T(8,128)S(1)}, f32[8,256]{1,0:T(8,128)S(1)}, u32[]{:S(2)}, u32[]{:S(2)}) collective-permute-start(f32[8,256]{1,0:T(8,128)S(1)} %pad_maximum_fusion.refs_6_), channel_id=1, source_target_pairs={{0,6},{1,7},{2,0},{3,1},{4,2},{5,3},{6,4},{7,5},{8,14},{9,15},{10,... | collective-permute-start | bytes 24584 | tf_op jit(solution)/shard_map/ppermute | solution.py:369
  14.3 17.0 %collective-permute-done.22.refs_7_ = f32[8,256]{1,0:T(8,128)S(1)} collective-permute-done((f32[8,256]{1,0:T(8,128)S(1)}, f32[8,256]{1,0:T(8,128)S(1)}, u32[]{:S(2)}, u32[]{:S(2)}) %collective-permute-start.22) | collective-permute-done | bytes 8224 | tf_op jit(solution)/shard_map/ppermute | solution.py:369
  32.0 3.9 %collective-permute-done.3.refs_4_.refs_2_ = f32[8,256]{1,0:T(8,128)S(1)} collective-permute-done((f32[8,256]{1,0:T(8,128)S(1)}, f32[8,256]{1,0:T(8,128)S(1)}, u32[]{:S(2)}, u32[]{:S(2)}) %collective-permute-start.3) | collective-permute-done | bytes 8224 | tf_op jit(solution)/shard_map/ppermute | solution.py:369
  35.8 1.7 %collective-permute-start.12 = (bf16[128,1536]{1,0:T(8,128)(2,1)}, bf16[128,1536]{1,0:T(8,128)(2,1)S(1)}, u32[]{:S(2)}, u32[]{:S(2)}) collective-permute-start(bf16[128,1536]{1,0:T(8,128)(2,1)} %tokens.1), channel_id=1, source_target_pairs={{0,6},{1,7},{2,0},{3,1},{4,2},{5,3},{6,4},{7,5},{8,14},{9,15},{10,... | collective-permute-start | bytes 1179656 | tf_op jit(solution)/shard_map/ppermute | solution.py:369
  37.6 1.6 %collective-permute-start.16 = (bf16[384,768]{1,0:T(8,128)(2,1)S(1)}, bf16[384,768]{1,0:T(8,128)(2,1)S(1)}, u32[]{:S(2)}, u32[]{:S(2)}) collective-permute-start(bf16[384,768]{1,0:T(8,128)(2,1)S(1)} %bitcast.7), channel_id=1, source_target_pairs={{0,8},{8,0},{16,24},{24,16},{1,9},{9,1},{17,25},{25,17},{2,10},{10... | collective-permute-start | bytes 1769480 | tf_op jit(solution)/shard_map/ppermute | solution.py:372
  39.2 1.5 %collective-permute-start.17 = (bf16[384,768]{1,0:T(8,128)(2,1)S(1)}, bf16[384,768]{1,0:T(8,128)(2,1)S(1)}, u32[]{:S(2)}, u32[]{:S(2)}) collective-permute-start(bf16[384,768]{1,0:T(8,128)(2,1)S(1)} %bitcast.8), channel_id=1, source_target_pairs={{0,16},{8,24},{16,0},{24,8},{1,17},{9,25},{17,1},{25,9},{2,18},{10... | collective-permute-start | bytes 1769480 | tf_op jit(solution)/shard_map/ppermute | solution.py:372
  40.7 4.4 %collective-permute-done.12.refs_4_ = bf16[128,1536]{1,0:T(8,128)(2,1)S(1)} collective-permute-done((bf16[128,1536]{1,0:T(8,128)(2,1)}, bf16[128,1536]{1,0:T(8,128)(2,1)S(1)}, u32[]{:S(2)}, u32[]{:S(2)}) %collective-permute-start.12) | collective-permute-done | bytes 393248 | tf_op jit(solution)/shard_map/ppermute | solution.py:369
  46.4 6.9 %collective-permute-done.16.refs_5_.refs_7_ = bf16[384,768]{1,0:T(8,128)(2,1)S(1)} collective-permute-done((bf16[384,768]{1,0:T(8,128)(2,1)S(1)}, bf16[384,768]{1,0:T(8,128)(2,1)S(1)}, u32[]{:S(2)}, u32[]{:S(2)}) %collective-permute-start.16) | collective-permute-done | bytes 589856 | tf_op jit(solution)/shard_map/ppermute | solution.py:372
  55.4 1.6 %collective-permute-start.18 = (bf16[384,768]{1,0:T(8,128)(2,1)S(1)}, bf16[384,768]{1,0:T(8,128)(2,1)S(1)}, u32[]{:S(2)}, u32[]{:S(2)}) collective-permute-start(bf16[384,768]{1,0:T(8,128)(2,1)S(1)} %collective-permute-done.16.refs_5_.refs_7_), channel_id=1, source_target_pairs={{0,16},{8,24},{16,0},{24,8},{1,17},{9,25},{17,1},{25,9},{2,18},{10... | collective-permute-start | bytes 1769480 | tf_op jit(solution)/shard_map/ppermute | solution.py:372
  57.2 7.3 %collective-permute-done.7.refs_1_ = bf16[128,1152]{1,0:T(8,128)(2,1)S(1)} collective-permute-done((bf16[128,1152]{1,0:T(8,128)(2,1)S(1)}, bf16[128,1152]{1,0:T(8,128)(2,1)S(1)}, u32[]{:S(2)}, u32[]{:S(2)}) %collective-permute-start.7) | collective-permute-done | bytes 294944 | tf_op jit(solution)/shard_map/ppermute | solution.py:369
  65.1 2.9 %collective-permute-done.28.refs_2_.refs_9_ = bf16[768,384]{1,0:T(8,128)(2,1)S(1)} collective-permute-done((bf16[768,384]{1,0:T(8,128)(2,1)}, bf16[768,384]{1,0:T(8,128)(2,1)S(1)}, u32[]{:S(2)}, u32[]{:S(2)}) %collective-permute-start.28) | collective-permute-done | bytes 589856 | tf_op jit(solution)/shard_map/ppermute | solution.py:372
  70.0 1.5 %collective-permute-start.29 = (bf16[768,384]{1,0:T(8,128)(2,1)S(1)}, bf16[768,384]{1,0:T(8,128)(2,1)S(1)}, u32[]{:S(2)}, u32[]{:S(2)}) collective-permute-start(bf16[768,384]{1,0:T(8,128)(2,1)S(1)} %collective-permute-done.28.refs_2_.refs_9_), channel_id=1, source_target_pairs={{0,8},{8,0},{16,24},{24,16},{1,9},{9,1},{17,25},{25,17},{2,10},{10... | collective-permute-start | bytes 1769480 | tf_op jit(solution)/shard_map/ppermute | solution.py:372
  71.5 7.9 %collective-permute-done.13.refs_1_ = bf16[128,1536]{1,0:T(8,128)(2,1)S(1)} collective-permute-done((bf16[128,1536]{1,0:T(8,128)(2,1)S(1)}, bf16[128,1536]{1,0:T(8,128)(2,1)S(1)}, u32[]{:S(2)}, u32[]{:S(2)}) %collective-permute-start.13) | collective-permute-done | bytes 393248 | tf_op jit(solution)/shard_map/ppermute | solution.py:369
  80.0 1.6 %shard_map.79 = (bf16[768,768]{1,0:T(8,128)(2,1)S(1)}, bf16[1536,768]{1,0:T(8,128)(2,1)S(1)}, f32[768,768]{1,0:T(8,128)S(1)}) custom-call(bf16[128,1536]{1,0:T(8,128)(2,1)S(1)} %get-tuple-element.43.refs_0_, bf16[128,1536]{1,0:T(8,128)(2,1)S(1)} %collective-permute-done.24.refs_1_, bf16[128,1536]{1,0:T(8,128)(2,1)S(1)} %collective-permute-done.10.refs_2_, ...), custom_call_target="tpu_custom_call" | custom-call | flops 905969664 | bytes 9437184 | tf_op jit(solution)/shard_map/pallas_call | solution.py:247
  81.6 3.5 %shard_map.80 = (bf16[768,1152]{1,0:T(8,128)(2,1)S(1)}, bf16[768,768]{1,0:T(8,128)(2,1)S(1)}, f32[768,768]{1,0:T(8,128)S(1)}, f32[768,384]{1,0:T(8,128)S(1)}, f3...) custom-call(bf16[128,1152]{1,0:T(8,128)(2,1)S(1)} %get-tuple-element.40.refs_0_, ...), custom_call_target="tpu_custom_call" | custom-call | flops 2264924160 | bytes 15360000 | tf_op jit(solution)/shard_map/pallas_call | solution.py:247
  85.5 3.5 %collective-permute-start.33 = (bf16[128,384]{1,0:T(8,128)(2,1)S(1)}, bf16[128,384]{1,0:T(8,128)(2,1)S(1)}, u32[]{:S(2)}, u32[]{:S(2)}) collective-permute-start(bf16[128,384]{1,0:T(8,128)(2,1)S(1)} %get-tuple-element.39.refs_0_), channel_id=1, source_target_pairs={{0,6},{1,7},{2,0},{3,1},{4,2},{5,3},{6,4},{7,5},{8,14},{9,15},{10,... | collective-permute-start | bytes 294920 | tf_op jit(solution)/shard_map/ppermute | solution.py:369
  91.2 1.5 %collective-permute-done.31.refs_2_ = bf16[128,384]{1,0:T(8,128)(2,1)S(1)} collective-permute-done((bf16[128,384]{1,0:T(8,128)(2,1)S(1)}, bf16[128,384]{1,0:T(8,128)(2,1)S(1)}, u32[]{:S(2)}, u32[]{:S(2)}) %collective-permute-start.31) | collective-permute-done | bytes 98336 | tf_op jit(solution)/shard_map/ppermute | solution.py:369
  94.0 2.7 %collective-permute-done.refs_0_ = bf16[128,384]{1,0:T(8,128)(2,1)S(1)} collective-permute-done((bf16[128,384]{1,0:T(8,128)(2,1)S(1)}, bf16[128,384]{1,0:T(8,128)(2,1)S(1)}, u32[]{:S(2)}, u32[]{:S(2)}) %collective-permute-start) | collective-permute-done | bytes 98336 | tf_op jit(solution)/shard_map/ppermute | solution.py:369
  98.0 1.5 %collective-permute-start.45 = (bf16[384,384]{1,0:T(8,128)(2,1)S(1)}, bf16[384,384]{1,0:T(8,128)(2,1)S(1)}, u32[]{:S(2)}, u32[]{:S(2)}) collective-permute-start(bf16[384,384]{1,0:T(8,128)(2,1)S(1)} %get-tuple-element.75), channel_id=1, source_target_pairs={{0,16},{8,24},{16,0},{24,8},{1,17},{9,25},{17,1},{25,9},{2,18},{10... | collective-permute-start | bytes 884744 | tf_op jit(solution)/shard_map/ppermute | solution.py:372
  99.5 2.0 %shard_map.82.refs_9_ = f32[768,768]{1,0:T(8,128)S(1)} custom-call(bf16[768,1152]{1,0:T(8,128)(2,1)S(1)} %get-tuple-element.53.g, bf16[768,384]{1,0:T(8,128)(2,1)S(1)} %collective-permute-done.29.refs_0_.refs_10_, bf16[768,384]{1,0:T(8,128)(2,1)S(1)} %collective-permute-done.27.refs_1_.refs_8_, bf16[768,384]{1,0:T(8,128)(2,1)S(1)} %collective-permute-done.28.refs_2_.refs_9_), custom_call_target="tpu_custom_call" | custom-call | flops 1358954496 | bytes 5898240 | tf_op jit(solution)/shard_map/pallas_call | solution.py:247
  104.1 3.4 %shard_map.83 = (f32[384,768]{1,0:T(8,128)S(1)}, f32[384,768]{1,0:T(8,128)S(1)}, f32[384,768]{1,0:T(8,128)S(1)}, f32[384,768]{1,0:T(8,128)S(1)}, f32[768,384]{1,0:T(8,128)S(1)}) custom-call(bf16[128,384]{1,0:T(8,128)(2,1)S(1)} %get-tuple-element.39.refs_0_, bf16[128,384]{1,0:T(8,128)(2,1)S(1)} %collective-permute-done.30.refs_1_, ...), custom_call_target="tpu_custom_call" | custom-call | flops 2717908992 | bytes 15360000 | tf_op jit(solution)/shard_map/pallas_call | solution.py:247
  107.5 2.4 %shard_map.84 = (bf16[192,768]{1,0:T(8,128)(2,1)S(1)}, bf16[192,768]{1,0:T(8,128)(2,1)S(1)}, bf16[192,768]{1,0:T(8,128)(2,1)S(1)}, bf16[192,768]{1,0:T(8,128)(2,...) custom-call(bf16[128,384]{1,0:T(8,128)(2,1)S(1)} %collective-permute-, ...), custom_call_target="tpu_custom_call" | custom-call | flops 1358954496 | bytes 15736832 | tf_op jit(solution)/shard_map/pallas_call | solution.py:247
  109.9 1.6 %collective-permute-start.39 = (bf16[192,768]{1,0:T(8,128)(2,1)S(1)}, bf16[192,768]{1,0:T(8,128)(2,1)S(1)}, u32[]{:S(2)}, u32[]{:S(2)}) collective-permute-start(bf16[192,768]{1,0:T(8,128)(2,1)S(1)} %get-tuple-element.68), channel_id=1, source_target_pairs={{0,16},{8,24},{16,0},{24,8},{1,17},{9,25},{17,1},{25,9},{2,18},{10... | collective-permute-start | bytes 884744 | tf_op jit(solution)/shard_map/ppermute | solution.py:372
  112.1 1.6 %collective-permute-start.35 = (bf16[192,768]{1,0:T(8,128)(2,1)S(1)}, bf16[192,768]{1,0:T(8,128)(2,1)S(1)}, u32[]{:S(2)}, u32[]{:S(2)}) collective-permute-start(bf16[192,768]{1,0:T(8,128)(2,1)S(1)} %get-tuple-element.63), channel_id=1, source_target_pairs={{0,8},{8,0},{16,24},{24,16},{1,9},{9,1},{17,25},{25,17},{2,10},{10... | collective-permute-start | bytes 884744 | tf_op jit(solution)/shard_map/ppermute | solution.py:372
  113.8 5.3 %collective-permute-done.39 = bf16[192,768]{1,0:T(8,128)(2,1)S(1)} collective-permute-done((bf16[192,768]{1,0:T(8,128)(2,1)S(1)}, bf16[192,768]{1,0:T(8,128)(2,1)S(1)}, u32[]{:S(2)}, u32[]{:S(2)}) %collective-permute-start.39) | collective-permute-done | bytes 294944 | tf_op jit(solution)/shard_map/ppermute | solution.py:372
  119.7 4.4 %collective-permute-done.37 = bf16[192,768]{1,0:T(8,128)(2,1)S(1)} collective-permute-done((bf16[192,768]{1,0:T(8,128)(2,1)S(1)}, bf16[192,768]{1,0:T(8,128)(2,1)S(1)}, u32[]{:S(2)}, u32[]{:S(2)}) %collective-permute-start.37) | collective-permute-done | bytes 294944 | tf_op jit(solution)/shard_map/ppermute | solution.py:372
  124.7 1.6 %collective-permute-start.36 = (bf16[192,768]{1,0:T(8,128)(2,1)S(1)}, bf16[192,768]{1,0:T(8,128)(2,1)S(1)}, u32[]{:S(2)}, u32[]{:S(2)}) collective-permute-start(bf16[192,768]{1,0:T(8,128)(2,1)S(1)} %get-tuple-element.64), channel_id=1, source_target_pairs={{0,16},{8,24},{16,0},{24,8},{1,17},{9,25},{17,1},{25,9},{2,18},{10... | collective-permute-start | bytes 884744 | tf_op jit(solution)/shard_map/ppermute | solution.py:372
  126.8 9.9 %collective-permute-done.46.far_b = bf16[384,384]{1,0:T(8,128)(2,1)S(1)} collective-permute-done((bf16[384,384]{1,0:T(8,128)(2,1)S(1)}, bf16[384,384]{1,0:T(8,128)(2,1)S(1)}, u32[]{:S(2)}, u32[]{:S(2)}) %collective-permute-start.46) | collective-permute-done | bytes 294944 | tf_op jit(solution)/shard_map/ppermute | solution.py:372
  138.3 3.1 %collective-permute-done.40.far_b = bf16[192,768]{1,0:T(8,128)(2,1)S(1)} collective-permute-done((bf16[192,768]{1,0:T(8,128)(2,1)S(1)}, bf16[192,768]{1,0:T(8,128)(2,1)S(1)}, u32[]{:S(2)}, u32[]{:S(2)}) %collective-permute-start.40) | collective-permute-done | bytes 294944 | tf_op jit(solution)/shard_map/ppermute | solution.py:372
  141.4 2.1 %collective-permute-done.38.far_a = bf16[192,768]{1,0:T(8,128)(2,1)S(1)} collective-permute-done((bf16[192,768]{1,0:T(8,128)(2,1)S(1)}, bf16[192,768]{1,0:T(8,128)(2,1)S(1)}, u32[]{:S(2)}, u32[]{:S(2)}) %collective-permute-start.38) | collective-permute-done | bytes 294944 | tf_op jit(solution)/shard_map/ppermute | solution.py:372
  (87 shorter events, 25.0 us)
Async XLA Ops:
  4.1 33.5 %collective-permute-start.4 = (bf16[128,1152]{1,0:T(8,128)(2,1)S(1)}, bf16[128,1152]{1,0:T(8,128)(2,1)S(1)}, u32[]{:S(2)}, u32[]{:S(2)}) collective-permute-start(bf16[128,1152]{1,0:T(8,128)(2,1)S(1)} %get-tuple-element.40.refs_0_), channel_id=1, source_target_pairs={{0,2},{1,3},{2,4},{3,5},{4,6},{5,7},{6,0},{7,1},{8,10},{9,11},{10,... | collective-permute-start | bytes 884744 | tf_op jit(solution)/shard_map/ppermute | solution.py:369
  7.2 30.4 %collective-permute-start.6 = (bf16[128,1152]{1,0:T(8,128)(2,1)S(1)}, bf16[128,1152]{1,0:T(8,128)(2,1)S(1)}, u32[]{:S(2)}, u32[]{:S(2)}) collective-permute-start(bf16[128,1152]{1,0:T(8,128)(2,1)S(1)} %get-tuple-element.40.refs_0_), channel_id=1, source_target_pairs={{0,6},{1,7},{2,0},{3,1},{4,2},{5,3},{6,4},{7,5},{8,14},{9,15},{10,... | collective-permute-start | bytes 884744 | tf_op jit(solution)/shard_map/ppermute | solution.py:369
  9.4 31.3 %collective-permute-start.10 = (bf16[128,1536]{1,0:T(8,128)(2,1)}, bf16[128,1536]{1,0:T(8,128)(2,1)S(1)}, u32[]{:S(2)}, u32[]{:S(2)}) collective-permute-start(bf16[128,1536]{1,0:T(8,128)(2,1)} %tokens.1), channel_id=1, source_target_pairs={{0,2},{1,3},{2,4},{3,5},{4,6},{5,7},{6,0},{7,1},{8,10},{9,11},{10,... | collective-permute-start | bytes 1179656 | tf_op jit(solution)/shard_map/ppermute | solution.py:369
  10.5 20.8 %collective-permute-start.22 = (f32[8,256]{1,0:T(8,128)S(1)}, f32[8,256]{1,0:T(8,128)S(1)}, u32[]{:S(2)}, u32[]{:S(2)}) collective-permute-start(f32[8,256]{1,0:T(8,128)S(1)} %pad_maximum_fusion.refs_6_), channel_id=1, source_target_pairs={{0,2},{1,3},{2,4},{3,5},{4,6},{5,7},{6,0},{7,1},{8,10},{9,11},{10,... | collective-permute-start | bytes 24584 | tf_op jit(solution)/shard_map/ppermute | solution.py:369
  10.9 21.0 %collective-permute-start.23 = (f32[8,256]{1,0:T(8,128)S(1)}, f32[8,256]{1,0:T(8,128)S(1)}, u32[]{:S(2)}, u32[]{:S(2)}) collective-permute-start(f32[8,256]{1,0:T(8,128)S(1)} %pad_maximum_fusion.refs_6_), channel_id=1, source_target_pairs={{0,6},{1,7},{2,0},{3,1},{4,2},{5,3},{6,4},{7,5},{8,14},{9,15},{10,... | collective-permute-start | bytes 24584 | tf_op jit(solution)/shard_map/ppermute | solution.py:369
  35.8 9.3 %collective-permute-start.12 = (bf16[128,1536]{1,0:T(8,128)(2,1)}, bf16[128,1536]{1,0:T(8,128)(2,1)S(1)}, u32[]{:S(2)}, u32[]{:S(2)}) collective-permute-start(bf16[128,1536]{1,0:T(8,128)(2,1)} %tokens.1), channel_id=1, source_target_pairs={{0,6},{1,7},{2,0},{3,1},{4,2},{5,3},{6,4},{7,5},{8,14},{9,15},{10,... | collective-permute-start | bytes 1179656 | tf_op jit(solution)/shard_map/ppermute | solution.py:369
  37.6 15.7 %collective-permute-start.16 = (bf16[384,768]{1,0:T(8,128)(2,1)S(1)}, bf16[384,768]{1,0:T(8,128)(2,1)S(1)}, u32[]{:S(2)}, u32[]{:S(2)}) collective-permute-start(bf16[384,768]{1,0:T(8,128)(2,1)S(1)} %bitcast.7), channel_id=1, source_target_pairs={{0,8},{8,0},{16,24},{24,16},{1,9},{9,1},{17,25},{25,17},{2,10},{10... | collective-permute-start | bytes 1769480 | tf_op jit(solution)/shard_map/ppermute | solution.py:372
  39.2 16.3 %collective-permute-start.17 = (bf16[384,768]{1,0:T(8,128)(2,1)S(1)}, bf16[384,768]{1,0:T(8,128)(2,1)S(1)}, u32[]{:S(2)}, u32[]{:S(2)}) collective-permute-start(bf16[384,768]{1,0:T(8,128)(2,1)S(1)} %bitcast.8), channel_id=1, source_target_pairs={{0,16},{8,24},{16,0},{24,8},{1,17},{9,25},{17,1},{25,9},{2,18},{10... | collective-permute-start | bytes 1769480 | tf_op jit(solution)/shard_map/ppermute | solution.py:372
  40.7 13.3 %collective-permute-start.20 = (bf16[128,1152]{1,0:T(8,128)(2,1)S(1)}, bf16[128,1152]{1,0:T(8,128)(2,1)S(1)}, u32[]{:S(2)}, u32[]{:S(2)}) collective-permute-start(bf16[128,1152]{1,0:T(8,128)(2,1)S(1)} %collective-permute-done.4.refs_2_), channel_id=1, source_target_pairs={{0,1},{1,0},{2,3},{3,2},{4,5},{5,4},{6,7},{7,6},{8,9},{9,8},{10,11... | collective-permute-start | bytes 884744 | tf_op jit(solution)/shard_map/ppermute | solution.py:369
  45.1 22.9 %collective-permute-start.28 = (bf16[768,384]{1,0:T(8,128)(2,1)}, bf16[768,384]{1,0:T(8,128)(2,1)S(1)}, u32[]{:S(2)}, u32[]{:S(2)}) collective-permute-start(bf16[768,384]{1,0:T(8,128)(2,1)} %bitcast.1.down), channel_id=1, source_target_pairs={{0,16},{8,24},{16,0},{24,8},{1,17},{9,25},{17,1},{25,9},{2,18},{10... | collective-permute-start | bytes 1769480 | tf_op jit(solution)/shard_map/ppermute | solution.py:372
  46.4 8.9 %collective-permute-start.21 = (bf16[128,1152]{1,0:T(8,128)(2,1)S(1)}, bf16[128,1152]{1,0:T(8,128)(2,1)S(1)}, u32[]{:S(2)}, u32[]{:S(2)}) collective-permute-start(bf16[128,1152]{1,0:T(8,128)(2,1)S(1)} %collective-permute-done.6.refs_4_), channel_id=1, source_target_pairs={{0,1},{1,0},{2,3},{3,2},{4,5},{5,4},{6,7},{7,6},{8,9},{9,8},{10,11... | collective-permute-start | bytes 884744 | tf_op jit(solution)/shard_map/ppermute | solution.py:369
  54.0 10.4 %collective-permute-start.7 = (bf16[128,1152]{1,0:T(8,128)(2,1)S(1)}, bf16[128,1152]{1,0:T(8,128)(2,1)S(1)}, u32[]{:S(2)}, u32[]{:S(2)}) collective-permute-start(bf16[128,1152]{1,0:T(8,128)(2,1)S(1)} %collective-permute-done.6.refs_4_), channel_id=1, source_target_pairs={{2,0},{3,1},{4,2},{5,3},{10,8},{11,9},{12,10},{13,11},{18,16},{19,... | collective-permute-start | bytes 884744 | tf_op jit(solution)/shard_map/ppermute | solution.py:369
  55.3 14.0 %collective-permute-start.25 = (bf16[128,1536]{1,0:T(8,128)(2,1)S(1)}, bf16[128,1536]{1,0:T(8,128)(2,1)S(1)}, u32[]{:S(2)}, u32[]{:S(2)}) collective-permute-start(bf16[128,1536]{1,0:T(8,128)(2,1)S(1)} %collective-permute-done.10.refs_2_), channel_id=1, source_target_pairs={{0,1},{1,0},{2,3},{3,2},{4,5},{5,4},{6,7},{7,6},{8,9},{9,8},{10,11... | collective-permute-start | bytes 1179656 | tf_op jit(solution)/shard_map/ppermute | solution.py:369
  55.4 24.5 %collective-permute-start.18 = (bf16[384,768]{1,0:T(8,128)(2,1)S(1)}, bf16[384,768]{1,0:T(8,128)(2,1)S(1)}, u32[]{:S(2)}, u32[]{:S(2)}) collective-permute-start(bf16[384,768]{1,0:T(8,128)(2,1)S(1)} %collective-permute-done.16.refs_5_.refs_7_), channel_id=1, source_target_pairs={{0,16},{8,24},{16,0},{24,8},{1,17},{9,25},{17,1},{25,9},{2,18},{10... | collective-permute-start | bytes 1769480 | tf_op jit(solution)/shard_map/ppermute | solution.py:372
  57.0 12.4 %collective-permute-start.26 = (bf16[128,1536]{1,0:T(8,128)(2,1)S(1)}, bf16[128,1536]{1,0:T(8,128)(2,1)S(1)}, u32[]{:S(2)}, u32[]{:S(2)}) collective-permute-start(bf16[128,1536]{1,0:T(8,128)(2,1)S(1)} %collective-permute-done.12.refs_4_), channel_id=1, source_target_pairs={{0,1},{1,0},{2,3},{3,2},{4,5},{5,4},{6,7},{7,6},{8,9},{9,8},{10,11... | collective-permute-start | bytes 1179656 | tf_op jit(solution)/shard_map/ppermute | solution.py:369
  68.0 11.4 %collective-permute-start.13 = (bf16[128,1536]{1,0:T(8,128)(2,1)S(1)}, bf16[128,1536]{1,0:T(8,128)(2,1)S(1)}, u32[]{:S(2)}, u32[]{:S(2)}) collective-permute-start(bf16[128,1536]{1,0:T(8,128)(2,1)S(1)} %collective-permute-done.12.refs_4_), channel_id=1, source_target_pairs={{2,0},{3,1},{4,2},{5,3},{10,8},{11,9},{12,10},{13,11},{18,16},{19,... | collective-permute-start | bytes 1179656 | tf_op jit(solution)/shard_map/ppermute | solution.py:369
  69.3 10.1 %collective-permute-start.8 = (bf16[128,1152]{1,0:T(8,128)(2,1)S(1)}, bf16[128,1152]{1,0:T(8,128)(2,1)S(1)}, u32[]{:S(2)}, u32[]{:S(2)}) collective-permute-start(bf16[128,1152]{1,0:T(8,128)(2,1)S(1)} %collective-permute-done.5.refs_0_), channel_id=1, source_target_pairs={{0,1},{1,0},{2,3},{3,2},{4,5},{5,4},{6,7},{7,6},{8,9},{9,8},{10,11... | collective-permute-start | bytes 884744 | tf_op jit(solution)/shard_map/ppermute | solution.py:369
  69.4 27.4 %collective-permute-start.27 = (bf16[768,384]{1,0:T(8,128)(2,1)}, bf16[768,384]{1,0:T(8,128)(2,1)S(1)}, u32[]{:S(2)}, u32[]{:S(2)}) collective-permute-start(bf16[768,384]{1,0:T(8,128)(2,1)} %bitcast.1.down), channel_id=1, source_target_pairs={{0,8},{8,0},{16,24},{24,16},{1,9},{9,1},{17,25},{25,17},{2,10},{10... | collective-permute-start | bytes 1769480 | tf_op jit(solution)/shard_map/ppermute | solution.py:372
  70.0 28.0 %collective-permute-start.29 = (bf16[768,384]{1,0:T(8,128)(2,1)S(1)}, bf16[768,384]{1,0:T(8,128)(2,1)S(1)}, u32[]{:S(2)}, u32[]{:S(2)}) collective-permute-start(bf16[768,384]{1,0:T(8,128)(2,1)S(1)} %collective-permute-done.28.refs_2_.refs_9_), channel_id=1, source_target_pairs={{0,8},{8,0},{16,24},{24,16},{1,9},{9,1},{17,25},{25,17},{2,10},{10... | collective-permute-start | bytes 1769480 | tf_op jit(solution)/shard_map/ppermute | solution.py:372
  79.4 9.6 %collective-permute-start.15 = (bf16[128,1536]{1,0:T(8,128)(2,1)S(1)}, bf16[128,1536]{1,0:T(8,128)(2,1)S(1)}, u32[]{:S(2)}, u32[]{:S(2)}) collective-permute-start(bf16[128,1536]{1,0:T(8,128)(2,1)S(1)} %collective-permute-done.13.refs_1_), channel_id=1, source_target_pairs={{0,1},{1,0},{2,3},{3,2},{4,5},{5,4},{6,7},{7,6},{8,9},{9,8},{10,11... | collective-permute-start | bytes 1179656 | tf_op jit(solution)/shard_map/ppermute | solution.py:369
  96.7 10.8 %collective-permute-start.1 = (bf16[128,384]{1,0:T(8,128)(2,1)S(1)}, bf16[128,384]{1,0:T(8,128)(2,1)S(1)}, u32[]{:S(2)}, u32[]{:S(2)}) collective-permute-start(bf16[128,384]{1,0:T(8,128)(2,1)S(1)} %collective-permute-done.refs_0_), channel_id=1, source_target_pairs={{0,1},{1,0},{2,3},{3,2},{4,5},{5,4},{6,7},{7,6},{8,9},{9,8},{10,11... | collective-permute-start | bytes 294920 | tf_op jit(solution)/shard_map/ppermute | solution.py:369
  98.0 13.6 %collective-permute-start.45 = (bf16[384,384]{1,0:T(8,128)(2,1)S(1)}, bf16[384,384]{1,0:T(8,128)(2,1)S(1)}, u32[]{:S(2)}, u32[]{:S(2)}) collective-permute-start(bf16[384,384]{1,0:T(8,128)(2,1)S(1)} %get-tuple-element.75), channel_id=1, source_target_pairs={{0,16},{8,24},{16,0},{24,8},{1,17},{9,25},{17,1},{25,9},{2,18},{10... | collective-permute-start | bytes 884744 | tf_op jit(solution)/shard_map/ppermute | solution.py:372
  101.5 10.6 %collective-permute-start.43 = (bf16[384,384]{1,0:T(8,128)(2,1)S(1)}, bf16[384,384]{1,0:T(8,128)(2,1)S(1)}, u32[]{:S(2)}, u32[]{:S(2)}) collective-permute-start(bf16[384,384]{1,0:T(8,128)(2,1)S(1)} %get-tuple-element.73), channel_id=1, source_target_pairs={{0,8},{8,0},{16,24},{24,16},{1,9},{9,1},{17,25},{25,17},{2,10},{10... | collective-permute-start | bytes 884744 | tf_op jit(solution)/shard_map/ppermute | solution.py:372
  102.1 22.6 %collective-permute-start.41 = (bf16[384,384]{1,0:T(8,128)(2,1)S(1)}, bf16[384,384]{1,0:T(8,128)(2,1)S(1)}, u32[]{:S(2)}, u32[]{:S(2)}) collective-permute-start(bf16[384,384]{1,0:T(8,128)(2,1)S(1)} %get-tuple-element.70), channel_id=1, source_target_pairs={{0,8},{8,0},{16,24},{24,16},{1,9},{9,1},{17,25},{25,17},{2,10},{10... | collective-permute-start | bytes 884744 | tf_op jit(solution)/shard_map/ppermute | solution.py:372
  103.6 22.7 %collective-permute-start.42 = (bf16[384,384]{1,0:T(8,128)(2,1)S(1)}, bf16[384,384]{1,0:T(8,128)(2,1)S(1)}, u32[]{:S(2)}, u32[]{:S(2)}) collective-permute-start(bf16[384,384]{1,0:T(8,128)(2,1)S(1)} %get-tuple-element.71), channel_id=1, source_target_pairs={{0,16},{8,24},{16,0},{24,8},{1,17},{9,25},{17,1},{25,9},{2,18},{10... | collective-permute-start | bytes 884744 | tf_op jit(solution)/shard_map/ppermute | solution.py:372
  109.9 9.1 %collective-permute-start.39 = (bf16[192,768]{1,0:T(8,128)(2,1)S(1)}, bf16[192,768]{1,0:T(8,128)(2,1)S(1)}, u32[]{:S(2)}, u32[]{:S(2)}) collective-permute-start(bf16[192,768]{1,0:T(8,128)(2,1)S(1)} %get-tuple-element.68), channel_id=1, source_target_pairs={{0,16},{8,24},{16,0},{24,8},{1,17},{9,25},{17,1},{25,9},{2,18},{10... | collective-permute-start | bytes 884744 | tf_op jit(solution)/shard_map/ppermute | solution.py:372
  111.5 12.6 %collective-permute-start.37 = (bf16[192,768]{1,0:T(8,128)(2,1)S(1)}, bf16[192,768]{1,0:T(8,128)(2,1)S(1)}, u32[]{:S(2)}, u32[]{:S(2)}) collective-permute-start(bf16[192,768]{1,0:T(8,128)(2,1)S(1)} %get-tuple-element.66), channel_id=1, source_target_pairs={{0,8},{8,0},{16,24},{24,16},{1,9},{9,1},{17,25},{25,17},{2,10},{10... | collective-permute-start | bytes 884744 | tf_op jit(solution)/shard_map/ppermute | solution.py:372
  112.1 26.2 %collective-permute-start.35 = (bf16[192,768]{1,0:T(8,128)(2,1)S(1)}, bf16[192,768]{1,0:T(8,128)(2,1)S(1)}, u32[]{:S(2)}, u32[]{:S(2)}) collective-permute-start(bf16[192,768]{1,0:T(8,128)(2,1)S(1)} %get-tuple-element.63), channel_id=1, source_target_pairs={{0,8},{8,0},{16,24},{24,16},{1,9},{9,1},{17,25},{25,17},{2,10},{10... | collective-permute-start | bytes 884744 | tf_op jit(solution)/shard_map/ppermute | solution.py:372
  119.1 17.6 %collective-permute-start.46 = (bf16[384,384]{1,0:T(8,128)(2,1)S(1)}, bf16[384,384]{1,0:T(8,128)(2,1)S(1)}, u32[]{:S(2)}, u32[]{:S(2)}) collective-permute-start(bf16[384,384]{1,0:T(8,128)(2,1)S(1)} %add_convert_fusion), channel_id=1, source_target_pairs={{0,8},{8,0},{16,24},{24,16},{1,9},{9,1},{17,25},{25,17},{2,10},{10... | collective-permute-start | bytes 884744 | tf_op jit(solution)/shard_map/ppermute | solution.py:372
  124.1 13.2 %collective-permute-start.44 = (bf16[384,384]{1,0:T(8,128)(2,1)S(1)}, bf16[384,384]{1,0:T(8,128)(2,1)S(1)}, u32[]{:S(2)}, u32[]{:S(2)}) collective-permute-start(bf16[384,384]{1,0:T(8,128)(2,1)S(1)} %add_convert_fusion.1), channel_id=1, source_target_pairs={{0,16},{8,24},{16,0},{24,8},{1,17},{9,25},{17,1},{25,9},{2,18},{10... | collective-permute-start | bytes 884744 | tf_op jit(solution)/shard_map/ppermute | solution.py:372
  124.7 13.6 %collective-permute-start.36 = (bf16[192,768]{1,0:T(8,128)(2,1)S(1)}, bf16[192,768]{1,0:T(8,128)(2,1)S(1)}, u32[]{:S(2)}, u32[]{:S(2)}) collective-permute-start(bf16[192,768]{1,0:T(8,128)(2,1)S(1)} %get-tuple-element.64), channel_id=1, source_target_pairs={{0,16},{8,24},{16,0},{24,8},{1,17},{9,25},{17,1},{25,9},{2,18},{10... | collective-permute-start | bytes 884744 | tf_op jit(solution)/shard_map/ppermute | solution.py:372
  126.3 15.1 %collective-permute-start.40 = (bf16[192,768]{1,0:T(8,128)(2,1)S(1)}, bf16[192,768]{1,0:T(8,128)(2,1)S(1)}, u32[]{:S(2)}, u32[]{:S(2)}) collective-permute-start(bf16[192,768]{1,0:T(8,128)(2,1)S(1)} %add_convert_fusion.2), channel_id=1, source_target_pairs={{0,8},{8,0},{16,24},{24,16},{1,9},{9,1},{17,25},{25,17},{2,10},{10... | collective-permute-start | bytes 884744 | tf_op jit(solution)/shard_map/ppermute | solution.py:372
  (19 other events, 113.9 us)

commit v5 on v4

--- a/solution.py
+++ b/solution.py
@@ -233,10 +233,25 @@
     down_own[...] = dot_rows(act_turned[...], kept[...]) + down_sum[...]
 
 
-def finish_kernel(own, near_a, near_b, far_a, far_b, out):
+def finish_kernel(parts, near_sum, far_a, far_b, out, stage, sems):
+    rows = near_sum.shape[0]
+    step = rows // parts
+    copies = []
+    for i in range(parts):
+        here = slice(i * step, (i + 1) * step)
+        far, base = (far_a, 0) if i * 2 < parts else (far_b, rows // 2)
+        got = far[i * step - base : (i + 1) * step - base, :]
+        stage[here, :] = (near_sum[here, :] + got.astype(F32)).astype(BF16)
+        copies.append(pltpu.make_async_copy(stage.at[pl.ds(i * step, step), :], out.at[pl.ds(i * step, step), :], sems.at[i]))
+        copies[-1].start()
+    for c in copies:
+        c.wait()
+
+
+def near_kernel(own, near_a, near_b, out):
     middle = own.shape[0] // 2
-    out[:middle, :] = (own[:middle, :] + near_a[...].astype(F32) + far_a[...].astype(F32)).astype(BF16)
-    out[middle:, :] = (own[middle:, :] + near_b[...].astype(F32) + far_b[...].astype(F32)).astype(BF16)
+    out[:middle, :] = own[:middle, :] + near_a[...].astype(F32)
+    out[middle:, :] = own[middle:, :] + near_b[...].astype(F32)
 
 
 VMEM = pl.BlockSpec(memory_space=pltpu.VMEM)
@@ -354,8 +369,21 @@
     )
 
 
-def finish(own, near_a, near_b, far_a, far_b):
-    return local_call(finish_kernel, [shape(*own.shape, BF16)], (own, near_a, near_b, far_a, far_b))[0]
+def with_near(own, near_a, near_b):
+    return local_call(near_kernel, [shape(*own.shape, F32)], (own, near_a, near_b))[0]
+
+
+def finish(near_sum, far_a, far_b):
+    parts = 4
+    return pl.pallas_call(
+        functools.partial(finish_kernel, parts),
+        out_shape=shape(*near_sum.shape, BF16),
+        in_specs=[VMEM] * 3,
+        out_specs=pl.BlockSpec(memory_space=pl.ANY),
+        scratch_shapes=[pltpu.VMEM(near_sum.shape, BF16), pltpu.SemaphoreType.DMA((parts,))],
+        compiler_params=pltpu.CompilerParams(vmem_limit_bytes=GRANT * MIB),
+        cost_estimate=pl.CostEstimate(flops=near_sum.size, bytes_accessed=10 * near_sum.size, transcendentals=0),
+    )(near_sum, far_a, far_b)
 
 
 def dense_shards(tokens, grad_out, expert_ids, gate_q, w_up, w_down):
@@ -444,8 +472,10 @@
 
     down_got = exchange(*down_parts)
     up_got = exchange(*up_parts)
-    dw_down = finish(down_own, *down_got)
-    dw_up = finish(up_own, *up_got)
+    down_sum = with_near(down_own, *down_got[:2])
+    dw_down = finish(down_sum, *down_got[2:])
+    up_sum = with_near(up_own, *up_got[:2])
+    dw_up = finish(up_sum, *up_got[2:])
     return dw_up[None], dw_down[None]
 
 

time: 145 us -> 143 us (0.986)
  waiting for transfers between devices: 82.5 us -> 79.4 us
    ppermute x18, waiting for transfers between devices: 35.4 us -> 32.3 us  [dp(): return lax.ppermute(value, 'dp', xor_perm(4, bits))]
    pallas_call x10, Pallas kernels: 18.5 us -> 16.7 us  [local_call(): pl.pallas_call(kernel, out_shape=outs, in_specs=[VMEM] * len(args), out_s...]
    pallas_call x0 -> x2, Pallas kernels: none -> 1.75 us  [finish(): pl.pallas_call(functools.partial(finish_kernel, parts), out_shape=shape(*...]
where the time goes in v5:
time: 143 us; the launch traced here: 142 us
  waiting for transfers between devices  79.4 us (56%)
  starting transfers between devices  41.2 us (29%)
  Pallas kernels  18.4 us (13%)
  local copies, waits for them, and re-layouts  2.07 us (1%)
    ppermute x29, waiting for transfers between devices, ex(): return lax.ppermute(value, 'expert', perm)  47.1 us
    ppermute x18, waiting for transfers between devices, dp(): return lax.ppermute(value, 'dp', xor_perm(4, bits))  32.3 us
    ppermute x29, starting transfers between devices, ex(): return lax.ppermute(value, 'expert', perm)  20.7 us
    ppermute x18, starting transfers between devices, dp(): return lax.ppermute(value, 'dp', xor_perm(4, bits))  20.5 us
    pallas_call x10, Pallas kernels, local_call(): pl.pallas_call(kernel, out_shape=outs, in_specs=[VMEM] * len(args), out_s...  16.7 us
  transfers between devices with their start and end apart: 47, of which 17 were waited for; matrix products, arithmetic and copies ran while one was open for 0% of the time, Pallas kernels for 11%

profile of v5, /device:TPU:0, one launch (start us, length us, event | category | flops | bytes accessed | tf_op | source)
XLA Modules:
  0.0 142.4 jit_solution(2226469468092153553)
XLA Ops:
  4.1 3.1 %collective-permute-start.4 = (bf16[128,1152]{1,0:T(8,128)(2,1)S(1)}, bf16[128,1152]{1,0:T(8,128)(2,1)S(1)}, u32[]{:S(2)}, u32[]{:S(2)}) collective-permute-start(bf16[128,1152]{1,0:T(8,128)(2,1)S(1)} %get-tuple-element.40.refs_0_), channel_id=1, source_target_pairs={{0,2},{1,3},{2,4},{3,5},{4,6},{5,7},{6,0},{7,1},{8,10},{9,11},{10,... | collective-permute-start | bytes 884744 | tf_op jit(solution)/shard_map/ppermute | solution.py:397
  7.2 2.1 %collective-permute-start.6 = (bf16[128,1152]{1,0:T(8,128)(2,1)S(1)}, bf16[128,1152]{1,0:T(8,128)(2,1)S(1)}, u32[]{:S(2)}, u32[]{:S(2)}) collective-permute-start(bf16[128,1152]{1,0:T(8,128)(2,1)S(1)} %get-tuple-element.40.refs_0_), channel_id=1, source_target_pairs={{0,6},{1,7},{2,0},{3,1},{4,2},{5,3},{6,4},{7,5},{8,14},{9,15},{10,... | collective-permute-start | bytes 884744 | tf_op jit(solution)/shard_map/ppermute | solution.py:397
  10.9 3.4 %collective-permute-start.23 = (f32[8,256]{1,0:T(8,128)S(1)}, f32[8,256]{1,0:T(8,128)S(1)}, u32[]{:S(2)}, u32[]{:S(2)}) collective-permute-start(f32[8,256]{1,0:T(8,128)S(1)} %pad_maximum_fusion.refs_6_), channel_id=1, source_target_pairs={{0,6},{1,7},{2,0},{3,1},{4,2},{5,3},{6,4},{7,5},{8,14},{9,15},{10,... | collective-permute-start | bytes 24584 | tf_op jit(solution)/shard_map/ppermute | solution.py:397
  14.3 17.0 %collective-permute-done.22.refs_7_ = f32[8,256]{1,0:T(8,128)S(1)} collective-permute-done((f32[8,256]{1,0:T(8,128)S(1)}, f32[8,256]{1,0:T(8,128)S(1)}, u32[]{:S(2)}, u32[]{:S(2)}) %collective-permute-start.22) | collective-permute-done | bytes 8224 | tf_op jit(solution)/shard_map/ppermute | solution.py:397
  32.0 3.9 %collective-permute-done.3.refs_4_.refs_2_ = f32[8,256]{1,0:T(8,128)S(1)} collective-permute-done((f32[8,256]{1,0:T(8,128)S(1)}, f32[8,256]{1,0:T(8,128)S(1)}, u32[]{:S(2)}, u32[]{:S(2)}) %collective-permute-start.3) | collective-permute-done | bytes 8224 | tf_op jit(solution)/shard_map/ppermute | solution.py:397
  35.8 1.7 %collective-permute-start.12 = (bf16[128,1536]{1,0:T(8,128)(2,1)}, bf16[128,1536]{1,0:T(8,128)(2,1)S(1)}, u32[]{:S(2)}, u32[]{:S(2)}) collective-permute-start(bf16[128,1536]{1,0:T(8,128)(2,1)} %tokens.1), channel_id=1, source_target_pairs={{0,6},{1,7},{2,0},{3,1},{4,2},{5,3},{6,4},{7,5},{8,14},{9,15},{10,... | collective-permute-start | bytes 1179656 | tf_op jit(solution)/shard_map/ppermute | solution.py:397
  37.6 1.6 %collective-permute-start.16 = (bf16[384,768]{1,0:T(8,128)(2,1)S(1)}, bf16[384,768]{1,0:T(8,128)(2,1)S(1)}, u32[]{:S(2)}, u32[]{:S(2)}) collective-permute-start(bf16[384,768]{1,0:T(8,128)(2,1)S(1)} %bitcast.7), channel_id=1, source_target_pairs={{0,8},{8,0},{16,24},{24,16},{1,9},{9,1},{17,25},{25,17},{2,10},{10... | collective-permute-start | bytes 1769480 | tf_op jit(solution)/shard_map/ppermute | solution.py:400
  39.2 1.5 %collective-permute-start.17 = (bf16[384,768]{1,0:T(8,128)(2,1)S(1)}, bf16[384,768]{1,0:T(8,128)(2,1)S(1)}, u32[]{:S(2)}, u32[]{:S(2)}) collective-permute-start(bf16[384,768]{1,0:T(8,128)(2,1)S(1)} %bitcast.8), channel_id=1, source_target_pairs={{0,16},{8,24},{16,0},{24,8},{1,17},{9,25},{17,1},{25,9},{2,18},{10... | collective-permute-start | bytes 1769480 | tf_op jit(solution)/shard_map/ppermute | solution.py:400
  40.7 4.4 %collective-permute-done.12.refs_4_ = bf16[128,1536]{1,0:T(8,128)(2,1)S(1)} collective-permute-done((bf16[128,1536]{1,0:T(8,128)(2,1)}, bf16[128,1536]{1,0:T(8,128)(2,1)S(1)}, u32[]{:S(2)}, u32[]{:S(2)}) %collective-permute-start.12) | collective-permute-done | bytes 393248 | tf_op jit(solution)/shard_map/ppermute | solution.py:397
  46.4 6.9 %collective-permute-done.16.refs_5_.refs_7_ = bf16[384,768]{1,0:T(8,128)(2,1)S(1)} collective-permute-done((bf16[384,768]{1,0:T(8,128)(2,1)S(1)}, bf16[384,768]{1,0:T(8,128)(2,1)S(1)}, u32[]{:S(2)}, u32[]{:S(2)}) %collective-permute-start.16) | collective-permute-done | bytes 589856 | tf_op jit(solution)/shard_map/ppermute | solution.py:400
  55.4 1.6 %collective-permute-start.18 = (bf16[384,768]{1,0:T(8,128)(2,1)S(1)}, bf16[384,768]{1,0:T(8,128)(2,1)S(1)}, u32[]{:S(2)}, u32[]{:S(2)}) collective-permute-start(bf16[384,768]{1,0:T(8,128)(2,1)S(1)} %collective-permute-done.16.refs_5_.refs_7_), channel_id=1, source_target_pairs={{0,16},{8,24},{16,0},{24,8},{1,17},{9,25},{17,1},{25,9},{2,18},{10... | collective-permute-start | bytes 1769480 | tf_op jit(solution)/shard_map/ppermute | solution.py:400
  57.2 7.3 %collective-permute-done.7.refs_1_ = bf16[128,1152]{1,0:T(8,128)(2,1)S(1)} collective-permute-done((bf16[128,1152]{1,0:T(8,128)(2,1)S(1)}, bf16[128,1152]{1,0:T(8,128)(2,1)S(1)}, u32[]{:S(2)}, u32[]{:S(2)}) %collective-permute-start.7) | collective-permute-done | bytes 294944 | tf_op jit(solution)/shard_map/ppermute | solution.py:397
  65.1 2.9 %collective-permute-done.28.refs_2_.refs_9_ = bf16[768,384]{1,0:T(8,128)(2,1)S(1)} collective-permute-done((bf16[768,384]{1,0:T(8,128)(2,1)}, bf16[768,384]{1,0:T(8,128)(2,1)S(1)}, u32[]{:S(2)}, u32[]{:S(2)}) %collective-permute-start.28) | collective-permute-done | bytes 589856 | tf_op jit(solution)/shard_map/ppermute | solution.py:400
  71.5 7.9 %collective-permute-done.13.refs_1_ = bf16[128,1536]{1,0:T(8,128)(2,1)S(1)} collective-permute-done((bf16[128,1536]{1,0:T(8,128)(2,1)S(1)}, bf16[128,1536]{1,0:T(8,128)(2,1)S(1)}, u32[]{:S(2)}, u32[]{:S(2)}) %collective-permute-start.13) | collective-permute-done | bytes 393248 | tf_op jit(solution)/shard_map/ppermute | solution.py:397
  80.0 1.6 %shard_map.79 = (bf16[768,768]{1,0:T(8,128)(2,1)S(1)}, bf16[1536,768]{1,0:T(8,128)(2,1)S(1)}, f32[768,768]{1,0:T(8,128)S(1)}) custom-call(bf16[128,1536]{1,0:T(8,128)(2,1)S(1)} %get-tuple-element.43.refs_0_, bf16[128,1536]{1,0:T(8,128)(2,1)S(1)} %collective-permute-done.24.refs_1_, bf16[128,1536]{1,0:T(8,128)(2,1)S(1)} %collective-permute-done.10.refs_2_, ...), custom_call_target="tpu_custom_call" | custom-call | flops 905969664 | bytes 9437184 | tf_op jit(solution)/shard_map/pallas_call | solution.py:262
  81.6 3.5 %shard_map.80 = (bf16[768,1152]{1,0:T(8,128)(2,1)S(1)}, bf16[768,768]{1,0:T(8,128)(2,1)S(1)}, f32[768,768]{1,0:T(8,128)S(1)}, f32[768,384]{1,0:T(8,128)S(1)}, f3...) custom-call(bf16[128,1152]{1,0:T(8,128)(2,1)S(1)} %get-tuple-element.40.refs_0_, ...), custom_call_target="tpu_custom_call" | custom-call | flops 2264924160 | bytes 15360000 | tf_op jit(solution)/shard_map/pallas_call | solution.py:262
  85.5 3.5 %collective-permute-start.33 = (bf16[128,384]{1,0:T(8,128)(2,1)S(1)}, bf16[128,384]{1,0:T(8,128)(2,1)S(1)}, u32[]{:S(2)}, u32[]{:S(2)}) collective-permute-start(bf16[128,384]{1,0:T(8,128)(2,1)S(1)} %get-tuple-element.39.refs_0_), channel_id=1, source_target_pairs={{0,6},{1,7},{2,0},{3,1},{4,2},{5,3},{6,4},{7,5},{8,14},{9,15},{10,... | collective-permute-start | bytes 294920 | tf_op jit(solution)/shard_map/ppermute | solution.py:397
  91.2 1.5 %collective-permute-done.31.refs_2_ = bf16[128,384]{1,0:T(8,128)(2,1)S(1)} collective-permute-done((bf16[128,384]{1,0:T(8,128)(2,1)S(1)}, bf16[128,384]{1,0:T(8,128)(2,1)S(1)}, u32[]{:S(2)}, u32[]{:S(2)}) %collective-permute-start.31) | collective-permute-done | bytes 98336 | tf_op jit(solution)/shard_map/ppermute | solution.py:397
  94.0 2.7 %collective-permute-done.refs_0_ = bf16[128,384]{1,0:T(8,128)(2,1)S(1)} collective-permute-done((bf16[128,384]{1,0:T(8,128)(2,1)S(1)}, bf16[128,384]{1,0:T(8,128)(2,1)S(1)}, u32[]{:S(2)}, u32[]{:S(2)}) %collective-permute-start) | collective-permute-done | bytes 98336 | tf_op jit(solution)/shard_map/ppermute | solution.py:397
  98.0 1.5 %collective-permute-start.45 = (bf16[384,384]{1,0:T(8,128)(2,1)S(1)}, bf16[384,384]{1,0:T(8,128)(2,1)S(1)}, u32[]{:S(2)}, u32[]{:S(2)}) collective-permute-start(bf16[384,384]{1,0:T(8,128)(2,1)S(1)} %get-tuple-element.75), channel_id=1, source_target_pairs={{0,16},{8,24},{16,0},{24,8},{1,17},{9,25},{17,1},{25,9},{2,18},{10... | collective-permute-start | bytes 884744 | tf_op jit(solution)/shard_map/ppermute | solution.py:400
  99.5 2.0 %shard_map.82.refs_9_ = f32[768,768]{1,0:T(8,128)S(1)} custom-call(bf16[768,1152]{1,0:T(8,128)(2,1)S(1)} %get-tuple-element.53.g, bf16[768,384]{1,0:T(8,128)(2,1)S(1)} %collective-permute-done.29.refs_0_.refs_10_, bf16[768,384]{1,0:T(8,128)(2,1)S(1)} %collective-permute-done.27.refs_1_.refs_8_, bf16[768,384]{1,0:T(8,128)(2,1)S(1)} %collective-permute-done.28.refs_2_.refs_9_), custom_call_target="tpu_custom_call" | custom-call | flops 1358954496 | bytes 5898240 | tf_op jit(solution)/shard_map/pallas_call | solution.py:262
  104.1 3.4 %shard_map.83 = (f32[384,768]{1,0:T(8,128)S(1)}, f32[384,768]{1,0:T(8,128)S(1)}, f32[384,768]{1,0:T(8,128)S(1)}, f32[384,768]{1,0:T(8,128)S(1)}, f32[768,384]{1,0:T(8,128)S(1)}) custom-call(bf16[128,384]{1,0:T(8,128)(2,1)S(1)} %get-tuple-element.39.refs_0_, bf16[128,384]{1,0:T(8,128)(2,1)S(1)} %collective-permute-done.30.refs_1_, ...), custom_call_target="tpu_custom_call" | custom-call | flops 2717908992 | bytes 15360000 | tf_op jit(solution)/shard_map/pallas_call | solution.py:262
  107.5 2.4 %shard_map.84 = (bf16[192,768]{1,0:T(8,128)(2,1)S(1)}, bf16[192,768]{1,0:T(8,128)(2,1)S(1)}, bf16[192,768]{1,0:T(8,128)(2,1)S(1)}, bf16[192,768]{1,0:T(8,128)(2,...) custom-call(bf16[128,384]{1,0:T(8,128)(2,1)S(1)} %collective-permute-, ...), custom_call_target="tpu_custom_call" | custom-call | flops 1358954496 | bytes 15736832 | tf_op jit(solution)/shard_map/pallas_call | solution.py:262
  109.9 1.6 %collective-permute-start.39 = (bf16[192,768]{1,0:T(8,128)(2,1)S(1)}, bf16[192,768]{1,0:T(8,128)(2,1)S(1)}, u32[]{:S(2)}, u32[]{:S(2)}) collective-permute-start(bf16[192,768]{1,0:T(8,128)(2,1)S(1)} %get-tuple-element.68), channel_id=1, source_target_pairs={{0,16},{8,24},{16,0},{24,8},{1,17},{9,25},{17,1},{25,9},{2,18},{10... | collective-permute-start | bytes 884744 | tf_op jit(solution)/shard_map/ppermute | solution.py:400
  112.1 1.6 %collective-permute-start.35 = (bf16[192,768]{1,0:T(8,128)(2,1)S(1)}, bf16[192,768]{1,0:T(8,128)(2,1)S(1)}, u32[]{:S(2)}, u32[]{:S(2)}) collective-permute-start(bf16[192,768]{1,0:T(8,128)(2,1)S(1)} %get-tuple-element.63), channel_id=1, source_target_pairs={{0,8},{8,0},{16,24},{24,16},{1,9},{9,1},{17,25},{25,17},{2,10},{10... | collective-permute-start | bytes 884744 | tf_op jit(solution)/shard_map/ppermute | solution.py:400
  113.8 5.3 %collective-permute-done.39 = bf16[192,768]{1,0:T(8,128)(2,1)S(1)} collective-permute-done((bf16[192,768]{1,0:T(8,128)(2,1)S(1)}, bf16[192,768]{1,0:T(8,128)(2,1)S(1)}, u32[]{:S(2)}, u32[]{:S(2)}) %collective-permute-start.39) | collective-permute-done | bytes 294944 | tf_op jit(solution)/shard_map/ppermute | solution.py:400
  119.1 1.5 %collective-permute-start.36 = (bf16[192,768]{1,0:T(8,128)(2,1)S(1)}, bf16[192,768]{1,0:T(8,128)(2,1)S(1)}, u32[]{:S(2)}, u32[]{:S(2)}) collective-permute-start(bf16[192,768]{1,0:T(8,128)(2,1)S(1)} %get-tuple-element.64), channel_id=1, source_target_pairs={{0,16},{8,24},{16,0},{24,8},{1,17},{9,25},{17,1},{25,9},{2,18},{10... | collective-permute-start | bytes 884744 | tf_op jit(solution)/shard_map/ppermute | solution.py:400
  120.7 3.4 %collective-permute-done.37 = bf16[192,768]{1,0:T(8,128)(2,1)S(1)} collective-permute-done((bf16[192,768]{1,0:T(8,128)(2,1)S(1)}, bf16[192,768]{1,0:T(8,128)(2,1)S(1)}, u32[]{:S(2)}, u32[]{:S(2)}) %collective-permute-start.37) | collective-permute-done | bytes 294944 | tf_op jit(solution)/shard_map/ppermute | solution.py:400
  125.3 1.5 %collective-permute-start.40 = (bf16[192,768]{1,0:T(8,128)(2,1)S(1)}, bf16[192,768]{1,0:T(8,128)(2,1)S(1)}, u32[]{:S(2)}, u32[]{:S(2)}) collective-permute-start(bf16[192,768]{1,0:T(8,128)(2,1)S(1)} %add_convert_fusion.2), channel_id=1, source_target_pairs={{0,8},{8,0},{16,24},{24,16},{1,9},{9,1},{17,25},{25,17},{2,10},{10... | collective-permute-start | bytes 884744 | tf_op jit(solution)/shard_map/ppermute | solution.py:400
  126.8 3.6 %collective-permute-done.35.near_a = bf16[192,768]{1,0:T(8,128)(2,1)S(1)} collective-permute-done((bf16[192,768]{1,0:T(8,128)(2,1)S(1)}, bf16[192,768]{1,0:T(8,128)(2,1)S(1)}, u32[]{:S(2)}, u32[]{:S(2)}) %collective-permute-start.35) | collective-permute-done | bytes 294944 | tf_op jit(solution)/shard_map/ppermute | solution.py:400
  131.2 5.5 %collective-permute-done.46.far_b = bf16[384,384]{1,0:T(8,128)(2,1)S(1)} collective-permute-done((bf16[384,384]{1,0:T(8,128)(2,1)S(1)}, bf16[384,384]{1,0:T(8,128)(2,1)S(1)}, u32[]{:S(2)}, u32[]{:S(2)}) %collective-permute-start.46) | collective-permute-done | bytes 294944 | tf_op jit(solution)/shard_map/ppermute | solution.py:400
  137.6 3.8 %collective-permute-done.40.far_b = bf16[192,768]{1,0:T(8,128)(2,1)S(1)} collective-permute-done((bf16[192,768]{1,0:T(8,128)(2,1)S(1)}, bf16[192,768]{1,0:T(8,128)(2,1)S(1)}, u32[]{:S(2)}, u32[]{:S(2)}) %collective-permute-start.40) | collective-permute-done | bytes 294944 | tf_op jit(solution)/shard_map/ppermute | solution.py:400
  (89 shorter events, 26.0 us)
Async XLA Ops:
  4.1 33.5 %collective-permute-start.4 = (bf16[128,1152]{1,0:T(8,128)(2,1)S(1)}, bf16[128,1152]{1,0:T(8,128)(2,1)S(1)}, u32[]{:S(2)}, u32[]{:S(2)}) collective-permute-start(bf16[128,1152]{1,0:T(8,128)(2,1)S(1)} %get-tuple-element.40.refs_0_), channel_id=1, source_target_pairs={{0,2},{1,3},{2,4},{3,5},{4,6},{5,7},{6,0},{7,1},{8,10},{9,11},{10,... | collective-permute-start | bytes 884744 | tf_op jit(solution)/shard_map/ppermute | solution.py:397
  7.2 30.4 %collective-permute-start.6 = (bf16[128,1152]{1,0:T(8,128)(2,1)S(1)}, bf16[128,1152]{1,0:T(8,128)(2,1)S(1)}, u32[]{:S(2)}, u32[]{:S(2)}) collective-permute-start(bf16[128,1152]{1,0:T(8,128)(2,1)S(1)} %get-tuple-element.40.refs_0_), channel_id=1, source_target_pairs={{0,6},{1,7},{2,0},{3,1},{4,2},{5,3},{6,4},{7,5},{8,14},{9,15},{10,... | collective-permute-start | bytes 884744 | tf_op jit(solution)/shard_map/ppermute | solution.py:397
  9.4 31.3 %collective-permute-start.10 = (bf16[128,1536]{1,0:T(8,128)(2,1)}, bf16[128,1536]{1,0:T(8,128)(2,1)S(1)}, u32[]{:S(2)}, u32[]{:S(2)}) collective-permute-start(bf16[128,1536]{1,0:T(8,128)(2,1)} %tokens.1), channel_id=1, source_target_pairs={{0,2},{1,3},{2,4},{3,5},{4,6},{5,7},{6,0},{7,1},{8,10},{9,11},{10,... | collective-permute-start | bytes 1179656 | tf_op jit(solution)/shard_map/ppermute | solution.py:397
  10.5 20.8 %collective-permute-start.22 = (f32[8,256]{1,0:T(8,128)S(1)}, f32[8,256]{1,0:T(8,128)S(1)}, u32[]{:S(2)}, u32[]{:S(2)}) collective-permute-start(f32[8,256]{1,0:T(8,128)S(1)} %pad_maximum_fusion.refs_6_), channel_id=1, source_target_pairs={{0,2},{1,3},{2,4},{3,5},{4,6},{5,7},{6,0},{7,1},{8,10},{9,11},{10,... | collective-permute-start | bytes 24584 | tf_op jit(solution)/shard_map/ppermute | solution.py:397
  10.9 21.0 %collective-permute-start.23 = (f32[8,256]{1,0:T(8,128)S(1)}, f32[8,256]{1,0:T(8,128)S(1)}, u32[]{:S(2)}, u32[]{:S(2)}) collective-permute-start(f32[8,256]{1,0:T(8,128)S(1)} %pad_maximum_fusion.refs_6_), channel_id=1, source_target_pairs={{0,6},{1,7},{2,0},{3,1},{4,2},{5,3},{6,4},{7,5},{8,14},{9,15},{10,... | collective-permute-start | bytes 24584 | tf_op jit(solution)/shard_map/ppermute | solution.py:397
  35.8 9.3 %collective-permute-start.12 = (bf16[128,1536]{1,0:T(8,128)(2,1)}, bf16[128,1536]{1,0:T(8,128)(2,1)S(1)}, u32[]{:S(2)}, u32[]{:S(2)}) collective-permute-start(bf16[128,1536]{1,0:T(8,128)(2,1)} %tokens.1), channel_id=1, source_target_pairs={{0,6},{1,7},{2,0},{3,1},{4,2},{5,3},{6,4},{7,5},{8,14},{9,15},{10,... | collective-permute-start | bytes 1179656 | tf_op jit(solution)/shard_map/ppermute | solution.py:397
  37.6 15.7 %collective-permute-start.16 = (bf16[384,768]{1,0:T(8,128)(2,1)S(1)}, bf16[384,768]{1,0:T(8,128)(2,1)S(1)}, u32[]{:S(2)}, u32[]{:S(2)}) collective-permute-start(bf16[384,768]{1,0:T(8,128)(2,1)S(1)} %bitcast.7), channel_id=1, source_target_pairs={{0,8},{8,0},{16,24},{24,16},{1,9},{9,1},{17,25},{25,17},{2,10},{10... | collective-permute-start | bytes 1769480 | tf_op jit(solution)/shard_map/ppermute | solution.py:400
  39.2 16.3 %collective-permute-start.17 = (bf16[384,768]{1,0:T(8,128)(2,1)S(1)}, bf16[384,768]{1,0:T(8,128)(2,1)S(1)}, u32[]{:S(2)}, u32[]{:S(2)}) collective-permute-start(bf16[384,768]{1,0:T(8,128)(2,1)S(1)} %bitcast.8), channel_id=1, source_target_pairs={{0,16},{8,24},{16,0},{24,8},{1,17},{9,25},{17,1},{25,9},{2,18},{10... | collective-permute-start | bytes 1769480 | tf_op jit(solution)/shard_map/ppermute | solution.py:400
  40.7 13.3 %collective-permute-start.20 = (bf16[128,1152]{1,0:T(8,128)(2,1)S(1)}, bf16[128,1152]{1,0:T(8,128)(2,1)S(1)}, u32[]{:S(2)}, u32[]{:S(2)}) collective-permute-start(bf16[128,1152]{1,0:T(8,128)(2,1)S(1)} %collective-permute-done.4.refs_2_), channel_id=1, source_target_pairs={{0,1},{1,0},{2,3},{3,2},{4,5},{5,4},{6,7},{7,6},{8,9},{9,8},{10,11... | collective-permute-start | bytes 884744 | tf_op jit(solution)/shard_map/ppermute | solution.py:397
  45.1 22.9 %collective-permute-start.28 = (bf16[768,384]{1,0:T(8,128)(2,1)}, bf16[768,384]{1,0:T(8,128)(2,1)S(1)}, u32[]{:S(2)}, u32[]{:S(2)}) collective-permute-start(bf16[768,384]{1,0:T(8,128)(2,1)} %bitcast.1.down), channel_id=1, source_target_pairs={{0,16},{8,24},{16,0},{24,8},{1,17},{9,25},{17,1},{25,9},{2,18},{10... | collective-permute-start | bytes 1769480 | tf_op jit(solution)/shard_map/ppermute | solution.py:400
  54.0 10.4 %collective-permute-start.7 = (bf16[128,1152]{1,0:T(8,128)(2,1)S(1)}, bf16[128,1152]{1,0:T(8,128)(2,1)S(1)}, u32[]{:S(2)}, u32[]{:S(2)}) collective-permute-start(bf16[128,1152]{1,0:T(8,128)(2,1)S(1)} %collective-permute-done.6.refs_4_), channel_id=1, source_target_pairs={{2,0},{3,1},{4,2},{5,3},{10,8},{11,9},{12,10},{13,11},{18,16},{19,... | collective-permute-start | bytes 884744 | tf_op jit(solution)/shard_map/ppermute | solution.py:397
  55.3 14.0 %collective-permute-start.25 = (bf16[128,1536]{1,0:T(8,128)(2,1)S(1)}, bf16[128,1536]{1,0:T(8,128)(2,1)S(1)}, u32[]{:S(2)}, u32[]{:S(2)}) collective-permute-start(bf16[128,1536]{1,0:T(8,128)(2,1)S(1)} %collective-permute-done.10.refs_2_), channel_id=1, source_target_pairs={{0,1},{1,0},{2,3},{3,2},{4,5},{5,4},{6,7},{7,6},{8,9},{9,8},{10,11... | collective-permute-start | bytes 1179656 | tf_op jit(solution)/shard_map/ppermute | solution.py:397
  55.4 24.5 %collective-permute-start.18 = (bf16[384,768]{1,0:T(8,128)(2,1)S(1)}, bf16[384,768]{1,0:T(8,128)(2,1)S(1)}, u32[]{:S(2)}, u32[]{:S(2)}) collective-permute-start(bf16[384,768]{1,0:T(8,128)(2,1)S(1)} %collective-permute-done.16.refs_5_.refs_7_), channel_id=1, source_target_pairs={{0,16},{8,24},{16,0},{24,8},{1,17},{9,25},{17,1},{25,9},{2,18},{10... | collective-permute-start | bytes 1769480 | tf_op jit(solution)/shard_map/ppermute | solution.py:400
  57.0 12.4 %collective-permute-start.26 = (bf16[128,1536]{1,0:T(8,128)(2,1)S(1)}, bf16[128,1536]{1,0:T(8,128)(2,1)S(1)}, u32[]{:S(2)}, u32[]{:S(2)}) collective-permute-start(bf16[128,1536]{1,0:T(8,128)(2,1)S(1)} %collective-permute-done.12.refs_4_), channel_id=1, source_target_pairs={{0,1},{1,0},{2,3},{3,2},{4,5},{5,4},{6,7},{7,6},{8,9},{9,8},{10,11... | collective-permute-start | bytes 1179656 | tf_op jit(solution)/shard_map/ppermute | solution.py:397
  68.0 11.4 %collective-permute-start.13 = (bf16[128,1536]{1,0:T(8,128)(2,1)S(1)}, bf16[128,1536]{1,0:T(8,128)(2,1)S(1)}, u32[]{:S(2)}, u32[]{:S(2)}) collective-permute-start(bf16[128,1536]{1,0:T(8,128)(2,1)S(1)} %collective-permute-done.12.refs_4_), channel_id=1, source_target_pairs={{2,0},{3,1},{4,2},{5,3},{10,8},{11,9},{12,10},{13,11},{18,16},{19,... | collective-permute-start | bytes 1179656 | tf_op jit(solution)/shard_map/ppermute | solution.py:397
  69.3 10.1 %collective-permute-start.8 = (bf16[128,1152]{1,0:T(8,128)(2,1)S(1)}, bf16[128,1152]{1,0:T(8,128)(2,1)S(1)}, u32[]{:S(2)}, u32[]{:S(2)}) collective-permute-start(bf16[128,1152]{1,0:T(8,128)(2,1)S(1)} %collective-permute-done.5.refs_0_), channel_id=1, source_target_pairs={{0,1},{1,0},{2,3},{3,2},{4,5},{5,4},{6,7},{7,6},{8,9},{9,8},{10,11... | collective-permute-start | bytes 884744 | tf_op jit(solution)/shard_map/ppermute | solution.py:397
  69.4 27.4 %collective-permute-start.27 = (bf16[768,384]{1,0:T(8,128)(2,1)}, bf16[768,384]{1,0:T(8,128)(2,1)S(1)}, u32[]{:S(2)}, u32[]{:S(2)}) collective-permute-start(bf16[768,384]{1,0:T(8,128)(2,1)} %bitcast.1.down), channel_id=1, source_target_pairs={{0,8},{8,0},{16,24},{24,16},{1,9},{9,1},{17,25},{25,17},{2,10},{10... | collective-permute-start | bytes 1769480 | tf_op jit(solution)/shard_map/ppermute | solution.py:400
  70.0 28.0 %collective-permute-start.29 = (bf16[768,384]{1,0:T(8,128)(2,1)S(1)}, bf16[768,384]{1,0:T(8,128)(2,1)S(1)}, u32[]{:S(2)}, u32[]{:S(2)}) collective-permute-start(bf16[768,384]{1,0:T(8,128)(2,1)S(1)} %collective-permute-done.28.refs_2_.refs_9_), channel_id=1, source_target_pairs={{0,8},{8,0},{16,24},{24,16},{1,9},{9,1},{17,25},{25,17},{2,10},{10... | collective-permute-start | bytes 1769480 | tf_op jit(solution)/shard_map/ppermute | solution.py:400
  79.4 9.6 %collective-permute-start.15 = (bf16[128,1536]{1,0:T(8,128)(2,1)S(1)}, bf16[128,1536]{1,0:T(8,128)(2,1)S(1)}, u32[]{:S(2)}, u32[]{:S(2)}) collective-permute-start(bf16[128,1536]{1,0:T(8,128)(2,1)S(1)} %collective-permute-done.13.refs_1_), channel_id=1, source_target_pairs={{0,1},{1,0},{2,3},{3,2},{4,5},{5,4},{6,7},{7,6},{8,9},{9,8},{10,11... | collective-permute-start | bytes 1179656 | tf_op jit(solution)/shard_map/ppermute | solution.py:397
  96.7 10.8 %collective-permute-start.1 = (bf16[128,384]{1,0:T(8,128)(2,1)S(1)}, bf16[128,384]{1,0:T(8,128)(2,1)S(1)}, u32[]{:S(2)}, u32[]{:S(2)}) collective-permute-start(bf16[128,384]{1,0:T(8,128)(2,1)S(1)} %collective-permute-done.refs_0_), channel_id=1, source_target_pairs={{0,1},{1,0},{2,3},{3,2},{4,5},{5,4},{6,7},{7,6},{8,9},{9,8},{10,11... | collective-permute-start | bytes 294920 | tf_op jit(solution)/shard_map/ppermute | solution.py:397
  98.0 13.6 %collective-permute-start.45 = (bf16[384,384]{1,0:T(8,128)(2,1)S(1)}, bf16[384,384]{1,0:T(8,128)(2,1)S(1)}, u32[]{:S(2)}, u32[]{:S(2)}) collective-permute-start(bf16[384,384]{1,0:T(8,128)(2,1)S(1)} %get-tuple-element.75), channel_id=1, source_target_pairs={{0,16},{8,24},{16,0},{24,8},{1,17},{9,25},{17,1},{25,9},{2,18},{10... | collective-permute-start | bytes 884744 | tf_op jit(solution)/shard_map/ppermute | solution.py:400
  101.5 10.6 %collective-permute-start.43 = (bf16[384,384]{1,0:T(8,128)(2,1)S(1)}, bf16[384,384]{1,0:T(8,128)(2,1)S(1)}, u32[]{:S(2)}, u32[]{:S(2)}) collective-permute-start(bf16[384,384]{1,0:T(8,128)(2,1)S(1)} %get-tuple-element.73), channel_id=1, source_target_pairs={{0,8},{8,0},{16,24},{24,16},{1,9},{9,1},{17,25},{25,17},{2,10},{10... | collective-permute-start | bytes 884744 | tf_op jit(solution)/shard_map/ppermute | solution.py:400
  102.1 22.6 %collective-permute-start.41 = (bf16[384,384]{1,0:T(8,128)(2,1)S(1)}, bf16[384,384]{1,0:T(8,128)(2,1)S(1)}, u32[]{:S(2)}, u32[]{:S(2)}) collective-permute-start(bf16[384,384]{1,0:T(8,128)(2,1)S(1)} %get-tuple-element.70), channel_id=1, source_target_pairs={{0,8},{8,0},{16,24},{24,16},{1,9},{9,1},{17,25},{25,17},{2,10},{10... | collective-permute-start | bytes 884744 | tf_op jit(solution)/shard_map/ppermute | solution.py:400
  103.6 21.7 %collective-permute-start.42 = (bf16[384,384]{1,0:T(8,128)(2,1)S(1)}, bf16[384,384]{1,0:T(8,128)(2,1)S(1)}, u32[]{:S(2)}, u32[]{:S(2)}) collective-permute-start(bf16[384,384]{1,0:T(8,128)(2,1)S(1)} %get-tuple-element.71), channel_id=1, source_target_pairs={{0,16},{8,24},{16,0},{24,8},{1,17},{9,25},{17,1},{25,9},{2,18},{10... | collective-permute-start | bytes 884744 | tf_op jit(solution)/shard_map/ppermute | solution.py:400
  109.9 9.1 %collective-permute-start.39 = (bf16[192,768]{1,0:T(8,128)(2,1)S(1)}, bf16[192,768]{1,0:T(8,128)(2,1)S(1)}, u32[]{:S(2)}, u32[]{:S(2)}) collective-permute-start(bf16[192,768]{1,0:T(8,128)(2,1)S(1)} %get-tuple-element.68), channel_id=1, source_target_pairs={{0,16},{8,24},{16,0},{24,8},{1,17},{9,25},{17,1},{25,9},{2,18},{10... | collective-permute-start | bytes 884744 | tf_op jit(solution)/shard_map/ppermute | solution.py:400
  111.5 12.6 %collective-permute-start.37 = (bf16[192,768]{1,0:T(8,128)(2,1)S(1)}, bf16[192,768]{1,0:T(8,128)(2,1)S(1)}, u32[]{:S(2)}, u32[]{:S(2)}) collective-permute-start(bf16[192,768]{1,0:T(8,128)(2,1)S(1)} %get-tuple-element.66), channel_id=1, source_target_pairs={{0,8},{8,0},{16,24},{24,16},{1,9},{9,1},{17,25},{25,17},{2,10},{10... | collective-permute-start | bytes 884744 | tf_op jit(solution)/shard_map/ppermute | solution.py:400
  112.1 18.3 %collective-permute-start.35 = (bf16[192,768]{1,0:T(8,128)(2,1)S(1)}, bf16[192,768]{1,0:T(8,128)(2,1)S(1)}, u32[]{:S(2)}, u32[]{:S(2)}) collective-permute-start(bf16[192,768]{1,0:T(8,128)(2,1)S(1)} %get-tuple-element.63), channel_id=1, source_target_pairs={{0,8},{8,0},{16,24},{24,16},{1,9},{9,1},{17,25},{25,17},{2,10},{10... | collective-permute-start | bytes 884744 | tf_op jit(solution)/shard_map/ppermute | solution.py:400
  119.1 11.9 %collective-permute-start.36 = (bf16[192,768]{1,0:T(8,128)(2,1)S(1)}, bf16[192,768]{1,0:T(8,128)(2,1)S(1)}, u32[]{:S(2)}, u32[]{:S(2)}) collective-permute-start(bf16[192,768]{1,0:T(8,128)(2,1)S(1)} %get-tuple-element.64), channel_id=1, source_target_pairs={{0,16},{8,24},{16,0},{24,8},{1,17},{9,25},{17,1},{25,9},{2,18},{10... | collective-permute-start | bytes 884744 | tf_op jit(solution)/shard_map/ppermute | solution.py:400
  124.1 12.6 %collective-permute-start.46 = (bf16[384,384]{1,0:T(8,128)(2,1)S(1)}, bf16[384,384]{1,0:T(8,128)(2,1)S(1)}, u32[]{:S(2)}, u32[]{:S(2)}) collective-permute-start(bf16[384,384]{1,0:T(8,128)(2,1)S(1)} %add_convert_fusion), channel_id=1, source_target_pairs={{0,8},{8,0},{16,24},{24,16},{1,9},{9,1},{17,25},{25,17},{2,10},{10... | collective-permute-start | bytes 884744 | tf_op jit(solution)/shard_map/ppermute | solution.py:400
  124.7 12.0 %collective-permute-start.44 = (bf16[384,384]{1,0:T(8,128)(2,1)S(1)}, bf16[384,384]{1,0:T(8,128)(2,1)S(1)}, u32[]{:S(2)}, u32[]{:S(2)}) collective-permute-start(bf16[384,384]{1,0:T(8,128)(2,1)S(1)} %add_convert_fusion.1), channel_id=1, source_target_pairs={{0,16},{8,24},{16,0},{24,8},{1,17},{9,25},{17,1},{25,9},{2,18},{10... | collective-permute-start | bytes 884744 | tf_op jit(solution)/shard_map/ppermute | solution.py:400
  125.3 16.1 %collective-permute-start.40 = (bf16[192,768]{1,0:T(8,128)(2,1)S(1)}, bf16[192,768]{1,0:T(8,128)(2,1)S(1)}, u32[]{:S(2)}, u32[]{:S(2)}) collective-permute-start(bf16[192,768]{1,0:T(8,128)(2,1)S(1)} %add_convert_fusion.2), channel_id=1, source_target_pairs={{0,8},{8,0},{16,24},{24,16},{1,9},{9,1},{17,25},{25,17},{2,10},{10... | collective-permute-start | bytes 884744 | tf_op jit(solution)/shard_map/ppermute | solution.py:400
  130.4 11.0 %collective-permute-start.38 = (bf16[192,768]{1,0:T(8,128)(2,1)S(1)}, bf16[192,768]{1,0:T(8,128)(2,1)S(1)}, u32[]{:S(2)}, u32[]{:S(2)}) collective-permute-start(bf16[192,768]{1,0:T(8,128)(2,1)S(1)} %add_convert_fusion.3), channel_id=1, source_target_pairs={{0,16},{8,24},{16,0},{24,8},{1,17},{9,25},{17,1},{25,9},{2,18},{10... | collective-permute-start | bytes 884744 | tf_op jit(solution)/shard_map/ppermute | solution.py:400
  (19 other events, 116.1 us)

commit v6 on v5

--- a/solution.py
+++ b/solution.py
@@ -160,21 +160,27 @@
     act_turned[...] = jnp.transpose(act)
 
 
-def last_down_kernel(block, *refs):
-    shards, table, act_turned, sums = refs[0:4], refs[4], refs[5], refs[6:9]
-    g, far_a, far_b, near_a, near_b, side_a, side_b = refs[9:]
+def last_far_kernel(block, *refs):
+    shards, table, act_turned, far_sum = refs[0:4], refs[4], refs[5], refs[6]
+    g, far_a, far_b = refs[7:]
     expert = lax.axis_index("expert")
     for half in range(2):
         gate = pick_gate(table, half, expert)
         g[half * SHARD : (half + 1) * SHARD, :] = scale_rows(gate, shards[2 * half][...] + shards[2 * half + 1][...])
     middle = act_turned.shape[0] // 2
-    total = dot_rows(act_turned[...], g[:, :block]) + sums[0][...]
+    total = dot_rows(act_turned[...], g[:, :block]) + far_sum[...]
     far_a[...] = total[:middle].astype(BF16)
     far_b[...] = total[middle:].astype(BF16)
-    total = dot_rows(act_turned[...], g[:, block : 2 * block]) + sums[1][...]
+
+
+def last_near_kernel(block, *refs):
+    g, act_turned, sum_x, sum_y = refs[:4]
+    near_a, near_b, side_a, side_b = refs[4:]
+    middle = act_turned.shape[0] // 2
+    total = dot_rows(act_turned[...], g[:, block : 2 * block]) + sum_x[...]
     near_a[...] = total[:middle].astype(BF16)
     side_b[...] = total[middle:]
-    total = dot_rows(act_turned[...], g[:, 2 * block :]) + sums[2][...]
+    total = dot_rows(act_turned[...], g[:, 2 * block :]) + sum_y[...]
     side_a[...] = total[:middle]
     near_b[...] = total[middle:].astype(BF16)
 
@@ -323,13 +329,23 @@
     return [shape(rows // 2, cols, BF16)] * 4 + [shape(rows // 2, cols, F32)] * 2
 
 
-def last_down(shards, table, act_turned, sums):
-    hidden, block = sums[0].shape
-    return local_call(
-        functools.partial(last_down_kernel, block),
-        [shape(2 * SHARD, 3 * block, BF16)] + exchanged(hidden, block),
-        (*shards, table, act_turned, *sums),
-        flops=12 * SHARD * block * hidden,
+def last_far(shards, table, act_turned, far_sum):
+    hidden, block = far_sum.shape
+    return local_call(
+        functools.partial(last_far_kernel, block),
+        [shape(2 * SHARD, 3 * block, BF16)] + exchanged(hidden, block)[:2],
+        (*shards, table, act_turned, far_sum),
+        flops=4 * SHARD * block * hidden,
+    )
+
+
+def last_near(g, act_turned, sum_x, sum_y):
+    hidden, block = sum_x.shape
+    return local_call(
+        functools.partial(last_near_kernel, block),
+        exchanged(hidden, block)[2:],
+        (g, act_turned, sum_x, sum_y),
+        flops=8 * SHARD * block * hidden,
     )
 
 
@@ -456,7 +472,8 @@
     x_tail, x_turned, pre_part = early_forward((tokens_here, t0b, t1, t1b, t3, t3b), ups)
     g_ab, act_ab, slope_ab, *down_sums = most_down((ga, ga0b, ga1, ga1b, ga3, ga3b), tables, x_tail, pre_part, up_y, up_d)
     x_c, act_c, slope_c = last_forward((t2u, t2d, t2ub, t2db), ups)
-    g_c, *down_parts = last_down((ga2u, ga2d, ga2ub, ga2db), c2, act_c, down_sums)
+    g_c, *down_far = last_far((ga2u, ga2d, ga2ub, ga2db), c2, act_c, down_sums[0])
+    down_parts = (*down_far, *last_near(g_c, act_c, *down_sums[1:]))
     grad_part = early_backward(g_ab, downs)
     up_sums, down_sum = most_up((gb, gb0b, gb1, gb1b, gb3, gb3b), tables, grad_part, slope_ab, x_turned, act_ab, down_here)
     *up_parts, up_own, down_own = last_up((gb2, gb2b), c2, g_c, slope_c, x_c, act_c, downs, up_sums, down_sum)

time: 143 us -> 143 us (level)
    pallas_call x10 -> x11, Pallas kernels: 16.7 us -> 16.8 us  [local_call(): pl.pallas_call(kernel, out_shape=outs, in_specs=[VMEM] * len(args), out_s...]
where the time goes in v6:
time: 143 us; the launch traced here: 142 us
  waiting for transfers between devices  79.2 us (55%)
  starting transfers between devices  41.2 us (29%)
  Pallas kernels  18.5 us (13%)
  local copies, waits for them, and re-layouts  2.07 us (1%)
    ppermute x29, waiting for transfers between devices, ex(): return lax.ppermute(value, 'expert', perm)  47 us
    ppermute x18, waiting for transfers between devices, dp(): return lax.ppermute(value, 'dp', xor_perm(4, bits))  32.2 us
    ppermute x29, starting transfers between devices, ex(): return lax.ppermute(value, 'expert', perm)  20.7 us
    ppermute x18, starting transfers between devices, dp(): return lax.ppermute(value, 'dp', xor_perm(4, bits))  20.5 us
    pallas_call x11, Pallas kernels, local_call(): pl.pallas_call(kernel, out_shape=outs, in_specs=[VMEM] * len(args), out_s...  16.8 us
  transfers between devices with their start and end apart: 47, of which 17 were waited for; matrix products, arithmetic and copies ran while one was open for 0% of the time, Pallas kernels for 11%

profile of v6, /device:TPU:0, one launch (start us, length us, event | category | flops | bytes accessed | tf_op | source)
XLA Modules:
  0.0 142.4 jit_solution(17194046890530254484)
XLA Ops:
  4.1 3.1 %collective-permute-start.4 = (bf16[128,1152]{1,0:T(8,128)(2,1)S(1)}, bf16[128,1152]{1,0:T(8,128)(2,1)S(1)}, u32[]{:S(2)}, u32[]{:S(2)}) collective-permute-start(bf16[128,1152]{1,0:T(8,128)(2,1)S(1)} %get-tuple-element.40.refs_0_), channel_id=1, source_target_pairs={{0,2},{1,3},{2,4},{3,5},{4,6},{5,7},{6,0},{7,1},{8,10},{9,11},{10,... | collective-permute-start | bytes 884744 | tf_op jit(solution)/shard_map/ppermute | solution.py:413
  7.2 2.1 %collective-permute-start.6 = (bf16[128,1152]{1,0:T(8,128)(2,1)S(1)}, bf16[128,1152]{1,0:T(8,128)(2,1)S(1)}, u32[]{:S(2)}, u32[]{:S(2)}) collective-permute-start(bf16[128,1152]{1,0:T(8,128)(2,1)S(1)} %get-tuple-element.40.refs_0_), channel_id=1, source_target_pairs={{0,6},{1,7},{2,0},{3,1},{4,2},{5,3},{6,4},{7,5},{8,14},{9,15},{10,... | collective-permute-start | bytes 884744 | tf_op jit(solution)/shard_map/ppermute | solution.py:413
  10.9 3.4 %collective-permute-start.23 = (f32[8,256]{1,0:T(8,128)S(1)}, f32[8,256]{1,0:T(8,128)S(1)}, u32[]{:S(2)}, u32[]{:S(2)}) collective-permute-start(f32[8,256]{1,0:T(8,128)S(1)} %pad_maximum_fusion.refs_6_), channel_id=1, source_target_pairs={{0,6},{1,7},{2,0},{3,1},{4,2},{5,3},{6,4},{7,5},{8,14},{9,15},{10,... | collective-permute-start | bytes 24584 | tf_op jit(solution)/shard_map/ppermute | solution.py:413
  14.3 17.0 %collective-permute-done.22.refs_7_ = f32[8,256]{1,0:T(8,128)S(1)} collective-permute-done((f32[8,256]{1,0:T(8,128)S(1)}, f32[8,256]{1,0:T(8,128)S(1)}, u32[]{:S(2)}, u32[]{:S(2)}) %collective-permute-start.22) | collective-permute-done | bytes 8224 | tf_op jit(solution)/shard_map/ppermute | solution.py:413
  32.0 3.9 %collective-permute-done.3.refs_4_.refs_2_ = f32[8,256]{1,0:T(8,128)S(1)} collective-permute-done((f32[8,256]{1,0:T(8,128)S(1)}, f32[8,256]{1,0:T(8,128)S(1)}, u32[]{:S(2)}, u32[]{:S(2)}) %collective-permute-start.3) | collective-permute-done | bytes 8224 | tf_op jit(solution)/shard_map/ppermute | solution.py:413
  35.8 1.7 %collective-permute-start.12 = (bf16[128,1536]{1,0:T(8,128)(2,1)}, bf16[128,1536]{1,0:T(8,128)(2,1)S(1)}, u32[]{:S(2)}, u32[]{:S(2)}) collective-permute-start(bf16[128,1536]{1,0:T(8,128)(2,1)} %tokens.1), channel_id=1, source_target_pairs={{0,6},{1,7},{2,0},{3,1},{4,2},{5,3},{6,4},{7,5},{8,14},{9,15},{10,... | collective-permute-start | bytes 1179656 | tf_op jit(solution)/shard_map/ppermute | solution.py:413
  37.6 1.6 %collective-permute-start.16 = (bf16[384,768]{1,0:T(8,128)(2,1)S(1)}, bf16[384,768]{1,0:T(8,128)(2,1)S(1)}, u32[]{:S(2)}, u32[]{:S(2)}) collective-permute-start(bf16[384,768]{1,0:T(8,128)(2,1)S(1)} %bitcast.7), channel_id=1, source_target_pairs={{0,8},{8,0},{16,24},{24,16},{1,9},{9,1},{17,25},{25,17},{2,10},{10... | collective-permute-start | bytes 1769480 | tf_op jit(solution)/shard_map/ppermute | solution.py:416
  39.2 1.5 %collective-permute-start.17 = (bf16[384,768]{1,0:T(8,128)(2,1)S(1)}, bf16[384,768]{1,0:T(8,128)(2,1)S(1)}, u32[]{:S(2)}, u32[]{:S(2)}) collective-permute-start(bf16[384,768]{1,0:T(8,128)(2,1)S(1)} %bitcast.8), channel_id=1, source_target_pairs={{0,16},{8,24},{16,0},{24,8},{1,17},{9,25},{17,1},{25,9},{2,18},{10... | collective-permute-start | bytes 1769480 | tf_op jit(solution)/shard_map/ppermute | solution.py:416
  40.7 4.4 %collective-permute-done.12.refs_4_ = bf16[128,1536]{1,0:T(8,128)(2,1)S(1)} collective-permute-done((bf16[128,1536]{1,0:T(8,128)(2,1)}, bf16[128,1536]{1,0:T(8,128)(2,1)S(1)}, u32[]{:S(2)}, u32[]{:S(2)}) %collective-permute-start.12) | collective-permute-done | bytes 393248 | tf_op jit(solution)/shard_map/ppermute | solution.py:413
  46.4 6.9 %collective-permute-done.16.refs_5_.refs_7_ = bf16[384,768]{1,0:T(8,128)(2,1)S(1)} collective-permute-done((bf16[384,768]{1,0:T(8,128)(2,1)S(1)}, bf16[384,768]{1,0:T(8,128)(2,1)S(1)}, u32[]{:S(2)}, u32[]{:S(2)}) %collective-permute-start.16) | collective-permute-done | bytes 589856 | tf_op jit(solution)/shard_map/ppermute | solution.py:416
  55.4 1.6 %collective-permute-start.18 = (bf16[384,768]{1,0:T(8,128)(2,1)S(1)}, bf16[384,768]{1,0:T(8,128)(2,1)S(1)}, u32[]{:S(2)}, u32[]{:S(2)}) collective-permute-start(bf16[384,768]{1,0:T(8,128)(2,1)S(1)} %collective-permute-done.16.refs_5_.refs_7_), channel_id=1, source_target_pairs={{0,16},{8,24},{16,0},{24,8},{1,17},{9,25},{17,1},{25,9},{2,18},{10... | collective-permute-start | bytes 1769480 | tf_op jit(solution)/shard_map/ppermute | solution.py:416
  57.2 7.3 %collective-permute-done.7.refs_1_ = bf16[128,1152]{1,0:T(8,128)(2,1)S(1)} collective-permute-done((bf16[128,1152]{1,0:T(8,128)(2,1)S(1)}, bf16[128,1152]{1,0:T(8,128)(2,1)S(1)}, u32[]{:S(2)}, u32[]{:S(2)}) %collective-permute-start.7) | collective-permute-done | bytes 294944 | tf_op jit(solution)/shard_map/ppermute | solution.py:413
  65.1 2.9 %collective-permute-done.28.refs_2_.refs_9_ = bf16[768,384]{1,0:T(8,128)(2,1)S(1)} collective-permute-done((bf16[768,384]{1,0:T(8,128)(2,1)}, bf16[768,384]{1,0:T(8,128)(2,1)S(1)}, u32[]{:S(2)}, u32[]{:S(2)}) %collective-permute-start.28) | collective-permute-done | bytes 589856 | tf_op jit(solution)/shard_map/ppermute | solution.py:416
  70.0 1.5 %collective-permute-start.29 = (bf16[768,384]{1,0:T(8,128)(2,1)S(1)}, bf16[768,384]{1,0:T(8,128)(2,1)S(1)}, u32[]{:S(2)}, u32[]{:S(2)}) collective-permute-start(bf16[768,384]{1,0:T(8,128)(2,1)S(1)} %collective-permute-done.28.refs_2_.refs_9_), channel_id=1, source_target_pairs={{0,8},{8,0},{16,24},{24,16},{1,9},{9,1},{17,25},{25,17},{2,10},{10... | collective-permute-start | bytes 1769480 | tf_op jit(solution)/shard_map/ppermute | solution.py:416
  71.5 7.9 %collective-permute-done.13.refs_1_ = bf16[128,1536]{1,0:T(8,128)(2,1)S(1)} collective-permute-done((bf16[128,1536]{1,0:T(8,128)(2,1)S(1)}, bf16[128,1536]{1,0:T(8,128)(2,1)S(1)}, u32[]{:S(2)}, u32[]{:S(2)}) %collective-permute-start.13) | collective-permute-done | bytes 393248 | tf_op jit(solution)/shard_map/ppermute | solution.py:413
  80.0 1.6 %shard_map.79 = (bf16[768,768]{1,0:T(8,128)(2,1)S(1)}, bf16[1536,768]{1,0:T(8,128)(2,1)S(1)}, f32[768,768]{1,0:T(8,128)S(1)}) custom-call(bf16[128,1536]{1,0:T(8,128)(2,1)S(1)} %get-tuple-element.43.refs_0_, bf16[128,1536]{1,0:T(8,128)(2,1)S(1)} %collective-permute-done.24.refs_1_, bf16[128,1536]{1,0:T(8,128)(2,1)S(1)} %collective-permute-done.10.refs_2_, ...), custom_call_target="tpu_custom_call" | custom-call | flops 905969664 | bytes 9437184 | tf_op jit(solution)/shard_map/pallas_call | solution.py:268
  81.6 3.5 %shard_map.80 = (bf16[768,1152]{1,0:T(8,128)(2,1)S(1)}, bf16[768,768]{1,0:T(8,128)(2,1)S(1)}, f32[768,768]{1,0:T(8,128)S(1)}, f32[768,384]{1,0:T(8,128)S(1)}, f3...) custom-call(bf16[128,1152]{1,0:T(8,128)(2,1)S(1)} %get-tuple-element.40.refs_0_, ...), custom_call_target="tpu_custom_call" | custom-call | flops 2264924160 | bytes 15360000 | tf_op jit(solution)/shard_map/pallas_call | solution.py:268
  85.5 3.5 %collective-permute-start.33 = (bf16[128,384]{1,0:T(8,128)(2,1)S(1)}, bf16[128,384]{1,0:T(8,128)(2,1)S(1)}, u32[]{:S(2)}, u32[]{:S(2)}) collective-permute-start(bf16[128,384]{1,0:T(8,128)(2,1)S(1)} %get-tuple-element.39.refs_0_), channel_id=1, source_target_pairs={{0,6},{1,7},{2,0},{3,1},{4,2},{5,3},{6,4},{7,5},{8,14},{9,15},{10,... | collective-permute-start | bytes 294920 | tf_op jit(solution)/shard_map/ppermute | solution.py:413
  94.0 2.7 %collective-permute-done.refs_0_ = bf16[128,384]{1,0:T(8,128)(2,1)S(1)} collective-permute-done((bf16[128,384]{1,0:T(8,128)(2,1)S(1)}, bf16[128,384]{1,0:T(8,128)(2,1)S(1)}, u32[]{:S(2)}, u32[]{:S(2)}) %collective-permute-start) | collective-permute-done | bytes 98336 | tf_op jit(solution)/shard_map/ppermute | solution.py:413
  98.0 1.5 %collective-permute-start.45 = (bf16[384,384]{1,0:T(8,128)(2,1)S(1)}, bf16[384,384]{1,0:T(8,128)(2,1)S(1)}, u32[]{:S(2)}, u32[]{:S(2)}) collective-permute-start(bf16[384,384]{1,0:T(8,128)(2,1)S(1)} %get-tuple-element.75), channel_id=1, source_target_pairs={{0,16},{8,24},{16,0},{24,8},{1,17},{9,25},{17,1},{25,9},{2,18},{10... | collective-permute-start | bytes 884744 | tf_op jit(solution)/shard_map/ppermute | solution.py:416
  99.5 2.0 %shard_map.82.refs_9_ = f32[768,768]{1,0:T(8,128)S(1)} custom-call(bf16[768,1152]{1,0:T(8,128)(2,1)S(1)} %get-tuple-element.51.g, bf16[768,384]{1,0:T(8,128)(2,1)S(1)} %collective-permute-done.29.refs_0_.refs_10_, bf16[768,384]{1,0:T(8,128)(2,1)S(1)} %collective-permute-done.27.refs_1_.refs_8_, bf16[768,384]{1,0:T(8,128)(2,1)S(1)} %collective-permute-done.28.refs_2_.refs_9_), custom_call_target="tpu_custom_call" | custom-call | flops 1358954496 | bytes 5898240 | tf_op jit(solution)/shard_map/pallas_call | solution.py:268
  104.1 3.4 %shard_map.83 = (f32[384,768]{1,0:T(8,128)S(1)}, f32[384,768]{1,0:T(8,128)S(1)}, f32[384,768]{1,0:T(8,128)S(1)}, f32[384,768]{1,0:T(8,128)S(1)}, f32[768,384]{1,0:T(8,128)S(1)}) custom-call(bf16[128,384]{1,0:T(8,128)(2,1)S(1)} %get-tuple-element.39.refs_0_, bf16[128,384]{1,0:T(8,128)(2,1)S(1)} %collective-permute-done.30.refs_1_, ...), custom_call_target="tpu_custom_call" | custom-call | flops 2717908992 | bytes 15360000 | tf_op jit(solution)/shard_map/pallas_call | solution.py:268
  107.5 2.4 %shard_map.84 = (bf16[192,768]{1,0:T(8,128)(2,1)S(1)}, bf16[192,768]{1,0:T(8,128)(2,1)S(1)}, bf16[192,768]{1,0:T(8,128)(2,1)S(1)}, bf16[192,768]{1,0:T(8,128)(2,...) custom-call(bf16[128,384]{1,0:T(8,128)(2,1)S(1)} %collective-permute-, ...), custom_call_target="tpu_custom_call" | custom-call | flops 1358954496 | bytes 15736832 | tf_op jit(solution)/shard_map/pallas_call | solution.py:268
  109.9 1.6 %collective-permute-start.39 = (bf16[192,768]{1,0:T(8,128)(2,1)S(1)}, bf16[192,768]{1,0:T(8,128)(2,1)S(1)}, u32[]{:S(2)}, u32[]{:S(2)}) collective-permute-start(bf16[192,768]{1,0:T(8,128)(2,1)S(1)} %get-tuple-element.66), channel_id=1, source_target_pairs={{0,16},{8,24},{16,0},{24,8},{1,17},{9,25},{17,1},{25,9},{2,18},{10... | collective-permute-start | bytes 884744 | tf_op jit(solution)/shard_map/ppermute | solution.py:416
  112.1 1.5 %collective-permute-start.35 = (bf16[192,768]{1,0:T(8,128)(2,1)S(1)}, bf16[192,768]{1,0:T(8,128)(2,1)S(1)}, u32[]{:S(2)}, u32[]{:S(2)}) collective-permute-start(bf16[192,768]{1,0:T(8,128)(2,1)S(1)} %get-tuple-element.61), channel_id=1, source_target_pairs={{0,8},{8,0},{16,24},{24,16},{1,9},{9,1},{17,25},{25,17},{2,10},{10... | collective-permute-start | bytes 884744 | tf_op jit(solution)/shard_map/ppermute | solution.py:416
  113.8 5.3 %collective-permute-done.39 = bf16[192,768]{1,0:T(8,128)(2,1)S(1)} collective-permute-done((bf16[192,768]{1,0:T(8,128)(2,1)S(1)}, bf16[192,768]{1,0:T(8,128)(2,1)S(1)}, u32[]{:S(2)}, u32[]{:S(2)}) %collective-permute-start.39) | collective-permute-done | bytes 294944 | tf_op jit(solution)/shard_map/ppermute | solution.py:416
  119.1 1.5 %collective-permute-start.36 = (bf16[192,768]{1,0:T(8,128)(2,1)S(1)}, bf16[192,768]{1,0:T(8,128)(2,1)S(1)}, u32[]{:S(2)}, u32[]{:S(2)}) collective-permute-start(bf16[192,768]{1,0:T(8,128)(2,1)S(1)} %get-tuple-element.62), channel_id=1, source_target_pairs={{0,16},{8,24},{16,0},{24,8},{1,17},{9,25},{17,1},{25,9},{2,18},{10... | collective-permute-start | bytes 884744 | tf_op jit(solution)/shard_map/ppermute | solution.py:416
  120.7 3.4 %collective-permute-done.37 = bf16[192,768]{1,0:T(8,128)(2,1)S(1)} collective-permute-done((bf16[192,768]{1,0:T(8,128)(2,1)S(1)}, bf16[192,768]{1,0:T(8,128)(2,1)S(1)}, u32[]{:S(2)}, u32[]{:S(2)}) %collective-permute-start.37) | collective-permute-done | bytes 294944 | tf_op jit(solution)/shard_map/ppermute | solution.py:416
  125.3 1.5 %collective-permute-start.40 = (bf16[192,768]{1,0:T(8,128)(2,1)S(1)}, bf16[192,768]{1,0:T(8,128)(2,1)S(1)}, u32[]{:S(2)}, u32[]{:S(2)}) collective-permute-start(bf16[192,768]{1,0:T(8,128)(2,1)S(1)} %add_convert_fusion.2), channel_id=1, source_target_pairs={{0,8},{8,0},{16,24},{24,16},{1,9},{9,1},{17,25},{25,17},{2,10},{10... | collective-permute-start | bytes 884744 | tf_op jit(solution)/shard_map/ppermute | solution.py:416
  126.8 3.6 %collective-permute-done.35.near_a = bf16[192,768]{1,0:T(8,128)(2,1)S(1)} collective-permute-done((bf16[192,768]{1,0:T(8,128)(2,1)S(1)}, bf16[192,768]{1,0:T(8,128)(2,1)S(1)}, u32[]{:S(2)}, u32[]{:S(2)}) %collective-permute-start.35) | collective-permute-done | bytes 294944 | tf_op jit(solution)/shard_map/ppermute | solution.py:416
  131.2 5.5 %collective-permute-done.46.far_b = bf16[384,384]{1,0:T(8,128)(2,1)S(1)} collective-permute-done((bf16[384,384]{1,0:T(8,128)(2,1)S(1)}, bf16[384,384]{1,0:T(8,128)(2,1)S(1)}, u32[]{:S(2)}, u32[]{:S(2)}) %collective-permute-start.46) | collective-permute-done | bytes 294944 | tf_op jit(solution)/shard_map/ppermute | solution.py:416
  137.6 3.8 %collective-permute-done.40.far_b = bf16[192,768]{1,0:T(8,128)(2,1)S(1)} collective-permute-done((bf16[192,768]{1,0:T(8,128)(2,1)S(1)}, bf16[192,768]{1,0:T(8,128)(2,1)S(1)}, u32[]{:S(2)}, u32[]{:S(2)}) %collective-permute-start.40) | collective-permute-done | bytes 294944 | tf_op jit(solution)/shard_map/ppermute | solution.py:416
  (90 shorter events, 26.1 us)
Async XLA Ops:
  4.1 33.5 %collective-permute-start.4 = (bf16[128,1152]{1,0:T(8,128)(2,1)S(1)}, bf16[128,1152]{1,0:T(8,128)(2,1)S(1)}, u32[]{:S(2)}, u32[]{:S(2)}) collective-permute-start(bf16[128,1152]{1,0:T(8,128)(2,1)S(1)} %get-tuple-element.40.refs_0_), channel_id=1, source_target_pairs={{0,2},{1,3},{2,4},{3,5},{4,6},{5,7},{6,0},{7,1},{8,10},{9,11},{10,... | collective-permute-start | bytes 884744 | tf_op jit(solution)/shard_map/ppermute | solution.py:413
  7.2 30.4 %collective-permute-start.6 = (bf16[128,1152]{1,0:T(8,128)(2,1)S(1)}, bf16[128,1152]{1,0:T(8,128)(2,1)S(1)}, u32[]{:S(2)}, u32[]{:S(2)}) collective-permute-start(bf16[128,1152]{1,0:T(8,128)(2,1)S(1)} %get-tuple-element.40.refs_0_), channel_id=1, source_target_pairs={{0,6},{1,7},{2,0},{3,1},{4,2},{5,3},{6,4},{7,5},{8,14},{9,15},{10,... | collective-permute-start | bytes 884744 | tf_op jit(solution)/shard_map/ppermute | solution.py:413
  9.4 31.3 %collective-permute-start.10 = (bf16[128,1536]{1,0:T(8,128)(2,1)}, bf16[128,1536]{1,0:T(8,128)(2,1)S(1)}, u32[]{:S(2)}, u32[]{:S(2)}) collective-permute-start(bf16[128,1536]{1,0:T(8,128)(2,1)} %tokens.1), channel_id=1, source_target_pairs={{0,2},{1,3},{2,4},{3,5},{4,6},{5,7},{6,0},{7,1},{8,10},{9,11},{10,... | collective-permute-start | bytes 1179656 | tf_op jit(solution)/shard_map/ppermute | solution.py:413
  10.5 20.8 %collective-permute-start.22 = (f32[8,256]{1,0:T(8,128)S(1)}, f32[8,256]{1,0:T(8,128)S(1)}, u32[]{:S(2)}, u32[]{:S(2)}) collective-permute-start(f32[8,256]{1,0:T(8,128)S(1)} %pad_maximum_fusion.refs_6_), channel_id=1, source_target_pairs={{0,2},{1,3},{2,4},{3,5},{4,6},{5,7},{6,0},{7,1},{8,10},{9,11},{10,... | collective-permute-start | bytes 24584 | tf_op jit(solution)/shard_map/ppermute | solution.py:413
  10.9 21.0 %collective-permute-start.23 = (f32[8,256]{1,0:T(8,128)S(1)}, f32[8,256]{1,0:T(8,128)S(1)}, u32[]{:S(2)}, u32[]{:S(2)}) collective-permute-start(f32[8,256]{1,0:T(8,128)S(1)} %pad_maximum_fusion.refs_6_), channel_id=1, source_target_pairs={{0,6},{1,7},{2,0},{3,1},{4,2},{5,3},{6,4},{7,5},{8,14},{9,15},{10,... | collective-permute-start | bytes 24584 | tf_op jit(solution)/shard_map/ppermute | solution.py:413
  35.8 9.3 %collective-permute-start.12 = (bf16[128,1536]{1,0:T(8,128)(2,1)}, bf16[128,1536]{1,0:T(8,128)(2,1)S(1)}, u32[]{:S(2)}, u32[]{:S(2)}) collective-permute-start(bf16[128,1536]{1,0:T(8,128)(2,1)} %tokens.1), channel_id=1, source_target_pairs={{0,6},{1,7},{2,0},{3,1},{4,2},{5,3},{6,4},{7,5},{8,14},{9,15},{10,... | collective-permute-start | bytes 1179656 | tf_op jit(solution)/shard_map/ppermute | solution.py:413
  37.6 15.7 %collective-permute-start.16 = (bf16[384,768]{1,0:T(8,128)(2,1)S(1)}, bf16[384,768]{1,0:T(8,128)(2,1)S(1)}, u32[]{:S(2)}, u32[]{:S(2)}) collective-permute-start(bf16[384,768]{1,0:T(8,128)(2,1)S(1)} %bitcast.7), channel_id=1, source_target_pairs={{0,8},{8,0},{16,24},{24,16},{1,9},{9,1},{17,25},{25,17},{2,10},{10... | collective-permute-start | bytes 1769480 | tf_op jit(solution)/shard_map/ppermute | solution.py:416
  39.2 16.3 %collective-permute-start.17 = (bf16[384,768]{1,0:T(8,128)(2,1)S(1)}, bf16[384,768]{1,0:T(8,128)(2,1)S(1)}, u32[]{:S(2)}, u32[]{:S(2)}) collective-permute-start(bf16[384,768]{1,0:T(8,128)(2,1)S(1)} %bitcast.8), channel_id=1, source_target_pairs={{0,16},{8,24},{16,0},{24,8},{1,17},{9,25},{17,1},{25,9},{2,18},{10... | collective-permute-start | bytes 1769480 | tf_op jit(solution)/shard_map/ppermute | solution.py:416
  40.7 13.3 %collective-permute-start.20 = (bf16[128,1152]{1,0:T(8,128)(2,1)S(1)}, bf16[128,1152]{1,0:T(8,128)(2,1)S(1)}, u32[]{:S(2)}, u32[]{:S(2)}) collective-permute-start(bf16[128,1152]{1,0:T(8,128)(2,1)S(1)} %collective-permute-done.4.refs_2_), channel_id=1, source_target_pairs={{0,1},{1,0},{2,3},{3,2},{4,5},{5,4},{6,7},{7,6},{8,9},{9,8},{10,11... | collective-permute-start | bytes 884744 | tf_op jit(solution)/shard_map/ppermute | solution.py:413
  45.1 22.9 %collective-permute-start.28 = (bf16[768,384]{1,0:T(8,128)(2,1)}, bf16[768,384]{1,0:T(8,128)(2,1)S(1)}, u32[]{:S(2)}, u32[]{:S(2)}) collective-permute-start(bf16[768,384]{1,0:T(8,128)(2,1)} %bitcast.1.down), channel_id=1, source_target_pairs={{0,16},{8,24},{16,0},{24,8},{1,17},{9,25},{17,1},{25,9},{2,18},{10... | collective-permute-start | bytes 1769480 | tf_op jit(solution)/shard_map/ppermute | solution.py:416
  54.0 10.4 %collective-permute-start.7 = (bf16[128,1152]{1,0:T(8,128)(2,1)S(1)}, bf16[128,1152]{1,0:T(8,128)(2,1)S(1)}, u32[]{:S(2)}, u32[]{:S(2)}) collective-permute-start(bf16[128,1152]{1,0:T(8,128)(2,1)S(1)} %collective-permute-done.6.refs_4_), channel_id=1, source_target_pairs={{2,0},{3,1},{4,2},{5,3},{10,8},{11,9},{12,10},{13,11},{18,16},{19,... | collective-permute-start | bytes 884744 | tf_op jit(solution)/shard_map/ppermute | solution.py:413
  55.3 14.0 %collective-permute-start.25 = (bf16[128,1536]{1,0:T(8,128)(2,1)S(1)}, bf16[128,1536]{1,0:T(8,128)(2,1)S(1)}, u32[]{:S(2)}, u32[]{:S(2)}) collective-permute-start(bf16[128,1536]{1,0:T(8,128)(2,1)S(1)} %collective-permute-done.10.refs_2_), channel_id=1, source_target_pairs={{0,1},{1,0},{2,3},{3,2},{4,5},{5,4},{6,7},{7,6},{8,9},{9,8},{10,11... | collective-permute-start | bytes 1179656 | tf_op jit(solution)/shard_map/ppermute | solution.py:413
  55.4 24.5 %collective-permute-start.18 = (bf16[384,768]{1,0:T(8,128)(2,1)S(1)}, bf16[384,768]{1,0:T(8,128)(2,1)S(1)}, u32[]{:S(2)}, u32[]{:S(2)}) collective-permute-start(bf16[384,768]{1,0:T(8,128)(2,1)S(1)} %collective-permute-done.16.refs_5_.refs_7_), channel_id=1, source_target_pairs={{0,16},{8,24},{16,0},{24,8},{1,17},{9,25},{17,1},{25,9},{2,18},{10... | collective-permute-start | bytes 1769480 | tf_op jit(solution)/shard_map/ppermute | solution.py:416
  57.0 12.4 %collective-permute-start.26 = (bf16[128,1536]{1,0:T(8,128)(2,1)S(1)}, bf16[128,1536]{1,0:T(8,128)(2,1)S(1)}, u32[]{:S(2)}, u32[]{:S(2)}) collective-permute-start(bf16[128,1536]{1,0:T(8,128)(2,1)S(1)} %collective-permute-done.12.refs_4_), channel_id=1, source_target_pairs={{0,1},{1,0},{2,3},{3,2},{4,5},{5,4},{6,7},{7,6},{8,9},{9,8},{10,11... | collective-permute-start | bytes 1179656 | tf_op jit(solution)/shard_map/ppermute | solution.py:413
  68.0 11.4 %collective-permute-start.13 = (bf16[128,1536]{1,0:T(8,128)(2,1)S(1)}, bf16[128,1536]{1,0:T(8,128)(2,1)S(1)}, u32[]{:S(2)}, u32[]{:S(2)}) collective-permute-start(bf16[128,1536]{1,0:T(8,128)(2,1)S(1)} %collective-permute-done.12.refs_4_), channel_id=1, source_target_pairs={{2,0},{3,1},{4,2},{5,3},{10,8},{11,9},{12,10},{13,11},{18,16},{19,... | collective-permute-start | bytes 1179656 | tf_op jit(solution)/shard_map/ppermute | solution.py:413
  69.3 10.1 %collective-permute-start.8 = (bf16[128,1152]{1,0:T(8,128)(2,1)S(1)}, bf16[128,1152]{1,0:T(8,128)(2,1)S(1)}, u32[]{:S(2)}, u32[]{:S(2)}) collective-permute-start(bf16[128,1152]{1,0:T(8,128)(2,1)S(1)} %collective-permute-done.5.refs_0_), channel_id=1, source_target_pairs={{0,1},{1,0},{2,3},{3,2},{4,5},{5,4},{6,7},{7,6},{8,9},{9,8},{10,11... | collective-permute-start | bytes 884744 | tf_op jit(solution)/shard_map/ppermute | solution.py:413
  69.4 27.4 %collective-permute-start.27 = (bf16[768,384]{1,0:T(8,128)(2,1)}, bf16[768,384]{1,0:T(8,128)(2,1)S(1)}, u32[]{:S(2)}, u32[]{:S(2)}) collective-permute-start(bf16[768,384]{1,0:T(8,128)(2,1)} %bitcast.1.down), channel_id=1, source_target_pairs={{0,8},{8,0},{16,24},{24,16},{1,9},{9,1},{17,25},{25,17},{2,10},{10... | collective-permute-start | bytes 1769480 | tf_op jit(solution)/shard_map/ppermute | solution.py:416
  70.0 28.0 %collective-permute-start.29 = (bf16[768,384]{1,0:T(8,128)(2,1)S(1)}, bf16[768,384]{1,0:T(8,128)(2,1)S(1)}, u32[]{:S(2)}, u32[]{:S(2)}) collective-permute-start(bf16[768,384]{1,0:T(8,128)(2,1)S(1)} %collective-permute-done.28.refs_2_.refs_9_), channel_id=1, source_target_pairs={{0,8},{8,0},{16,24},{24,16},{1,9},{9,1},{17,25},{25,17},{2,10},{10... | collective-permute-start | bytes 1769480 | tf_op jit(solution)/shard_map/ppermute | solution.py:416
  79.4 9.6 %collective-permute-start.15 = (bf16[128,1536]{1,0:T(8,128)(2,1)S(1)}, bf16[128,1536]{1,0:T(8,128)(2,1)S(1)}, u32[]{:S(2)}, u32[]{:S(2)}) collective-permute-start(bf16[128,1536]{1,0:T(8,128)(2,1)S(1)} %collective-permute-done.13.refs_1_), channel_id=1, source_target_pairs={{0,1},{1,0},{2,3},{3,2},{4,5},{5,4},{6,7},{7,6},{8,9},{9,8},{10,11... | collective-permute-start | bytes 1179656 | tf_op jit(solution)/shard_map/ppermute | solution.py:413
  96.8 10.8 %collective-permute-start.1 = (bf16[128,384]{1,0:T(8,128)(2,1)S(1)}, bf16[128,384]{1,0:T(8,128)(2,1)S(1)}, u32[]{:S(2)}, u32[]{:S(2)}) collective-permute-start(bf16[128,384]{1,0:T(8,128)(2,1)S(1)} %collective-permute-done.refs_0_), channel_id=1, source_target_pairs={{0,1},{1,0},{2,3},{3,2},{4,5},{5,4},{6,7},{7,6},{8,9},{9,8},{10,11... | collective-permute-start | bytes 294920 | tf_op jit(solution)/shard_map/ppermute | solution.py:413
  98.0 13.5 %collective-permute-start.45 = (bf16[384,384]{1,0:T(8,128)(2,1)S(1)}, bf16[384,384]{1,0:T(8,128)(2,1)S(1)}, u32[]{:S(2)}, u32[]{:S(2)}) collective-permute-start(bf16[384,384]{1,0:T(8,128)(2,1)S(1)} %get-tuple-element.75), channel_id=1, source_target_pairs={{0,16},{8,24},{16,0},{24,8},{1,17},{9,25},{17,1},{25,9},{2,18},{10... | collective-permute-start | bytes 884744 | tf_op jit(solution)/shard_map/ppermute | solution.py:416
  101.5 10.6 %collective-permute-start.43 = (bf16[384,384]{1,0:T(8,128)(2,1)S(1)}, bf16[384,384]{1,0:T(8,128)(2,1)S(1)}, u32[]{:S(2)}, u32[]{:S(2)}) collective-permute-start(bf16[384,384]{1,0:T(8,128)(2,1)S(1)} %get-tuple-element.73), channel_id=1, source_target_pairs={{0,8},{8,0},{16,24},{24,16},{1,9},{9,1},{17,25},{25,17},{2,10},{10... | collective-permute-start | bytes 884744 | tf_op jit(solution)/shard_map/ppermute | solution.py:416
  102.1 22.6 %collective-permute-start.41 = (bf16[384,384]{1,0:T(8,128)(2,1)S(1)}, bf16[384,384]{1,0:T(8,128)(2,1)S(1)}, u32[]{:S(2)}, u32[]{:S(2)}) collective-permute-start(bf16[384,384]{1,0:T(8,128)(2,1)S(1)} %get-tuple-element.70), channel_id=1, source_target_pairs={{0,8},{8,0},{16,24},{24,16},{1,9},{9,1},{17,25},{25,17},{2,10},{10... | collective-permute-start | bytes 884744 | tf_op jit(solution)/shard_map/ppermute | solution.py:416
  103.6 21.7 %collective-permute-start.42 = (bf16[384,384]{1,0:T(8,128)(2,1)S(1)}, bf16[384,384]{1,0:T(8,128)(2,1)S(1)}, u32[]{:S(2)}, u32[]{:S(2)}) collective-permute-start(bf16[384,384]{1,0:T(8,128)(2,1)S(1)} %get-tuple-element.71), channel_id=1, source_target_pairs={{0,16},{8,24},{16,0},{24,8},{1,17},{9,25},{17,1},{25,9},{2,18},{10... | collective-permute-start | bytes 884744 | tf_op jit(solution)/shard_map/ppermute | solution.py:416
  109.9 9.2 %collective-permute-start.39 = (bf16[192,768]{1,0:T(8,128)(2,1)S(1)}, bf16[192,768]{1,0:T(8,128)(2,1)S(1)}, u32[]{:S(2)}, u32[]{:S(2)}) collective-permute-start(bf16[192,768]{1,0:T(8,128)(2,1)S(1)} %get-tuple-element.66), channel_id=1, source_target_pairs={{0,16},{8,24},{16,0},{24,8},{1,17},{9,25},{17,1},{25,9},{2,18},{10... | collective-permute-start | bytes 884744 | tf_op jit(solution)/shard_map/ppermute | solution.py:416
  111.5 12.6 %collective-permute-start.37 = (bf16[192,768]{1,0:T(8,128)(2,1)S(1)}, bf16[192,768]{1,0:T(8,128)(2,1)S(1)}, u32[]{:S(2)}, u32[]{:S(2)}) collective-permute-start(bf16[192,768]{1,0:T(8,128)(2,1)S(1)} %get-tuple-element.64), channel_id=1, source_target_pairs={{0,8},{8,0},{16,24},{24,16},{1,9},{9,1},{17,25},{25,17},{2,10},{10... | collective-permute-start | bytes 884744 | tf_op jit(solution)/shard_map/ppermute | solution.py:416
  112.1 18.3 %collective-permute-start.35 = (bf16[192,768]{1,0:T(8,128)(2,1)S(1)}, bf16[192,768]{1,0:T(8,128)(2,1)S(1)}, u32[]{:S(2)}, u32[]{:S(2)}) collective-permute-start(bf16[192,768]{1,0:T(8,128)(2,1)S(1)} %get-tuple-element.61), channel_id=1, source_target_pairs={{0,8},{8,0},{16,24},{24,16},{1,9},{9,1},{17,25},{25,17},{2,10},{10... | collective-permute-start | bytes 884744 | tf_op jit(solution)/shard_map/ppermute | solution.py:416
  119.1 11.9 %collective-permute-start.36 = (bf16[192,768]{1,0:T(8,128)(2,1)S(1)}, bf16[192,768]{1,0:T(8,128)(2,1)S(1)}, u32[]{:S(2)}, u32[]{:S(2)}) collective-permute-start(bf16[192,768]{1,0:T(8,128)(2,1)S(1)} %get-tuple-element.62), channel_id=1, source_target_pairs={{0,16},{8,24},{16,0},{24,8},{1,17},{9,25},{17,1},{25,9},{2,18},{10... | collective-permute-start | bytes 884744 | tf_op jit(solution)/shard_map/ppermute | solution.py:416
  124.1 12.6 %collective-permute-start.46 = (bf16[384,384]{1,0:T(8,128)(2,1)S(1)}, bf16[384,384]{1,0:T(8,128)(2,1)S(1)}, u32[]{:S(2)}, u32[]{:S(2)}) collective-permute-start(bf16[384,384]{1,0:T(8,128)(2,1)S(1)} %add_convert_fusion), channel_id=1, source_target_pairs={{0,8},{8,0},{16,24},{24,16},{1,9},{9,1},{17,25},{25,17},{2,10},{10... | collective-permute-start | bytes 884744 | tf_op jit(solution)/shard_map/ppermute | solution.py:416
  124.7 12.0 %collective-permute-start.44 = (bf16[384,384]{1,0:T(8,128)(2,1)S(1)}, bf16[384,384]{1,0:T(8,128)(2,1)S(1)}, u32[]{:S(2)}, u32[]{:S(2)}) collective-permute-start(bf16[384,384]{1,0:T(8,128)(2,1)S(1)} %add_convert_fusion.1), channel_id=1, source_target_pairs={{0,16},{8,24},{16,0},{24,8},{1,17},{9,25},{17,1},{25,9},{2,18},{10... | collective-permute-start | bytes 884744 | tf_op jit(solution)/shard_map/ppermute | solution.py:416
  125.3 16.1 %collective-permute-start.40 = (bf16[192,768]{1,0:T(8,128)(2,1)S(1)}, bf16[192,768]{1,0:T(8,128)(2,1)S(1)}, u32[]{:S(2)}, u32[]{:S(2)}) collective-permute-start(bf16[192,768]{1,0:T(8,128)(2,1)S(1)} %add_convert_fusion.2), channel_id=1, source_target_pairs={{0,8},{8,0},{16,24},{24,16},{1,9},{9,1},{17,25},{25,17},{2,10},{10... | collective-permute-start | bytes 884744 | tf_op jit(solution)/shard_map/ppermute | solution.py:416
  130.4 11.0 %collective-permute-start.38 = (bf16[192,768]{1,0:T(8,128)(2,1)S(1)}, bf16[192,768]{1,0:T(8,128)(2,1)S(1)}, u32[]{:S(2)}, u32[]{:S(2)}) collective-permute-start(bf16[192,768]{1,0:T(8,128)(2,1)S(1)} %add_convert_fusion.3), channel_id=1, source_target_pairs={{0,16},{8,24},{16,0},{24,8},{1,17},{9,25},{17,1},{25,9},{2,18},{10... | collective-permute-start | bytes 884744 | tf_op jit(solution)/shard_map/ppermute | solution.py:416
  (19 other events, 116.1 us)

commit v7 on v6

--- a/solution.py
+++ b/solution.py
@@ -143,15 +143,16 @@
         sums[place][...] = dot_rows(act_turned[...], g[:, place * block : (place + 1) * block])
 
 
+def merge_kernel(upper, lower, out):
+    out[...] = upper[...] + lower[...]
+
+
 def last_forward_kernel(block, *refs):
-    shards, ups = refs[0:4], refs[4:8]
-    x_turned, act_turned, slope, x = refs[8:]
+    shards, ups = refs[0:2], refs[2:6]
+    x_turned, act_turned, slope, x = refs[6:]
     for half in range(2):
         for bits in range(4):
-            cols = owner_columns(block, bits)
-            x[half * SHARD : (half + 1) * SHARD, bits * block : (bits + 1) * block] = (
-                shards[2 * half][:, cols] + shards[2 * half + 1][:, cols]
-            )
+            x[half * SHARD : (half + 1) * SHARD, bits * block : (bits + 1) * block] = shards[half][:, owner_columns(block, bits)]
     pre = dot_rows(x[:, :block], ups[0][...])
     for bits in (1, 2, 3):
         pre = pre + dot_rows(x[:, bits * block : (bits + 1) * block], ups[bits][...])
@@ -161,12 +162,11 @@
 
 
 def last_far_kernel(block, *refs):
-    shards, table, act_turned, far_sum = refs[0:4], refs[4], refs[5], refs[6]
-    g, far_a, far_b = refs[7:]
+    shards, table, act_turned, far_sum = refs[0:2], refs[2], refs[3], refs[4]
+    g, far_a, far_b = refs[5:]
     expert = lax.axis_index("expert")
     for half in range(2):
-        gate = pick_gate(table, half, expert)
-        g[half * SHARD : (half + 1) * SHARD, :] = scale_rows(gate, shards[2 * half][...] + shards[2 * half + 1][...])
+        g[half * SHARD : (half + 1) * SHARD, :] = scale_rows(pick_gate(table, half, expert), shards[half][...])
     middle = act_turned.shape[0] // 2
     total = dot_rows(act_turned[...], g[:, :block]) + far_sum[...]
     far_a[...] = total[:middle].astype(BF16)
@@ -313,6 +313,10 @@
     )
 
 
+def merged(upper, lower):
+    return local_call(merge_kernel, [shape(*upper.shape, BF16)], (upper, lower))[0]
+
+
 def last_forward(shards, ups):
     block, hidden = ups[0].shape
     rows, width = 2 * SHARD, 4 * block
@@ -458,10 +462,10 @@
     gb1 = ex(gb, ring(1))
     gb3 = ex(gb, ring(-1))
     gb2 = ex(gb, ring(2))
-    t2ub = ex(t2u, swap)
-    t2db = ex(t2d, swap)
-    ga2ub = ex(ga2u, swap)
-    ga2db = ex(ga2d, swap)
+    t2 = merged(t2u, t2d)
+    t2b = ex(t2, swap)
+    ga2 = merged(ga2u, ga2d)
+    ga2b = ex(ga2, swap)
     gb1b = ex(gb1, swap)
     gb3b = ex(gb3, swap)
     gb2b = ex(gb2, swap)
@@ -471,8 +475,8 @@
     tables = (c0, c1, c3)
     x_tail, x_turned, pre_part = early_forward((tokens_here, t0b, t1, t1b, t3, t3b), ups)
     g_ab, act_ab, slope_ab, *down_sums = most_down((ga, ga0b, ga1, ga1b, ga3, ga3b), tables, x_tail, pre_part, up_y, up_d)
-    x_c, act_c, slope_c = last_forward((t2u, t2d, t2ub, t2db), ups)
-    g_c, *down_far = last_far((ga2u, ga2d, ga2ub, ga2db), c2, act_c, down_sums[0])
+    x_c, act_c, slope_c = last_forward((t2, t2b), ups)
+    g_c, *down_far = last_far((ga2, ga2b), c2, act_c, down_sums[0])
     down_parts = (*down_far, *last_near(g_c, act_c, *down_sums[1:]))
     grad_part = early_backward(g_ab, downs)
     up_sums, down_sum = most_up((gb, gb0b, gb1, gb1b, gb3, gb3b), tables, grad_part, slope_ab, x_turned, act_ab, down_here)

time: 143 us -> 143 us (level)
    ppermute x29 -> x27, waiting for transfers between devices: 47 us -> 34.3 us  [ex(): return lax.ppermute(value, 'expert', perm)]
    ppermute x18, waiting for transfers between devices: 32.2 us -> 44.1 us  [dp(): return lax.ppermute(value, 'dp', xor_perm(4, bits))]
    unnamed x8 -> x10, local copies, waits for them, and re-layouts: 2.07 us -> 3.06 us
    ppermute x29 -> x27, starting transfers between devices: 20.7 us -> 21.2 us  [ex(): return lax.ppermute(value, 'expert', perm)]
    pallas_call x11 -> x13, Pallas kernels: 16.8 us -> 16.7 us  [local_call(): pl.pallas_call(kernel, out_shape=outs, in_specs=[VMEM] * len(args), out_s...]
  transfers between devices with their start and end apart: 47 -> 45, of which waited for: 17 -> 17; matrix products, arithmetic and copies ran while one was open for 0% -> 0% of each run, Pallas kernels for 11% -> 11%
where the time goes in v7:
time: 143 us
  waiting for transfers between devices  78.4 us (55%)
  starting transfers between devices  41.8 us (29%)
  Pallas kernels  18.4 us (13%)
  local copies, waits for them, and re-layouts  3.06 us (2%)
    ppermute x18, waiting for transfers between devices, dp(): return lax.ppermute(value, 'dp', xor_perm(4, bits))  44.1 us
    ppermute x27, waiting for transfers between devices, ex(): return lax.ppermute(value, 'expert', perm)  34.3 us
    ppermute x27, starting transfers between devices, ex(): return lax.ppermute(value, 'expert', perm)  21.2 us
    ppermute x18, starting transfers between devices, dp(): return lax.ppermute(value, 'dp', xor_perm(4, bits))  20.6 us
    pallas_call x13, Pallas kernels, local_call(): pl.pallas_call(kernel, out_shape=outs, in_specs=[VMEM] * len(args), out_s...  16.7 us
    unnamed x10, local copies, waits for them, and re-layouts  3.06 us
  transfers between devices with their start and end apart: 45, of which 17 were waited for; matrix products, arithmetic and copies ran while one was open for 0% of the time, Pallas kernels for 11%

profile of v7, /device:TPU:0, one launch (start us, length us, event | category | flops | bytes accessed | tf_op | source)
XLA Modules:
  0.0 143.1 jit_solution(3172170860401562913)
XLA Ops:
  4.9 3.1 %collective-permute-start.4 = (bf16[128,1152]{1,0:T(8,128)(2,1)S(1)}, bf16[128,1152]{1,0:T(8,128)(2,1)S(1)}, u32[]{:S(2)}, u32[]{:S(2)}) collective-permute-start(bf16[128,1152]{1,0:T(8,128)(2,1)S(1)} %get-tuple-element.40.refs_0_), channel_id=1, source_target_pairs={{0,2},{1,3},{2,4},{3,5},{4,6},{5,7},{6,0},{7,1},{8,10},{9,11},{10,... | collective-permute-start | bytes 884744 | tf_op jit(solution)/shard_map/ppermute | solution.py:417
  8.0 2.1 %collective-permute-start.6 = (bf16[128,1152]{1,0:T(8,128)(2,1)S(1)}, bf16[128,1152]{1,0:T(8,128)(2,1)S(1)}, u32[]{:S(2)}, u32[]{:S(2)}) collective-permute-start(bf16[128,1152]{1,0:T(8,128)(2,1)S(1)} %get-tuple-element.40.refs_0_), channel_id=1, source_target_pairs={{0,6},{1,7},{2,0},{3,1},{4,2},{5,3},{6,4},{7,5},{8,14},{9,15},{10,... | collective-permute-start | bytes 884744 | tf_op jit(solution)/shard_map/ppermute | solution.py:417
  12.0 20.1 %collective-permute-done.20.refs_7_ = f32[8,256]{1,0:T(8,128)S(1)} collective-permute-done((f32[8,256]{1,0:T(8,128)S(1)}, f32[8,256]{1,0:T(8,128)S(1)}, u32[]{:S(2)}, u32[]{:S(2)}) %collective-permute-start.20) | collective-permute-done | bytes 8224 | tf_op jit(solution)/shard_map/ppermute | solution.py:417
  32.0 1.7 %collective-permute-start.21 = (f32[8,256]{1,0:T(8,128)S(1)}, f32[8,256]{1,0:T(8,128)S(1)}, u32[]{:S(2)}, u32[]{:S(2)}) collective-permute-start(f32[8,256]{1,0:T(8,128)S(1)} %pad_maximum_fusion.refs_6_), channel_id=1, source_target_pairs={{0,6},{1,7},{2,0},{3,1},{4,2},{5,3},{6,4},{7,5},{8,14},{9,15},{10,... | collective-permute-start | bytes 24584 | tf_op jit(solution)/shard_map/ppermute | solution.py:417
  33.7 2.0 %collective-permute-done.21.refs_8_ = f32[8,256]{1,0:T(8,128)S(1)} collective-permute-done((f32[8,256]{1,0:T(8,128)S(1)}, f32[8,256]{1,0:T(8,128)S(1)}, u32[]{:S(2)}, u32[]{:S(2)}) %collective-permute-start.21) | collective-permute-done | bytes 8224 | tf_op jit(solution)/shard_map/ppermute | solution.py:417
  37.2 3.5 %collective-permute-start.11 = (bf16[128,1536]{1,0:T(8,128)(2,1)S(1)}, bf16[128,1536]{1,0:T(8,128)(2,1)S(1)}, u32[]{:S(2)}, u32[]{:S(2)}) collective-permute-start(bf16[128,1536]{1,0:T(8,128)(2,1)S(1)} %copy-done.2), channel_id=1, source_target_pairs={{0,6},{1,7},{2,0},{3,1},{4,2},{5,3},{6,4},{7,5},{8,14},{9,15},{10,... | collective-permute-start | bytes 1179656 | tf_op jit(solution)/shard_map/ppermute | solution.py:417
  40.7 1.6 %collective-permute-start.15 = (bf16[384,768]{1,0:T(8,128)(2,1)S(1)}, bf16[384,768]{1,0:T(8,128)(2,1)S(1)}, u32[]{:S(2)}, u32[]{:S(2)}) collective-permute-start(bf16[384,768]{1,0:T(8,128)(2,1)S(1)} %bitcast.8), channel_id=1, source_target_pairs={{0,16},{8,24},{16,0},{24,8},{1,17},{9,25},{17,1},{25,9},{2,18},{10... | collective-permute-start | bytes 1769480 | tf_op jit(solution)/shard_map/ppermute | solution.py:420
  42.4 4.3 %collective-permute-done.11.refs_4_ = bf16[128,1536]{1,0:T(8,128)(2,1)S(1)} collective-permute-done((bf16[128,1536]{1,0:T(8,128)(2,1)S(1)}, bf16[128,1536]{1,0:T(8,128)(2,1)S(1)}, u32[]{:S(2)}, u32[]{:S(2)}) %collective-permute-start.11) | collective-permute-done | bytes 393248 | tf_op jit(solution)/shard_map/ppermute | solution.py:417
  46.8 1.5 %collective-permute-start.26 = (bf16[768,384]{1,0:T(8,128)(2,1)}, bf16[768,384]{1,0:T(8,128)(2,1)S(1)}, u32[]{:S(2)}, u32[]{:S(2)}) collective-permute-start(bf16[768,384]{1,0:T(8,128)(2,1)} %bitcast.1.down), channel_id=1, source_target_pairs={{0,16},{8,24},{16,0},{24,8},{1,17},{9,25},{17,1},{25,9},{2,18},{10... | collective-permute-start | bytes 1769480 | tf_op jit(solution)/shard_map/ppermute | solution.py:420
  51.7 5.2 %collective-permute-done.15.refs_4_.refs_11_ = bf16[384,768]{1,0:T(8,128)(2,1)S(1)} collective-permute-done((bf16[384,768]{1,0:T(8,128)(2,1)S(1)}, bf16[384,768]{1,0:T(8,128)(2,1)S(1)}, u32[]{:S(2)}, u32[]{:S(2)}) %collective-permute-start.15) | collective-permute-done | bytes 589856 | tf_op jit(solution)/shard_map/ppermute | solution.py:420
  58.3 1.6 %collective-permute-start.16 = (bf16[384,768]{1,0:T(8,128)(2,1)S(1)}, bf16[384,768]{1,0:T(8,128)(2,1)S(1)}, u32[]{:S(2)}, u32[]{:S(2)}) collective-permute-start(bf16[384,768]{1,0:T(8,128)(2,1)S(1)} %collective-permute-done.14.refs_3_.refs_7_), channel_id=1, source_target_pairs={{0,16},{8,24},{16,0},{24,8},{1,17},{9,25},{17,1},{25,9},{2,18},{10... | collective-permute-start | bytes 1769480 | tf_op jit(solution)/shard_map/ppermute | solution.py:420
  59.8 1.6 %collective-permute-done.7.lower = bf16[128,1152]{1,0:T(8,128)(2,1)S(1)} collective-permute-done((bf16[128,1152]{1,0:T(8,128)(2,1)S(1)}, bf16[128,1152]{1,0:T(8,128)(2,1)S(1)}, u32[]{:S(2)}, u32[]{:S(2)}) %collective-permute-start.7) | collective-permute-done | bytes 294944 | tf_op jit(solution)/shard_map/ppermute | solution.py:417
  61.4 8.2 %collective-permute-done.26.refs_2_.refs_9_ = bf16[768,384]{1,0:T(8,128)(2,1)S(1)} collective-permute-done((bf16[768,384]{1,0:T(8,128)(2,1)}, bf16[768,384]{1,0:T(8,128)(2,1)S(1)}, u32[]{:S(2)}, u32[]{:S(2)}) %collective-permute-start.26) | collective-permute-done | bytes 589856 | tf_op jit(solution)/shard_map/ppermute | solution.py:420
  70.1 1.5 %collective-permute-start.27 = (bf16[768,384]{1,0:T(8,128)(2,1)S(1)}, bf16[768,384]{1,0:T(8,128)(2,1)S(1)}, u32[]{:S(2)}, u32[]{:S(2)}) collective-permute-start(bf16[768,384]{1,0:T(8,128)(2,1)S(1)} %collective-permute-done.26.refs_2_.refs_9_), channel_id=1, source_target_pairs={{0,8},{8,0},{16,24},{24,16},{1,9},{9,1},{17,25},{25,17},{2,10},{10... | collective-permute-start | bytes 1769480 | tf_op jit(solution)/shard_map/ppermute | solution.py:420
  72.4 1.6 %shard_map.81 = (bf16[768,768]{1,0:T(8,128)(2,1)S(1)}, bf16[1536,768]{1,0:T(8,128)(2,1)S(1)}, f32[768,768]{1,0:T(8,128)S(1)}) custom-call(bf16[128,1536]{1,0:T(8,128)(2,1)S(1)} %get-tuple-element.43.refs_0_, bf16[128,1536]{1,0:T(8,128)(2,1)S(1)} %collective-permute-done.22.refs_1_, bf16[128,1536]{1,0:T(8,128)(2,1)S(1)} %collective-permute-done.9.refs_2_, ...), custom_call_target="tpu_custom_call" | custom-call | flops 905969664 | bytes 9437184 | tf_op jit(solution)/shard_map/pallas_call | solution.py:268
  74.0 7.7 %collective-permute-done.16.refs_5_.refs_12_ = bf16[384,768]{1,0:T(8,128)(2,1)S(1)} collective-permute-done((bf16[384,768]{1,0:T(8,128)(2,1)S(1)}, bf16[384,768]{1,0:T(8,128)(2,1)S(1)}, u32[]{:S(2)}, u32[]{:S(2)}) %collective-permute-start.16) | collective-permute-done | bytes 589856 | tf_op jit(solution)/shard_map/ppermute | solution.py:420
  81.7 3.5 %shard_map.82 = (bf16[768,1152]{1,0:T(8,128)(2,1)S(1)}, bf16[768,768]{1,0:T(8,128)(2,1)S(1)}, f32[768,768]{1,0:T(8,128)S(1)}, f32[768,384]{1,0:T(8,128)S(1)}, f3...) custom-call(bf16[128,1152]{1,0:T(8,128)(2,1)S(1)} %get-tuple-element.40.refs_0_, ...), custom_call_target="tpu_custom_call" | custom-call | flops 2264924160 | bytes 15360000 | tf_op jit(solution)/shard_map/pallas_call | solution.py:268
  86.3 3.8 %collective-permute-start.31 = (bf16[128,384]{1,0:T(8,128)(2,1)S(1)}, bf16[128,384]{1,0:T(8,128)(2,1)S(1)}, u32[]{:S(2)}, u32[]{:S(2)}) collective-permute-start(bf16[128,384]{1,0:T(8,128)(2,1)S(1)} %get-tuple-element.39.refs_0_), channel_id=1, source_target_pairs={{0,6},{1,7},{2,0},{3,1},{4,2},{5,3},{6,4},{7,5},{8,14},{9,15},{10,... | collective-permute-start | bytes 294920 | tf_op jit(solution)/shard_map/ppermute | solution.py:417
  94.0 3.6 %collective-permute-done.refs_0_ = bf16[128,384]{1,0:T(8,128)(2,1)S(1)} collective-permute-done((bf16[128,384]{1,0:T(8,128)(2,1)S(1)}, bf16[128,384]{1,0:T(8,128)(2,1)S(1)}, u32[]{:S(2)}, u32[]{:S(2)}) %collective-permute-start) | collective-permute-done | bytes 98336 | tf_op jit(solution)/shard_map/ppermute | solution.py:417
  98.2 1.5 %collective-permute-start.43 = (bf16[384,384]{1,0:T(8,128)(2,1)S(1)}, bf16[384,384]{1,0:T(8,128)(2,1)S(1)}, u32[]{:S(2)}, u32[]{:S(2)}) collective-permute-start(bf16[384,384]{1,0:T(8,128)(2,1)S(1)} %get-tuple-element.75), channel_id=1, source_target_pairs={{0,16},{8,24},{16,0},{24,8},{1,17},{9,25},{17,1},{25,9},{2,18},{10... | collective-permute-start | bytes 884744 | tf_op jit(solution)/shard_map/ppermute | solution.py:420
  99.7 2.0 %shard_map.84.refs_9_ = f32[768,768]{1,0:T(8,128)S(1)} custom-call(bf16[768,1152]{1,0:T(8,128)(2,1)S(1)} %get-tuple-element.51.g, bf16[768,384]{1,0:T(8,128)(2,1)S(1)} %collective-permute-done.27.refs_0_.refs_10_, bf16[768,384]{1,0:T(8,128)(2,1)S(1)} %collective-permute-done.25.refs_1_.refs_8_, bf16[768,384]{1,0:T(8,128)(2,1)S(1)} %collective-permute-done.26.refs_2_.refs_9_), custom_call_target="tpu_custom_call" | custom-call | flops 1358954496 | bytes 5898240 | tf_op jit(solution)/shard_map/pallas_call | solution.py:268
  104.3 3.4 %shard_map.85 = (f32[384,768]{1,0:T(8,128)S(1)}, f32[384,768]{1,0:T(8,128)S(1)}, f32[384,768]{1,0:T(8,128)S(1)}, f32[384,768]{1,0:T(8,128)S(1)}, f32[768,384]{1,0:T(8,128)S(1)}) custom-call(bf16[128,384]{1,0:T(8,128)(2,1)S(1)} %get-tuple-element.39.refs_0_, bf16[128,384]{1,0:T(8,128)(2,1)S(1)} %collective-permute-done.28.refs_1_, ...), custom_call_target="tpu_custom_call" | custom-call | flops 2717908992 | bytes 15360000 | tf_op jit(solution)/shard_map/pallas_call | solution.py:268
  107.8 2.4 %shard_map.86 = (bf16[192,768]{1,0:T(8,128)(2,1)S(1)}, bf16[192,768]{1,0:T(8,128)(2,1)S(1)}, bf16[192,768]{1,0:T(8,128)(2,1)S(1)}, bf16[192,768]{1,0:T(8,128)(2,...) custom-call(bf16[128,384]{1,0:T(8,128)(2,1)S(1)} %collective-permute-, ...), custom_call_target="tpu_custom_call" | custom-call | flops 1358954496 | bytes 15736832 | tf_op jit(solution)/shard_map/pallas_call | solution.py:268
  110.2 1.6 %collective-permute-start.37 = (bf16[192,768]{1,0:T(8,128)(2,1)S(1)}, bf16[192,768]{1,0:T(8,128)(2,1)S(1)}, u32[]{:S(2)}, u32[]{:S(2)}) collective-permute-start(bf16[192,768]{1,0:T(8,128)(2,1)S(1)} %get-tuple-element.66), channel_id=1, source_target_pairs={{0,16},{8,24},{16,0},{24,8},{1,17},{9,25},{17,1},{25,9},{2,18},{10... | collective-permute-start | bytes 884744 | tf_op jit(solution)/shard_map/ppermute | solution.py:420
  112.4 1.6 %collective-permute-start.33 = (bf16[192,768]{1,0:T(8,128)(2,1)S(1)}, bf16[192,768]{1,0:T(8,128)(2,1)S(1)}, u32[]{:S(2)}, u32[]{:S(2)}) collective-permute-start(bf16[192,768]{1,0:T(8,128)(2,1)S(1)} %get-tuple-element.61), channel_id=1, source_target_pairs={{0,8},{8,0},{16,24},{24,16},{1,9},{9,1},{17,25},{25,17},{2,10},{10... | collective-permute-start | bytes 884744 | tf_op jit(solution)/shard_map/ppermute | solution.py:420
  114.0 5.8 %collective-permute-done.37 = bf16[192,768]{1,0:T(8,128)(2,1)S(1)} collective-permute-done((bf16[192,768]{1,0:T(8,128)(2,1)S(1)}, bf16[192,768]{1,0:T(8,128)(2,1)S(1)}, u32[]{:S(2)}, u32[]{:S(2)}) %collective-permute-start.37) | collective-permute-done | bytes 294944 | tf_op jit(solution)/shard_map/ppermute | solution.py:420
  119.8 1.5 %collective-permute-start.34 = (bf16[192,768]{1,0:T(8,128)(2,1)S(1)}, bf16[192,768]{1,0:T(8,128)(2,1)S(1)}, u32[]{:S(2)}, u32[]{:S(2)}) collective-permute-start(bf16[192,768]{1,0:T(8,128)(2,1)S(1)} %get-tuple-element.62), channel_id=1, source_target_pairs={{0,16},{8,24},{16,0},{24,8},{1,17},{9,25},{17,1},{25,9},{2,18},{10... | collective-permute-start | bytes 884744 | tf_op jit(solution)/shard_map/ppermute | solution.py:420
  121.4 2.9 %collective-permute-done.35 = bf16[192,768]{1,0:T(8,128)(2,1)S(1)} collective-permute-done((bf16[192,768]{1,0:T(8,128)(2,1)S(1)}, bf16[192,768]{1,0:T(8,128)(2,1)S(1)}, u32[]{:S(2)}, u32[]{:S(2)}) %collective-permute-start.35) | collective-permute-done | bytes 294944 | tf_op jit(solution)/shard_map/ppermute | solution.py:420
  125.5 1.5 %collective-permute-start.38 = (bf16[192,768]{1,0:T(8,128)(2,1)S(1)}, bf16[192,768]{1,0:T(8,128)(2,1)S(1)}, u32[]{:S(2)}, u32[]{:S(2)}) collective-permute-start(bf16[192,768]{1,0:T(8,128)(2,1)S(1)} %add_convert_fusion.2), channel_id=1, source_target_pairs={{0,8},{8,0},{16,24},{24,16},{1,9},{9,1},{17,25},{25,17},{2,10},{10... | collective-permute-start | bytes 884744 | tf_op jit(solution)/shard_map/ppermute | solution.py:420
  127.0 3.6 %collective-permute-done.33.near_a = bf16[192,768]{1,0:T(8,128)(2,1)S(1)} collective-permute-done((bf16[192,768]{1,0:T(8,128)(2,1)S(1)}, bf16[192,768]{1,0:T(8,128)(2,1)S(1)}, u32[]{:S(2)}, u32[]{:S(2)}) %collective-permute-start.33) | collective-permute-done | bytes 294944 | tf_op jit(solution)/shard_map/ppermute | solution.py:420
  131.4 5.5 %collective-permute-done.44.far_b = bf16[384,384]{1,0:T(8,128)(2,1)S(1)} collective-permute-done((bf16[384,384]{1,0:T(8,128)(2,1)S(1)}, bf16[384,384]{1,0:T(8,128)(2,1)S(1)}, u32[]{:S(2)}, u32[]{:S(2)}) %collective-permute-start.44) | collective-permute-done | bytes 294944 | tf_op jit(solution)/shard_map/ppermute | solution.py:420
  137.8 4.2 %collective-permute-done.38.far_b = bf16[192,768]{1,0:T(8,128)(2,1)S(1)} collective-permute-done((bf16[192,768]{1,0:T(8,128)(2,1)S(1)}, bf16[192,768]{1,0:T(8,128)(2,1)S(1)}, u32[]{:S(2)}, u32[]{:S(2)}) %collective-permute-start.38) | collective-permute-done | bytes 294944 | tf_op jit(solution)/shard_map/ppermute | solution.py:420
  (90 shorter events, 26.3 us)
Async XLA Ops:
  4.9 32.3 %collective-permute-start.4 = (bf16[128,1152]{1,0:T(8,128)(2,1)S(1)}, bf16[128,1152]{1,0:T(8,128)(2,1)S(1)}, u32[]{:S(2)}, u32[]{:S(2)}) collective-permute-start(bf16[128,1152]{1,0:T(8,128)(2,1)S(1)} %get-tuple-element.40.refs_0_), channel_id=1, source_target_pairs={{0,2},{1,3},{2,4},{3,5},{4,6},{5,7},{6,0},{7,1},{8,10},{9,11},{10,... | collective-permute-start | bytes 884744 | tf_op jit(solution)/shard_map/ppermute | solution.py:417
  8.0 32.6 %collective-permute-start.6 = (bf16[128,1152]{1,0:T(8,128)(2,1)S(1)}, bf16[128,1152]{1,0:T(8,128)(2,1)S(1)}, u32[]{:S(2)}, u32[]{:S(2)}) collective-permute-start(bf16[128,1152]{1,0:T(8,128)(2,1)S(1)} %get-tuple-element.40.refs_0_), channel_id=1, source_target_pairs={{0,6},{1,7},{2,0},{3,1},{4,2},{5,3},{6,4},{7,5},{8,14},{9,15},{10,... | collective-permute-start | bytes 884744 | tf_op jit(solution)/shard_map/ppermute | solution.py:417
  10.2 32.0 %collective-permute-start.9 = (bf16[128,1536]{1,0:T(8,128)(2,1)S(1)}, bf16[128,1536]{1,0:T(8,128)(2,1)S(1)}, u32[]{:S(2)}, u32[]{:S(2)}) collective-permute-start(bf16[128,1536]{1,0:T(8,128)(2,1)S(1)} %copy-done.2), channel_id=1, source_target_pairs={{0,2},{1,3},{2,4},{3,5},{4,6},{5,7},{6,0},{7,1},{8,10},{9,11},{10,... | collective-permute-start | bytes 1179656 | tf_op jit(solution)/shard_map/ppermute | solution.py:417
  10.3 30.4 %collective-permute-start.17 = (bf16[128,1152]{1,0:T(8,128)(2,1)S(1)}, bf16[128,1152]{1,0:T(8,128)(2,1)S(1)}, u32[]{:S(2)}, u32[]{:S(2)}) collective-permute-start(bf16[128,1152]{1,0:T(8,128)(2,1)S(1)} %get-tuple-element.40.refs_0_), channel_id=1, source_target_pairs={{0,1},{1,0},{2,3},{3,2},{4,5},{5,4},{6,7},{7,6},{8,9},{9,8},{10,11... | collective-permute-start | bytes 884744 | tf_op jit(solution)/shard_map/ppermute | solution.py:417
  11.4 20.6 %collective-permute-start.20 = (f32[8,256]{1,0:T(8,128)S(1)}, f32[8,256]{1,0:T(8,128)S(1)}, u32[]{:S(2)}, u32[]{:S(2)}) collective-permute-start(f32[8,256]{1,0:T(8,128)S(1)} %pad_maximum_fusion.refs_6_), channel_id=1, source_target_pairs={{0,2},{1,3},{2,4},{3,5},{4,6},{5,7},{6,0},{7,1},{8,10},{9,11},{10,... | collective-permute-start | bytes 24584 | tf_op jit(solution)/shard_map/ppermute | solution.py:417
  35.7 13.3 %collective-permute-start.14 = (bf16[384,768]{1,0:T(8,128)(2,1)S(1)}, bf16[384,768]{1,0:T(8,128)(2,1)S(1)}, u32[]{:S(2)}, u32[]{:S(2)}) collective-permute-start(bf16[384,768]{1,0:T(8,128)(2,1)S(1)} %bitcast.7), channel_id=1, source_target_pairs={{0,8},{8,0},{16,24},{24,16},{1,9},{9,1},{17,25},{25,17},{2,10},{10... | collective-permute-start | bytes 1769480 | tf_op jit(solution)/shard_map/ppermute | solution.py:420
  37.2 9.6 %collective-permute-start.11 = (bf16[128,1536]{1,0:T(8,128)(2,1)S(1)}, bf16[128,1536]{1,0:T(8,128)(2,1)S(1)}, u32[]{:S(2)}, u32[]{:S(2)}) collective-permute-start(bf16[128,1536]{1,0:T(8,128)(2,1)S(1)} %copy-done.2), channel_id=1, source_target_pairs={{0,6},{1,7},{2,0},{3,1},{4,2},{5,3},{6,4},{7,5},{8,14},{9,15},{10,... | collective-permute-start | bytes 1179656 | tf_op jit(solution)/shard_map/ppermute | solution.py:417
  40.7 16.3 %collective-permute-start.15 = (bf16[384,768]{1,0:T(8,128)(2,1)S(1)}, bf16[384,768]{1,0:T(8,128)(2,1)S(1)}, u32[]{:S(2)}, u32[]{:S(2)}) collective-permute-start(bf16[384,768]{1,0:T(8,128)(2,1)S(1)} %bitcast.8), channel_id=1, source_target_pairs={{0,16},{8,24},{16,0},{24,8},{1,17},{9,25},{17,1},{25,9},{2,18},{10... | collective-permute-start | bytes 1769480 | tf_op jit(solution)/shard_map/ppermute | solution.py:420
  46.8 22.8 %collective-permute-start.26 = (bf16[768,384]{1,0:T(8,128)(2,1)}, bf16[768,384]{1,0:T(8,128)(2,1)S(1)}, u32[]{:S(2)}, u32[]{:S(2)}) collective-permute-start(bf16[768,384]{1,0:T(8,128)(2,1)} %bitcast.1.down), channel_id=1, source_target_pairs={{0,16},{8,24},{16,0},{24,8},{1,17},{9,25},{17,1},{25,9},{2,18},{10... | collective-permute-start | bytes 1769480 | tf_op jit(solution)/shard_map/ppermute | solution.py:420
  49.0 9.2 %collective-permute-start.5 = (bf16[128,1152]{1,0:T(8,128)(2,1)S(1)}, bf16[128,1152]{1,0:T(8,128)(2,1)S(1)}, u32[]{:S(2)}, u32[]{:S(2)}) collective-permute-start(bf16[128,1152]{1,0:T(8,128)(2,1)S(1)} %collective-permute-done.4.refs_2_), channel_id=1, source_target_pairs={{2,4},{3,5},{4,6},{5,7},{10,12},{11,13},{12,14},{13,15},{18,20},{1... | collective-permute-start | bytes 884744 | tf_op jit(solution)/shard_map/ppermute | solution.py:417
  49.7 11.7 %collective-permute-start.7 = (bf16[128,1152]{1,0:T(8,128)(2,1)S(1)}, bf16[128,1152]{1,0:T(8,128)(2,1)S(1)}, u32[]{:S(2)}, u32[]{:S(2)}) collective-permute-start(bf16[128,1152]{1,0:T(8,128)(2,1)S(1)} %collective-permute-done.6.refs_4_), channel_id=1, source_target_pairs={{2,0},{3,1},{4,2},{5,3},{10,8},{11,9},{12,10},{13,11},{18,16},{19,... | collective-permute-start | bytes 884744 | tf_op jit(solution)/shard_map/ppermute | solution.py:417
  51.0 18.6 %collective-permute-start.10 = (bf16[128,1536]{1,0:T(8,128)(2,1)S(1)}, bf16[128,1536]{1,0:T(8,128)(2,1)S(1)}, u32[]{:S(2)}, u32[]{:S(2)}) collective-permute-start(bf16[128,1536]{1,0:T(8,128)(2,1)S(1)} %collective-permute-done.9.refs_2_), channel_id=1, source_target_pairs={{2,4},{3,5},{4,6},{5,7},{10,12},{11,13},{12,14},{13,15},{18,20},{1... | collective-permute-start | bytes 1179656 | tf_op jit(solution)/shard_map/ppermute | solution.py:417
  57.0 13.2 %collective-permute-start.12 = (bf16[128,1536]{1,0:T(8,128)(2,1)S(1)}, bf16[128,1536]{1,0:T(8,128)(2,1)S(1)}, u32[]{:S(2)}, u32[]{:S(2)}) collective-permute-start(bf16[128,1536]{1,0:T(8,128)(2,1)S(1)} %collective-permute-done.11.refs_4_), channel_id=1, source_target_pairs={{2,0},{3,1},{4,2},{5,3},{10,8},{11,9},{12,10},{13,11},{18,16},{19,... | collective-permute-start | bytes 1179656 | tf_op jit(solution)/shard_map/ppermute | solution.py:417
  58.3 23.5 %collective-permute-start.16 = (bf16[384,768]{1,0:T(8,128)(2,1)S(1)}, bf16[384,768]{1,0:T(8,128)(2,1)S(1)}, u32[]{:S(2)}, u32[]{:S(2)}) collective-permute-start(bf16[384,768]{1,0:T(8,128)(2,1)S(1)} %collective-permute-done.14.refs_3_.refs_7_), channel_id=1, source_target_pairs={{0,16},{8,24},{16,0},{24,8},{1,17},{9,25},{17,1},{25,9},{2,18},{10... | collective-permute-start | bytes 1769480 | tf_op jit(solution)/shard_map/ppermute | solution.py:420
  61.4 10.3 %collective-permute-start.23 = (bf16[128,1536]{1,0:T(8,128)(2,1)S(1)}, bf16[128,1536]{1,0:T(8,128)(2,1)S(1)}, u32[]{:S(2)}, u32[]{:S(2)}) collective-permute-start(bf16[128,1536]{1,0:T(8,128)(2,1)S(1)} %collective-permute-done.9.refs_2_), channel_id=1, source_target_pairs={{0,1},{1,0},{2,3},{3,2},{4,5},{5,4},{6,7},{7,6},{8,9},{9,8},{10,11... | collective-permute-start | bytes 1179656 | tf_op jit(solution)/shard_map/ppermute | solution.py:417
  69.6 28.0 %collective-permute-start.25 = (bf16[768,384]{1,0:T(8,128)(2,1)}, bf16[768,384]{1,0:T(8,128)(2,1)S(1)}, u32[]{:S(2)}, u32[]{:S(2)}) collective-permute-start(bf16[768,384]{1,0:T(8,128)(2,1)} %bitcast.1.down), channel_id=1, source_target_pairs={{0,8},{8,0},{16,24},{24,16},{1,9},{9,1},{17,25},{25,17},{2,10},{10... | collective-permute-start | bytes 1769480 | tf_op jit(solution)/shard_map/ppermute | solution.py:420
  70.1 28.1 %collective-permute-start.27 = (bf16[768,384]{1,0:T(8,128)(2,1)S(1)}, bf16[768,384]{1,0:T(8,128)(2,1)S(1)}, u32[]{:S(2)}, u32[]{:S(2)}) collective-permute-start(bf16[768,384]{1,0:T(8,128)(2,1)S(1)} %collective-permute-done.26.refs_2_.refs_9_), channel_id=1, source_target_pairs={{0,8},{8,0},{16,24},{24,16},{1,9},{9,1},{17,25},{25,17},{2,10},{10... | collective-permute-start | bytes 1769480 | tf_op jit(solution)/shard_map/ppermute | solution.py:420
  71.7 18.4 %collective-permute-start.13 = (bf16[128,1536]{1,0:T(8,128)(2,1)S(1)}, bf16[128,1536]{1,0:T(8,128)(2,1)S(1)}, u32[]{:S(2)}, u32[]{:S(2)}) collective-permute-start(bf16[128,1536]{1,0:T(8,128)(2,1)S(1)} %shard_map.79.refs_0_), channel_id=1, source_target_pairs={{0,1},{1,0},{2,3},{3,2},{4,5},{5,4},{6,7},{7,6},{8,9},{9,8},{10,11... | collective-permute-start | bytes 1179656 | tf_op jit(solution)/shard_map/ppermute | solution.py:417
  71.8 14.4 %collective-permute-start.8 = (bf16[128,1152]{1,0:T(8,128)(2,1)S(1)}, bf16[128,1152]{1,0:T(8,128)(2,1)S(1)}, u32[]{:S(2)}, u32[]{:S(2)}) collective-permute-start(bf16[128,1152]{1,0:T(8,128)(2,1)S(1)} %shard_map.78.refs_0_), channel_id=1, source_target_pairs={{0,1},{1,0},{2,3},{3,2},{4,5},{5,4},{6,7},{7,6},{8,9},{9,8},{10,11... | collective-permute-start | bytes 884744 | tf_op jit(solution)/shard_map/ppermute | solution.py:417
  97.6 10.1 %collective-permute-start.1 = (bf16[128,384]{1,0:T(8,128)(2,1)S(1)}, bf16[128,384]{1,0:T(8,128)(2,1)S(1)}, u32[]{:S(2)}, u32[]{:S(2)}) collective-permute-start(bf16[128,384]{1,0:T(8,128)(2,1)S(1)} %collective-permute-done.refs_0_), channel_id=1, source_target_pairs={{0,1},{1,0},{2,3},{3,2},{4,5},{5,4},{6,7},{7,6},{8,9},{9,8},{10,11... | collective-permute-start | bytes 294920 | tf_op jit(solution)/shard_map/ppermute | solution.py:417
  98.2 13.6 %collective-permute-start.43 = (bf16[384,384]{1,0:T(8,128)(2,1)S(1)}, bf16[384,384]{1,0:T(8,128)(2,1)S(1)}, u32[]{:S(2)}, u32[]{:S(2)}) collective-permute-start(bf16[384,384]{1,0:T(8,128)(2,1)S(1)} %get-tuple-element.75), channel_id=1, source_target_pairs={{0,16},{8,24},{16,0},{24,8},{1,17},{9,25},{17,1},{25,9},{2,18},{10... | collective-permute-start | bytes 884744 | tf_op jit(solution)/shard_map/ppermute | solution.py:420
  101.7 10.6 %collective-permute-start.41 = (bf16[384,384]{1,0:T(8,128)(2,1)S(1)}, bf16[384,384]{1,0:T(8,128)(2,1)S(1)}, u32[]{:S(2)}, u32[]{:S(2)}) collective-permute-start(bf16[384,384]{1,0:T(8,128)(2,1)S(1)} %get-tuple-element.73), channel_id=1, source_target_pairs={{0,8},{8,0},{16,24},{24,16},{1,9},{9,1},{17,25},{25,17},{2,10},{10... | collective-permute-start | bytes 884744 | tf_op jit(solution)/shard_map/ppermute | solution.py:420
  102.3 22.6 %collective-permute-start.39 = (bf16[384,384]{1,0:T(8,128)(2,1)S(1)}, bf16[384,384]{1,0:T(8,128)(2,1)S(1)}, u32[]{:S(2)}, u32[]{:S(2)}) collective-permute-start(bf16[384,384]{1,0:T(8,128)(2,1)S(1)} %get-tuple-element.70), channel_id=1, source_target_pairs={{0,8},{8,0},{16,24},{24,16},{1,9},{9,1},{17,25},{25,17},{2,10},{10... | collective-permute-start | bytes 884744 | tf_op jit(solution)/shard_map/ppermute | solution.py:420
  103.8 21.7 %collective-permute-start.40 = (bf16[384,384]{1,0:T(8,128)(2,1)S(1)}, bf16[384,384]{1,0:T(8,128)(2,1)S(1)}, u32[]{:S(2)}, u32[]{:S(2)}) collective-permute-start(bf16[384,384]{1,0:T(8,128)(2,1)S(1)} %get-tuple-element.71), channel_id=1, source_target_pairs={{0,16},{8,24},{16,0},{24,8},{1,17},{9,25},{17,1},{25,9},{2,18},{10... | collective-permute-start | bytes 884744 | tf_op jit(solution)/shard_map/ppermute | solution.py:420
  110.2 9.6 %collective-permute-start.37 = (bf16[192,768]{1,0:T(8,128)(2,1)S(1)}, bf16[192,768]{1,0:T(8,128)(2,1)S(1)}, u32[]{:S(2)}, u32[]{:S(2)}) collective-permute-start(bf16[192,768]{1,0:T(8,128)(2,1)S(1)} %get-tuple-element.66), channel_id=1, source_target_pairs={{0,16},{8,24},{16,0},{24,8},{1,17},{9,25},{17,1},{25,9},{2,18},{10... | collective-permute-start | bytes 884744 | tf_op jit(solution)/shard_map/ppermute | solution.py:420
  111.8 12.6 %collective-permute-start.35 = (bf16[192,768]{1,0:T(8,128)(2,1)S(1)}, bf16[192,768]{1,0:T(8,128)(2,1)S(1)}, u32[]{:S(2)}, u32[]{:S(2)}) collective-permute-start(bf16[192,768]{1,0:T(8,128)(2,1)S(1)} %get-tuple-element.64), channel_id=1, source_target_pairs={{0,8},{8,0},{16,24},{24,16},{1,9},{9,1},{17,25},{25,17},{2,10},{10... | collective-permute-start | bytes 884744 | tf_op jit(solution)/shard_map/ppermute | solution.py:420
  112.4 18.3 %collective-permute-start.33 = (bf16[192,768]{1,0:T(8,128)(2,1)S(1)}, bf16[192,768]{1,0:T(8,128)(2,1)S(1)}, u32[]{:S(2)}, u32[]{:S(2)}) collective-permute-start(bf16[192,768]{1,0:T(8,128)(2,1)S(1)} %get-tuple-element.61), channel_id=1, source_target_pairs={{0,8},{8,0},{16,24},{24,16},{1,9},{9,1},{17,25},{25,17},{2,10},{10... | collective-permute-start | bytes 884744 | tf_op jit(solution)/shard_map/ppermute | solution.py:420
  119.8 11.5 %collective-permute-start.34 = (bf16[192,768]{1,0:T(8,128)(2,1)S(1)}, bf16[192,768]{1,0:T(8,128)(2,1)S(1)}, u32[]{:S(2)}, u32[]{:S(2)}) collective-permute-start(bf16[192,768]{1,0:T(8,128)(2,1)S(1)} %get-tuple-element.62), channel_id=1, source_target_pairs={{0,16},{8,24},{16,0},{24,8},{1,17},{9,25},{17,1},{25,9},{2,18},{10... | collective-permute-start | bytes 884744 | tf_op jit(solution)/shard_map/ppermute | solution.py:420
  124.3 12.6 %collective-permute-start.44 = (bf16[384,384]{1,0:T(8,128)(2,1)S(1)}, bf16[384,384]{1,0:T(8,128)(2,1)S(1)}, u32[]{:S(2)}, u32[]{:S(2)}) collective-permute-start(bf16[384,384]{1,0:T(8,128)(2,1)S(1)} %add_convert_fusion), channel_id=1, source_target_pairs={{0,8},{8,0},{16,24},{24,16},{1,9},{9,1},{17,25},{25,17},{2,10},{10... | collective-permute-start | bytes 884744 | tf_op jit(solution)/shard_map/ppermute | solution.py:420
  124.9 12.0 %collective-permute-start.42 = (bf16[384,384]{1,0:T(8,128)(2,1)S(1)}, bf16[384,384]{1,0:T(8,128)(2,1)S(1)}, u32[]{:S(2)}, u32[]{:S(2)}) collective-permute-start(bf16[384,384]{1,0:T(8,128)(2,1)S(1)} %add_convert_fusion.1), channel_id=1, source_target_pairs={{0,16},{8,24},{16,0},{24,8},{1,17},{9,25},{17,1},{25,9},{2,18},{10... | collective-permute-start | bytes 884744 | tf_op jit(solution)/shard_map/ppermute | solution.py:420
  125.5 16.6 %collective-permute-start.38 = (bf16[192,768]{1,0:T(8,128)(2,1)S(1)}, bf16[192,768]{1,0:T(8,128)(2,1)S(1)}, u32[]{:S(2)}, u32[]{:S(2)}) collective-permute-start(bf16[192,768]{1,0:T(8,128)(2,1)S(1)} %add_convert_fusion.2), channel_id=1, source_target_pairs={{0,8},{8,0},{16,24},{24,16},{1,9},{9,1},{17,25},{25,17},{2,10},{10... | collective-permute-start | bytes 884744 | tf_op jit(solution)/shard_map/ppermute | solution.py:420
  130.6 11.4 %collective-permute-start.36 = (bf16[192,768]{1,0:T(8,128)(2,1)S(1)}, bf16[192,768]{1,0:T(8,128)(2,1)S(1)}, u32[]{:S(2)}, u32[]{:S(2)}) collective-permute-start(bf16[192,768]{1,0:T(8,128)(2,1)S(1)} %add_convert_fusion.3), channel_id=1, source_target_pairs={{0,16},{8,24},{16,0},{24,8},{1,17},{9,25},{17,1},{25,9},{2,18},{10... | collective-permute-start | bytes 884744 | tf_op jit(solution)/shard_map/ppermute | solution.py:420
  (18 other events, 93.7 us)

commit v8 on v7

--- a/solution.py
+++ b/solution.py
@@ -89,6 +89,10 @@
     return lax.dot_general(left, right, LAST, preferred_element_type=F32)
 
 
+def first_part(rows):
+    return rows // 2 + rows // 24 // 32 * 32
+
+
 def owner_columns(block, bits):
     return pl.ds(pl.multiple_of((lax.axis_index("dp") ^ bits) * block, block), block)
 
@@ -167,7 +171,7 @@
     expert = lax.axis_index("expert")
     for half in range(2):
         g[half * SHARD : (half + 1) * SHARD, :] = scale_rows(pick_gate(table, half, expert), shards[half][...])
-    middle = act_turned.shape[0] // 2
+    middle = first_part(act_turned.shape[0])
     total = dot_rows(act_turned[...], g[:, :block]) + far_sum[...]
     far_a[...] = total[:middle].astype(BF16)
     far_b[...] = total[middle:].astype(BF16)
@@ -176,7 +180,7 @@
 def last_near_kernel(block, *refs):
     g, act_turned, sum_x, sum_y = refs[:4]
     near_a, near_b, side_a, side_b = refs[4:]
-    middle = act_turned.shape[0] // 2
+    middle = first_part(act_turned.shape[0])
     total = dot_rows(act_turned[...], g[:, block : 2 * block]) + sum_x[...]
     near_a[...] = total[:middle].astype(BF16)
     side_b[...] = total[middle:]
@@ -225,7 +229,7 @@
     for place, bits in enumerate(SENT):
         grad = grad + dot_last(g[:, place * block : (place + 1) * block], downs[bits][...])
     back[...] = (grad * slope[...]).astype(BF16)
-    middle = block // 2
+    middle = first_part(block)
     total = dot_rows(x_turned[3 * block :, :], back[...]) + sums[3][...]
     far_a[...] = total[:middle].astype(BF16)
     far_b[...] = total[middle:].astype(BF16)
@@ -239,23 +243,24 @@
     down_own[...] = dot_rows(act_turned[...], kept[...]) + down_sum[...]
 
 
-def finish_kernel(parts, near_sum, far_a, far_b, out, stage, sems):
+def finish_kernel(near_sum, far_a, far_b, out, stage, sems):
     rows = near_sum.shape[0]
-    step = rows // parts
+    middle = first_part(rows)
     copies = []
-    for i in range(parts):
-        here = slice(i * step, (i + 1) * step)
-        far, base = (far_a, 0) if i * 2 < parts else (far_b, rows // 2)
-        got = far[i * step - base : (i + 1) * step - base, :]
-        stage[here, :] = (near_sum[here, :] + got.astype(F32)).astype(BF16)
-        copies.append(pltpu.make_async_copy(stage.at[pl.ds(i * step, step), :], out.at[pl.ds(i * step, step), :], sems.at[i]))
-        copies[-1].start()
+    for far, start, end in ((far_a, 0, middle), (far_b, middle, rows)):
+        step = (end - start) // 2
+        for i in range(2):
+            here = slice(start + i * step, start + (i + 1) * step)
+            stage[here, :] = (near_sum[here, :] + far[i * step : (i + 1) * step, :].astype(F32)).astype(BF16)
+            place = pl.ds(start + i * step, step)
+            copies.append(pltpu.make_async_copy(stage.at[place, :], out.at[place, :], sems.at[len(copies)]))
+            copies[-1].start()
     for c in copies:
         c.wait()
 
 
 def near_kernel(own, near_a, near_b, out):
-    middle = own.shape[0] // 2
+    middle = first_part(own.shape[0])
     out[:middle, :] = own[:middle, :] + near_a[...].astype(F32)
     out[middle:, :] = own[middle:, :] + near_b[...].astype(F32)
 
@@ -330,7 +335,9 @@
 
 
 def exchanged(rows, cols):
-    return [shape(rows // 2, cols, BF16)] * 4 + [shape(rows // 2, cols, F32)] * 2
+    first = first_part(rows)
+    a, b = (shape(first, cols, BF16), shape(rows - first, cols, BF16))
+    return [a, b, a, b, shape(first, cols, F32), shape(rows - first, cols, F32)]
 
 
 def last_far(shards, table, act_turned, far_sum):
@@ -394,13 +401,12 @@
 
 
 def finish(near_sum, far_a, far_b):
-    parts = 4
     return pl.pallas_call(
-        functools.partial(finish_kernel, parts),
+        finish_kernel,
         out_shape=shape(*near_sum.shape, BF16),
         in_specs=[VMEM] * 3,
         out_specs=pl.BlockSpec(memory_space=pl.ANY),
-        scratch_shapes=[pltpu.VMEM(near_sum.shape, BF16), pltpu.SemaphoreType.DMA((parts,))],
+        scratch_shapes=[pltpu.VMEM(near_sum.shape, BF16), pltpu.SemaphoreType.DMA((4,))],
         compiler_params=pltpu.CompilerParams(vmem_limit_bytes=GRANT * MIB),
         cost_estimate=pl.CostEstimate(flops=near_sum.size, bytes_accessed=10 * near_sum.size, transcendentals=0),
     )(near_sum, far_a, far_b)

time: 143 us -> 151 us (1.056)
  starting transfers between devices: 41.8 us -> 49.1 us
    ppermute x18, waiting for transfers between devices: 44.1 us -> 36.6 us  [dp(): return lax.ppermute(value, 'dp', xor_perm(4, bits))]
    ppermute x27, waiting for transfers between devices: 34.3 us -> 41.7 us  [ex(): return lax.ppermute(value, 'expert', perm)]
    ppermute x27, starting transfers between devices: 21.2 us -> 26.5 us  [ex(): return lax.ppermute(value, 'expert', perm)]
    ppermute x18, starting transfers between devices: 20.6 us -> 22.7 us  [dp(): return lax.ppermute(value, 'dp', xor_perm(4, bits))]
  transfers between devices with their start and end apart: 45 -> 45, of which waited for: 17 -> 15; matrix products, arithmetic and copies ran while one was open for 0% -> 0% of each run, Pallas kernels for 11% -> 9%
where the time goes in v8:
time: 151 us; the launch traced here: 150 us
  waiting for transfers between devices  78.2 us (52%)
  starting transfers between devices  49.1 us (33%)
  Pallas kernels  18.4 us (12%)
  local copies, waits for them, and re-layouts  3.06 us (2%)
    ppermute x27, waiting for transfers between devices, ex(): return lax.ppermute(value, 'expert', perm)  41.7 us
    ppermute x18, waiting for transfers between devices, dp(): return lax.ppermute(value, 'dp', xor_perm(4, bits))  36.6 us
    ppermute x27, starting transfers between devices, ex(): return lax.ppermute(value, 'expert', perm)  26.5 us
    ppermute x18, starting transfers between devices, dp(): return lax.ppermute(value, 'dp', xor_perm(4, bits))  22.7 us
    pallas_call x13, Pallas kernels, local_call(): pl.pallas_call(kernel, out_shape=outs, in_specs=[VMEM] * len(args), out_s...  16.7 us
    unnamed x10, local copies, waits for them, and re-layouts  3.06 us
  transfers between devices with their start and end apart: 45, of which 15 were waited for; matrix products, arithmetic and copies ran while one was open for 0% of the time, Pallas kernels for 9%

profile of v8, /device:TPU:0, one launch (start us, length us, event | category | flops | bytes accessed | tf_op | source)
XLA Modules:
  0.0 150.3 jit_solution(9702656564208235163)
XLA Ops:
  4.9 3.1 %collective-permute-start.4 = (bf16[128,1152]{1,0:T(8,128)(2,1)S(1)}, bf16[128,1152]{1,0:T(8,128)(2,1)S(1)}, u32[]{:S(2)}, u32[]{:S(2)}) collective-permute-start(bf16[128,1152]{1,0:T(8,128)(2,1)S(1)} %get-tuple-element.40.refs_0_), channel_id=1, source_target_pairs={{0,2},{1,3},{2,4},{3,5},{4,6},{5,7},{6,0},{7,1},{8,10},{9,11},{10,... | collective-permute-start | bytes 884744 | tf_op jit(solution)/shard_map/ppermute | solution.py:423
  8.0 2.1 %collective-permute-start.6 = (bf16[128,1152]{1,0:T(8,128)(2,1)S(1)}, bf16[128,1152]{1,0:T(8,128)(2,1)S(1)}, u32[]{:S(2)}, u32[]{:S(2)}) collective-permute-start(bf16[128,1152]{1,0:T(8,128)(2,1)S(1)} %get-tuple-element.40.refs_0_), channel_id=1, source_target_pairs={{0,6},{1,7},{2,0},{3,1},{4,2},{5,3},{6,4},{7,5},{8,14},{9,15},{10,... | collective-permute-start | bytes 884744 | tf_op jit(solution)/shard_map/ppermute | solution.py:423
  12.2 11.5 %collective-permute-done.20.refs_7_ = f32[8,256]{1,0:T(8,128)S(1)} collective-permute-done((f32[8,256]{1,0:T(8,128)S(1)}, f32[8,256]{1,0:T(8,128)S(1)}, u32[]{:S(2)}, u32[]{:S(2)}) %collective-permute-start.20) | collective-permute-done | bytes 8224 | tf_op jit(solution)/shard_map/ppermute | solution.py:423
  25.3 2.0 %collective-permute-done.21.refs_8_ = f32[8,256]{1,0:T(8,128)S(1)} collective-permute-done((f32[8,256]{1,0:T(8,128)S(1)}, f32[8,256]{1,0:T(8,128)S(1)}, u32[]{:S(2)}, u32[]{:S(2)}) %collective-permute-start.21) | collective-permute-done | bytes 8224 | tf_op jit(solution)/shard_map/ppermute | solution.py:423
  27.4 3.8 %collective-permute-start.11 = (bf16[128,1536]{1,0:T(8,128)(2,1)S(1)}, bf16[128,1536]{1,0:T(8,128)(2,1)S(1)}, u32[]{:S(2)}, u32[]{:S(2)}) collective-permute-start(bf16[128,1536]{1,0:T(8,128)(2,1)S(1)} %copy-done.2), channel_id=1, source_target_pairs={{0,6},{1,7},{2,0},{3,1},{4,2},{5,3},{6,4},{7,5},{8,14},{9,15},{10,... | collective-permute-start | bytes 1179656 | tf_op jit(solution)/shard_map/ppermute | solution.py:423
  32.8 8.4 %collective-permute-done.9.refs_2_ = bf16[128,1536]{1,0:T(8,128)(2,1)S(1)} collective-permute-done((bf16[128,1536]{1,0:T(8,128)(2,1)S(1)}, bf16[128,1536]{1,0:T(8,128)(2,1)S(1)}, u32[]{:S(2)}, u32[]{:S(2)}) %collective-permute-start.9) | collective-permute-done | bytes 393248 | tf_op jit(solution)/shard_map/ppermute | solution.py:423
  41.1 3.7 %collective-permute-done.11.refs_4_ = bf16[128,1536]{1,0:T(8,128)(2,1)S(1)} collective-permute-done((bf16[128,1536]{1,0:T(8,128)(2,1)S(1)}, bf16[128,1536]{1,0:T(8,128)(2,1)S(1)}, u32[]{:S(2)}, u32[]{:S(2)}) %collective-permute-start.11) | collective-permute-done | bytes 393248 | tf_op jit(solution)/shard_map/ppermute | solution.py:423
  48.1 8.2 %collective-permute-done.7.lower = bf16[128,1152]{1,0:T(8,128)(2,1)S(1)} collective-permute-done((bf16[128,1152]{1,0:T(8,128)(2,1)S(1)}, bf16[128,1152]{1,0:T(8,128)(2,1)S(1)}, u32[]{:S(2)}, u32[]{:S(2)}) %collective-permute-start.7) | collective-permute-done | bytes 294944 | tf_op jit(solution)/shard_map/ppermute | solution.py:423
  57.6 2.2 %collective-permute-start.15 = (bf16[384,768]{1,0:T(8,128)(2,1)S(1)}, bf16[384,768]{1,0:T(8,128)(2,1)S(1)}, u32[]{:S(2)}, u32[]{:S(2)}) collective-permute-start(bf16[384,768]{1,0:T(8,128)(2,1)S(1)} %bitcast.8), channel_id=1, source_target_pairs={{0,16},{8,24},{16,0},{24,8},{1,17},{9,25},{17,1},{25,9},{2,18},{10... | collective-permute-start | bytes 1769480 | tf_op jit(solution)/shard_map/ppermute | solution.py:426
  60.0 1.9 %collective-permute-start.25 = (bf16[768,384]{1,0:T(8,128)(2,1)}, bf16[768,384]{1,0:T(8,128)(2,1)S(1)}, u32[]{:S(2)}, u32[]{:S(2)}) collective-permute-start(bf16[768,384]{1,0:T(8,128)(2,1)} %bitcast.1.down), channel_id=1, source_target_pairs={{0,8},{8,0},{16,24},{24,16},{1,9},{9,1},{17,25},{25,17},{2,10},{10... | collective-permute-start | bytes 1769480 | tf_op jit(solution)/shard_map/ppermute | solution.py:426
  62.0 5.2 %collective-permute-done.12.lower = bf16[128,1536]{1,0:T(8,128)(2,1)S(1)} collective-permute-done((bf16[128,1536]{1,0:T(8,128)(2,1)S(1)}, bf16[128,1536]{1,0:T(8,128)(2,1)S(1)}, u32[]{:S(2)}, u32[]{:S(2)}) %collective-permute-start.12) | collective-permute-done | bytes 393248 | tf_op jit(solution)/shard_map/ppermute | solution.py:423
  68.9 1.8 %collective-permute-start.29 = (bf16[128,384]{1,0:T(8,128)(2,1)S(1)}, bf16[128,384]{1,0:T(8,128)(2,1)S(1)}, u32[]{:S(2)}, u32[]{:S(2)}) collective-permute-start(bf16[128,384]{1,0:T(8,128)(2,1)S(1)} %get-tuple-element.39.refs_0_), channel_id=1, source_target_pairs={{0,2},{1,3},{2,4},{3,5},{4,6},{5,7},{6,0},{7,1},{8,10},{9,11},{10,... | collective-permute-start | bytes 294920 | tf_op jit(solution)/shard_map/ppermute | solution.py:423
  70.7 3.3 %collective-permute-done.15.refs_4_.refs_11_ = bf16[384,768]{1,0:T(8,128)(2,1)S(1)} collective-permute-done((bf16[384,768]{1,0:T(8,128)(2,1)S(1)}, bf16[384,768]{1,0:T(8,128)(2,1)S(1)}, u32[]{:S(2)}, u32[]{:S(2)}) %collective-permute-start.15) | collective-permute-done | bytes 589856 | tf_op jit(solution)/shard_map/ppermute | solution.py:426
  74.0 2.1 %collective-permute-start.31 = (bf16[128,384]{1,0:T(8,128)(2,1)S(1)}, bf16[128,384]{1,0:T(8,128)(2,1)S(1)}, u32[]{:S(2)}, u32[]{:S(2)}) collective-permute-start(bf16[128,384]{1,0:T(8,128)(2,1)S(1)} %get-tuple-element.39.refs_0_), channel_id=1, source_target_pairs={{0,6},{1,7},{2,0},{3,1},{4,2},{5,3},{6,4},{7,5},{8,14},{9,15},{10,... | collective-permute-start | bytes 294920 | tf_op jit(solution)/shard_map/ppermute | solution.py:423
  76.1 7.7 %collective-permute-done.16.refs_5_.refs_12_ = bf16[384,768]{1,0:T(8,128)(2,1)S(1)} collective-permute-done((bf16[384,768]{1,0:T(8,128)(2,1)S(1)}, bf16[384,768]{1,0:T(8,128)(2,1)S(1)}, u32[]{:S(2)}, u32[]{:S(2)}) %collective-permute-start.16) | collective-permute-done | bytes 589856 | tf_op jit(solution)/shard_map/ppermute | solution.py:426
  83.8 3.5 %shard_map.82 = (bf16[768,1152]{1,0:T(8,128)(2,1)S(1)}, bf16[768,768]{1,0:T(8,128)(2,1)S(1)}, f32[768,768]{1,0:T(8,128)S(1)}, f32[768,384]{1,0:T(8,128)S(1)}, f3...) custom-call(bf16[128,1152]{1,0:T(8,128)(2,1)S(1)} %get-tuple-element.40.refs_0_, ...), custom_call_target="tpu_custom_call" | custom-call | flops 2264924160 | bytes 15360000 | tf_op jit(solution)/shard_map/pallas_call | solution.py:273
  87.9 5.5 %collective-permute-start = (bf16[128,384]{1,0:T(8,128)(2,1)S(1)}, bf16[128,384]{1,0:T(8,128)(2,1)S(1)}, u32[]{:S(2)}, u32[]{:S(2)}) collective-permute-start(bf16[128,384]{1,0:T(8,128)(2,1)S(1)} %get-tuple-element.39.refs_0_), channel_id=1, source_target_pairs={{0,4},{1,5},{2,6},{3,7},{4,0},{5,1},{6,2},{7,3},{8,12},{9,13},{10,... | collective-permute-start | bytes 294920 | tf_op jit(solution)/shard_map/ppermute | solution.py:423
  93.8 2.0 %shard_map.84.refs_9_ = f32[768,768]{1,0:T(8,128)S(1)} custom-call(bf16[768,1152]{1,0:T(8,128)(2,1)S(1)} %get-tuple-element.51.g, bf16[768,384]{1,0:T(8,128)(2,1)S(1)} %collective-permute-done.27.refs_0_.refs_10_, bf16[768,384]{1,0:T(8,128)(2,1)S(1)} %collective-permute-done.25.refs_1_.refs_8_, bf16[768,384]{1,0:T(8,128)(2,1)S(1)} %collective-permute-done.26.refs_2_.refs_9_), custom_call_target="tpu_custom_call" | custom-call | flops 1358954496 | bytes 5898240 | tf_op jit(solution)/shard_map/pallas_call | solution.py:273
  96.0 2.6 %collective-permute-done.refs_0_ = bf16[128,384]{1,0:T(8,128)(2,1)S(1)} collective-permute-done((bf16[128,384]{1,0:T(8,128)(2,1)S(1)}, bf16[128,384]{1,0:T(8,128)(2,1)S(1)}, u32[]{:S(2)}, u32[]{:S(2)}) %collective-permute-start) | collective-permute-done | bytes 98336 | tf_op jit(solution)/shard_map/ppermute | solution.py:423
  99.1 3.4 %shard_map.85 = (f32[384,768]{1,0:T(8,128)S(1)}, f32[384,768]{1,0:T(8,128)S(1)}, f32[384,768]{1,0:T(8,128)S(1)}, f32[384,768]{1,0:T(8,128)S(1)}, f32[768,384]{1,0:T(8,128)S(1)}) custom-call(bf16[128,384]{1,0:T(8,128)(2,1)S(1)} %get-tuple-element.39.refs_0_, bf16[128,384]{1,0:T(8,128)(2,1)S(1)} %collective-permute-done.28.refs_1_, ...), custom_call_target="tpu_custom_call" | custom-call | flops 2717908992 | bytes 15360000 | tf_op jit(solution)/shard_map/pallas_call | solution.py:273
  104.2 2.4 %shard_map.86 = (bf16[192,768]{1,0:T(8,128)(2,1)S(1)}, bf16[192,768]{1,0:T(8,128)(2,1)S(1)}, bf16[192,768]{1,0:T(8,128)(2,1)S(1)}, bf16[192,768]{1,0:T(8,128)(2,...) custom-call(bf16[128,384]{1,0:T(8,128)(2,1)S(1)} %collective-permute-, ...), custom_call_target="tpu_custom_call" | custom-call | flops 1358954496 | bytes 15736832 | tf_op jit(solution)/shard_map/pallas_call | solution.py:273
  106.6 1.8 %collective-permute-start.37 = (bf16[192,768]{1,0:T(8,128)(2,1)S(1)}, bf16[192,768]{1,0:T(8,128)(2,1)S(1)}, u32[]{:S(2)}, u32[]{:S(2)}) collective-permute-start(bf16[192,768]{1,0:T(8,128)(2,1)S(1)} %get-tuple-element.66), channel_id=1, source_target_pairs={{0,16},{8,24},{16,0},{24,8},{1,17},{9,25},{17,1},{25,9},{2,18},{10... | collective-permute-start | bytes 884744 | tf_op jit(solution)/shard_map/ppermute | solution.py:426
  111.3 1.8 %collective-permute-start.39 = (bf16[416,384]{1,0:T(8,128)(2,1)S(1)}, bf16[416,384]{1,0:T(8,128)(2,1)S(1)}, u32[]{:S(2)}, u32[]{:S(2)}) collective-permute-start(bf16[416,384]{1,0:T(8,128)(2,1)S(1)} %get-tuple-element.70), channel_id=1, source_target_pairs={{0,8},{8,0},{16,24},{24,16},{1,9},{9,1},{17,25},{25,17},{2,10},{10... | collective-permute-start | bytes 958472 | tf_op jit(solution)/shard_map/ppermute | solution.py:426
  113.1 3.5 %collective-permute-done.37 = bf16[192,768]{1,0:T(8,128)(2,1)S(1)} collective-permute-done((bf16[192,768]{1,0:T(8,128)(2,1)S(1)}, bf16[192,768]{1,0:T(8,128)(2,1)S(1)}, u32[]{:S(2)}, u32[]{:S(2)}) %collective-permute-start.37) | collective-permute-done | bytes 294944 | tf_op jit(solution)/shard_map/ppermute | solution.py:426
  116.6 1.7 %collective-permute-start.40 = (bf16[352,384]{1,0:T(8,128)(2,1)S(1)}, bf16[352,384]{1,0:T(8,128)(2,1)S(1)}, u32[]{:S(2)}, u32[]{:S(2)}) collective-permute-start(bf16[352,384]{1,0:T(8,128)(2,1)S(1)} %get-tuple-element.71), channel_id=1, source_target_pairs={{0,16},{8,24},{16,0},{24,8},{1,17},{9,25},{17,1},{25,9},{2,18},{10... | collective-permute-start | bytes 811016 | tf_op jit(solution)/shard_map/ppermute | solution.py:426
  120.0 5.2 %collective-permute-done.41 = bf16[416,384]{1,0:T(8,128)(2,1)S(1)} collective-permute-done((bf16[416,384]{1,0:T(8,128)(2,1)S(1)}, bf16[416,384]{1,0:T(8,128)(2,1)S(1)}, u32[]{:S(2)}, u32[]{:S(2)}) %collective-permute-start.41) | collective-permute-done | bytes 319520 | tf_op jit(solution)/shard_map/ppermute | solution.py:426
  125.5 1.8 %collective-permute-start.38 = (bf16[192,768]{1,0:T(8,128)(2,1)S(1)}, bf16[192,768]{1,0:T(8,128)(2,1)S(1)}, u32[]{:S(2)}, u32[]{:S(2)}) collective-permute-start(bf16[192,768]{1,0:T(8,128)(2,1)S(1)} %add_convert_fusion.1), channel_id=1, source_target_pairs={{0,8},{8,0},{16,24},{24,16},{1,9},{9,1},{17,25},{25,17},{2,10},{10... | collective-permute-start | bytes 884744 | tf_op jit(solution)/shard_map/ppermute | solution.py:426
  128.2 1.7 %collective-permute-start.36 = (bf16[192,768]{1,0:T(8,128)(2,1)S(1)}, bf16[192,768]{1,0:T(8,128)(2,1)S(1)}, u32[]{:S(2)}, u32[]{:S(2)}) collective-permute-start(bf16[192,768]{1,0:T(8,128)(2,1)S(1)} %add_convert_fusion.2), channel_id=1, source_target_pairs={{0,16},{8,24},{16,0},{24,8},{1,17},{9,25},{17,1},{25,9},{2,18},{10... | collective-permute-start | bytes 884744 | tf_op jit(solution)/shard_map/ppermute | solution.py:426
  129.9 8.4 %collective-permute-done.33.near_a = bf16[192,768]{1,0:T(8,128)(2,1)S(1)} collective-permute-done((bf16[192,768]{1,0:T(8,128)(2,1)S(1)}, bf16[192,768]{1,0:T(8,128)(2,1)S(1)}, u32[]{:S(2)}, u32[]{:S(2)}) %collective-permute-start.33) | collective-permute-done | bytes 294944 | tf_op jit(solution)/shard_map/ppermute | solution.py:426
  138.7 1.8 %collective-permute-start.44 = (bf16[352,384]{1,0:T(8,128)(2,1)S(1)}, bf16[352,384]{1,0:T(8,128)(2,1)S(1)}, u32[]{:S(2)}, u32[]{:S(2)}) collective-permute-start(bf16[352,384]{1,0:T(8,128)(2,1)S(1)} %add_convert_fusion.3), channel_id=1, source_target_pairs={{0,8},{8,0},{16,24},{24,16},{1,9},{9,1},{17,25},{25,17},{2,10},{10... | collective-permute-start | bytes 811016 | tf_op jit(solution)/shard_map/ppermute | solution.py:426
  140.7 3.9 %collective-permute-done.38.far_b = bf16[192,768]{1,0:T(8,128)(2,1)S(1)} collective-permute-done((bf16[192,768]{1,0:T(8,128)(2,1)S(1)}, bf16[192,768]{1,0:T(8,128)(2,1)S(1)}, u32[]{:S(2)}, u32[]{:S(2)}) %collective-permute-start.38) | collective-permute-done | bytes 294944 | tf_op jit(solution)/shard_map/ppermute | solution.py:426
  145.5 3.7 %collective-permute-done.44.far_b = bf16[352,384]{1,0:T(8,128)(2,1)S(1)} collective-permute-done((bf16[352,384]{1,0:T(8,128)(2,1)S(1)}, bf16[352,384]{1,0:T(8,128)(2,1)S(1)}, u32[]{:S(2)}, u32[]{:S(2)}) %collective-permute-start.44) | collective-permute-done | bytes 270368 | tf_op jit(solution)/shard_map/ppermute | solution.py:426
  (90 shorter events, 27.5 us)
Async XLA Ops:
  4.9 22.4 %collective-permute-start.4 = (bf16[128,1152]{1,0:T(8,128)(2,1)S(1)}, bf16[128,1152]{1,0:T(8,128)(2,1)S(1)}, u32[]{:S(2)}, u32[]{:S(2)}) collective-permute-start(bf16[128,1152]{1,0:T(8,128)(2,1)S(1)} %get-tuple-element.40.refs_0_), channel_id=1, source_target_pairs={{0,2},{1,3},{2,4},{3,5},{4,6},{5,7},{6,0},{7,1},{8,10},{9,11},{10,... | collective-permute-start | bytes 884744 | tf_op jit(solution)/shard_map/ppermute | solution.py:423
  8.0 23.1 %collective-permute-start.6 = (bf16[128,1152]{1,0:T(8,128)(2,1)S(1)}, bf16[128,1152]{1,0:T(8,128)(2,1)S(1)}, u32[]{:S(2)}, u32[]{:S(2)}) collective-permute-start(bf16[128,1152]{1,0:T(8,128)(2,1)S(1)} %get-tuple-element.40.refs_0_), channel_id=1, source_target_pairs={{0,6},{1,7},{2,0},{3,1},{4,2},{5,3},{6,4},{7,5},{8,14},{9,15},{10,... | collective-permute-start | bytes 884744 | tf_op jit(solution)/shard_map/ppermute | solution.py:423
  10.2 36.6 %collective-permute-start.14 = (bf16[384,768]{1,0:T(8,128)(2,1)S(1)}, bf16[384,768]{1,0:T(8,128)(2,1)S(1)}, u32[]{:S(2)}, u32[]{:S(2)}) collective-permute-start(bf16[384,768]{1,0:T(8,128)(2,1)S(1)} %bitcast.7), channel_id=1, source_target_pairs={{0,8},{8,0},{16,24},{24,16},{1,9},{9,1},{17,25},{25,17},{2,10},{10... | collective-permute-start | bytes 1769480 | tf_op jit(solution)/shard_map/ppermute | solution.py:426
  12.0 11.7 %collective-permute-start.20 = (f32[8,256]{1,0:T(8,128)S(1)}, f32[8,256]{1,0:T(8,128)S(1)}, u32[]{:S(2)}, u32[]{:S(2)}) collective-permute-start(f32[8,256]{1,0:T(8,128)S(1)} %pad_maximum_fusion.refs_6_), channel_id=1, source_target_pairs={{0,2},{1,3},{2,4},{3,5},{4,6},{5,7},{6,0},{7,1},{8,10},{9,11},{10,... | collective-permute-start | bytes 24584 | tf_op jit(solution)/shard_map/ppermute | solution.py:423
  12.0 19.2 %collective-permute-start.17 = (bf16[128,1152]{1,0:T(8,128)(2,1)S(1)}, bf16[128,1152]{1,0:T(8,128)(2,1)S(1)}, u32[]{:S(2)}, u32[]{:S(2)}) collective-permute-start(bf16[128,1152]{1,0:T(8,128)(2,1)S(1)} %get-tuple-element.40.refs_0_), channel_id=1, source_target_pairs={{0,1},{1,0},{2,3},{3,2},{4,5},{5,4},{6,7},{7,6},{8,9},{9,8},{10,11... | collective-permute-start | bytes 884744 | tf_op jit(solution)/shard_map/ppermute | solution.py:423
  27.4 13.8 %collective-permute-start.9 = (bf16[128,1536]{1,0:T(8,128)(2,1)S(1)}, bf16[128,1536]{1,0:T(8,128)(2,1)S(1)}, u32[]{:S(2)}, u32[]{:S(2)}) collective-permute-start(bf16[128,1536]{1,0:T(8,128)(2,1)S(1)} %copy-done.2), channel_id=1, source_target_pairs={{0,2},{1,3},{2,4},{3,5},{4,6},{5,7},{6,0},{7,1},{8,10},{9,11},{10,... | collective-permute-start | bytes 1179656 | tf_op jit(solution)/shard_map/ppermute | solution.py:423
  27.4 17.5 %collective-permute-start.11 = (bf16[128,1536]{1,0:T(8,128)(2,1)S(1)}, bf16[128,1536]{1,0:T(8,128)(2,1)S(1)}, u32[]{:S(2)}, u32[]{:S(2)}) collective-permute-start(bf16[128,1536]{1,0:T(8,128)(2,1)S(1)} %copy-done.2), channel_id=1, source_target_pairs={{0,6},{1,7},{2,0},{3,1},{4,2},{5,3},{6,4},{7,5},{8,14},{9,15},{10,... | collective-permute-start | bytes 1179656 | tf_op jit(solution)/shard_map/ppermute | solution.py:423
  31.2 14.3 %collective-permute-start.22 = (bf16[128,1536]{1,0:T(8,128)(2,1)S(1)}, bf16[128,1536]{1,0:T(8,128)(2,1)S(1)}, u32[]{:S(2)}, u32[]{:S(2)}) collective-permute-start(bf16[128,1536]{1,0:T(8,128)(2,1)S(1)} %copy-done.2), channel_id=1, source_target_pairs={{0,1},{1,0},{2,3},{3,2},{4,5},{5,4},{6,7},{7,6},{8,9},{9,8},{10,11... | collective-permute-start | bytes 1179656 | tf_op jit(solution)/shard_map/ppermute | solution.py:423
  31.2 26.4 %collective-permute-start.26 = (bf16[768,384]{1,0:T(8,128)(2,1)}, bf16[768,384]{1,0:T(8,128)(2,1)S(1)}, u32[]{:S(2)}, u32[]{:S(2)}) collective-permute-start(bf16[768,384]{1,0:T(8,128)(2,1)} %bitcast.1.down), channel_id=1, source_target_pairs={{0,16},{8,24},{16,0},{24,8},{1,17},{9,25},{17,1},{25,9},{2,18},{10... | collective-permute-start | bytes 1769480 | tf_op jit(solution)/shard_map/ppermute | solution.py:426
  45.5 10.8 %collective-permute-start.7 = (bf16[128,1152]{1,0:T(8,128)(2,1)S(1)}, bf16[128,1152]{1,0:T(8,128)(2,1)S(1)}, u32[]{:S(2)}, u32[]{:S(2)}) collective-permute-start(bf16[128,1152]{1,0:T(8,128)(2,1)S(1)} %collective-permute-done.6.refs_4_), channel_id=1, source_target_pairs={{2,0},{3,1},{4,2},{5,3},{10,8},{11,9},{12,10},{13,11},{18,16},{19,... | collective-permute-start | bytes 884744 | tf_op jit(solution)/shard_map/ppermute | solution.py:423
  46.8 13.0 %collective-permute-start.23 = (bf16[128,1536]{1,0:T(8,128)(2,1)S(1)}, bf16[128,1536]{1,0:T(8,128)(2,1)S(1)}, u32[]{:S(2)}, u32[]{:S(2)}) collective-permute-start(bf16[128,1536]{1,0:T(8,128)(2,1)S(1)} %collective-permute-done.9.refs_2_), channel_id=1, source_target_pairs={{0,1},{1,0},{2,3},{3,2},{4,5},{5,4},{6,7},{7,6},{8,9},{9,8},{10,11... | collective-permute-start | bytes 1179656 | tf_op jit(solution)/shard_map/ppermute | solution.py:423
  46.9 13.0 %collective-permute-start.24 = (bf16[128,1536]{1,0:T(8,128)(2,1)S(1)}, bf16[128,1536]{1,0:T(8,128)(2,1)S(1)}, u32[]{:S(2)}, u32[]{:S(2)}) collective-permute-start(bf16[128,1536]{1,0:T(8,128)(2,1)S(1)} %collective-permute-done.11.refs_4_), channel_id=1, source_target_pairs={{0,1},{1,0},{2,3},{3,2},{4,5},{5,4},{6,7},{7,6},{8,9},{9,8},{10,11... | collective-permute-start | bytes 1179656 | tf_op jit(solution)/shard_map/ppermute | solution.py:423
  47.4 14.5 %collective-permute-start.10 = (bf16[128,1536]{1,0:T(8,128)(2,1)S(1)}, bf16[128,1536]{1,0:T(8,128)(2,1)S(1)}, u32[]{:S(2)}, u32[]{:S(2)}) collective-permute-start(bf16[128,1536]{1,0:T(8,128)(2,1)S(1)} %collective-permute-done.9.refs_2_), channel_id=1, source_target_pairs={{2,4},{3,5},{4,6},{5,7},{10,12},{11,13},{12,14},{13,15},{18,20},{1... | collective-permute-start | bytes 1179656 | tf_op jit(solution)/shard_map/ppermute | solution.py:423
  56.3 10.9 %collective-permute-start.12 = (bf16[128,1536]{1,0:T(8,128)(2,1)S(1)}, bf16[128,1536]{1,0:T(8,128)(2,1)S(1)}, u32[]{:S(2)}, u32[]{:S(2)}) collective-permute-start(bf16[128,1536]{1,0:T(8,128)(2,1)S(1)} %collective-permute-done.11.refs_4_), channel_id=1, source_target_pairs={{2,0},{3,1},{4,2},{5,3},{10,8},{11,9},{12,10},{13,11},{18,16},{19,... | collective-permute-start | bytes 1179656 | tf_op jit(solution)/shard_map/ppermute | solution.py:423
  57.6 16.4 %collective-permute-start.15 = (bf16[384,768]{1,0:T(8,128)(2,1)S(1)}, bf16[384,768]{1,0:T(8,128)(2,1)S(1)}, u32[]{:S(2)}, u32[]{:S(2)}) collective-permute-start(bf16[384,768]{1,0:T(8,128)(2,1)S(1)} %bitcast.8), channel_id=1, source_target_pairs={{0,16},{8,24},{16,0},{24,8},{1,17},{9,25},{17,1},{25,9},{2,18},{10... | collective-permute-start | bytes 1769480 | tf_op jit(solution)/shard_map/ppermute | solution.py:426
  59.9 23.9 %collective-permute-start.16 = (bf16[384,768]{1,0:T(8,128)(2,1)S(1)}, bf16[384,768]{1,0:T(8,128)(2,1)S(1)}, u32[]{:S(2)}, u32[]{:S(2)}) collective-permute-start(bf16[384,768]{1,0:T(8,128)(2,1)S(1)} %collective-permute-done.14.refs_3_.refs_7_), channel_id=1, source_target_pairs={{0,16},{8,24},{16,0},{24,8},{1,17},{9,25},{17,1},{25,9},{2,18},{10... | collective-permute-start | bytes 1769480 | tf_op jit(solution)/shard_map/ppermute | solution.py:426
  60.0 33.4 %collective-permute-start.25 = (bf16[768,384]{1,0:T(8,128)(2,1)}, bf16[768,384]{1,0:T(8,128)(2,1)S(1)}, u32[]{:S(2)}, u32[]{:S(2)}) collective-permute-start(bf16[768,384]{1,0:T(8,128)(2,1)} %bitcast.1.down), channel_id=1, source_target_pairs={{0,8},{8,0},{16,24},{24,16},{1,9},{9,1},{17,25},{25,17},{2,10},{10... | collective-permute-start | bytes 1769480 | tf_op jit(solution)/shard_map/ppermute | solution.py:426
  61.9 31.5 %collective-permute-start.27 = (bf16[768,384]{1,0:T(8,128)(2,1)S(1)}, bf16[768,384]{1,0:T(8,128)(2,1)S(1)}, u32[]{:S(2)}, u32[]{:S(2)}) collective-permute-start(bf16[768,384]{1,0:T(8,128)(2,1)S(1)} %collective-permute-done.26.refs_2_.refs_9_), channel_id=1, source_target_pairs={{0,8},{8,0},{16,24},{24,16},{1,9},{9,1},{17,25},{25,17},{2,10},{10... | collective-permute-start | bytes 1769480 | tf_op jit(solution)/shard_map/ppermute | solution.py:426
  68.9 18.4 %collective-permute-start.29 = (bf16[128,384]{1,0:T(8,128)(2,1)S(1)}, bf16[128,384]{1,0:T(8,128)(2,1)S(1)}, u32[]{:S(2)}, u32[]{:S(2)}) collective-permute-start(bf16[128,384]{1,0:T(8,128)(2,1)S(1)} %get-tuple-element.39.refs_0_), channel_id=1, source_target_pairs={{0,2},{1,3},{2,4},{3,5},{4,6},{5,7},{6,0},{7,1},{8,10},{9,11},{10,... | collective-permute-start | bytes 294920 | tf_op jit(solution)/shard_map/ppermute | solution.py:423
  74.0 13.8 %collective-permute-start.31 = (bf16[128,384]{1,0:T(8,128)(2,1)S(1)}, bf16[128,384]{1,0:T(8,128)(2,1)S(1)}, u32[]{:S(2)}, u32[]{:S(2)}) collective-permute-start(bf16[128,384]{1,0:T(8,128)(2,1)S(1)} %get-tuple-element.39.refs_0_), channel_id=1, source_target_pairs={{0,6},{1,7},{2,0},{3,1},{4,2},{5,3},{6,4},{7,5},{8,14},{9,15},{10,... | collective-permute-start | bytes 294920 | tf_op jit(solution)/shard_map/ppermute | solution.py:423
  83.8 18.7 %collective-permute-start.13 = (bf16[128,1536]{1,0:T(8,128)(2,1)S(1)}, bf16[128,1536]{1,0:T(8,128)(2,1)S(1)}, u32[]{:S(2)}, u32[]{:S(2)}) collective-permute-start(bf16[128,1536]{1,0:T(8,128)(2,1)S(1)} %shard_map.79.refs_0_), channel_id=1, source_target_pairs={{0,1},{1,0},{2,3},{3,2},{4,5},{5,4},{6,7},{7,6},{8,9},{9,8},{10,11... | collective-permute-start | bytes 1179656 | tf_op jit(solution)/shard_map/ppermute | solution.py:423
  87.9 10.7 %collective-permute-start = (bf16[128,384]{1,0:T(8,128)(2,1)S(1)}, bf16[128,384]{1,0:T(8,128)(2,1)S(1)}, u32[]{:S(2)}, u32[]{:S(2)}) collective-permute-start(bf16[128,384]{1,0:T(8,128)(2,1)S(1)} %get-tuple-element.39.refs_0_), channel_id=1, source_target_pairs={{0,4},{1,5},{2,6},{3,7},{4,0},{5,1},{6,2},{7,3},{8,12},{9,13},{10,... | collective-permute-start | bytes 294920 | tf_op jit(solution)/shard_map/ppermute | solution.py:423
  109.9 15.6 %collective-permute-start.43 = (bf16[352,384]{1,0:T(8,128)(2,1)S(1)}, bf16[352,384]{1,0:T(8,128)(2,1)S(1)}, u32[]{:S(2)}, u32[]{:S(2)}) collective-permute-start(bf16[352,384]{1,0:T(8,128)(2,1)S(1)} %get-tuple-element.75), channel_id=1, source_target_pairs={{0,16},{8,24},{16,0},{24,8},{1,17},{9,25},{17,1},{25,9},{2,18},{10... | collective-permute-start | bytes 811016 | tf_op jit(solution)/shard_map/ppermute | solution.py:426
  110.4 14.7 %collective-permute-start.41 = (bf16[416,384]{1,0:T(8,128)(2,1)S(1)}, bf16[416,384]{1,0:T(8,128)(2,1)S(1)}, u32[]{:S(2)}, u32[]{:S(2)}) collective-permute-start(bf16[416,384]{1,0:T(8,128)(2,1)S(1)} %get-tuple-element.73), channel_id=1, source_target_pairs={{0,8},{8,0},{16,24},{24,16},{1,9},{9,1},{17,25},{25,17},{2,10},{10... | collective-permute-start | bytes 958472 | tf_op jit(solution)/shard_map/ppermute | solution.py:426
  111.3 29.2 %collective-permute-start.39 = (bf16[416,384]{1,0:T(8,128)(2,1)S(1)}, bf16[416,384]{1,0:T(8,128)(2,1)S(1)}, u32[]{:S(2)}, u32[]{:S(2)}) collective-permute-start(bf16[416,384]{1,0:T(8,128)(2,1)S(1)} %get-tuple-element.70), channel_id=1, source_target_pairs={{0,8},{8,0},{16,24},{24,16},{1,9},{9,1},{17,25},{25,17},{2,10},{10... | collective-permute-start | bytes 958472 | tf_op jit(solution)/shard_map/ppermute | solution.py:426
  116.6 11.6 %collective-permute-start.40 = (bf16[352,384]{1,0:T(8,128)(2,1)S(1)}, bf16[352,384]{1,0:T(8,128)(2,1)S(1)}, u32[]{:S(2)}, u32[]{:S(2)}) collective-permute-start(bf16[352,384]{1,0:T(8,128)(2,1)S(1)} %get-tuple-element.71), channel_id=1, source_target_pairs={{0,16},{8,24},{16,0},{24,8},{1,17},{9,25},{17,1},{25,9},{2,18},{10... | collective-permute-start | bytes 811016 | tf_op jit(solution)/shard_map/ppermute | solution.py:426
  118.4 19.9 %collective-permute-start.33 = (bf16[192,768]{1,0:T(8,128)(2,1)S(1)}, bf16[192,768]{1,0:T(8,128)(2,1)S(1)}, u32[]{:S(2)}, u32[]{:S(2)}) collective-permute-start(bf16[192,768]{1,0:T(8,128)(2,1)S(1)} %get-tuple-element.61), channel_id=1, source_target_pairs={{0,8},{8,0},{16,24},{24,16},{1,9},{9,1},{17,25},{25,17},{2,10},{10... | collective-permute-start | bytes 884744 | tf_op jit(solution)/shard_map/ppermute | solution.py:426
  125.2 13.5 %collective-permute-start.34 = (bf16[192,768]{1,0:T(8,128)(2,1)S(1)}, bf16[192,768]{1,0:T(8,128)(2,1)S(1)}, u32[]{:S(2)}, u32[]{:S(2)}) collective-permute-start(bf16[192,768]{1,0:T(8,128)(2,1)S(1)} %get-tuple-element.62), channel_id=1, source_target_pairs={{0,16},{8,24},{16,0},{24,8},{1,17},{9,25},{17,1},{25,9},{2,18},{10... | collective-permute-start | bytes 884744 | tf_op jit(solution)/shard_map/ppermute | solution.py:426
  125.5 19.1 %collective-permute-start.38 = (bf16[192,768]{1,0:T(8,128)(2,1)S(1)}, bf16[192,768]{1,0:T(8,128)(2,1)S(1)}, u32[]{:S(2)}, u32[]{:S(2)}) collective-permute-start(bf16[192,768]{1,0:T(8,128)(2,1)S(1)} %add_convert_fusion.1), channel_id=1, source_target_pairs={{0,8},{8,0},{16,24},{24,16},{1,9},{9,1},{17,25},{25,17},{2,10},{10... | collective-permute-start | bytes 884744 | tf_op jit(solution)/shard_map/ppermute | solution.py:426
  128.2 16.5 %collective-permute-start.36 = (bf16[192,768]{1,0:T(8,128)(2,1)S(1)}, bf16[192,768]{1,0:T(8,128)(2,1)S(1)}, u32[]{:S(2)}, u32[]{:S(2)}) collective-permute-start(bf16[192,768]{1,0:T(8,128)(2,1)S(1)} %add_convert_fusion.2), channel_id=1, source_target_pairs={{0,16},{8,24},{16,0},{24,8},{1,17},{9,25},{17,1},{25,9},{2,18},{10... | collective-permute-start | bytes 884744 | tf_op jit(solution)/shard_map/ppermute | solution.py:426
  138.3 10.9 %collective-permute-start.42 = (bf16[416,384]{1,0:T(8,128)(2,1)S(1)}, bf16[416,384]{1,0:T(8,128)(2,1)S(1)}, u32[]{:S(2)}, u32[]{:S(2)}) collective-permute-start(bf16[416,384]{1,0:T(8,128)(2,1)S(1)} %add_convert_fusion), channel_id=1, source_target_pairs={{0,16},{8,24},{16,0},{24,8},{1,17},{9,25},{17,1},{25,9},{2,18},{10... | collective-permute-start | bytes 958472 | tf_op jit(solution)/shard_map/ppermute | solution.py:426
  138.7 10.5 %collective-permute-start.44 = (bf16[352,384]{1,0:T(8,128)(2,1)S(1)}, bf16[352,384]{1,0:T(8,128)(2,1)S(1)}, u32[]{:S(2)}, u32[]{:S(2)}) collective-permute-start(bf16[352,384]{1,0:T(8,128)(2,1)S(1)} %add_convert_fusion.3), channel_id=1, source_target_pairs={{0,8},{8,0},{16,24},{24,16},{1,9},{9,1},{17,25},{25,17},{2,10},{10... | collective-permute-start | bytes 811016 | tf_op jit(solution)/shard_map/ppermute | solution.py:426
  (18 other events, 92.5 us)

commit v9 on v8

--- a/solution.py
+++ b/solution.py
@@ -170,16 +170,21 @@
     g, far_a, far_b = refs[5:]
     expert = lax.axis_index("expert")
     for half in range(2):
-        g[half * SHARD : (half + 1) * SHARD, :] = scale_rows(pick_gate(table, half, expert), shards[half][...])
+        g[half * SHARD : (half + 1) * SHARD, :] = scale_rows(pick_gate(table, half, expert), shards[half][:, :block])
     middle = first_part(act_turned.shape[0])
-    total = dot_rows(act_turned[...], g[:, :block]) + far_sum[...]
+    total = dot_rows(act_turned[...], g[...]) + far_sum[...]
     far_a[...] = total[:middle].astype(BF16)
     far_b[...] = total[middle:].astype(BF16)
 
 
 def last_near_kernel(block, *refs):
-    g, act_turned, sum_x, sum_y = refs[:4]
-    near_a, near_b, side_a, side_b = refs[4:]
+    shards, table, g_far, act_turned, sum_x, sum_y = refs[0:2], refs[2], refs[3], refs[4], refs[5], refs[6]
+    g, near_a, near_b, side_a, side_b = refs[7:]
+    expert = lax.axis_index("expert")
+    g[:, :block] = g_far[...]
+    for half in range(2):
+        rows = slice(half * SHARD, (half + 1) * SHARD)
+        g[rows, block:] = scale_rows(pick_gate(table, half, expert), shards[half][:, block:])
     middle = first_part(act_turned.shape[0])
     total = dot_rows(act_turned[...], g[:, block : 2 * block]) + sum_x[...]
     near_a[...] = total[:middle].astype(BF16)
@@ -344,18 +349,18 @@
     hidden, block = far_sum.shape
     return local_call(
         functools.partial(last_far_kernel, block),
-        [shape(2 * SHARD, 3 * block, BF16)] + exchanged(hidden, block)[:2],
+        [shape(2 * SHARD, block, BF16)] + exchanged(hidden, block)[:2],
         (*shards, table, act_turned, far_sum),
         flops=4 * SHARD * block * hidden,
     )
 
 
-def last_near(g, act_turned, sum_x, sum_y):
+def last_near(shards, table, g_far, act_turned, sum_x, sum_y):
     hidden, block = sum_x.shape
     return local_call(
         functools.partial(last_near_kernel, block),
-        exchanged(hidden, block)[2:],
-        (g, act_turned, sum_x, sum_y),
+        [shape(2 * SHARD, 3 * block, BF16)] + exchanged(hidden, block)[2:],
+        (*shards, table, g_far, act_turned, sum_x, sum_y),
         flops=8 * SHARD * block * hidden,
     )
 
@@ -482,8 +487,9 @@
     x_tail, x_turned, pre_part = early_forward((tokens_here, t0b, t1, t1b, t3, t3b), ups)
     g_ab, act_ab, slope_ab, *down_sums = most_down((ga, ga0b, ga1, ga1b, ga3, ga3b), tables, x_tail, pre_part, up_y, up_d)
     x_c, act_c, slope_c = last_forward((t2, t2b), ups)
-    g_c, *down_far = last_far((ga2, ga2b), c2, act_c, down_sums[0])
-    down_parts = (*down_far, *last_near(g_c, act_c, *down_sums[1:]))
+    g_far, *down_far = last_far((ga2, ga2b), c2, act_c, down_sums[0])
+    g_c, *down_near = last_near((ga2, ga2b), c2, g_far, act_c, *down_sums[1:])
+    down_parts = (*down_far, *down_near)
     grad_part = early_backward(g_ab, downs)
     up_sums, down_sum = most_up((gb, gb0b, gb1, gb1b, gb3, gb3b), tables, grad_part, slope_ab, x_turned, act_ab, down_here)
     *up_parts, up_own, down_own = last_up((gb2, gb2b), c2, g_c, slope_c, x_c, act_c, downs, up_sums, down_sum)

time: 151 us -> 151 us (level)
  no operation moved by 1% of the time
where the time goes in v9:
time: 151 us
  waiting for transfers between devices  78.9 us (52%)
  starting transfers between devices  49.1 us (33%)
  Pallas kernels  18.5 us (12%)
  local copies, waits for them, and re-layouts  3.06 us (2%)
    ppermute x27, waiting for transfers between devices, ex(): return lax.ppermute(value, 'expert', perm)  41.7 us
    ppermute x18, waiting for transfers between devices, dp(): return lax.ppermute(value, 'dp', xor_perm(4, bits))  37.2 us
    ppermute x27, starting transfers between devices, ex(): return lax.ppermute(value, 'expert', perm)  26.5 us
    ppermute x18, starting transfers between devices, dp(): return lax.ppermute(value, 'dp', xor_perm(4, bits))  22.6 us
    pallas_call x13, Pallas kernels, local_call(): pl.pallas_call(kernel, out_shape=outs, in_specs=[VMEM] * len(args), out_s...  16.8 us
    unnamed x10, local copies, waits for them, and re-layouts  3.06 us
  transfers between devices with their start and end apart: 45, of which 15 were waited for; matrix products, arithmetic and copies ran while one was open for 0% of the time, Pallas kernels for 9%

profile of v9, /device:TPU:0, one launch (start us, length us, event | category | flops | bytes accessed | tf_op | source)
XLA Modules:
  0.0 150.9 jit_solution(17961923513418111261)
XLA Ops:
  4.9 3.1 %collective-permute-start.4 = (bf16[128,1152]{1,0:T(8,128)(2,1)S(1)}, bf16[128,1152]{1,0:T(8,128)(2,1)S(1)}, u32[]{:S(2)}, u32[]{:S(2)}) collective-permute-start(bf16[128,1152]{1,0:T(8,128)(2,1)S(1)} %get-tuple-element.41.refs_0_), channel_id=1, source_target_pairs={{0,2},{1,3},{2,4},{3,5},{4,6},{5,7},{6,0},{7,1},{8,10},{9,11},{10,... | collective-permute-start | bytes 884744 | tf_op jit(solution)/shard_map/ppermute | solution.py:428
  8.0 2.1 %collective-permute-start.6 = (bf16[128,1152]{1,0:T(8,128)(2,1)S(1)}, bf16[128,1152]{1,0:T(8,128)(2,1)S(1)}, u32[]{:S(2)}, u32[]{:S(2)}) collective-permute-start(bf16[128,1152]{1,0:T(8,128)(2,1)S(1)} %get-tuple-element.41.refs_0_), channel_id=1, source_target_pairs={{0,6},{1,7},{2,0},{3,1},{4,2},{5,3},{6,4},{7,5},{8,14},{9,15},{10,... | collective-permute-start | bytes 884744 | tf_op jit(solution)/shard_map/ppermute | solution.py:428
  10.2 1.7 %collective-permute-start.14 = (bf16[384,768]{1,0:T(8,128)(2,1)S(1)}, bf16[384,768]{1,0:T(8,128)(2,1)S(1)}, u32[]{:S(2)}, u32[]{:S(2)}) collective-permute-start(bf16[384,768]{1,0:T(8,128)(2,1)S(1)} %bitcast.7), channel_id=1, source_target_pairs={{0,8},{8,0},{16,24},{24,16},{1,9},{9,1},{17,25},{25,17},{2,10},{10... | collective-permute-start | bytes 1769480 | tf_op jit(solution)/shard_map/ppermute | solution.py:431
  12.2 11.5 %collective-permute-done.20.refs_7_ = f32[8,256]{1,0:T(8,128)S(1)} collective-permute-done((f32[8,256]{1,0:T(8,128)S(1)}, f32[8,256]{1,0:T(8,128)S(1)}, u32[]{:S(2)}, u32[]{:S(2)}) %collective-permute-start.20) | collective-permute-done | bytes 8224 | tf_op jit(solution)/shard_map/ppermute | solution.py:428
  25.3 2.0 %collective-permute-done.21.refs_8_ = f32[8,256]{1,0:T(8,128)S(1)} collective-permute-done((f32[8,256]{1,0:T(8,128)S(1)}, f32[8,256]{1,0:T(8,128)S(1)}, u32[]{:S(2)}, u32[]{:S(2)}) %collective-permute-start.21) | collective-permute-done | bytes 8224 | tf_op jit(solution)/shard_map/ppermute | solution.py:428
  27.4 3.8 %collective-permute-start.11 = (bf16[128,1536]{1,0:T(8,128)(2,1)S(1)}, bf16[128,1536]{1,0:T(8,128)(2,1)S(1)}, u32[]{:S(2)}, u32[]{:S(2)}) collective-permute-start(bf16[128,1536]{1,0:T(8,128)(2,1)S(1)} %copy-done.2), channel_id=1, source_target_pairs={{0,6},{1,7},{2,0},{3,1},{4,2},{5,3},{6,4},{7,5},{8,14},{9,15},{10,... | collective-permute-start | bytes 1179656 | tf_op jit(solution)/shard_map/ppermute | solution.py:428
  32.8 8.4 %collective-permute-done.9.refs_2_ = bf16[128,1536]{1,0:T(8,128)(2,1)S(1)} collective-permute-done((bf16[128,1536]{1,0:T(8,128)(2,1)S(1)}, bf16[128,1536]{1,0:T(8,128)(2,1)S(1)}, u32[]{:S(2)}, u32[]{:S(2)}) %collective-permute-start.9) | collective-permute-done | bytes 393248 | tf_op jit(solution)/shard_map/ppermute | solution.py:428
  41.1 3.7 %collective-permute-done.11.refs_4_ = bf16[128,1536]{1,0:T(8,128)(2,1)S(1)} collective-permute-done((bf16[128,1536]{1,0:T(8,128)(2,1)S(1)}, bf16[128,1536]{1,0:T(8,128)(2,1)S(1)}, u32[]{:S(2)}, u32[]{:S(2)}) %collective-permute-start.11) | collective-permute-done | bytes 393248 | tf_op jit(solution)/shard_map/ppermute | solution.py:428
  48.1 8.2 %collective-permute-done.7.lower = bf16[128,1152]{1,0:T(8,128)(2,1)S(1)} collective-permute-done((bf16[128,1152]{1,0:T(8,128)(2,1)S(1)}, bf16[128,1152]{1,0:T(8,128)(2,1)S(1)}, u32[]{:S(2)}, u32[]{:S(2)}) %collective-permute-start.7) | collective-permute-done | bytes 294944 | tf_op jit(solution)/shard_map/ppermute | solution.py:428
  57.6 2.2 %collective-permute-start.15 = (bf16[384,768]{1,0:T(8,128)(2,1)S(1)}, bf16[384,768]{1,0:T(8,128)(2,1)S(1)}, u32[]{:S(2)}, u32[]{:S(2)}) collective-permute-start(bf16[384,768]{1,0:T(8,128)(2,1)S(1)} %bitcast.8), channel_id=1, source_target_pairs={{0,16},{8,24},{16,0},{24,8},{1,17},{9,25},{17,1},{25,9},{2,18},{10... | collective-permute-start | bytes 1769480 | tf_op jit(solution)/shard_map/ppermute | solution.py:431
  60.0 1.9 %collective-permute-start.25 = (bf16[768,384]{1,0:T(8,128)(2,1)}, bf16[768,384]{1,0:T(8,128)(2,1)S(1)}, u32[]{:S(2)}, u32[]{:S(2)}) collective-permute-start(bf16[768,384]{1,0:T(8,128)(2,1)} %bitcast.1.down), channel_id=1, source_target_pairs={{0,8},{8,0},{16,24},{24,16},{1,9},{9,1},{17,25},{25,17},{2,10},{10... | collective-permute-start | bytes 1769480 | tf_op jit(solution)/shard_map/ppermute | solution.py:431
  62.0 5.2 %collective-permute-done.12.lower = bf16[128,1536]{1,0:T(8,128)(2,1)S(1)} collective-permute-done((bf16[128,1536]{1,0:T(8,128)(2,1)S(1)}, bf16[128,1536]{1,0:T(8,128)(2,1)S(1)}, u32[]{:S(2)}, u32[]{:S(2)}) %collective-permute-start.12) | collective-permute-done | bytes 393248 | tf_op jit(solution)/shard_map/ppermute | solution.py:428
  68.9 1.8 %collective-permute-start.29 = (bf16[128,384]{1,0:T(8,128)(2,1)S(1)}, bf16[128,384]{1,0:T(8,128)(2,1)S(1)}, u32[]{:S(2)}, u32[]{:S(2)}) collective-permute-start(bf16[128,384]{1,0:T(8,128)(2,1)S(1)} %get-tuple-element.40.refs_0_), channel_id=1, source_target_pairs={{0,2},{1,3},{2,4},{3,5},{4,6},{5,7},{6,0},{7,1},{8,10},{9,11},{10,... | collective-permute-start | bytes 294920 | tf_op jit(solution)/shard_map/ppermute | solution.py:428
  70.7 3.3 %collective-permute-done.15.refs_4_.refs_11_ = bf16[384,768]{1,0:T(8,128)(2,1)S(1)} collective-permute-done((bf16[384,768]{1,0:T(8,128)(2,1)S(1)}, bf16[384,768]{1,0:T(8,128)(2,1)S(1)}, u32[]{:S(2)}, u32[]{:S(2)}) %collective-permute-start.15) | collective-permute-done | bytes 589856 | tf_op jit(solution)/shard_map/ppermute | solution.py:431
  74.0 2.1 %collective-permute-start.31 = (bf16[128,384]{1,0:T(8,128)(2,1)S(1)}, bf16[128,384]{1,0:T(8,128)(2,1)S(1)}, u32[]{:S(2)}, u32[]{:S(2)}) collective-permute-start(bf16[128,384]{1,0:T(8,128)(2,1)S(1)} %get-tuple-element.40.refs_0_), channel_id=1, source_target_pairs={{0,6},{1,7},{2,0},{3,1},{4,2},{5,3},{6,4},{7,5},{8,14},{9,15},{10,... | collective-permute-start | bytes 294920 | tf_op jit(solution)/shard_map/ppermute | solution.py:428
  76.1 7.7 %collective-permute-done.16.refs_5_.refs_12_ = bf16[384,768]{1,0:T(8,128)(2,1)S(1)} collective-permute-done((bf16[384,768]{1,0:T(8,128)(2,1)S(1)}, bf16[384,768]{1,0:T(8,128)(2,1)S(1)}, u32[]{:S(2)}, u32[]{:S(2)}) %collective-permute-start.16) | collective-permute-done | bytes 589856 | tf_op jit(solution)/shard_map/ppermute | solution.py:431
  83.8 3.5 %shard_map.82 = (bf16[768,1152]{1,0:T(8,128)(2,1)S(1)}, bf16[768,768]{1,0:T(8,128)(2,1)S(1)}, f32[768,768]{1,0:T(8,128)S(1)}, f32[768,384]{1,0:T(8,128)S(1)}, f3...) custom-call(bf16[128,1152]{1,0:T(8,128)(2,1)S(1)} %get-tuple-element.41.refs_0_, ...), custom_call_target="tpu_custom_call" | custom-call | flops 2264924160 | bytes 15360000 | tf_op jit(solution)/shard_map/pallas_call | solution.py:278
  87.9 5.5 %collective-permute-start = (bf16[128,384]{1,0:T(8,128)(2,1)S(1)}, bf16[128,384]{1,0:T(8,128)(2,1)S(1)}, u32[]{:S(2)}, u32[]{:S(2)}) collective-permute-start(bf16[128,384]{1,0:T(8,128)(2,1)S(1)} %get-tuple-element.40.refs_0_), channel_id=1, source_target_pairs={{0,4},{1,5},{2,6},{3,7},{4,0},{5,1},{6,2},{7,3},{8,12},{9,13},{10,... | collective-permute-start | bytes 294920 | tf_op jit(solution)/shard_map/ppermute | solution.py:428
  93.8 2.0 %shard_map.85.refs_9_ = f32[768,768]{1,0:T(8,128)S(1)} custom-call(bf16[768,1152]{1,0:T(8,128)(2,1)S(1)} %get-tuple-element.55.g, bf16[768,384]{1,0:T(8,128)(2,1)S(1)} %collective-permute-done.27.refs_0_.refs_10_, bf16[768,384]{1,0:T(8,128)(2,1)S(1)} %collective-permute-done.25.refs_1_.refs_8_, bf16[768,384]{1,0:T(8,128)(2,1)S(1)} %collective-permute-done.26.refs_2_.refs_9_), custom_call_target="tpu_custom_call" | custom-call | flops 1358954496 | bytes 5898240 | tf_op jit(solution)/shard_map/pallas_call | solution.py:278
  96.0 2.6 %collective-permute-done.refs_0_ = bf16[128,384]{1,0:T(8,128)(2,1)S(1)} collective-permute-done((bf16[128,384]{1,0:T(8,128)(2,1)S(1)}, bf16[128,384]{1,0:T(8,128)(2,1)S(1)}, u32[]{:S(2)}, u32[]{:S(2)}) %collective-permute-start) | collective-permute-done | bytes 98336 | tf_op jit(solution)/shard_map/ppermute | solution.py:428
  99.1 3.4 %shard_map.86 = (f32[384,768]{1,0:T(8,128)S(1)}, f32[384,768]{1,0:T(8,128)S(1)}, f32[384,768]{1,0:T(8,128)S(1)}, f32[384,768]{1,0:T(8,128)S(1)}, f32[768,384]{1,0:T(8,128)S(1)}) custom-call(bf16[128,384]{1,0:T(8,128)(2,1)S(1)} %get-tuple-element.40.refs_0_, bf16[128,384]{1,0:T(8,128)(2,1)S(1)} %collective-permute-done.28.refs_1_, ...), custom_call_target="tpu_custom_call" | custom-call | flops 2717908992 | bytes 15360000 | tf_op jit(solution)/shard_map/pallas_call | solution.py:278
  104.9 2.4 %shard_map.87 = (bf16[192,768]{1,0:T(8,128)(2,1)S(1)}, bf16[192,768]{1,0:T(8,128)(2,1)S(1)}, bf16[192,768]{1,0:T(8,128)(2,1)S(1)}, bf16[192,768]{1,0:T(8,128)(2,...) custom-call(bf16[128,384]{1,0:T(8,128)(2,1)S(1)} %collective-permute-, ...), custom_call_target="tpu_custom_call" | custom-call | flops 1358954496 | bytes 15736832 | tf_op jit(solution)/shard_map/pallas_call | solution.py:278
  107.3 1.8 %collective-permute-start.37 = (bf16[192,768]{1,0:T(8,128)(2,1)S(1)}, bf16[192,768]{1,0:T(8,128)(2,1)S(1)}, u32[]{:S(2)}, u32[]{:S(2)}) collective-permute-start(bf16[192,768]{1,0:T(8,128)(2,1)S(1)} %get-tuple-element.70), channel_id=1, source_target_pairs={{0,16},{8,24},{16,0},{24,8},{1,17},{9,25},{17,1},{25,9},{2,18},{10... | collective-permute-start | bytes 884744 | tf_op jit(solution)/shard_map/ppermute | solution.py:431
  113.1 4.1 %collective-permute-done.37 = bf16[192,768]{1,0:T(8,128)(2,1)S(1)} collective-permute-done((bf16[192,768]{1,0:T(8,128)(2,1)S(1)}, bf16[192,768]{1,0:T(8,128)(2,1)S(1)}, u32[]{:S(2)}, u32[]{:S(2)}) %collective-permute-start.37) | collective-permute-done | bytes 294944 | tf_op jit(solution)/shard_map/ppermute | solution.py:431
  117.2 1.8 %collective-permute-start.40 = (bf16[352,384]{1,0:T(8,128)(2,1)S(1)}, bf16[352,384]{1,0:T(8,128)(2,1)S(1)}, u32[]{:S(2)}, u32[]{:S(2)}) collective-permute-start(bf16[352,384]{1,0:T(8,128)(2,1)S(1)} %get-tuple-element.73), channel_id=1, source_target_pairs={{0,16},{8,24},{16,0},{24,8},{1,17},{9,25},{17,1},{25,9},{2,18},{10... | collective-permute-start | bytes 811016 | tf_op jit(solution)/shard_map/ppermute | solution.py:431
  120.7 5.2 %collective-permute-done.41 = bf16[416,384]{1,0:T(8,128)(2,1)S(1)} collective-permute-done((bf16[416,384]{1,0:T(8,128)(2,1)S(1)}, bf16[416,384]{1,0:T(8,128)(2,1)S(1)}, u32[]{:S(2)}, u32[]{:S(2)}) %collective-permute-start.41) | collective-permute-done | bytes 319520 | tf_op jit(solution)/shard_map/ppermute | solution.py:431
  126.2 1.8 %collective-permute-start.38 = (bf16[192,768]{1,0:T(8,128)(2,1)S(1)}, bf16[192,768]{1,0:T(8,128)(2,1)S(1)}, u32[]{:S(2)}, u32[]{:S(2)}) collective-permute-start(bf16[192,768]{1,0:T(8,128)(2,1)S(1)} %add_convert_fusion.1), channel_id=1, source_target_pairs={{0,8},{8,0},{16,24},{24,16},{1,9},{9,1},{17,25},{25,17},{2,10},{10... | collective-permute-start | bytes 884744 | tf_op jit(solution)/shard_map/ppermute | solution.py:431
  128.8 1.8 %collective-permute-start.36 = (bf16[192,768]{1,0:T(8,128)(2,1)S(1)}, bf16[192,768]{1,0:T(8,128)(2,1)S(1)}, u32[]{:S(2)}, u32[]{:S(2)}) collective-permute-start(bf16[192,768]{1,0:T(8,128)(2,1)S(1)} %add_convert_fusion.2), channel_id=1, source_target_pairs={{0,16},{8,24},{16,0},{24,8},{1,17},{9,25},{17,1},{25,9},{2,18},{10... | collective-permute-start | bytes 884744 | tf_op jit(solution)/shard_map/ppermute | solution.py:431
  130.6 8.4 %collective-permute-done.33.near_a = bf16[192,768]{1,0:T(8,128)(2,1)S(1)} collective-permute-done((bf16[192,768]{1,0:T(8,128)(2,1)S(1)}, bf16[192,768]{1,0:T(8,128)(2,1)S(1)}, u32[]{:S(2)}, u32[]{:S(2)}) %collective-permute-start.33) | collective-permute-done | bytes 294944 | tf_op jit(solution)/shard_map/ppermute | solution.py:431
  139.4 1.8 %collective-permute-start.44 = (bf16[352,384]{1,0:T(8,128)(2,1)S(1)}, bf16[352,384]{1,0:T(8,128)(2,1)S(1)}, u32[]{:S(2)}, u32[]{:S(2)}) collective-permute-start(bf16[352,384]{1,0:T(8,128)(2,1)S(1)} %add_convert_fusion.3), channel_id=1, source_target_pairs={{0,8},{8,0},{16,24},{24,16},{1,9},{9,1},{17,25},{25,17},{2,10},{10... | collective-permute-start | bytes 811016 | tf_op jit(solution)/shard_map/ppermute | solution.py:431
  141.4 3.9 %collective-permute-done.38.far_b = bf16[192,768]{1,0:T(8,128)(2,1)S(1)} collective-permute-done((bf16[192,768]{1,0:T(8,128)(2,1)S(1)}, bf16[192,768]{1,0:T(8,128)(2,1)S(1)}, u32[]{:S(2)}, u32[]{:S(2)}) %collective-permute-start.38) | collective-permute-done | bytes 294944 | tf_op jit(solution)/shard_map/ppermute | solution.py:431
  146.2 3.7 %collective-permute-done.44.far_b = bf16[352,384]{1,0:T(8,128)(2,1)S(1)} collective-permute-done((bf16[352,384]{1,0:T(8,128)(2,1)S(1)}, bf16[352,384]{1,0:T(8,128)(2,1)S(1)}, u32[]{:S(2)}, u32[]{:S(2)}) %collective-permute-start.44) | collective-permute-done | bytes 270368 | tf_op jit(solution)/shard_map/ppermute | solution.py:431
  (90 shorter events, 27.6 us)
Async XLA Ops:
  4.9 22.4 %collective-permute-start.4 = (bf16[128,1152]{1,0:T(8,128)(2,1)S(1)}, bf16[128,1152]{1,0:T(8,128)(2,1)S(1)}, u32[]{:S(2)}, u32[]{:S(2)}) collective-permute-start(bf16[128,1152]{1,0:T(8,128)(2,1)S(1)} %get-tuple-element.41.refs_0_), channel_id=1, source_target_pairs={{0,2},{1,3},{2,4},{3,5},{4,6},{5,7},{6,0},{7,1},{8,10},{9,11},{10,... | collective-permute-start | bytes 884744 | tf_op jit(solution)/shard_map/ppermute | solution.py:428
  8.0 23.1 %collective-permute-start.6 = (bf16[128,1152]{1,0:T(8,128)(2,1)S(1)}, bf16[128,1152]{1,0:T(8,128)(2,1)S(1)}, u32[]{:S(2)}, u32[]{:S(2)}) collective-permute-start(bf16[128,1152]{1,0:T(8,128)(2,1)S(1)} %get-tuple-element.41.refs_0_), channel_id=1, source_target_pairs={{0,6},{1,7},{2,0},{3,1},{4,2},{5,3},{6,4},{7,5},{8,14},{9,15},{10,... | collective-permute-start | bytes 884744 | tf_op jit(solution)/shard_map/ppermute | solution.py:428
  10.2 36.6 %collective-permute-start.14 = (bf16[384,768]{1,0:T(8,128)(2,1)S(1)}, bf16[384,768]{1,0:T(8,128)(2,1)S(1)}, u32[]{:S(2)}, u32[]{:S(2)}) collective-permute-start(bf16[384,768]{1,0:T(8,128)(2,1)S(1)} %bitcast.7), channel_id=1, source_target_pairs={{0,8},{8,0},{16,24},{24,16},{1,9},{9,1},{17,25},{25,17},{2,10},{10... | collective-permute-start | bytes 1769480 | tf_op jit(solution)/shard_map/ppermute | solution.py:431
  12.0 11.7 %collective-permute-start.20 = (f32[8,256]{1,0:T(8,128)S(1)}, f32[8,256]{1,0:T(8,128)S(1)}, u32[]{:S(2)}, u32[]{:S(2)}) collective-permute-start(f32[8,256]{1,0:T(8,128)S(1)} %pad_maximum_fusion.refs_6_), channel_id=1, source_target_pairs={{0,2},{1,3},{2,4},{3,5},{4,6},{5,7},{6,0},{7,1},{8,10},{9,11},{10,... | collective-permute-start | bytes 24584 | tf_op jit(solution)/shard_map/ppermute | solution.py:428
  12.0 19.2 %collective-permute-start.17 = (bf16[128,1152]{1,0:T(8,128)(2,1)S(1)}, bf16[128,1152]{1,0:T(8,128)(2,1)S(1)}, u32[]{:S(2)}, u32[]{:S(2)}) collective-permute-start(bf16[128,1152]{1,0:T(8,128)(2,1)S(1)} %get-tuple-element.41.refs_0_), channel_id=1, source_target_pairs={{0,1},{1,0},{2,3},{3,2},{4,5},{5,4},{6,7},{7,6},{8,9},{9,8},{10,11... | collective-permute-start | bytes 884744 | tf_op jit(solution)/shard_map/ppermute | solution.py:428
  27.4 13.8 %collective-permute-start.9 = (bf16[128,1536]{1,0:T(8,128)(2,1)S(1)}, bf16[128,1536]{1,0:T(8,128)(2,1)S(1)}, u32[]{:S(2)}, u32[]{:S(2)}) collective-permute-start(bf16[128,1536]{1,0:T(8,128)(2,1)S(1)} %copy-done.2), channel_id=1, source_target_pairs={{0,2},{1,3},{2,4},{3,5},{4,6},{5,7},{6,0},{7,1},{8,10},{9,11},{10,... | collective-permute-start | bytes 1179656 | tf_op jit(solution)/shard_map/ppermute | solution.py:428
  27.4 17.5 %collective-permute-start.11 = (bf16[128,1536]{1,0:T(8,128)(2,1)S(1)}, bf16[128,1536]{1,0:T(8,128)(2,1)S(1)}, u32[]{:S(2)}, u32[]{:S(2)}) collective-permute-start(bf16[128,1536]{1,0:T(8,128)(2,1)S(1)} %copy-done.2), channel_id=1, source_target_pairs={{0,6},{1,7},{2,0},{3,1},{4,2},{5,3},{6,4},{7,5},{8,14},{9,15},{10,... | collective-permute-start | bytes 1179656 | tf_op jit(solution)/shard_map/ppermute | solution.py:428
  31.2 14.3 %collective-permute-start.22 = (bf16[128,1536]{1,0:T(8,128)(2,1)S(1)}, bf16[128,1536]{1,0:T(8,128)(2,1)S(1)}, u32[]{:S(2)}, u32[]{:S(2)}) collective-permute-start(bf16[128,1536]{1,0:T(8,128)(2,1)S(1)} %copy-done.2), channel_id=1, source_target_pairs={{0,1},{1,0},{2,3},{3,2},{4,5},{5,4},{6,7},{7,6},{8,9},{9,8},{10,11... | collective-permute-start | bytes 1179656 | tf_op jit(solution)/shard_map/ppermute | solution.py:428
  31.2 26.4 %collective-permute-start.26 = (bf16[768,384]{1,0:T(8,128)(2,1)}, bf16[768,384]{1,0:T(8,128)(2,1)S(1)}, u32[]{:S(2)}, u32[]{:S(2)}) collective-permute-start(bf16[768,384]{1,0:T(8,128)(2,1)} %bitcast.1.down), channel_id=1, source_target_pairs={{0,16},{8,24},{16,0},{24,8},{1,17},{9,25},{17,1},{25,9},{2,18},{10... | collective-permute-start | bytes 1769480 | tf_op jit(solution)/shard_map/ppermute | solution.py:431
  45.5 10.8 %collective-permute-start.7 = (bf16[128,1152]{1,0:T(8,128)(2,1)S(1)}, bf16[128,1152]{1,0:T(8,128)(2,1)S(1)}, u32[]{:S(2)}, u32[]{:S(2)}) collective-permute-start(bf16[128,1152]{1,0:T(8,128)(2,1)S(1)} %collective-permute-done.6.refs_4_), channel_id=1, source_target_pairs={{2,0},{3,1},{4,2},{5,3},{10,8},{11,9},{12,10},{13,11},{18,16},{19,... | collective-permute-start | bytes 884744 | tf_op jit(solution)/shard_map/ppermute | solution.py:428
  46.8 13.0 %collective-permute-start.23 = (bf16[128,1536]{1,0:T(8,128)(2,1)S(1)}, bf16[128,1536]{1,0:T(8,128)(2,1)S(1)}, u32[]{:S(2)}, u32[]{:S(2)}) collective-permute-start(bf16[128,1536]{1,0:T(8,128)(2,1)S(1)} %collective-permute-done.9.refs_2_), channel_id=1, source_target_pairs={{0,1},{1,0},{2,3},{3,2},{4,5},{5,4},{6,7},{7,6},{8,9},{9,8},{10,11... | collective-permute-start | bytes 1179656 | tf_op jit(solution)/shard_map/ppermute | solution.py:428
  46.9 13.0 %collective-permute-start.24 = (bf16[128,1536]{1,0:T(8,128)(2,1)S(1)}, bf16[128,1536]{1,0:T(8,128)(2,1)S(1)}, u32[]{:S(2)}, u32[]{:S(2)}) collective-permute-start(bf16[128,1536]{1,0:T(8,128)(2,1)S(1)} %collective-permute-done.11.refs_4_), channel_id=1, source_target_pairs={{0,1},{1,0},{2,3},{3,2},{4,5},{5,4},{6,7},{7,6},{8,9},{9,8},{10,11... | collective-permute-start | bytes 1179656 | tf_op jit(solution)/shard_map/ppermute | solution.py:428
  47.4 14.5 %collective-permute-start.10 = (bf16[128,1536]{1,0:T(8,128)(2,1)S(1)}, bf16[128,1536]{1,0:T(8,128)(2,1)S(1)}, u32[]{:S(2)}, u32[]{:S(2)}) collective-permute-start(bf16[128,1536]{1,0:T(8,128)(2,1)S(1)} %collective-permute-done.9.refs_2_), channel_id=1, source_target_pairs={{2,4},{3,5},{4,6},{5,7},{10,12},{11,13},{12,14},{13,15},{18,20},{1... | collective-permute-start | bytes 1179656 | tf_op jit(solution)/shard_map/ppermute | solution.py:428
  56.3 10.9 %collective-permute-start.12 = (bf16[128,1536]{1,0:T(8,128)(2,1)S(1)}, bf16[128,1536]{1,0:T(8,128)(2,1)S(1)}, u32[]{:S(2)}, u32[]{:S(2)}) collective-permute-start(bf16[128,1536]{1,0:T(8,128)(2,1)S(1)} %collective-permute-done.11.refs_4_), channel_id=1, source_target_pairs={{2,0},{3,1},{4,2},{5,3},{10,8},{11,9},{12,10},{13,11},{18,16},{19,... | collective-permute-start | bytes 1179656 | tf_op jit(solution)/shard_map/ppermute | solution.py:428
  57.6 16.4 %collective-permute-start.15 = (bf16[384,768]{1,0:T(8,128)(2,1)S(1)}, bf16[384,768]{1,0:T(8,128)(2,1)S(1)}, u32[]{:S(2)}, u32[]{:S(2)}) collective-permute-start(bf16[384,768]{1,0:T(8,128)(2,1)S(1)} %bitcast.8), channel_id=1, source_target_pairs={{0,16},{8,24},{16,0},{24,8},{1,17},{9,25},{17,1},{25,9},{2,18},{10... | collective-permute-start | bytes 1769480 | tf_op jit(solution)/shard_map/ppermute | solution.py:431
  59.9 23.9 %collective-permute-start.16 = (bf16[384,768]{1,0:T(8,128)(2,1)S(1)}, bf16[384,768]{1,0:T(8,128)(2,1)S(1)}, u32[]{:S(2)}, u32[]{:S(2)}) collective-permute-start(bf16[384,768]{1,0:T(8,128)(2,1)S(1)} %collective-permute-done.14.refs_3_.refs_7_), channel_id=1, source_target_pairs={{0,16},{8,24},{16,0},{24,8},{1,17},{9,25},{17,1},{25,9},{2,18},{10... | collective-permute-start | bytes 1769480 | tf_op jit(solution)/shard_map/ppermute | solution.py:431
  60.0 33.4 %collective-permute-start.25 = (bf16[768,384]{1,0:T(8,128)(2,1)}, bf16[768,384]{1,0:T(8,128)(2,1)S(1)}, u32[]{:S(2)}, u32[]{:S(2)}) collective-permute-start(bf16[768,384]{1,0:T(8,128)(2,1)} %bitcast.1.down), channel_id=1, source_target_pairs={{0,8},{8,0},{16,24},{24,16},{1,9},{9,1},{17,25},{25,17},{2,10},{10... | collective-permute-start | bytes 1769480 | tf_op jit(solution)/shard_map/ppermute | solution.py:431
  61.9 31.5 %collective-permute-start.27 = (bf16[768,384]{1,0:T(8,128)(2,1)S(1)}, bf16[768,384]{1,0:T(8,128)(2,1)S(1)}, u32[]{:S(2)}, u32[]{:S(2)}) collective-permute-start(bf16[768,384]{1,0:T(8,128)(2,1)S(1)} %collective-permute-done.26.refs_2_.refs_9_), channel_id=1, source_target_pairs={{0,8},{8,0},{16,24},{24,16},{1,9},{9,1},{17,25},{25,17},{2,10},{10... | collective-permute-start | bytes 1769480 | tf_op jit(solution)/shard_map/ppermute | solution.py:431
  68.9 18.4 %collective-permute-start.29 = (bf16[128,384]{1,0:T(8,128)(2,1)S(1)}, bf16[128,384]{1,0:T(8,128)(2,1)S(1)}, u32[]{:S(2)}, u32[]{:S(2)}) collective-permute-start(bf16[128,384]{1,0:T(8,128)(2,1)S(1)} %get-tuple-element.40.refs_0_), channel_id=1, source_target_pairs={{0,2},{1,3},{2,4},{3,5},{4,6},{5,7},{6,0},{7,1},{8,10},{9,11},{10,... | collective-permute-start | bytes 294920 | tf_op jit(solution)/shard_map/ppermute | solution.py:428
  74.0 13.8 %collective-permute-start.31 = (bf16[128,384]{1,0:T(8,128)(2,1)S(1)}, bf16[128,384]{1,0:T(8,128)(2,1)S(1)}, u32[]{:S(2)}, u32[]{:S(2)}) collective-permute-start(bf16[128,384]{1,0:T(8,128)(2,1)S(1)} %get-tuple-element.40.refs_0_), channel_id=1, source_target_pairs={{0,6},{1,7},{2,0},{3,1},{4,2},{5,3},{6,4},{7,5},{8,14},{9,15},{10,... | collective-permute-start | bytes 294920 | tf_op jit(solution)/shard_map/ppermute | solution.py:428
  83.8 18.7 %collective-permute-start.13 = (bf16[128,1536]{1,0:T(8,128)(2,1)S(1)}, bf16[128,1536]{1,0:T(8,128)(2,1)S(1)}, u32[]{:S(2)}, u32[]{:S(2)}) collective-permute-start(bf16[128,1536]{1,0:T(8,128)(2,1)S(1)} %shard_map.79.refs_0_), channel_id=1, source_target_pairs={{0,1},{1,0},{2,3},{3,2},{4,5},{5,4},{6,7},{7,6},{8,9},{9,8},{10,11... | collective-permute-start | bytes 1179656 | tf_op jit(solution)/shard_map/ppermute | solution.py:428
  87.9 10.7 %collective-permute-start = (bf16[128,384]{1,0:T(8,128)(2,1)S(1)}, bf16[128,384]{1,0:T(8,128)(2,1)S(1)}, u32[]{:S(2)}, u32[]{:S(2)}) collective-permute-start(bf16[128,384]{1,0:T(8,128)(2,1)S(1)} %get-tuple-element.40.refs_0_), channel_id=1, source_target_pairs={{0,4},{1,5},{2,6},{3,7},{4,0},{5,1},{6,2},{7,3},{8,12},{9,13},{10,... | collective-permute-start | bytes 294920 | tf_op jit(solution)/shard_map/ppermute | solution.py:428
  110.6 15.6 %collective-permute-start.43 = (bf16[352,384]{1,0:T(8,128)(2,1)S(1)}, bf16[352,384]{1,0:T(8,128)(2,1)S(1)}, u32[]{:S(2)}, u32[]{:S(2)}) collective-permute-start(bf16[352,384]{1,0:T(8,128)(2,1)S(1)} %get-tuple-element.77), channel_id=1, source_target_pairs={{0,16},{8,24},{16,0},{24,8},{1,17},{9,25},{17,1},{25,9},{2,18},{10... | collective-permute-start | bytes 811016 | tf_op jit(solution)/shard_map/ppermute | solution.py:431
  111.1 14.7 %collective-permute-start.41 = (bf16[416,384]{1,0:T(8,128)(2,1)S(1)}, bf16[416,384]{1,0:T(8,128)(2,1)S(1)}, u32[]{:S(2)}, u32[]{:S(2)}) collective-permute-start(bf16[416,384]{1,0:T(8,128)(2,1)S(1)} %get-tuple-element.75), channel_id=1, source_target_pairs={{0,8},{8,0},{16,24},{24,16},{1,9},{9,1},{17,25},{25,17},{2,10},{10... | collective-permute-start | bytes 958472 | tf_op jit(solution)/shard_map/ppermute | solution.py:431
  111.4 29.9 %collective-permute-start.39 = (bf16[416,384]{1,0:T(8,128)(2,1)S(1)}, bf16[416,384]{1,0:T(8,128)(2,1)S(1)}, u32[]{:S(2)}, u32[]{:S(2)}) collective-permute-start(bf16[416,384]{1,0:T(8,128)(2,1)S(1)} %get-tuple-element.72), channel_id=1, source_target_pairs={{0,8},{8,0},{16,24},{24,16},{1,9},{9,1},{17,25},{25,17},{2,10},{10... | collective-permute-start | bytes 958472 | tf_op jit(solution)/shard_map/ppermute | solution.py:431
  117.2 11.6 %collective-permute-start.40 = (bf16[352,384]{1,0:T(8,128)(2,1)S(1)}, bf16[352,384]{1,0:T(8,128)(2,1)S(1)}, u32[]{:S(2)}, u32[]{:S(2)}) collective-permute-start(bf16[352,384]{1,0:T(8,128)(2,1)S(1)} %get-tuple-element.73), channel_id=1, source_target_pairs={{0,16},{8,24},{16,0},{24,8},{1,17},{9,25},{17,1},{25,9},{2,18},{10... | collective-permute-start | bytes 811016 | tf_op jit(solution)/shard_map/ppermute | solution.py:431
  119.1 19.9 %collective-permute-start.33 = (bf16[192,768]{1,0:T(8,128)(2,1)S(1)}, bf16[192,768]{1,0:T(8,128)(2,1)S(1)}, u32[]{:S(2)}, u32[]{:S(2)}) collective-permute-start(bf16[192,768]{1,0:T(8,128)(2,1)S(1)} %get-tuple-element.65), channel_id=1, source_target_pairs={{0,8},{8,0},{16,24},{24,16},{1,9},{9,1},{17,25},{25,17},{2,10},{10... | collective-permute-start | bytes 884744 | tf_op jit(solution)/shard_map/ppermute | solution.py:431
  125.8 13.5 %collective-permute-start.34 = (bf16[192,768]{1,0:T(8,128)(2,1)S(1)}, bf16[192,768]{1,0:T(8,128)(2,1)S(1)}, u32[]{:S(2)}, u32[]{:S(2)}) collective-permute-start(bf16[192,768]{1,0:T(8,128)(2,1)S(1)} %get-tuple-element.66), channel_id=1, source_target_pairs={{0,16},{8,24},{16,0},{24,8},{1,17},{9,25},{17,1},{25,9},{2,18},{10... | collective-permute-start | bytes 884744 | tf_op jit(solution)/shard_map/ppermute | solution.py:431
  126.2 19.1 %collective-permute-start.38 = (bf16[192,768]{1,0:T(8,128)(2,1)S(1)}, bf16[192,768]{1,0:T(8,128)(2,1)S(1)}, u32[]{:S(2)}, u32[]{:S(2)}) collective-permute-start(bf16[192,768]{1,0:T(8,128)(2,1)S(1)} %add_convert_fusion.1), channel_id=1, source_target_pairs={{0,8},{8,0},{16,24},{24,16},{1,9},{9,1},{17,25},{25,17},{2,10},{10... | collective-permute-start | bytes 884744 | tf_op jit(solution)/shard_map/ppermute | solution.py:431
  128.8 16.5 %collective-permute-start.36 = (bf16[192,768]{1,0:T(8,128)(2,1)S(1)}, bf16[192,768]{1,0:T(8,128)(2,1)S(1)}, u32[]{:S(2)}, u32[]{:S(2)}) collective-permute-start(bf16[192,768]{1,0:T(8,128)(2,1)S(1)} %add_convert_fusion.2), channel_id=1, source_target_pairs={{0,16},{8,24},{16,0},{24,8},{1,17},{9,25},{17,1},{25,9},{2,18},{10... | collective-permute-start | bytes 884744 | tf_op jit(solution)/shard_map/ppermute | solution.py:431
  139.0 10.9 %collective-permute-start.42 = (bf16[416,384]{1,0:T(8,128)(2,1)S(1)}, bf16[416,384]{1,0:T(8,128)(2,1)S(1)}, u32[]{:S(2)}, u32[]{:S(2)}) collective-permute-start(bf16[416,384]{1,0:T(8,128)(2,1)S(1)} %add_convert_fusion), channel_id=1, source_target_pairs={{0,16},{8,24},{16,0},{24,8},{1,17},{9,25},{17,1},{25,9},{2,18},{10... | collective-permute-start | bytes 958472 | tf_op jit(solution)/shard_map/ppermute | solution.py:431
  139.4 10.5 %collective-permute-start.44 = (bf16[352,384]{1,0:T(8,128)(2,1)S(1)}, bf16[352,384]{1,0:T(8,128)(2,1)S(1)}, u32[]{:S(2)}, u32[]{:S(2)}) collective-permute-start(bf16[352,384]{1,0:T(8,128)(2,1)S(1)} %add_convert_fusion.3), channel_id=1, source_target_pairs={{0,8},{8,0},{16,24},{24,16},{1,9},{9,1},{17,25},{25,17},{2,10},{10... | collective-permute-start | bytes 811016 | tf_op jit(solution)/shard_map/ppermute | solution.py:431
  (18 other events, 93.2 us)
